TPU v7x, 32 devices: a whole 2x2x4 slice. The times are simulated.
32 devices in a mesh: seq: 16 (over z, y, core), row: 2 (over x).
Axes of the slice: x: 2, y: 2, z: 4, core: 2. Of those that a mesh axis runs over, the one named last changes fastest.
Arguments:
- latents: bfloat16 [192, 8, 32, 320], P('seq', 'row'), may hold values from -6 to 6
- clip_lengths: int32 [4], replicated, may hold values from 1 to 96, 192 in all
- timesteps: int32 [4], replicated, may hold values from 0 to 999
- spatial_weight: bfloat16 [3, 3, 320, 320], replicated, may hold values from -0.109375 to 0.109375
- time_weight: bfloat16 [320, 320], replicated, may hold values from -0.3125 to 0.3125
- query_weight: bfloat16 [320, 320], replicated, may hold values from -3 to 3
- key_weight: bfloat16 [320, 320], replicated, may hold values from -3 to 3
- value_weight: bfloat16 [320, 320], replicated, may hold values from -0.3125 to 0.3125
- out_weight: bfloat16 [320, 320], replicated, may hold values from -0.3125 to 0.3125
- temporal_weight: bfloat16 [3, 320, 320], replicated, may hold values from -0.1875 to 0.1875
- cotangent: bfloat16 [192, 8, 32, 320], P('seq', 'row'), may hold values from -0.02734375 to 0.02734375
Outputs:
- block_out: bfloat16 [192, 8, 32, 320], P('seq', 'row')
- temporal_grad: float32 [3, 320, 320], replicated
Inputs may be any that keep to these rules, and one draw needn't show every extreme that they name: `clip_lengths`: clip frame counts in packing order; they sum to 192 and the largest is exactly 96.
All inputs are finite; a program needn't handle non-finite values.
Results may differ from a plain program's by a relative error of at most 0.011.
Values may be sent and summed in bfloat16 or wider, within the bound.
No kernel may reach another device: no remote copies, remote signals or barrier semaphores. Data moves between devices by JAX's collectives and lax.ppermute only.
A program may use at most 128 MiB of HBM per device.

v0:
```python
import math

import jax
import jax.numpy as jnp
from jax import lax
from jax.experimental import pallas as pl
from jax.experimental.pallas import tpu as pltpu
from jax.sharding import Mesh
from jax.sharding import PartitionSpec as P

HEADS = 8
CLIPS = 4
SEQ = ("z", "y", "c")
PLANE = ("y", "x")
BF16 = jnp.bfloat16
F32 = jnp.float32
VMEM = pltpu.VMEM
SMEM = pltpu.SMEM
PIX = 8


def time_table(timesteps, time_weight):
    half_width = time_weight.shape[0] // 2
    frequency = jnp.exp(-math.log(10000.0) * jnp.arange(half_width, dtype=F32) / half_width)
    angles = timesteps.astype(F32)[:, None] * frequency[None, :]
    embedded = jnp.concatenate([jnp.cos(angles), jnp.sin(angles)], axis=1)
    return jnp.dot(embedded, time_weight.astype(F32), precision=lax.Precision.HIGHEST)


def call(kernel, out_shape, in_spaces, scratch=(), flops=0, bytes_accessed=0, grid=None, **kw):
    return pl.pallas_call(
        kernel,
        out_shape=out_shape,
        in_specs=[pl.BlockSpec(memory_space=s) for s in in_spaces],
        out_specs=jax.tree.map(lambda _: pl.BlockSpec(memory_space=VMEM), out_shape),
        scratch_shapes=scratch,
        cost_estimate=pl.CostEstimate(
            flops=flops, bytes_accessed=bytes_accessed, transcendentals=0
        ),
        compiler_params=pltpu.CompilerParams(vmem_limit_bytes=56 * 2**20),
        **kw,
    )


def pack_pair(ref, index, first, second):
    wide = first.shape[-1] // 128 * 128
    ref[index + (slice(None), slice(0, wide))] = first[:, :wide]
    ref[index + (slice(None), slice(wide, 2 * wide))] = second[:, :wide]
    ref[index + (slice(None), slice(2 * wide, 2 * first.shape[-1]))] = jnp.concatenate(
        [first[:, wide:], second[:, wide:]], axis=-1
    )


def clip_ids(frame, len_ref):
    bound = jnp.int32(0)
    ids = jnp.zeros(frame.shape, jnp.int32)
    for k in range(CLIPS):
        bound = bound + len_ref[k]
        ids = ids + jnp.where(frame >= bound, 1, 0)
    return ids


def take(row, g, real):
    if real == PIX:
        return row[g * PIX : (g + 1) * PIX]
    piece = row[g * real : (g + 1) * real].astype(F32)
    return jnp.concatenate([piece, jnp.zeros((PIX - real, row.shape[-1]), F32)], 0).astype(BF16)


def pack_kernel(x_ref, o_ref):
    frames, rows, across, ch = x_ref.shape
    half = frames // 2
    groups = o_ref.shape[0] // rows
    real = across // groups

    def step(t, _):
        for i in range(rows):
            first, second = x_ref[t, i], x_ref[t + half, i]
            for g in range(groups):
                pack_pair(
                    o_ref, (i * groups + g, t), take(first, g, real), take(second, g, real)
                )
        return 0

    lax.fori_loop(0, half, step, 0)


def unpack_kernel(x_ref, o_ref):
    frames, rows, across, ch = o_ref.shape
    half = frames // 2
    groups = x_ref.shape[0] // rows
    real = across // groups
    wide = ch // 128 * 128

    def join(blocks, low, high):
        if real == PIX:
            return jnp.concatenate([b[:, low:high] for b in blocks], 0)
        return jnp.concatenate([b[:real, low:high].astype(F32) for b in blocks], 0).astype(BF16)

    def step(t, _):
        for i in range(rows):
            blocks = [x_ref[i * groups + g, t] for g in range(groups)]
            o_ref[t, i, :, 0:wide] = join(blocks, 0, wide)
            o_ref[t, i, :, wide:ch] = join(blocks, 2 * wide, wide + ch)
            o_ref[t + half, i, :, 0:wide] = join(blocks, wide, 2 * wide)
            o_ref[t + half, i, :, wide:ch] = join(blocks, wide + ch, 2 * ch)
        return 0

    lax.fori_loop(0, half, step, 0)


def conv_kernel(flag_ref, id_ref, lat_ref, top_ref, bot_ref, w_ref, table_ref, o_ref):
    frames, rows, across, ch = lat_ref.shape
    half = frames // 2
    groups = o_ref.shape[0] // rows
    real = across // groups

    def step(t, _):
        kept = []
        for base in (0, half):
            top = top_ref[t + base]
            bot = bot_ref[t + base]
            top = jnp.where(flag_ref[0] > 0, top, jnp.zeros_like(top))
            bot = jnp.where(flag_ref[1] > 0, bot, jnp.zeros_like(bot))
            lat = [lat_ref[t + base, i] for i in range(rows)]
            kept.append([top] + lat + [bot])
        n_rows = 2 * rows * across
        sums = []
        windows = [
            jnp.concatenate([r for s in kept for r in s[a : a + rows]], axis=0) for a in range(3)
        ]
        for b in range(3):
            acc = jnp.zeros((n_rows, ch), F32)
            for a in range(3):
                acc = acc + jnp.dot(windows[a], w_ref[a, b], preferred_element_type=F32)
            sums.append(acc)
        col = lax.broadcasted_iota(jnp.int32, (n_rows, ch), 0) & (across - 1)
        left = jnp.where(col == 0, 0.0, pltpu.roll(sums[0], 1, 0))
        right = jnp.where(col == across - 1, 0.0, pltpu.roll(sums[2], n_rows - 1, 0))
        spatial = sums[1] + left + right
        per = rows * across
        outs = []
        for k, base in enumerate((0, half)):
            emb = table_ref[pl.ds(id_ref[t + base], 1), :]
            v = spatial[k * per : (k + 1) * per] + emb
            silu = 0.5 * v * (1.0 + jnp.tanh(0.5 * v))
            res = windows[1][k * per : (k + 1) * per].astype(F32)
            outs.append((res + silu).astype(BF16))
        for d in range(rows * groups):
            pack_pair(o_ref, (d, t), take(outs[0], d, real), take(outs[1], d, real))
        return 0

    lax.fori_loop(0, half, step, 0)


def unpack_rows(blk, ch):
    wide = ch // 128 * 128
    blk = blk.astype(F32).reshape(-1, 2 * ch)
    first = (blk[:, :wide], blk[:, 2 * wide : wide + ch])
    second = (blk[:, wide : 2 * wide], blk[:, wide + ch : 2 * ch])
    return first, second


def attention_kernel(
    len_ref, act_ref, wq_ref, wk_ref, wv_ref, wo_ref, tw_ref, o_ref, m_ref, x32, n32, a32, m32, wqkv
):
    shards, half, _, ch2 = act_ref.shape
    ch = ch2 // 2
    wide = ch // 128 * 128
    frames = shards * half * 2
    rows = frames * PIX
    per = half * PIX
    head = ch // HEADS
    pad = n32.shape[0] * 128
    wqkv[...] = jnp.zeros_like(wqkv)
    for j, ref in enumerate((wq_ref, wk_ref, wv_ref)):
        wqkv[0:ch, j * pad : j * pad + ch] = ref[...]

    def load(s, _):
        first, second = unpack_rows(act_ref[s], ch)
        for k, part in enumerate((first, second)):
            at = pl.ds(pl.multiple_of((2 * s + k) * per, 8), per)
            x32[at, 0:wide] = part[0]
            x32[at, wide:ch] = part[1]
        at = pl.ds(pl.multiple_of(2 * s * per, 8), 2 * per)
        v = x32[at, :]
        center = v - jnp.mean(v, axis=-1, keepdims=True)
        spread = jnp.mean(center * center, axis=-1, keepdims=True)
        n = (center * lax.rsqrt(spread + 1e-05)).astype(BF16).astype(F32)
        n = jnp.concatenate([n, jnp.zeros((2 * per, pad - ch), F32)], axis=-1)
        for c in range(pad // 128):
            n32[c, at, :] = n[:, c * 128 : (c + 1) * 128]
        return 0

    lax.fori_loop(0, shards, load, 0)

    f_row = lax.broadcasted_iota(jnp.int32, (frames, frames), 0)
    f_col = lax.broadcasted_iota(jnp.int32, (frames, frames), 1)
    same = clip_ids(f_row, len_ref) == clip_ids(f_col, len_ref)
    scale = head ** (-0.5)
    lane = lax.broadcasted_iota(jnp.int32, (1, pad), 1)

    def pixel(p, _):
        at = pl.ds(p, frames, stride=PIX)
        n = jnp.concatenate([n32[c, at, :] for c in range(pad // 128)], axis=-1).astype(BF16)
        qkv = jnp.dot(n, wqkv[...], preferred_element_type=F32).astype(BF16)
        q, k, v = (qkv[:, j * pad : (j + 1) * pad] for j in range(3))
        acc = [jnp.zeros((frames, 256), F32), jnp.zeros((frames, 256), F32)]
        for h in range(HEADS):
            w = 0 if (h + 1) * head <= 256 else 1
            win = slice(w * 128, w * 128 + 256)
            mine = jnp.where((lane >= h * head) & (lane < (h + 1) * head), 1.0, 0.0).astype(BF16)
            s = lax.dot_general(
                (q * mine)[:, win],
                k[:, win],
                (((1,), (1,)), ((), ())),
                preferred_element_type=F32,
            )
            s = jnp.where(same, s * scale, -1e30)
            e = jnp.exp(s - jnp.max(s, axis=-1, keepdims=True))
            prob = (e * (1.0 / jnp.sum(e, axis=-1, keepdims=True))).astype(BF16)
            acc[w] = acc[w] + jnp.dot(prob, (v * mine)[:, win], preferred_element_type=F32)
        a32[0, at, :] = acc[0][:, :128]
        a32[1, at, :] = acc[0][:, 128:] + acc[1][:, :128]
        a32[2, at, :] = acc[1][:, 128:]
        return 0

    lax.fori_loop(0, PIX, pixel, 0)

    step_rows = 4 * 2 * per
    steps = rows // step_rows
    m32[0:PIX, :] = jnp.zeros((PIX, ch), F32)
    m32[rows + PIX : rows + 2 * PIX, :] = jnp.zeros((PIX, ch), F32)

    def mix(i, _):
        at = pl.ds(pl.multiple_of(i * step_rows, 8), step_rows)
        att = jnp.concatenate([a32[c, at, :] for c in range(pad // 128)], axis=-1)
        att = att[:, :ch].astype(BF16)
        m = (x32[at, :] + jnp.dot(att, wo_ref[...], preferred_element_type=F32)).astype(BF16)
        m_ref[at, :] = m
        m32[pl.ds(pl.multiple_of(i * step_rows + PIX, 8), step_rows), :] = m.astype(F32)
        return 0

    lax.fori_loop(0, steps, mix, 0)

    def temporal(i, _):
        r0 = pl.multiple_of(i * step_rows, 8)
        f = (r0 + lax.broadcasted_iota(jnp.int32, (step_rows, 1), 0)) >> 3
        here = clip_ids(f, len_ref)
        before = jnp.where((clip_ids(f - 1, len_ref) == here) & (f > 0), 1.0, 0.0)
        after = jnp.where((clip_ids(f + 1, len_ref) == here) & (f < frames - 1), 1.0, 0.0)
        prev = (m32[pl.ds(r0, step_rows), :] * before).astype(BF16)
        cur32 = m32[pl.ds(pl.multiple_of(r0 + PIX, 8), step_rows), :]
        nxt = (m32[pl.ds(pl.multiple_of(r0 + 2 * PIX, 8), step_rows), :] * after).astype(BF16)
        total = cur32 + jnp.dot(prev, tw_ref[0], preferred_element_type=F32)
        total = total + jnp.dot(cur32.astype(BF16), tw_ref[1], preferred_element_type=F32)
        total = total + jnp.dot(nxt, tw_ref[2], preferred_element_type=F32)
        for k in range(4):
            base = k * 2 * per
            a = total[base : base + per].astype(BF16).reshape(half, PIX, ch)
            b = total[base + per : base + 2 * per].astype(BF16).reshape(half, PIX, ch)
            d = i * 4 + k
            o_ref[d, :, :, 0:wide] = a[:, :, :wide]
            o_ref[d, :, :, wide : 2 * wide] = b[:, :, :wide]
            o_ref[d, :, :, 2 * wide : 2 * ch] = jnp.concatenate([a[:, :, wide:], b[:, :, wide:]], -1)
        return 0

    lax.fori_loop(0, steps, temporal, 0)


def grad_kernel(len_ref, m_ref, cot_ref, o_ref, c32):
    shards, half, _, ch2 = cot_ref.shape
    ch = ch2 // 2
    wide = ch // 128 * 128
    frames = shards * half * 2
    rows = frames * PIX
    per = half * PIX
    c32[0:PIX, :] = jnp.zeros((PIX, ch), F32)
    c32[rows + PIX : rows + 2 * PIX, :] = jnp.zeros((PIX, ch), F32)

    def load(s, _):
        first, second = unpack_rows(cot_ref[s], ch)
        for k, part in enumerate((first, second)):
            at = pl.ds(pl.multiple_of((2 * s + k) * per + PIX, 8), per)
            c32[at, 0:wide] = part[0]
            c32[at, wide:ch] = part[1]
        return 0

    lax.fori_loop(0, shards, load, 0)
    step_rows = 4 * 2 * per
    o_ref[...] = jnp.zeros_like(o_ref)

    def step(i, _):
        r0 = pl.multiple_of(i * step_rows, 8)
        f = (r0 + lax.broadcasted_iota(jnp.int32, (step_rows, 1), 0)) >> 3
        here = clip_ids(f, len_ref)
        before = jnp.where((clip_ids(f - 1, len_ref) == here) & (f > 0), 1.0, 0.0)
        after = jnp.where((clip_ids(f + 1, len_ref) == here) & (f < frames - 1), 1.0, 0.0)
        m = m_ref[pl.ds(r0, step_rows), :]
        pieces = (
            (c32[pl.ds(pl.multiple_of(r0 + 2 * PIX, 8), step_rows), :] * after).astype(BF16),
            c32[pl.ds(pl.multiple_of(r0 + PIX, 8), step_rows), :].astype(BF16),
            (c32[pl.ds(r0, step_rows), :] * before).astype(BF16),
        )
        for j, piece in enumerate(pieces):
            at = slice(j * ch, (j + 1) * ch)
            o_ref[at, :] += lax.dot_general(
                m, piece, (((0,), (0,)), ((), ())), preferred_element_type=F32
            )
        return 0

    lax.fori_loop(0, rows // step_rows, step, 0)


def tree(parts):
    while len(parts) > 1:
        parts = [parts[i] + parts[i + 1] for i in range(0, len(parts), 2)]
    return parts[0]


def swaps(n, k):
    return [(i, i ^ k) for i in range(n)]


def reduce_all(g):
    core = lax.axis_index("c")
    n_plane = lax.axis_size("y") * lax.axis_size("x")
    place = lax.axis_index("y") * lax.axis_size("x") + lax.axis_index("x")
    n_z = lax.axis_size("z")
    half = g.shape[0] // 2
    share = half // n_plane

    def cut(v, i, size):
        return lax.dynamic_slice_in_dim(v, i * size, size, 0)

    other = lax.ppermute(cut(g, 1 - core, half).astype(BF16), "c", swaps(2, 1))
    g = cut(g, core, half) + other.astype(F32)
    parts = [cut(g, place, share)]
    for k in range(1, n_plane):
        sent = cut(g, place ^ k, share).astype(BF16)
        parts.append(lax.ppermute(sent, PLANE, swaps(n_plane, k)).astype(F32))
    mine = tree(parts).astype(BF16)
    parts = [mine.astype(F32)]
    for k in range(1, n_z):
        parts.append(lax.ppermute(mine, "z", swaps(n_z, k)).astype(F32))
    total = tree(parts).astype(BF16)
    parts = [total] + [lax.ppermute(total, PLANE, swaps(n_plane, k)) for k in range(1, n_plane)]
    stacked = jnp.stack(parts)
    ordered = jnp.concatenate(
        [lax.dynamic_index_in_dim(stacked, place ^ j, 0, False) for j in range(n_plane)], 0
    )
    other = lax.ppermute(ordered, "c", swaps(2, 1))
    low = jnp.where(core == 0, ordered, other)
    high = jnp.where(core == 0, other, ordered)
    return jnp.concatenate([low, high], 0).astype(F32)


def exchange(x):
    shape = x.shape
    flat = x.reshape(shape[0], shape[1] * shape[2], shape[3])
    flat = lax.all_to_all(flat, SEQ, split_axis=0, concat_axis=0, tiled=True)
    return flat.reshape(shape)


def body(
    latents,
    clip_lengths,
    timesteps,
    spatial_weight,
    time_weight,
    query_weight,
    key_weight,
    value_weight,
    out_weight,
    temporal_weight,
    cotangent,
):
    f_dev, rows, across, ch = latents.shape
    shards = lax.axis_size("z") * lax.axis_size("y") * lax.axis_size("c")
    n_rows = lax.axis_size("x")
    assert rows * across <= shards * PIX and shards % rows == 0 and f_dev % 2 == 0
    half = f_dev // 2
    packed = jax.ShapeDtypeStruct((shards, half, PIX, 2 * ch), BF16)
    positions = f_dev * rows * across
    size = positions * ch * 2
    dense = 2 * positions * ch * ch

    row = lax.axis_index("x")
    if n_rows == 2:
        edge = jnp.where(row == 0, latents[:, rows - 1], latents[:, 0])
        got = lax.ppermute(edge, "x", swaps(2, 1))
        top, bot = got, got
    else:
        up = [(i, i + 1) for i in range(n_rows - 1)]
        top = lax.ppermute(latents[:, rows - 1], "x", up)
        bot = lax.ppermute(latents[:, 0], "x", [(j, i) for i, j in up])
    flags = jnp.stack([row > 0, row < n_rows - 1]).astype(jnp.int32)

    table = time_table(timesteps, time_weight)
    seq = (lax.axis_index("z") * lax.axis_size("y") + lax.axis_index("y")) * 2 + lax.axis_index("c")
    frame = seq * f_dev + jnp.arange(f_dev, dtype=jnp.int32)
    local_ids = jnp.sum(
        (frame[:, None] >= jnp.cumsum(clip_lengths)[None, :]).astype(jnp.int32), axis=1
    )
    active = call(
        conv_kernel,
        packed,
        [SMEM, SMEM, VMEM, VMEM, VMEM, VMEM, VMEM],
        flops=9 * dense,
        bytes_accessed=2 * size + 9 * ch * ch * 2,
    )(flags, local_ids, latents, top, bot, spatial_weight, table)
    active = exchange(active)

    cot = call(pack_kernel, packed, [VMEM], bytes_accessed=2 * size)(cotangent)
    cot, active = lax.optimization_barrier((cot, active))
    cot = exchange(cot)

    total_rows = shards * f_dev * PIX
    tiles = -(-ch // 128)
    columns = pltpu.VMEM((tiles, total_rows, 128), F32)
    block, mixed = call(
        attention_kernel,
        (packed, jax.ShapeDtypeStruct((total_rows, ch), BF16)),
        [SMEM] + [VMEM] * 6,
        scratch=[
            pltpu.VMEM((total_rows, ch), F32),
            columns,
            columns,
            pltpu.VMEM((total_rows + 2 * PIX, ch), F32),
            pltpu.VMEM((tiles * 128, 3 * tiles * 128), BF16),
        ],
        flops=10 * dense,
        bytes_accessed=3 * size,
    )(
        clip_lengths,
        active,
        query_weight,
        key_weight,
        value_weight,
        out_weight,
        temporal_weight,
    )
    block = exchange(block)
    grads = call(
        grad_kernel,
        jax.ShapeDtypeStruct((3 * ch, ch), F32),
        [SMEM, VMEM, VMEM],
        scratch=[pltpu.VMEM((total_rows + 2 * PIX, ch), F32)],
        flops=3 * dense,
        bytes_accessed=2 * size + 3 * ch * ch * 4,
    )(clip_lengths, mixed, cot)
    grads = reduce_all(grads).reshape(3, ch, ch)
    block_out = call(
        unpack_kernel,
        jax.ShapeDtypeStruct(latents.shape, BF16),
        [VMEM],
        bytes_accessed=2 * size,
    )(block)
    return block_out, grads


def solution(mesh):
    n_seq, n_row = mesh.devices.shape
    grid = Mesh(mesh.devices.reshape(n_seq // 4, 2, 2, n_row), ("z", "y", "c", "x"))
    spread = P(SEQ, "x", None, None)
    in_specs = (spread,) + (P(),) * 9 + (spread,)
    return jax.shard_map(
        body, mesh=grid, in_specs=in_specs, out_specs=(spread, P()), check_vma=False
    )
```

profile of v0, /device:TPU:0, one launch (start us, length us, event | category | flops | bytes accessed | tf_op | source)
XLA Modules:
  0.0 143.7 jit_solution(1075530948339179801)
XLA Ops:
  0.7 1.1 fusion
  1.8 3.0 %collective-permute-start = (bf16[12,32,320]{2,1,0:T(8,128)(2,1)S(1)}, bf16[12,32,320]{2,1,0:T(8,128)(2,1)S(1)}, u32[]{:S(2)}, u32[]{:S(2)}) collective-permute-start(bf16[12,32,320]{2,1,0:T(8,128)(2,1)S(1)} %fusion), channel_id=1, source_target_pairs={{0,1},{1,0},{2,3},{3,2},{4,5},{5,4},{6,7},{7,6},{8,9},{9,8},{10,11... | collective-permute-start | bytes 737288 | tf_op jit(solution)/shard_map/ppermute | solution.py:391
  4.8 0.8 reduce-window.8
  6.3 0.7 convert_reduce_fusion.id_ref
  7.7 0.9 fusion.1.table_ref
  8.6 3.2 %collective-permute-done.top_ref.bot_ref = bf16[12,32,320]{2,1,0:T(8,128)(2,1)S(1)} collective-permute-done((bf16[12,32,320]{2,1,0:T(8,128)(2,1)S(1)}, bf16[12,32,320]{2,1,0:T(8,128)(2,1)S(1)}, u32[]{:S(2)}, u32[]{:S(2)}) %collective-permute-start) | collective-permute-done | bytes 245792 | tf_op jit(solution)/shard_map/ppermute | solution.py:391
  11.8 0.7 copy-done.5
  12.5 11.3 %shard_map.123 = bf16[16,6,8,640]{3,2,1,0:T(8,128)(2,1)} custom-call(s32[2]{0:T(128)} %add_convert_fusion.2.flag_ref, s32[12]{0:T(128)} %convert_reduce_fusion.id_ref, bf16[12,4,32,320]{3,2,1,0:T(8,128)(2,1)} %lat_ref.1, bf16[12,32,320]{2,1,0:T(8,128)(2,1)} %copy-done.5, bf16[12,32,320]{2,1,0:T(8,128)(2,1)} %copy-done.5, bf16[3,3,320,320]{3,2,1,0:T(8,128)(2,1)} %w_ref.1, ...), custom_call_target="tpu_custom_call" | custom-call | flops 2831155200 | bytes 3809280 | tf_op jit(solution)/shard_map/pallas_call | solution.py:405
  23.8 6.2 %all-to-all-start = ((bf16[16,48,640]{2,1,0:T(8,128)(2,1)}), bf16[16,48,640]{2,1,0:T(8,128)(2,1)S(1)}, u32[]{:S(2)}, u32[]{:S(2)}) async-start(bf16[16,48,640]{2,1,0:T(8,128)(2,1)} %bitcast.39), calls=%async_computation | async-start | bytes 1966080 | tf_op jit(solution)/shard_map/all_to_all | solution.py:361
  30.0 2.7 %shard_map.122 = bf16[16,6,8,640]{3,2,1,0:T(8,128)(2,1)} custom-call(bf16[12,4,32,320]{3,2,1,0:T(8,128)(2,1)} %x_ref.1), custom_call_target="tpu_custom_call" | custom-call | bytes 1966080 | tf_op jit(solution)/shard_map/pallas_call | solution.py:414
  32.8 19.1 %all-to-all-done = bf16[16,48,640]{2,1,0:T(8,128)(2,1)S(1)} async-done(((bf16[16,48,640]{2,1,0:T(8,128)(2,1)}), bf16[16,48,640]{2,1,0:T(8,128)(2,1)S(1)}, u32[]{:S(2)}, u32[]{:S(2)}) %all-to-all-start) | async-done | bytes 983072 | tf_op jit(solution)/shard_map/all_to_all | solution.py:361
  51.9 6.5 %all-to-all-start.2 = ((bf16[16,48,640]{2,1,0:T(8,128)(2,1)}), bf16[16,48,640]{2,1,0:T(8,128)(2,1)S(1)}, u32[]{:S(2)}, u32[]{:S(2)}) async-start(bf16[16,48,640]{2,1,0:T(8,128)(2,1)} %bitcast.34), calls=%async_computation.2 | async-start | bytes 1966080 | tf_op jit(solution)/shard_map/all_to_all | solution.py:361
  58.5 24.0 %shard_map.124 = (bf16[16,6,8,640]{3,2,1,0:T(8,128)(2,1)}, bf16[1536,320]{1,0:T(8,128)(2,1)}) custom-call(s32[4]{0:T(128)} %len_ref.3, bf16[16,6,8,640]{3,2,1,0:T(8,128)(2,1)} %bitcast.38, bf16[320,320]{1,0:T(8,128)(2,1)} %wq_ref.1, bf16[320,320]{1,0:T(8,128)(2,1)} %wk_ref.1, bf16[320,320]{1,0:T(8,128)(2,1)} %wv_ref.1, bf16[320,320]{1,0:T(8,128)(2,1)} %wo_ref.1, ...), custom_call_target="tpu_custom_call" | custom-call | flops 3145728000 | bytes 2949120 | tf_op jit(solution)/shard_map/pallas_call | solution.py:421
  82.5 1.0 copy-done.3
  83.5 7.1 %shard_map.126 = f32[960,320]{1,0:T(8,128)} custom-call(s32[4]{0:T(128)} %len_ref.3, bf16[1536,320]{1,0:T(8,128)(2,1)} %get-tuple-element.8.m_ref, bf16[16,6,8,640]{3,2,1,0:T(8,128)(2,1)} %bitcast.35), custom_call_target="tpu_custom_call" | custom-call | flops 943718400 | bytes 3194880 | tf_op jit(solution)/shard_map/pallas_call | solution.py:444
  90.6 1.3 dynamic-slice_convert_fusion
  92.4 5.8 %all-to-all-start.1 = ((bf16[16,48,640]{2,1,0:T(8,128)(2,1)}), bf16[16,48,640]{2,1,0:T(8,128)(2,1)S(1)}, u32[]{:S(2)}, u32[]{:S(2)}) async-start(bf16[16,48,640]{2,1,0:T(8,128)(2,1)} %bitcast.37), calls=%async_computation.1 | async-start | bytes 1966080 | tf_op jit(solution)/shard_map/all_to_all | solution.py:361
  98.2 1.1 convert_add_fusion
  99.3 1.6 %collective-permute-start.2 = (bf16[120,320]{1,0:T(8,128)(2,1)S(1)}, bf16[120,320]{1,0:T(8,128)(2,1)S(1)}, u32[]{:S(2)}, u32[]{:S(2)}) collective-permute-start(bf16[120,320]{1,0:T(8,128)(2,1)S(1)} %get-tuple-element.12), channel_id=1, source_target_pairs={{0,1},{1,0},{4,5},{5,4},{2,3},{3,2},{6,7},{7,6},{8,9},{9,8},{12,13... | collective-permute-start | bytes 230408 | tf_op jit(solution)/shard_map/ppermute | solution.py:341
  100.9 1.9 %collective-permute-start.3 = (bf16[120,320]{1,0:T(8,128)(2,1)S(1)}, bf16[120,320]{1,0:T(8,128)(2,1)S(1)}, u32[]{:S(2)}, u32[]{:S(2)}) collective-permute-start(bf16[120,320]{1,0:T(8,128)(2,1)S(1)} %get-tuple-element.14), channel_id=1, source_target_pairs={{0,4},{1,5},{4,0},{5,1},{2,6},{3,7},{6,2},{7,3},{8,12},{9,13},{12,... | collective-permute-start | bytes 230408 | tf_op jit(solution)/shard_map/ppermute | solution.py:341
  102.9 1.4 collective-permute-done.2
  104.3 8.8 %collective-permute-done.3 = bf16[120,320]{1,0:T(8,128)(2,1)S(1)} collective-permute-done((bf16[120,320]{1,0:T(8,128)(2,1)S(1)}, bf16[120,320]{1,0:T(8,128)(2,1)S(1)}, u32[]{:S(2)}, u32[]{:S(2)}) %collective-permute-start.3) | collective-permute-done | bytes 76832 | tf_op jit(solution)/shard_map/ppermute | solution.py:341
  113.2 4.2 %collective-permute-start.6 = (bf16[120,320]{1,0:T(8,128)(2,1)S(1)}, bf16[120,320]{1,0:T(8,128)(2,1)S(1)}, u32[]{:S(2)}, u32[]{:S(2)}) collective-permute-start(bf16[120,320]{1,0:T(8,128)(2,1)S(1)} %add_convert_fusion.1), channel_id=1, source_target_pairs={{0,16},{8,24},{16,0},{24,8},{1,17},{9,25},{17,1},{25,9},{2,18},{10... | collective-permute-start | bytes 230408 | tf_op jit(solution)/shard_map/ppermute | solution.py:345
  118.0 11.6 %collective-permute-done.6 = bf16[120,320]{1,0:T(8,128)(2,1)S(1)} collective-permute-done((bf16[120,320]{1,0:T(8,128)(2,1)S(1)}, bf16[120,320]{1,0:T(8,128)(2,1)S(1)}, u32[]{:S(2)}, u32[]{:S(2)}) %collective-permute-start.6) | collective-permute-done | bytes 76832 | tf_op jit(solution)/shard_map/ppermute | solution.py:345
  129.7 1.6 %collective-permute-start.8 = (bf16[120,320]{1,0:T(8,128)(2,1)S(1)}, bf16[120,320]{1,0:T(8,128)(2,1)S(1)}, u32[]{:S(2)}, u32[]{:S(2)}) collective-permute-start(bf16[120,320]{1,0:T(8,128)(2,1)S(1)} %add_convert_fusion), channel_id=1, source_target_pairs={{0,1},{1,0},{4,5},{5,4},{2,3},{3,2},{6,7},{7,6},{8,9},{9,8},{12,13... | collective-permute-start | bytes 230408 | tf_op jit(solution)/shard_map/ppermute | solution.py:347
  131.3 1.5 %collective-permute-start.9 = (bf16[120,320]{1,0:T(8,128)(2,1)S(1)}, bf16[120,320]{1,0:T(8,128)(2,1)S(1)}, u32[]{:S(2)}, u32[]{:S(2)}) collective-permute-start(bf16[120,320]{1,0:T(8,128)(2,1)S(1)} %add_convert_fusion), channel_id=1, source_target_pairs={{0,4},{1,5},{4,0},{5,1},{2,6},{3,7},{6,2},{7,3},{8,12},{9,13},{12,... | collective-permute-start | bytes 230408 | tf_op jit(solution)/shard_map/ppermute | solution.py:347
  133.3 1.5 %collective-permute-done.8 = bf16[120,320]{1,0:T(8,128)(2,1)S(1)} collective-permute-done((bf16[120,320]{1,0:T(8,128)(2,1)S(1)}, bf16[120,320]{1,0:T(8,128)(2,1)S(1)}, u32[]{:S(2)}, u32[]{:S(2)}) %collective-permute-start.8) | collective-permute-done | bytes 76832 | tf_op jit(solution)/shard_map/ppermute | solution.py:347
  134.8 2.0 %collective-permute-done.9 = bf16[120,320]{1,0:T(8,128)(2,1)S(1)} collective-permute-done((bf16[120,320]{1,0:T(8,128)(2,1)S(1)}, bf16[120,320]{1,0:T(8,128)(2,1)S(1)}, u32[]{:S(2)}, u32[]{:S(2)}) %collective-permute-start.9) | collective-permute-done | bytes 76832 | tf_op jit(solution)/shard_map/ppermute | solution.py:347
  136.8 1.4 collective-permute-done.10
  138.5 0.9 copy-done.2
  139.5 2.8 %shard_map.125 = bf16[12,4,32,320]{3,2,1,0:T(8,128)(2,1)} custom-call(bf16[16,6,8,640]{3,2,1,0:T(8,128)(2,1)} %bitcast.33), custom_call_target="tpu_custom_call" | custom-call | bytes 1966080 | tf_op jit(solution)/shard_map/pallas_call | solution.py:453
  142.5 1.2 convert.1
  (35 shorter events, 3.9 us)
Async XLA Ops:
  0.6 7.1 %copy-start = (bf16[320,320]{1,0:T(8,128)(2,1)S(1)}, bf16[320,320]{1,0:T(8,128)(2,1)}, u32[]{:S(2)}) copy-start(bf16[320,320]{1,0:T(8,128)(2,1)} %param.15) | copy-start | bytes 614404
  1.8 10.0 %collective-permute-start = (bf16[12,32,320]{2,1,0:T(8,128)(2,1)S(1)}, bf16[12,32,320]{2,1,0:T(8,128)(2,1)S(1)}, u32[]{:S(2)}, u32[]{:S(2)}) collective-permute-start(bf16[12,32,320]{2,1,0:T(8,128)(2,1)S(1)} %fusion), channel_id=1, source_target_pairs={{0,1},{1,0},{2,3},{3,2},{4,5},{5,4},{6,7},{7,6},{8,9},{9,8},{10,11... | collective-permute-start | bytes 737288 | tf_op jit(solution)/shard_map/ppermute | solution.py:391
  11.8 0.7 copy-start.5
  23.8 28.1 %all-to-all-start = ((bf16[16,48,640]{2,1,0:T(8,128)(2,1)}), bf16[16,48,640]{2,1,0:T(8,128)(2,1)S(1)}, u32[]{:S(2)}, u32[]{:S(2)}) async-start(bf16[16,48,640]{2,1,0:T(8,128)(2,1)} %bitcast.39), calls=%async_computation | async-start | bytes 1966080 | tf_op jit(solution)/shard_map/all_to_all | solution.py:361
  51.9 6.5 %copy-start.4 = (bf16[16,48,640]{2,1,0:T(8,128)(2,1)}, bf16[16,48,640]{2,1,0:T(8,128)(2,1)S(1)}, u32[]{:S(2)}) copy-start(bf16[16,48,640]{2,1,0:T(8,128)(2,1)S(1)} %all-to-all-done) | copy-start | bytes 2949124
  51.9 30.6 %all-to-all-start.2 = ((bf16[16,48,640]{2,1,0:T(8,128)(2,1)}), bf16[16,48,640]{2,1,0:T(8,128)(2,1)S(1)}, u32[]{:S(2)}, u32[]{:S(2)}) async-start(bf16[16,48,640]{2,1,0:T(8,128)(2,1)} %bitcast.34), calls=%async_computation.2 | async-start | bytes 1966080 | tf_op jit(solution)/shard_map/all_to_all | solution.py:361
  82.5 1.0 copy-start.3
  90.6 7.6 %copy-start.1 = (f32[960,320]{1,0:T(8,128)S(1)}, f32[960,320]{1,0:T(8,128)}, u32[]{:S(2)}) copy-start(f32[960,320]{1,0:T(8,128)} %shard_map.126) | copy-start | bytes 3686404
  91.9 6.3 %collective-permute-start.1 = (bf16[480,320]{1,0:T(8,128)(2,1)S(1)}, bf16[480,320]{1,0:T(8,128)(2,1)}, u32[]{:S(2)}, u32[]{:S(2)}) collective-permute-start(bf16[480,320]{1,0:T(8,128)(2,1)S(1)} %dynamic-slice_convert_fusion), channel_id=1, source_target_pairs={{0,2},{2,0},{1,3},{3,1},{4,6},{6,4},{5,7},{7,5},{8,10},{10,8},{9,1... | collective-permute-start | bytes 921608 | tf_op jit(solution)/shard_map/ppermute | solution.py:336
  92.4 46.1 %all-to-all-start.1 = ((bf16[16,48,640]{2,1,0:T(8,128)(2,1)}), bf16[16,48,640]{2,1,0:T(8,128)(2,1)S(1)}, u32[]{:S(2)}, u32[]{:S(2)}) async-start(bf16[16,48,640]{2,1,0:T(8,128)(2,1)} %bitcast.37), calls=%async_computation.1 | async-start | bytes 1966080 | tf_op jit(solution)/shard_map/all_to_all | solution.py:361
  99.3 5.0 %collective-permute-start.2 = (bf16[120,320]{1,0:T(8,128)(2,1)S(1)}, bf16[120,320]{1,0:T(8,128)(2,1)S(1)}, u32[]{:S(2)}, u32[]{:S(2)}) collective-permute-start(bf16[120,320]{1,0:T(8,128)(2,1)S(1)} %get-tuple-element.12), channel_id=1, source_target_pairs={{0,1},{1,0},{4,5},{5,4},{2,3},{3,2},{6,7},{7,6},{8,9},{9,8},{12,13... | collective-permute-start | bytes 230408 | tf_op jit(solution)/shard_map/ppermute | solution.py:341
  100.9 12.2 %collective-permute-start.3 = (bf16[120,320]{1,0:T(8,128)(2,1)S(1)}, bf16[120,320]{1,0:T(8,128)(2,1)S(1)}, u32[]{:S(2)}, u32[]{:S(2)}) collective-permute-start(bf16[120,320]{1,0:T(8,128)(2,1)S(1)} %get-tuple-element.14), channel_id=1, source_target_pairs={{0,4},{1,5},{4,0},{5,1},{2,6},{3,7},{6,2},{7,3},{8,12},{9,13},{12,... | collective-permute-start | bytes 230408 | tf_op jit(solution)/shard_map/ppermute | solution.py:341
  102.7 10.4 %collective-permute-start.4 = (bf16[120,320]{1,0:T(8,128)(2,1)S(1)}, bf16[120,320]{1,0:T(8,128)(2,1)S(1)}, u32[]{:S(2)}, u32[]{:S(2)}) collective-permute-start(bf16[120,320]{1,0:T(8,128)(2,1)S(1)} %get-tuple-element.13), channel_id=1, source_target_pairs={{0,5},{1,4},{4,1},{5,0},{2,7},{3,6},{6,3},{7,2},{8,13},{9,12},{12,... | collective-permute-start | bytes 230408 | tf_op jit(solution)/shard_map/ppermute | solution.py:341
  113.2 4.9 %collective-permute-start.5 = (bf16[120,320]{1,0:T(8,128)(2,1)S(1)}, bf16[120,320]{1,0:T(8,128)(2,1)S(1)}, u32[]{:S(2)}, u32[]{:S(2)}) collective-permute-start(bf16[120,320]{1,0:T(8,128)(2,1)S(1)} %add_convert_fusion.1), channel_id=1, source_target_pairs={{0,8},{8,0},{16,24},{24,16},{1,9},{9,1},{17,25},{25,17},{2,10},{10... | collective-permute-start | bytes 230408 | tf_op jit(solution)/shard_map/ppermute | solution.py:345
  113.2 16.4 %collective-permute-start.6 = (bf16[120,320]{1,0:T(8,128)(2,1)S(1)}, bf16[120,320]{1,0:T(8,128)(2,1)S(1)}, u32[]{:S(2)}, u32[]{:S(2)}) collective-permute-start(bf16[120,320]{1,0:T(8,128)(2,1)S(1)} %add_convert_fusion.1), channel_id=1, source_target_pairs={{0,16},{8,24},{16,0},{24,8},{1,17},{9,25},{17,1},{25,9},{2,18},{10... | collective-permute-start | bytes 230408 | tf_op jit(solution)/shard_map/ppermute | solution.py:345
  117.4 12.3 %collective-permute-start.7 = (bf16[120,320]{1,0:T(8,128)(2,1)S(1)}, bf16[120,320]{1,0:T(8,128)(2,1)S(1)}, u32[]{:S(2)}, u32[]{:S(2)}) collective-permute-start(bf16[120,320]{1,0:T(8,128)(2,1)S(1)} %add_convert_fusion.1), channel_id=1, source_target_pairs={{0,24},{8,16},{16,8},{24,0},{1,25},{9,17},{17,9},{25,1},{2,26},{10... | collective-permute-start | bytes 230408 | tf_op jit(solution)/shard_map/ppermute | solution.py:345
  129.7 5.1 %collective-permute-start.8 = (bf16[120,320]{1,0:T(8,128)(2,1)S(1)}, bf16[120,320]{1,0:T(8,128)(2,1)S(1)}, u32[]{:S(2)}, u32[]{:S(2)}) collective-permute-start(bf16[120,320]{1,0:T(8,128)(2,1)S(1)} %add_convert_fusion), channel_id=1, source_target_pairs={{0,1},{1,0},{4,5},{5,4},{2,3},{3,2},{6,7},{7,6},{8,9},{9,8},{12,13... | collective-permute-start | bytes 230408 | tf_op jit(solution)/shard_map/ppermute | solution.py:347
  131.3 5.5 %collective-permute-start.9 = (bf16[120,320]{1,0:T(8,128)(2,1)S(1)}, bf16[120,320]{1,0:T(8,128)(2,1)S(1)}, u32[]{:S(2)}, u32[]{:S(2)}) collective-permute-start(bf16[120,320]{1,0:T(8,128)(2,1)S(1)} %add_convert_fusion), channel_id=1, source_target_pairs={{0,4},{1,5},{4,0},{5,1},{2,6},{3,7},{6,2},{7,3},{8,12},{9,13},{12,... | collective-permute-start | bytes 230408 | tf_op jit(solution)/shard_map/ppermute | solution.py:347
  132.7 5.5 %collective-permute-start.10 = (bf16[120,320]{1,0:T(8,128)(2,1)S(1)}, bf16[120,320]{1,0:T(8,128)(2,1)S(1)}, u32[]{:S(2)}, u32[]{:S(2)}) collective-permute-start(bf16[120,320]{1,0:T(8,128)(2,1)S(1)} %add_convert_fusion), channel_id=1, source_target_pairs={{0,5},{1,4},{4,1},{5,0},{2,7},{3,6},{6,3},{7,2},{8,13},{9,12},{12,... | collective-permute-start | bytes 230408 | tf_op jit(solution)/shard_map/ppermute | solution.py:347
  138.4 3.9 %collective-permute-start.11 = (bf16[480,320]{1,0:T(8,128)(2,1)S(1)}, bf16[480,320]{1,0:T(8,128)(2,1)S(1)}, u32[]{:S(2)}, u32[]{:S(2)}) collective-permute-start(bf16[480,320]{1,0:T(8,128)(2,1)S(1)} %pad_maximum_fusion.2), channel_id=1, source_target_pairs={{0,2},{2,0},{1,3},{3,1},{4,6},{6,4},{5,7},{7,5},{8,10},{10,8},{9,1... | collective-permute-start | bytes 921608 | tf_op jit(solution)/shard_map/ppermute | solution.py:352
  138.5 0.9 copy-start.2
where the time goes:
time: 144 us
  waiting for transfers between devices  49.6 us (34%)
  Pallas kernels  48.1 us (33%)
  starting transfers between devices  33.6 us (23%)
  other arithmetic  6.77 us (5%)
  local copies, waits for them, and re-layouts  4.01 us (3%)
    pallas_call x1, Pallas kernels, body(): call(attention_kernel, (packed, jax.ShapeDtypeStruct((total_rows, ch), BF...  24 us
    all_to_all x3, waiting for transfers between devices, exchange(): flat = lax.all_to_all(flat, SEQ, split_axis=0, concat_axis=0, tiled=True)  19.1 us
    all_to_all x3, starting transfers between devices, exchange(): flat = lax.all_to_all(flat, SEQ, split_axis=0, concat_axis=0, tiled=True)  18.5 us
    ppermute x3, waiting for transfers between devices, reduce_all(): parts.append(lax.ppermute(mine, 'z', swaps(n_z, k)).astype(F32))  12.1 us
    pallas_call x1, Pallas kernels, body(): call(conv_kernel, packed, [SMEM, SMEM, VMEM, VMEM, VMEM, VMEM, VMEM], flo...  11.3 us
    ppermute x3, waiting for transfers between devices, reduce_all(): parts.append(lax.ppermute(sent, PLANE, swaps(n_plane, k)).astype(F32))  10.2 us
    pallas_call x1, Pallas kernels, body(): call(grad_kernel, jax.ShapeDtypeStruct((3 * ch, ch), F32), [SMEM, VMEM, V...  7.14 us
    ppermute x3, waiting for transfers between devices, reduce_all(): lax.ppermute(total, PLANE, swaps(n_plane, k))  4.91 us
  transfers between devices with their start and end apart: 15, of which 9 were waited for; matrix products, arithmetic and copies ran while one was open for 4% of the time, Pallas kernels for 21%

commit v1 on v0

v1 whole, which is shorter than its diff:
```python
import math

import jax
import jax.numpy as jnp
from jax import lax
from jax.experimental import pallas as pl
from jax.experimental.pallas import tpu as pltpu
from jax.sharding import Mesh
from jax.sharding import PartitionSpec as P

HEADS = 8
CLIPS = 4
SEQ = ("z", "y", "c")
PLANE = ("y", "x")
BF16 = jnp.bfloat16
F32 = jnp.float32
VMEM = pltpu.VMEM
SMEM = pltpu.SMEM
PIX = 8


def time_table(timesteps, time_weight):
    half_width = time_weight.shape[0] // 2
    frequency = jnp.exp(-math.log(10000.0) * jnp.arange(half_width, dtype=F32) / half_width)
    angles = timesteps.astype(F32)[:, None] * frequency[None, :]
    embedded = jnp.concatenate([jnp.cos(angles), jnp.sin(angles)], axis=1)
    return jnp.dot(embedded, time_weight.astype(F32), precision=lax.Precision.HIGHEST)


def call(kernel, out_shape, in_spaces, scratch=(), flops=0, bytes_accessed=0, grid=None, **kw):
    return pl.pallas_call(
        kernel,
        out_shape=out_shape,
        in_specs=[pl.BlockSpec(memory_space=s) for s in in_spaces],
        out_specs=jax.tree.map(lambda _: pl.BlockSpec(memory_space=VMEM), out_shape),
        scratch_shapes=scratch,
        cost_estimate=pl.CostEstimate(
            flops=flops, bytes_accessed=bytes_accessed, transcendentals=0
        ),
        compiler_params=pltpu.CompilerParams(vmem_limit_bytes=56 * 2**20),
        **kw,
    )


def pack_pair(ref, index, first, second):
    wide = first.shape[-1] // 128 * 128
    ref[index + (slice(None), slice(0, wide))] = first[:, :wide]
    ref[index + (slice(None), slice(wide, 2 * wide))] = second[:, :wide]
    ref[index + (slice(None), slice(2 * wide, 2 * first.shape[-1]))] = jnp.concatenate(
        [first[:, wide:], second[:, wide:]], axis=-1
    )


def clip_ids(frame, len_ref):
    bound = jnp.int32(0)
    ids = jnp.zeros(frame.shape, jnp.int32)
    for k in range(CLIPS):
        bound = bound + len_ref[k]
        ids = ids + jnp.where(frame >= bound, 1, 0)
    return ids


def take(row, g, real):
    if real == PIX:
        return row[g * PIX : (g + 1) * PIX]
    piece = row[g * real : (g + 1) * real].astype(F32)
    return jnp.concatenate([piece, jnp.zeros((PIX - real, row.shape[-1]), F32)], 0).astype(BF16)


def pack_kernel(x_ref, o_ref):
    frames, rows, across, ch = x_ref.shape
    half = frames // 2
    groups = o_ref.shape[0] // rows
    real = across // groups

    def step(t, _):
        for i in range(rows):
            first, second = x_ref[2 * t, i], x_ref[2 * t + 1, i]
            for g in range(groups):
                pack_pair(
                    o_ref, (i * groups + g, t), take(first, g, real), take(second, g, real)
                )
        return 0

    lax.fori_loop(0, half, step, 0)


def unpack_kernel(x_ref, o_ref):
    frames, rows, across, ch = o_ref.shape
    half = frames // 2
    groups = x_ref.shape[0] // rows
    real = across // groups
    wide = ch // 128 * 128

    def join(blocks, low, high):
        if real == PIX:
            return jnp.concatenate([b[:, low:high] for b in blocks], 0)
        return jnp.concatenate([b[:real, low:high].astype(F32) for b in blocks], 0).astype(BF16)

    def step(t, _):
        for i in range(rows):
            blocks = [x_ref[i * groups + g, t] for g in range(groups)]
            o_ref[2 * t, i, :, 0:wide] = join(blocks, 0, wide)
            o_ref[2 * t, i, :, wide:ch] = join(blocks, 2 * wide, wide + ch)
            o_ref[2 * t + 1, i, :, 0:wide] = join(blocks, wide, 2 * wide)
            o_ref[2 * t + 1, i, :, wide:ch] = join(blocks, wide + ch, 2 * ch)
        return 0

    lax.fori_loop(0, half, step, 0)


def conv_kernel(flag_ref, id_ref, lat_ref, top_ref, bot_ref, w_ref, table_ref, o_ref):
    frames, rows, across, ch = lat_ref.shape
    half = frames // 2
    groups = o_ref.shape[0] // rows
    real = across // groups

    def step(t, _):
        kept = []
        for base in (0, 1):
            top = top_ref[2 * t + base]
            bot = bot_ref[2 * t + base]
            top = jnp.where(flag_ref[0] > 0, top, jnp.zeros_like(top))
            bot = jnp.where(flag_ref[1] > 0, bot, jnp.zeros_like(bot))
            lat = [lat_ref[2 * t + base, i] for i in range(rows)]
            kept.append([top] + lat + [bot])
        n_rows = 2 * rows * across
        sums = []
        windows = [
            jnp.concatenate([r for s in kept for r in s[a : a + rows]], axis=0) for a in range(3)
        ]
        for b in range(3):
            acc = jnp.zeros((n_rows, ch), F32)
            for a in range(3):
                acc = acc + jnp.dot(windows[a], w_ref[a, b], preferred_element_type=F32)
            sums.append(acc)
        col = lax.broadcasted_iota(jnp.int32, (n_rows, ch), 0) & (across - 1)
        left = jnp.where(col == 0, 0.0, pltpu.roll(sums[0], 1, 0))
        right = jnp.where(col == across - 1, 0.0, pltpu.roll(sums[2], n_rows - 1, 0))
        spatial = sums[1] + left + right
        per = rows * across
        outs = []
        for k in (0, 1):
            emb = table_ref[pl.ds(id_ref[2 * t + k], 1), :]
            v = spatial[k * per : (k + 1) * per] + emb
            silu = 0.5 * v * (1.0 + jnp.tanh(0.5 * v))
            res = windows[1][k * per : (k + 1) * per].astype(F32)
            outs.append((res + silu).astype(BF16))
        for d in range(rows * groups):
            pack_pair(o_ref, (d, t), take(outs[0], d, real), take(outs[1], d, real))
        return 0

    lax.fori_loop(0, half, step, 0)


def low_lanes():
    return lax.broadcasted_iota(jnp.int32, (1, 128), 1) < 64


def swap_halves(tail):
    return pltpu.roll(tail, 64, 1)


def split_pair(x):
    tail = x[:, 512:640]
    even = jnp.concatenate([x[:, 0:256], tail], axis=1)
    odd = jnp.concatenate([x[:, 256:512], swap_halves(tail)], axis=1)
    return even, odd


def join_pair(even, odd):
    tail = jnp.where(low_lanes(), even[:, 256:384], swap_halves(odd[:, 256:384]))
    return even[:, 0:256], odd[:, 0:256], tail


def pad_weight(dst, src, row, col):
    ch = src.shape[-1]
    dst[pl.ds(row, dst_tile(ch)), pl.ds(col, dst_tile(ch))] = jnp.zeros(
        (dst_tile(ch), dst_tile(ch)), BF16
    )
    dst[pl.ds(row, ch), pl.ds(col, ch)] = src


def dst_tile(ch):
    return -(-ch // 128) * 128


def sources(m32, r0, n, frames, len_ref):
    cur = split_pair(m32[pl.ds(pl.multiple_of(r0 + PIX, 8), n), :])
    before = split_pair(m32[pl.ds(pl.multiple_of(r0, 8), n), :])[1]
    after = split_pair(m32[pl.ds(pl.multiple_of(r0 + 2 * PIX, 8), n), :])[0]
    even = ((r0 + lax.broadcasted_iota(jnp.int32, (n, 1), 0)) >> 3) * 2
    ids = [clip_ids(even + k, len_ref) for k in (-1, 0, 1, 2)]
    into = jnp.where((ids[0] == ids[1]) & (even > 0), 1.0, 0.0)
    inside = jnp.where(ids[1] == ids[2], 1.0, 0.0)
    out = jnp.where((ids[2] == ids[3]) & (even < frames - 2), 1.0, 0.0)
    stack = lambda a, b: jnp.concatenate([a, b], axis=0)
    previous = stack(before * into, cur[0] * inside)
    following = stack(cur[1] * inside, after * out)
    return previous, stack(*cur), following


def attention_kernel(
    len_ref, act_ref, wq_ref, wk_ref, wv_ref, wo_ref, tw_ref, o_ref, m_ref,
    n5, d5, m32, bias, wqkv, wo, tw,
):
    rows, ch2 = act_ref.shape
    ch = ch2 // 2
    pad = dst_tile(ch)
    units = rows // PIX
    frames = units * 2
    head = ch // HEADS
    for j, ref in enumerate((wq_ref, wk_ref, wv_ref)):
        pad_weight(wqkv, ref[...], 0, j * pad)
    pad_weight(wo, wo_ref[...], 0, 0)
    for j in range(3):
        pad_weight(tw, tw_ref[j], j * pad, 0)

    place = lambda axis: lax.broadcasted_iota(jnp.int32, (frames, frames), axis)
    frame = lambda i: jnp.where(i < units, 2 * i, 2 * (i - units) + 1)
    same = clip_ids(frame(place(0)), len_ref) == clip_ids(frame(place(1)), len_ref)
    bias[...] = jnp.where(same, 0.0, -1e30)

    chunk = 96
    low = low_lanes()

    def norm(i, _):
        at = pl.ds(pl.multiple_of(i * chunk, 8), chunk)
        x = act_ref[at, :].astype(F32)
        cols = [x[:, c * 128 : (c + 1) * 128] for c in range(5)]

        def sums(v):
            a = v[0] + v[1] + jnp.where(low, v[4], 0.0)
            b = v[2] + v[3] + jnp.where(low, 0.0, v[4])
            return [jnp.sum(t, axis=-1, keepdims=True) * (1.0 / ch) for t in (a, b)]

        def spread_out(a, b):
            return [a, a, b, b, jnp.where(low, a, b)]

        center = [v - m for v, m in zip(cols, spread_out(*sums(cols)))]
        var = sums([v * v for v in center])
        gain = spread_out(*[lax.rsqrt(v + 1e-05) for v in var])
        for c in range(5):
            n5[c, at, :] = (center[c] * gain[c]).astype(BF16).astype(F32)
        return 0

    lax.fori_loop(0, rows // chunk, norm, 0)

    factor = head ** (-0.5) * math.log2(math.e)
    lane = lax.broadcasted_iota(jnp.int32, (1, pad), 1)
    group = 2

    def pixels(i, _):
        parts = []
        for g in range(group):
            at = pl.ds(i * group + g, units, stride=PIX)
            cols = [n5[c, at, :] for c in range(5)]
            parts.append(jnp.concatenate([cols[0], cols[1], cols[4]], axis=1))
            parts.append(jnp.concatenate([cols[2], cols[3], swap_halves(cols[4])], axis=1))
        n = jnp.concatenate(parts, axis=0).astype(BF16)
        qkv = jnp.dot(n, wqkv[...], preferred_element_type=F32).astype(BF16)
        att = []
        for g in range(group):
            q, k, v = (
                qkv[g * frames : (g + 1) * frames, j * pad : (j + 1) * pad] for j in range(3)
            )
            acc = [None, None]
            for h in range(HEADS):
                w = 0 if (h + 1) * head <= 256 else 1
                win = slice(w * 128, w * 128 + 256)
                mine = (lane >= h * head) & (lane < (h + 1) * head)
                mine = jnp.where(mine, 1.0, 0.0).astype(BF16)
                s = lax.dot_general(
                    (q * mine)[:, win],
                    k[:, win],
                    (((1,), (1,)), ((), ())),
                    preferred_element_type=F32,
                )
                s = s * factor + bias[...]
                e = jnp.exp2(s - jnp.max(s, axis=-1, keepdims=True))
                prob = (e * (1.0 / jnp.sum(e, axis=-1, keepdims=True))).astype(BF16)
                got = jnp.dot(prob, (v * mine)[:, win], preferred_element_type=F32)
                acc[w] = got if acc[w] is None else acc[w] + got
            att.append(
                jnp.concatenate(
                    [acc[0][:, :128], acc[0][:, 128:] + acc[1][:, :128], acc[1][:, 128:]], axis=1
                )
            )
        att = jnp.concatenate(att, axis=0).astype(BF16)
        delta = jnp.dot(att, wo[...], preferred_element_type=F32)
        for g in range(group):
            at = pl.ds(i * group + g, units, stride=PIX)
            base = g * frames
            even, odd = delta[base : base + units], delta[base + units : base + frames]
            d5[0, at, :] = even[:, 0:128]
            d5[1, at, :] = even[:, 128:256]
            d5[2, at, :] = odd[:, 0:128]
            d5[3, at, :] = odd[:, 128:256]
            d5[4, at, :] = even[:, 256:384] + swap_halves(odd[:, 256:384])
        return 0

    lax.fori_loop(0, PIX // group, pixels, 0)

    m32[0:PIX, :] = jnp.zeros((PIX, ch2), F32)
    m32[rows + PIX : rows + 2 * PIX, :] = jnp.zeros((PIX, ch2), F32)

    def mix(i, _):
        at = pl.ds(pl.multiple_of(i * chunk, 8), chunk)
        delta = jnp.concatenate([d5[c, at, :] for c in range(5)], axis=1)
        m = (act_ref[at, :].astype(F32) + delta).astype(BF16)
        m_ref[at, :] = m
        m32[pl.ds(pl.multiple_of(i * chunk + PIX, 8), chunk), :] = m.astype(F32)
        return 0

    lax.fori_loop(0, rows // chunk, mix, 0)
    big = 192

    def temporal(i, _):
        r0 = i * big
        src = sources(m32, r0, big, frames, len_ref)
        total = src[1] + jnp.dot(
            jnp.concatenate([v.astype(BF16) for v in src], axis=1),
            tw[...],
            preferred_element_type=F32,
        )
        even, odd, tail = join_pair(total[:big], total[big:])
        at = pl.ds(pl.multiple_of(r0, 8), big)
        o_ref[at, 0:256] = even.astype(BF16)
        o_ref[at, 256:512] = odd.astype(BF16)
        o_ref[at, 512:640] = tail.astype(BF16)
        return 0

    lax.fori_loop(0, rows // big, temporal, 0)


def grad_kernel(len_ref, m_ref, cot_ref, o_ref, m32, total):
    rows, ch2 = cot_ref.shape
    ch = ch2 // 2
    pad = dst_tile(ch)
    frames = rows // PIX * 2
    big = 192
    m32[0:PIX, :] = jnp.zeros((PIX, ch2), F32)
    m32[rows + PIX : rows + 2 * PIX, :] = jnp.zeros((PIX, ch2), F32)

    def load(i, _):
        at = pl.ds(pl.multiple_of(i * big, 8), big)
        m32[pl.ds(pl.multiple_of(i * big + PIX, 8), big), :] = m_ref[at, :].astype(F32)
        return 0

    lax.fori_loop(0, rows // big, load, 0)
    total[...] = jnp.zeros_like(total)

    def step(i, _):
        r0 = i * big
        src = sources(m32, r0, big, frames, len_ref)
        src = jnp.concatenate([v.astype(BF16) for v in src], axis=1)
        cot = split_pair(cot_ref[pl.ds(pl.multiple_of(r0, 8), big), :].astype(F32))
        cot = jnp.concatenate(cot, axis=0).astype(BF16)
        total[...] += lax.dot_general(
            cot, src, (((0,), (0,)), ((), ())), preferred_element_type=F32
        )
        return 0

    lax.fori_loop(0, rows // big, step, 0)
    for j in range(3):
        o_ref[j * ch : (j + 1) * ch, :] = total[:, j * pad : (j + 1) * pad].T[:ch, :ch]


def tree(parts):
    while len(parts) > 1:
        parts = [parts[i] + parts[i + 1] for i in range(0, len(parts), 2)]
    return parts[0]


def swaps(n, k):
    return [(i, i ^ k) for i in range(n)]


def reduce_all(g):
    core = lax.axis_index("c")
    n_plane = lax.axis_size("y") * lax.axis_size("x")
    place = lax.axis_index("y") * lax.axis_size("x") + lax.axis_index("x")
    n_z = lax.axis_size("z")
    half = g.shape[0] // 2
    share = half // n_plane

    def cut(v, i, size):
        return lax.dynamic_slice_in_dim(v, i * size, size, 0)

    other = lax.ppermute(cut(g, 1 - core, half).astype(BF16), "c", swaps(2, 1))
    g = cut(g, core, half) + other.astype(F32)
    parts = [cut(g, place, share)]
    for k in range(1, n_plane):
        sent = cut(g, place ^ k, share).astype(BF16)
        parts.append(lax.ppermute(sent, PLANE, swaps(n_plane, k)).astype(F32))
    mine = tree(parts).astype(BF16)
    parts = [mine.astype(F32)]
    for k in range(1, n_z):
        parts.append(lax.ppermute(mine, "z", swaps(n_z, k)).astype(F32))
    total = tree(parts).astype(BF16)
    parts = [total] + [lax.ppermute(total, PLANE, swaps(n_plane, k)) for k in range(1, n_plane)]
    stacked = jnp.stack(parts)
    ordered = jnp.concatenate(
        [lax.dynamic_index_in_dim(stacked, place ^ j, 0, False) for j in range(n_plane)], 0
    )
    other = lax.ppermute(ordered, "c", swaps(2, 1))
    low = jnp.where(core == 0, ordered, other)
    high = jnp.where(core == 0, other, ordered)
    return jnp.concatenate([low, high], 0).astype(F32)


def exchange(x):
    shape = x.shape
    flat = x.reshape(shape[0], shape[1] * shape[2], shape[3])
    flat = lax.all_to_all(flat, SEQ, split_axis=0, concat_axis=0, tiled=True)
    return flat.reshape(shape)


def body(
    latents,
    clip_lengths,
    timesteps,
    spatial_weight,
    time_weight,
    query_weight,
    key_weight,
    value_weight,
    out_weight,
    temporal_weight,
    cotangent,
):
    f_dev, rows, across, ch = latents.shape
    shards = lax.axis_size("z") * lax.axis_size("y") * lax.axis_size("c")
    n_rows = lax.axis_size("x")
    assert rows * across <= shards * PIX and shards % rows == 0 and f_dev % 2 == 0
    half = f_dev // 2
    packed = jax.ShapeDtypeStruct((shards, half, PIX, 2 * ch), BF16)
    positions = f_dev * rows * across
    size = positions * ch * 2
    dense = 2 * positions * ch * ch

    row = lax.axis_index("x")
    if n_rows == 2:
        edge = jnp.where(row == 0, latents[:, rows - 1], latents[:, 0])
        got = lax.ppermute(edge, "x", swaps(2, 1))
        top, bot = got, got
    else:
        up = [(i, i + 1) for i in range(n_rows - 1)]
        top = lax.ppermute(latents[:, rows - 1], "x", up)
        bot = lax.ppermute(latents[:, 0], "x", [(j, i) for i, j in up])
    flags = jnp.stack([row > 0, row < n_rows - 1]).astype(jnp.int32)

    table = time_table(timesteps, time_weight)
    seq = (lax.axis_index("z") * lax.axis_size("y") + lax.axis_index("y")) * 2 + lax.axis_index("c")
    frame = seq * f_dev + jnp.arange(f_dev, dtype=jnp.int32)
    local_ids = jnp.sum(
        (frame[:, None] >= jnp.cumsum(clip_lengths)[None, :]).astype(jnp.int32), axis=1
    )
    active = call(
        conv_kernel,
        packed,
        [SMEM, SMEM, VMEM, VMEM, VMEM, VMEM, VMEM],
        flops=9 * dense,
        bytes_accessed=2 * size + 9 * ch * ch * 2,
    )(flags, local_ids, latents, top, bot, spatial_weight, table)
    active = exchange(active)

    cot = call(pack_kernel, packed, [VMEM], bytes_accessed=2 * size)(cotangent)
    cot, active = lax.optimization_barrier((cot, active))
    cot = exchange(cot)

    n_packed = shards * half * PIX
    flat = jax.ShapeDtypeStruct((n_packed, 2 * ch), BF16)
    units = n_packed // PIX
    tiles = -(-ch // 128)
    columns = pltpu.VMEM((5, n_packed, 128), F32)
    shifted = pltpu.VMEM((n_packed + 2 * PIX, 2 * ch), F32)
    pad = tiles * 128
    block, mixed = call(
        attention_kernel,
        (flat, flat),
        [SMEM] + [VMEM] * 6,
        scratch=[
            columns,
            columns,
            shifted,
            pltpu.VMEM((2 * units, 2 * units), F32),
            pltpu.VMEM((pad, 3 * pad), BF16),
            pltpu.VMEM((pad, pad), BF16),
            pltpu.VMEM((3 * pad, pad), BF16),
        ],
        flops=10 * dense,
        bytes_accessed=3 * size,
    )(
        clip_lengths,
        active.reshape(flat.shape),
        query_weight,
        key_weight,
        value_weight,
        out_weight,
        temporal_weight,
    )
    block = exchange(block.reshape(packed.shape))
    grads = call(
        grad_kernel,
        jax.ShapeDtypeStruct((3 * ch, ch), F32),
        [SMEM, VMEM, VMEM],
        scratch=[shifted, pltpu.VMEM((pad, 3 * pad), F32)],
        flops=3 * dense,
        bytes_accessed=2 * size + 3 * ch * ch * 4,
    )(clip_lengths, mixed, cot.reshape(flat.shape))
    grads = reduce_all(grads).reshape(3, ch, ch)
    block_out = call(
        unpack_kernel,
        jax.ShapeDtypeStruct(latents.shape, BF16),
        [VMEM],
        bytes_accessed=2 * size,
    )(block)
    return block_out, grads


def solution(mesh):
    n_seq, n_row = mesh.devices.shape
    grid = Mesh(mesh.devices.reshape(n_seq // 4, 2, 2, n_row), ("z", "y", "c", "x"))
    spread = P(SEQ, "x", None, None)
    in_specs = (spread,) + (P(),) * 9 + (spread,)
    return jax.shard_map(
        body, mesh=grid, in_specs=in_specs, out_specs=(spread, P()), check_vma=False
    )
```

time: 144 us -> 142 us (0.986)
  Pallas kernels: 48.1 us -> 42.7 us
  waiting for transfers between devices: 49.6 us -> 52.3 us
    pallas_call x1, Pallas kernels: 24 us -> 19.1 us  [body(): call(attention_kernel, (flat, flat), [SMEM] + [VMEM] * 6, scratch=[column...]
    all_to_all x3, waiting for transfers between devices: 19.1 us -> 21.9 us  [exchange(): flat = lax.all_to_all(flat, SEQ, split_axis=0, concat_axis=0, tiled=True)]
  transfers between devices with their start and end apart: 15 -> 15, of which waited for: 9 -> 10; matrix products, arithmetic and copies ran while one was open for 4% -> 4% of each run, Pallas kernels for 21% -> 17%
where the time goes in v1:
time: 142 us
  waiting for transfers between devices  52.3 us (37%)
  Pallas kernels  42.7 us (30%)
  starting transfers between devices  34.3 us (24%)
  other arithmetic  6.77 us (5%)
  local copies, waits for them, and re-layouts  3.99 us (3%)
    all_to_all x3, waiting for transfers between devices, exchange(): flat = lax.all_to_all(flat, SEQ, split_axis=0, concat_axis=0, tiled=True)  21.9 us
    pallas_call x1, Pallas kernels, body(): call(attention_kernel, (flat, flat), [SMEM] + [VMEM] * 6, scratch=[column...  19.1 us
    all_to_all x3, starting transfers between devices, exchange(): flat = lax.all_to_all(flat, SEQ, split_axis=0, concat_axis=0, tiled=True)  19 us
    ppermute x3, waiting for transfers between devices, reduce_all(): parts.append(lax.ppermute(mine, 'z', swaps(n_z, k)).astype(F32))  12.1 us
    pallas_call x1, Pallas kernels, body(): call(conv_kernel, packed, [SMEM, SMEM, VMEM, VMEM, VMEM, VMEM, VMEM], flo...  11.3 us
    ppermute x3, waiting for transfers between devices, reduce_all(): parts.append(lax.ppermute(sent, PLANE, swaps(n_plane, k)).astype(F32))  10.2 us
    pallas_call x1, Pallas kernels, body(): call(grad_kernel, jax.ShapeDtypeStruct((3 * ch, ch), F32), [SMEM, VMEM, V...  6.73 us
    ppermute x3, waiting for transfers between devices, reduce_all(): lax.ppermute(total, PLANE, swaps(n_plane, k))  4.91 us
  transfers between devices with their start and end apart: 15, of which 10 were waited for; matrix products, arithmetic and copies ran while one was open for 4% of the time, Pallas kernels for 17%

profile of v1, /device:TPU:0, one launch (start us, length us, event | category | flops | bytes accessed | tf_op | source)
XLA Modules:
  0.0 141.8 jit_solution(9232247127754671029)
XLA Ops:
  0.7 1.1 fusion
  1.8 3.0 %collective-permute-start = (bf16[12,32,320]{2,1,0:T(8,128)(2,1)S(1)}, bf16[12,32,320]{2,1,0:T(8,128)(2,1)S(1)}, u32[]{:S(2)}, u32[]{:S(2)}) collective-permute-start(bf16[12,32,320]{2,1,0:T(8,128)(2,1)S(1)} %fusion), channel_id=1, source_target_pairs={{0,1},{1,0},{2,3},{3,2},{4,5},{5,4},{6,7},{7,6},{8,9},{9,8},{10,11... | collective-permute-start | bytes 737288 | tf_op jit(solution)/shard_map/ppermute | solution.py:445
  4.8 0.8 reduce-window.8
  7.7 0.9 fusion.1.table_ref
  8.6 3.2 %collective-permute-done.top_ref.bot_ref = bf16[12,32,320]{2,1,0:T(8,128)(2,1)S(1)} collective-permute-done((bf16[12,32,320]{2,1,0:T(8,128)(2,1)S(1)}, bf16[12,32,320]{2,1,0:T(8,128)(2,1)S(1)}, u32[]{:S(2)}, u32[]{:S(2)}) %collective-permute-start) | collective-permute-done | bytes 245792 | tf_op jit(solution)/shard_map/ppermute | solution.py:445
  11.8 0.7 copy-done.5
  12.5 11.3 %shard_map.123 = bf16[16,6,8,640]{3,2,1,0:T(8,128)(2,1)} custom-call(s32[2]{0:T(128)} %add_convert_fusion.2.flag_ref, s32[12]{0:T(128)} %convert_reduce_fusion.id_ref, bf16[12,4,32,320]{3,2,1,0:T(8,128)(2,1)} %lat_ref.1, bf16[12,32,320]{2,1,0:T(8,128)(2,1)} %copy-done.5, bf16[12,32,320]{2,1,0:T(8,128)(2,1)} %copy-done.5, bf16[3,3,320,320]{3,2,1,0:T(8,128)(2,1)} %w_ref.1, ...), custom_call_target="tpu_custom_call" | custom-call | flops 2831155200 | bytes 3809280 | tf_op jit(solution)/shard_map/pallas_call | solution.py:459
  23.8 6.2 %all-to-all-start = ((bf16[16,48,640]{2,1,0:T(8,128)(2,1)}), bf16[16,48,640]{2,1,0:T(8,128)(2,1)S(1)}, u32[]{:S(2)}, u32[]{:S(2)}) async-start(bf16[16,48,640]{2,1,0:T(8,128)(2,1)} %bitcast.39), calls=%async_computation | async-start | bytes 1966080 | tf_op jit(solution)/shard_map/all_to_all | solution.py:415
  30.0 2.7 %shard_map.122 = bf16[16,6,8,640]{3,2,1,0:T(8,128)(2,1)} custom-call(bf16[12,4,32,320]{3,2,1,0:T(8,128)(2,1)} %x_ref.1), custom_call_target="tpu_custom_call" | custom-call | bytes 1966080 | tf_op jit(solution)/shard_map/pallas_call | solution.py:468
  32.8 19.1 %all-to-all-done = bf16[16,48,640]{2,1,0:T(8,128)(2,1)S(1)} async-done(((bf16[16,48,640]{2,1,0:T(8,128)(2,1)}), bf16[16,48,640]{2,1,0:T(8,128)(2,1)S(1)}, u32[]{:S(2)}, u32[]{:S(2)}) %all-to-all-start) | async-done | bytes 983072 | tf_op jit(solution)/shard_map/all_to_all | solution.py:415
  51.9 6.5 %all-to-all-start.2 = ((bf16[16,48,640]{2,1,0:T(8,128)(2,1)}), bf16[16,48,640]{2,1,0:T(8,128)(2,1)S(1)}, u32[]{:S(2)}, u32[]{:S(2)}) async-start(bf16[16,48,640]{2,1,0:T(8,128)(2,1)} %bitcast.35), calls=%async_computation.2 | async-start | bytes 1966080 | tf_op jit(solution)/shard_map/all_to_all | solution.py:415
  58.5 19.1 %shard_map.124 = (bf16[768,640]{1,0:T(8,128)(2,1)}, bf16[768,640]{1,0:T(8,128)(2,1)}) custom-call(s32[4]{0:T(128)} %len_ref.3, bf16[768,640]{1,0:T(8,128)(2,1)} %bitcast.37, bf16[320,320]{1,0:T(8,128)(2,1)} %wq_ref.1, bf16[320,320]{1,0:T(8,128)(2,1)} %wk_ref.1, bf16[320,320]{1,0:T(8,128)(2,1)} %wv_ref.1, bf16[320,320]{1,0:T(8,128)(2,1)} %wo_ref.1, ...), custom_call_target="tpu_custom_call" | custom-call | flops 3145728000 | bytes 2949120 | tf_op jit(solution)/shard_map/pallas_call | solution.py:479
  77.6 2.7 %all-to-all-done.2 = bf16[16,48,640]{2,1,0:T(8,128)(2,1)S(1)} async-done(((bf16[16,48,640]{2,1,0:T(8,128)(2,1)}), bf16[16,48,640]{2,1,0:T(8,128)(2,1)S(1)}, u32[]{:S(2)}, u32[]{:S(2)}) %all-to-all-start.2) | async-done | bytes 983072 | tf_op jit(solution)/shard_map/all_to_all | solution.py:415
  80.3 0.9 copy-done.3
  81.2 6.7 %shard_map.126 = f32[960,320]{1,0:T(8,128)} custom-call(s32[4]{0:T(128)} %len_ref.3, bf16[768,640]{1,0:T(8,128)(2,1)} %get-tuple-element.8.m_ref, bf16[768,640]{1,0:T(8,128)(2,1)} %bitcast.38), custom_call_target="tpu_custom_call" | custom-call | flops 943718400 | bytes 3194880 | tf_op jit(solution)/shard_map/pallas_call | solution.py:504
  88.0 1.3 dynamic-slice_convert_fusion
  89.8 6.3 %all-to-all-start.1 = ((bf16[16,48,640]{2,1,0:T(8,128)(2,1)}), bf16[16,48,640]{2,1,0:T(8,128)(2,1)S(1)}, u32[]{:S(2)}, u32[]{:S(2)}) async-start(bf16[16,48,640]{2,1,0:T(8,128)(2,1)} %bitcast.8), calls=%async_computation.1 | async-start | bytes 1966080 | tf_op jit(solution)/shard_map/all_to_all | solution.py:415
  96.2 1.1 convert_add_fusion
  97.3 1.6 %collective-permute-start.2 = (bf16[120,320]{1,0:T(8,128)(2,1)S(1)}, bf16[120,320]{1,0:T(8,128)(2,1)S(1)}, u32[]{:S(2)}, u32[]{:S(2)}) collective-permute-start(bf16[120,320]{1,0:T(8,128)(2,1)S(1)} %get-tuple-element.12), channel_id=1, source_target_pairs={{0,1},{1,0},{4,5},{5,4},{2,3},{3,2},{6,7},{7,6},{8,9},{9,8},{12,13... | collective-permute-start | bytes 230408 | tf_op jit(solution)/shard_map/ppermute | solution.py:395
  98.9 1.9 %collective-permute-start.3 = (bf16[120,320]{1,0:T(8,128)(2,1)S(1)}, bf16[120,320]{1,0:T(8,128)(2,1)S(1)}, u32[]{:S(2)}, u32[]{:S(2)}) collective-permute-start(bf16[120,320]{1,0:T(8,128)(2,1)S(1)} %get-tuple-element.14), channel_id=1, source_target_pairs={{0,4},{1,5},{4,0},{5,1},{2,6},{3,7},{6,2},{7,3},{8,12},{9,13},{12,... | collective-permute-start | bytes 230408 | tf_op jit(solution)/shard_map/ppermute | solution.py:395
  100.9 1.4 %collective-permute-done.2 = bf16[120,320]{1,0:T(8,128)(2,1)S(1)} collective-permute-done((bf16[120,320]{1,0:T(8,128)(2,1)S(1)}, bf16[120,320]{1,0:T(8,128)(2,1)S(1)}, u32[]{:S(2)}, u32[]{:S(2)}) %collective-permute-start.2) | collective-permute-done | bytes 76832 | tf_op jit(solution)/shard_map/ppermute | solution.py:395
  102.3 8.8 %collective-permute-done.3 = bf16[120,320]{1,0:T(8,128)(2,1)S(1)} collective-permute-done((bf16[120,320]{1,0:T(8,128)(2,1)S(1)}, bf16[120,320]{1,0:T(8,128)(2,1)S(1)}, u32[]{:S(2)}, u32[]{:S(2)}) %collective-permute-start.3) | collective-permute-done | bytes 76832 | tf_op jit(solution)/shard_map/ppermute | solution.py:395
  111.3 4.2 %collective-permute-start.6 = (bf16[120,320]{1,0:T(8,128)(2,1)S(1)}, bf16[120,320]{1,0:T(8,128)(2,1)S(1)}, u32[]{:S(2)}, u32[]{:S(2)}) collective-permute-start(bf16[120,320]{1,0:T(8,128)(2,1)S(1)} %add_convert_fusion.1), channel_id=1, source_target_pairs={{0,16},{8,24},{16,0},{24,8},{1,17},{9,25},{17,1},{25,9},{2,18},{10... | collective-permute-start | bytes 230408 | tf_op jit(solution)/shard_map/ppermute | solution.py:399
  116.0 11.6 %collective-permute-done.6 = bf16[120,320]{1,0:T(8,128)(2,1)S(1)} collective-permute-done((bf16[120,320]{1,0:T(8,128)(2,1)S(1)}, bf16[120,320]{1,0:T(8,128)(2,1)S(1)}, u32[]{:S(2)}, u32[]{:S(2)}) %collective-permute-start.6) | collective-permute-done | bytes 76832 | tf_op jit(solution)/shard_map/ppermute | solution.py:399
  127.8 1.6 %collective-permute-start.8 = (bf16[120,320]{1,0:T(8,128)(2,1)S(1)}, bf16[120,320]{1,0:T(8,128)(2,1)S(1)}, u32[]{:S(2)}, u32[]{:S(2)}) collective-permute-start(bf16[120,320]{1,0:T(8,128)(2,1)S(1)} %add_convert_fusion), channel_id=1, source_target_pairs={{0,1},{1,0},{4,5},{5,4},{2,3},{3,2},{6,7},{7,6},{8,9},{9,8},{12,13... | collective-permute-start | bytes 230408 | tf_op jit(solution)/shard_map/ppermute | solution.py:401
  129.3 1.5 %collective-permute-start.9 = (bf16[120,320]{1,0:T(8,128)(2,1)S(1)}, bf16[120,320]{1,0:T(8,128)(2,1)S(1)}, u32[]{:S(2)}, u32[]{:S(2)}) collective-permute-start(bf16[120,320]{1,0:T(8,128)(2,1)S(1)} %add_convert_fusion), channel_id=1, source_target_pairs={{0,4},{1,5},{4,0},{5,1},{2,6},{3,7},{6,2},{7,3},{8,12},{9,13},{12,... | collective-permute-start | bytes 230408 | tf_op jit(solution)/shard_map/ppermute | solution.py:401
  131.3 1.5 %collective-permute-done.8 = bf16[120,320]{1,0:T(8,128)(2,1)S(1)} collective-permute-done((bf16[120,320]{1,0:T(8,128)(2,1)S(1)}, bf16[120,320]{1,0:T(8,128)(2,1)S(1)}, u32[]{:S(2)}, u32[]{:S(2)}) %collective-permute-start.8) | collective-permute-done | bytes 76832 | tf_op jit(solution)/shard_map/ppermute | solution.py:401
  132.8 2.0 %collective-permute-done.9 = bf16[120,320]{1,0:T(8,128)(2,1)S(1)} collective-permute-done((bf16[120,320]{1,0:T(8,128)(2,1)S(1)}, bf16[120,320]{1,0:T(8,128)(2,1)S(1)}, u32[]{:S(2)}, u32[]{:S(2)}) %collective-permute-start.9) | collective-permute-done | bytes 76832 | tf_op jit(solution)/shard_map/ppermute | solution.py:401
  134.8 1.4 collective-permute-done.10
  136.5 0.9 copy-done.1
  137.5 2.8 %shard_map.125 = bf16[12,4,32,320]{3,2,1,0:T(8,128)(2,1)} custom-call(bf16[16,6,8,640]{3,2,1,0:T(8,128)(2,1)} %bitcast.34), custom_call_target="tpu_custom_call" | custom-call | bytes 1966080 | tf_op jit(solution)/shard_map/pallas_call | solution.py:513
  140.6 1.2 convert.1
  (35 shorter events, 4.7 us)
Async XLA Ops:
  0.6 7.1 %copy-start = (bf16[320,320]{1,0:T(8,128)(2,1)S(1)}, bf16[320,320]{1,0:T(8,128)(2,1)}, u32[]{:S(2)}) copy-start(bf16[320,320]{1,0:T(8,128)(2,1)} %param.15) | copy-start | bytes 614404
  1.8 10.0 %collective-permute-start = (bf16[12,32,320]{2,1,0:T(8,128)(2,1)S(1)}, bf16[12,32,320]{2,1,0:T(8,128)(2,1)S(1)}, u32[]{:S(2)}, u32[]{:S(2)}) collective-permute-start(bf16[12,32,320]{2,1,0:T(8,128)(2,1)S(1)} %fusion), channel_id=1, source_target_pairs={{0,1},{1,0},{2,3},{3,2},{4,5},{5,4},{6,7},{7,6},{8,9},{9,8},{10,11... | collective-permute-start | bytes 737288 | tf_op jit(solution)/shard_map/ppermute | solution.py:445
  11.8 0.7 copy-start.5
  23.8 28.1 %all-to-all-start = ((bf16[16,48,640]{2,1,0:T(8,128)(2,1)}), bf16[16,48,640]{2,1,0:T(8,128)(2,1)S(1)}, u32[]{:S(2)}, u32[]{:S(2)}) async-start(bf16[16,48,640]{2,1,0:T(8,128)(2,1)} %bitcast.39), calls=%async_computation | async-start | bytes 1966080 | tf_op jit(solution)/shard_map/all_to_all | solution.py:415
  51.9 6.5 %copy-start.2 = (bf16[16,48,640]{2,1,0:T(8,128)(2,1)}, bf16[16,48,640]{2,1,0:T(8,128)(2,1)S(1)}, u32[]{:S(2)}) copy-start(bf16[16,48,640]{2,1,0:T(8,128)(2,1)S(1)} %all-to-all-done) | copy-start | bytes 2949124
  51.9 28.4 %all-to-all-start.2 = ((bf16[16,48,640]{2,1,0:T(8,128)(2,1)}), bf16[16,48,640]{2,1,0:T(8,128)(2,1)S(1)}, u32[]{:S(2)}, u32[]{:S(2)}) async-start(bf16[16,48,640]{2,1,0:T(8,128)(2,1)} %bitcast.35), calls=%async_computation.2 | async-start | bytes 1966080 | tf_op jit(solution)/shard_map/all_to_all | solution.py:415
  80.3 0.9 copy-start.3
  88.0 8.2 %copy-start.4 = (f32[960,320]{1,0:T(8,128)S(1)}, f32[960,320]{1,0:T(8,128)}, u32[]{:S(2)}) copy-start(f32[960,320]{1,0:T(8,128)} %shard_map.126) | copy-start | bytes 3686404
  89.3 6.9 %collective-permute-start.1 = (bf16[480,320]{1,0:T(8,128)(2,1)S(1)}, bf16[480,320]{1,0:T(8,128)(2,1)}, u32[]{:S(2)}, u32[]{:S(2)}) collective-permute-start(bf16[480,320]{1,0:T(8,128)(2,1)S(1)} %dynamic-slice_convert_fusion), channel_id=1, source_target_pairs={{0,2},{2,0},{1,3},{3,1},{4,6},{6,4},{5,7},{7,5},{8,10},{10,8},{9,1... | collective-permute-start | bytes 921608 | tf_op jit(solution)/shard_map/ppermute | solution.py:390
  89.8 46.7 %all-to-all-start.1 = ((bf16[16,48,640]{2,1,0:T(8,128)(2,1)}), bf16[16,48,640]{2,1,0:T(8,128)(2,1)S(1)}, u32[]{:S(2)}, u32[]{:S(2)}) async-start(bf16[16,48,640]{2,1,0:T(8,128)(2,1)} %bitcast.8), calls=%async_computation.1 | async-start | bytes 1966080 | tf_op jit(solution)/shard_map/all_to_all | solution.py:415
  97.3 5.0 %collective-permute-start.2 = (bf16[120,320]{1,0:T(8,128)(2,1)S(1)}, bf16[120,320]{1,0:T(8,128)(2,1)S(1)}, u32[]{:S(2)}, u32[]{:S(2)}) collective-permute-start(bf16[120,320]{1,0:T(8,128)(2,1)S(1)} %get-tuple-element.12), channel_id=1, source_target_pairs={{0,1},{1,0},{4,5},{5,4},{2,3},{3,2},{6,7},{7,6},{8,9},{9,8},{12,13... | collective-permute-start | bytes 230408 | tf_op jit(solution)/shard_map/ppermute | solution.py:395
  98.9 12.2 %collective-permute-start.3 = (bf16[120,320]{1,0:T(8,128)(2,1)S(1)}, bf16[120,320]{1,0:T(8,128)(2,1)S(1)}, u32[]{:S(2)}, u32[]{:S(2)}) collective-permute-start(bf16[120,320]{1,0:T(8,128)(2,1)S(1)} %get-tuple-element.14), channel_id=1, source_target_pairs={{0,4},{1,5},{4,0},{5,1},{2,6},{3,7},{6,2},{7,3},{8,12},{9,13},{12,... | collective-permute-start | bytes 230408 | tf_op jit(solution)/shard_map/ppermute | solution.py:395
  100.8 10.4 %collective-permute-start.4 = (bf16[120,320]{1,0:T(8,128)(2,1)S(1)}, bf16[120,320]{1,0:T(8,128)(2,1)S(1)}, u32[]{:S(2)}, u32[]{:S(2)}) collective-permute-start(bf16[120,320]{1,0:T(8,128)(2,1)S(1)} %get-tuple-element.13), channel_id=1, source_target_pairs={{0,5},{1,4},{4,1},{5,0},{2,7},{3,6},{6,3},{7,2},{8,13},{9,12},{12,... | collective-permute-start | bytes 230408 | tf_op jit(solution)/shard_map/ppermute | solution.py:395
  111.2 4.9 %collective-permute-start.5 = (bf16[120,320]{1,0:T(8,128)(2,1)S(1)}, bf16[120,320]{1,0:T(8,128)(2,1)S(1)}, u32[]{:S(2)}, u32[]{:S(2)}) collective-permute-start(bf16[120,320]{1,0:T(8,128)(2,1)S(1)} %add_convert_fusion.1), channel_id=1, source_target_pairs={{0,8},{8,0},{16,24},{24,16},{1,9},{9,1},{17,25},{25,17},{2,10},{10... | collective-permute-start | bytes 230408 | tf_op jit(solution)/shard_map/ppermute | solution.py:399
  111.3 16.4 %collective-permute-start.6 = (bf16[120,320]{1,0:T(8,128)(2,1)S(1)}, bf16[120,320]{1,0:T(8,128)(2,1)S(1)}, u32[]{:S(2)}, u32[]{:S(2)}) collective-permute-start(bf16[120,320]{1,0:T(8,128)(2,1)S(1)} %add_convert_fusion.1), channel_id=1, source_target_pairs={{0,16},{8,24},{16,0},{24,8},{1,17},{9,25},{17,1},{25,9},{2,18},{10... | collective-permute-start | bytes 230408 | tf_op jit(solution)/shard_map/ppermute | solution.py:399
  115.4 12.3 %collective-permute-start.7 = (bf16[120,320]{1,0:T(8,128)(2,1)S(1)}, bf16[120,320]{1,0:T(8,128)(2,1)S(1)}, u32[]{:S(2)}, u32[]{:S(2)}) collective-permute-start(bf16[120,320]{1,0:T(8,128)(2,1)S(1)} %add_convert_fusion.1), channel_id=1, source_target_pairs={{0,24},{8,16},{16,8},{24,0},{1,25},{9,17},{17,9},{25,1},{2,26},{10... | collective-permute-start | bytes 230408 | tf_op jit(solution)/shard_map/ppermute | solution.py:399
  127.8 5.1 %collective-permute-start.8 = (bf16[120,320]{1,0:T(8,128)(2,1)S(1)}, bf16[120,320]{1,0:T(8,128)(2,1)S(1)}, u32[]{:S(2)}, u32[]{:S(2)}) collective-permute-start(bf16[120,320]{1,0:T(8,128)(2,1)S(1)} %add_convert_fusion), channel_id=1, source_target_pairs={{0,1},{1,0},{4,5},{5,4},{2,3},{3,2},{6,7},{7,6},{8,9},{9,8},{12,13... | collective-permute-start | bytes 230408 | tf_op jit(solution)/shard_map/ppermute | solution.py:401
  129.3 5.5 %collective-permute-start.9 = (bf16[120,320]{1,0:T(8,128)(2,1)S(1)}, bf16[120,320]{1,0:T(8,128)(2,1)S(1)}, u32[]{:S(2)}, u32[]{:S(2)}) collective-permute-start(bf16[120,320]{1,0:T(8,128)(2,1)S(1)} %add_convert_fusion), channel_id=1, source_target_pairs={{0,4},{1,5},{4,0},{5,1},{2,6},{3,7},{6,2},{7,3},{8,12},{9,13},{12,... | collective-permute-start | bytes 230408 | tf_op jit(solution)/shard_map/ppermute | solution.py:401
  130.8 5.5 %collective-permute-start.10 = (bf16[120,320]{1,0:T(8,128)(2,1)S(1)}, bf16[120,320]{1,0:T(8,128)(2,1)S(1)}, u32[]{:S(2)}, u32[]{:S(2)}) collective-permute-start(bf16[120,320]{1,0:T(8,128)(2,1)S(1)} %add_convert_fusion), channel_id=1, source_target_pairs={{0,5},{1,4},{4,1},{5,0},{2,7},{3,6},{6,3},{7,2},{8,13},{9,12},{12,... | collective-permute-start | bytes 230408 | tf_op jit(solution)/shard_map/ppermute | solution.py:401
  136.4 3.9 %collective-permute-start.11 = (bf16[480,320]{1,0:T(8,128)(2,1)S(1)}, bf16[480,320]{1,0:T(8,128)(2,1)S(1)}, u32[]{:S(2)}, u32[]{:S(2)}) collective-permute-start(bf16[480,320]{1,0:T(8,128)(2,1)S(1)} %pad_maximum_fusion.2), channel_id=1, source_target_pairs={{0,2},{2,0},{1,3},{3,1},{4,6},{6,4},{5,7},{7,5},{8,10},{10,8},{9,1... | collective-permute-start | bytes 921608 | tf_op jit(solution)/shard_map/ppermute | solution.py:406
  136.5 0.9 copy-start.1

commit v2 on v1

--- a/solution.py
+++ b/solution.py
@@ -17,6 +17,7 @@
 VMEM = pltpu.VMEM
 SMEM = pltpu.SMEM
 PIX = 8
+BIG = 384
 
 
 def time_table(timesteps, time_weight):
@@ -37,17 +38,8 @@
         cost_estimate=pl.CostEstimate(
             flops=flops, bytes_accessed=bytes_accessed, transcendentals=0
         ),
-        compiler_params=pltpu.CompilerParams(vmem_limit_bytes=56 * 2**20),
+        compiler_params=pltpu.CompilerParams(vmem_limit_bytes=40 * 2**20),
         **kw,
-    )
-
-
-def pack_pair(ref, index, first, second):
-    wide = first.shape[-1] // 128 * 128
-    ref[index + (slice(None), slice(0, wide))] = first[:, :wide]
-    ref[index + (slice(None), slice(wide, 2 * wide))] = second[:, :wide]
-    ref[index + (slice(None), slice(2 * wide, 2 * first.shape[-1]))] = jnp.concatenate(
-        [first[:, wide:], second[:, wide:]], axis=-1
     )
 
 
@@ -67,22 +59,25 @@
     return jnp.concatenate([piece, jnp.zeros((PIX - real, row.shape[-1]), F32)], 0).astype(BF16)
 
 
-def pack_kernel(x_ref, o_ref):
+def pack_kernel(x_ref, early_ref, late_ref):
     frames, rows, across, ch = x_ref.shape
     half = frames // 2
-    groups = o_ref.shape[0] // rows
-    real = across // groups
-
-    def step(t, _):
-        for i in range(rows):
-            first, second = x_ref[2 * t, i], x_ref[2 * t + 1, i]
-            for g in range(groups):
-                pack_pair(
-                    o_ref, (i * groups + g, t), take(first, g, real), take(second, g, real)
-                )
-        return 0
-
-    lax.fori_loop(0, half, step, 0)
+    real = across * rows // early_ref.shape[0]
+    wide = 256
+    for o_ref, start in ((early_ref, 0), (late_ref, half // 2)):
+
+        def step(t, _, o_ref=o_ref, start=start):
+            flat = [
+                jnp.concatenate([x_ref[2 * (t + start) + q, i] for i in range(rows)], axis=0)
+                for q in range(2)
+            ]
+            for q in range(2):
+                store_groups(o_ref, t, slice(q * wide, (q + 1) * wide), flat[q][:, :wide], real)
+            tail = jnp.concatenate([flat[0][:, wide:], flat[1][:, wide:]], axis=1)
+            store_groups(o_ref, t, slice(2 * wide, 2 * ch), tail, real)
+            return 0
+
+        lax.fori_loop(0, half // 2, step, 0)
 
 
 def unpack_kernel(x_ref, o_ref):
@@ -109,48 +104,118 @@
     lax.fori_loop(0, half, step, 0)
 
 
-def conv_kernel(flag_ref, id_ref, lat_ref, top_ref, bot_ref, w_ref, table_ref, o_ref):
+def conv_weight_kernel(w_ref, o_ref):
+    ch = w_ref.shape[-1]
+    wide = 256
+    rest = ch - wide
+    none = jnp.zeros((ch, rest), BF16)
+    for a in range(3):
+        taps = [w_ref[a, b] for b in range(3)]
+        tails = [
+            jnp.concatenate([taps[0][:, wide:], taps[1][:, wide:]], axis=1),
+            jnp.concatenate([taps[2][:, wide:], none], axis=1),
+        ]
+        for src, dst, size in ((0, a * wide, wide), (wide, 3 * wide + a * rest, rest)):
+            rows = pl.ds(dst, size)
+            for b in range(3):
+                o_ref[rows, b * wide : (b + 1) * wide] = taps[b][src : src + size, :wide]
+            for k in range(2):
+                o_ref[rows, 3 * wide + k * 128 : 3 * wide + (k + 1) * 128] = tails[k][
+                    src : src + size
+                ]
+    o_ref[3 * wide + 3 * rest :, :] = jnp.zeros((rest, 4 * wide), BF16)
+
+
+def store_groups(o_ref, t, lanes, value, real):
+    shards = o_ref.shape[0]
+    value = value.astype(BF16)
+    if real == PIX:
+        o_ref[:, t, :, lanes] = value.reshape(shards, PIX, value.shape[-1])
+        return
+    for d in range(shards):
+        o_ref[d, t, :, lanes] = take(value, d, real)
+
+
+def silu(v):
+    return 0.5 * v * (1.0 + jnp.tanh(0.5 * v))
+
+
+def conv_kernel(flag_ref, len_ref, lat_ref, top_ref, bot_ref, w_ref, table_ref, o_ref):
     frames, rows, across, ch = lat_ref.shape
-    half = frames // 2
-    groups = o_ref.shape[0] // rows
-    real = across // groups
-
-    def step(t, _):
+    real = across * rows // o_ref.shape[0]
+    wide = 256
+    pos = rows * across
+    low = low_lanes()
+    pairs = 3 if (frames // 2) % 3 == 0 else 1
+    count = 2 * pairs
+
+    def clip_of(frame):
+        bound = jnp.int32(0)
+        place = jnp.int32(0)
+        for k in range(CLIPS):
+            bound = bound + len_ref[k]
+            place = place + jnp.where(frame >= bound, 1, 0)
+        return jnp.minimum(place, CLIPS - 1)
+
+    def step(g, _):
         kept = []
-        for base in (0, 1):
-            top = top_ref[2 * t + base]
-            bot = bot_ref[2 * t + base]
+        for k in range(count):
+            f = g * count + k
+            top, bot = top_ref[f], bot_ref[f]
             top = jnp.where(flag_ref[0] > 0, top, jnp.zeros_like(top))
             bot = jnp.where(flag_ref[1] > 0, bot, jnp.zeros_like(bot))
-            lat = [lat_ref[2 * t + base, i] for i in range(rows)]
-            kept.append([top] + lat + [bot])
-        n_rows = 2 * rows * across
-        sums = []
-        windows = [
-            jnp.concatenate([r for s in kept for r in s[a : a + rows]], axis=0) for a in range(3)
+            kept.append([top] + [lat_ref[f, i] for i in range(rows)] + [bot])
+        window = [
+            jnp.concatenate([r for lines in kept for r in lines[a : a + rows]], axis=0)
+            for a in range(3)
         ]
-        for b in range(3):
-            acc = jnp.zeros((n_rows, ch), F32)
-            for a in range(3):
-                acc = acc + jnp.dot(windows[a], w_ref[a, b], preferred_element_type=F32)
-            sums.append(acc)
-        col = lax.broadcasted_iota(jnp.int32, (n_rows, ch), 0) & (across - 1)
-        left = jnp.where(col == 0, 0.0, pltpu.roll(sums[0], 1, 0))
-        right = jnp.where(col == across - 1, 0.0, pltpu.roll(sums[2], n_rows - 1, 0))
-        spatial = sums[1] + left + right
-        per = rows * across
-        outs = []
-        for k in (0, 1):
-            emb = table_ref[pl.ds(id_ref[2 * t + k], 1), :]
-            v = spatial[k * per : (k + 1) * per] + emb
-            silu = 0.5 * v * (1.0 + jnp.tanh(0.5 * v))
-            res = windows[1][k * per : (k + 1) * per].astype(F32)
-            outs.append((res + silu).astype(BF16))
-        for d in range(rows * groups):
-            pack_pair(o_ref, (d, t), take(outs[0], d, real), take(outs[1], d, real))
+        tails = [w[:, wide:] for w in window]
+        x = jnp.concatenate(
+            [w[:, :wide] for w in window]
+            + [
+                jnp.concatenate([tails[0], tails[1]], axis=1),
+                jnp.concatenate([tails[2], jnp.zeros_like(tails[2])], axis=1),
+            ],
+            axis=1,
+        )
+        y = jnp.dot(x, w_ref[...], preferred_element_type=F32)
+        n = count * pos
+        col = lax.broadcasted_iota(jnp.int32, (n, 128), 0) & (across - 1)
+        first, last = col == 0, col == across - 1
+
+        def shifted(left, right):
+            return jnp.where(first, 0.0, pltpu.roll(left, 1, 0)) + jnp.where(
+                last, 0.0, pltpu.roll(right, n - 1, 0)
+            )
+
+        cols = []
+        for c in range(2):
+            at = lambda b: y[:, b * wide + c * 128 : b * wide + (c + 1) * 128]
+            cols.append(shifted(at(0), at(2)) + at(1))
+        mid = y[:, 3 * wide : 3 * wide + 128]
+        side = shifted(mid, y[:, 3 * wide + 128 :])
+        for k in range(pairs):
+            t = g * pairs + k
+            even = slice(2 * k * pos, (2 * k + 1) * pos)
+            odd = slice((2 * k + 1) * pos, (2 * k + 2) * pos)
+            base = flag_ref[2] + 2 * t
+            emb = [table_ref[pl.ds(clip_of(base + q), 1), :] for q in range(2)]
+            for q, rs in enumerate((even, odd)):
+                for c in range(2):
+                    lanes = slice(c * 128, (c + 1) * 128)
+                    v = cols[c][rs] + emb[q][:, lanes]
+                    got = window[1][rs, lanes].astype(F32) + silu(v)
+                    dst = slice(q * wide + c * 128, q * wide + (c + 1) * 128)
+                    store_groups(o_ref, t, dst, got, real)
+            tail = jnp.where(
+                low, side[even] + swap_halves(mid[even]), swap_halves(side[odd]) + mid[odd]
+            )
+            tail = tail + jnp.concatenate([emb[0][:, wide:], emb[1][:, wide:]], axis=1)
+            res = jnp.concatenate([tails[1][even], tails[1][odd]], axis=1).astype(F32)
+            store_groups(o_ref, t, slice(2 * wide, 2 * wide + 128), res + silu(tail), real)
         return 0
 
-    lax.fori_loop(0, half, step, 0)
+    lax.fori_loop(0, frames // count, step, 0)
 
 
 def low_lanes():
@@ -200,9 +265,23 @@
     return previous, stack(*cur), following
 
 
+def prepare_kernel(len_ref, wq_ref, wk_ref, wv_ref, wo_ref, tw_ref, wqkv, wo, tw, bias):
+    pad = wo.shape[0]
+    frames = bias.shape[0]
+    units = frames // 2
+    for j, ref in enumerate((wq_ref, wk_ref, wv_ref)):
+        pad_weight(wqkv, ref[...], 0, j * pad)
+    pad_weight(wo, wo_ref[...], 0, 0)
+    for j in range(3):
+        pad_weight(tw, tw_ref[j], j * pad, 0)
+    place = lambda axis: lax.broadcasted_iota(jnp.int32, (frames, frames), axis)
+    frame = lambda i: jnp.where(i < units, 2 * i, 2 * (i - units) + 1)
+    same = clip_ids(frame(place(0)), len_ref) == clip_ids(frame(place(1)), len_ref)
+    bias[...] = jnp.where(same, 0.0, -1e30)
+
+
 def attention_kernel(
-    len_ref, act_ref, wq_ref, wk_ref, wv_ref, wo_ref, tw_ref, o_ref, m_ref,
-    n5, d5, m32, bias, wqkv, wo, tw,
+    act_ref, wqkv, wo, bias, m_ref, n5, d5
 ):
     rows, ch2 = act_ref.shape
     ch = ch2 // 2
@@ -210,17 +289,6 @@
     units = rows // PIX
     frames = units * 2
     head = ch // HEADS
-    for j, ref in enumerate((wq_ref, wk_ref, wv_ref)):
-        pad_weight(wqkv, ref[...], 0, j * pad)
-    pad_weight(wo, wo_ref[...], 0, 0)
-    for j in range(3):
-        pad_weight(tw, tw_ref[j], j * pad, 0)
-
-    place = lambda axis: lax.broadcasted_iota(jnp.int32, (frames, frames), axis)
-    frame = lambda i: jnp.where(i < units, 2 * i, 2 * (i - units) + 1)
-    same = clip_ids(frame(place(0)), len_ref) == clip_ids(frame(place(1)), len_ref)
-    bias[...] = jnp.where(same, 0.0, -1e30)
-
     chunk = 96
     low = low_lanes()
 
@@ -248,7 +316,7 @@
 
     factor = head ** (-0.5) * math.log2(math.e)
     lane = lax.broadcasted_iota(jnp.int32, (1, pad), 1)
-    group = 2
+    group = 4
 
     def pixels(i, _):
         parts = []
@@ -301,27 +369,41 @@
 
     lax.fori_loop(0, PIX // group, pixels, 0)
 
-    m32[0:PIX, :] = jnp.zeros((PIX, ch2), F32)
-    m32[rows + PIX : rows + 2 * PIX, :] = jnp.zeros((PIX, ch2), F32)
-
     def mix(i, _):
         at = pl.ds(pl.multiple_of(i * chunk, 8), chunk)
         delta = jnp.concatenate([d5[c, at, :] for c in range(5)], axis=1)
-        m = (act_ref[at, :].astype(F32) + delta).astype(BF16)
-        m_ref[at, :] = m
-        m32[pl.ds(pl.multiple_of(i * chunk + PIX, 8), chunk), :] = m.astype(F32)
+        m_ref[at, :] = (act_ref[at, :].astype(F32) + delta).astype(BF16)
         return 0
 
     lax.fori_loop(0, rows // chunk, mix, 0)
-    big = 192
+
+
+def temporal_kernel(
+    core_ref, len_ref, m_ref, early_ref, late_ref, tw,
+    o_ref, mine_ref, other_ref, m32, grad, full
+):
+    rows, ch2 = m_ref.shape
+    ch = ch2 // 2
+    pad = dst_tile(ch)
+    frames = rows // PIX * 2
+    big = BIG
+    m32[0:PIX, :] = jnp.zeros((PIX, ch2), F32)
+    m32[rows + PIX : rows + 2 * PIX, :] = jnp.zeros((PIX, ch2), F32)
+    m32[PIX : rows + PIX, :] = m_ref[...].astype(F32)
+    grad[...] = jnp.zeros_like(grad)
 
     def temporal(i, _):
         r0 = i * big
         src = sources(m32, r0, big, frames, len_ref)
-        total = src[1] + jnp.dot(
-            jnp.concatenate([v.astype(BF16) for v in src], axis=1),
-            tw[...],
-            preferred_element_type=F32,
+        rounded = jnp.concatenate([v.astype(BF16) for v in src], axis=1)
+        total = src[1] + jnp.dot(rounded, tw[...], preferred_element_type=F32)
+        each = early_ref.shape[1]
+        spans = big // (2 * each)
+        cot = [ref[i * spans + k] for k in range(spans) for ref in (early_ref, late_ref)]
+        cot = split_pair(jnp.concatenate([c.astype(F32) for c in cot], axis=0))
+        cot = jnp.concatenate(cot, axis=0).astype(BF16)
+        grad[...] += lax.dot_general(
+            cot, rounded, (((0,), (0,)), ((), ())), preferred_element_type=F32
         )
         even, odd, tail = join_pair(total[:big], total[big:])
         at = pl.ds(pl.multiple_of(r0, 8), big)
@@ -331,39 +413,12 @@
         return 0
 
     lax.fori_loop(0, rows // big, temporal, 0)
-
-
-def grad_kernel(len_ref, m_ref, cot_ref, o_ref, m32, total):
-    rows, ch2 = cot_ref.shape
-    ch = ch2 // 2
-    pad = dst_tile(ch)
-    frames = rows // PIX * 2
-    big = 192
-    m32[0:PIX, :] = jnp.zeros((PIX, ch2), F32)
-    m32[rows + PIX : rows + 2 * PIX, :] = jnp.zeros((PIX, ch2), F32)
-
-    def load(i, _):
-        at = pl.ds(pl.multiple_of(i * big, 8), big)
-        m32[pl.ds(pl.multiple_of(i * big + PIX, 8), big), :] = m_ref[at, :].astype(F32)
-        return 0
-
-    lax.fori_loop(0, rows // big, load, 0)
-    total[...] = jnp.zeros_like(total)
-
-    def step(i, _):
-        r0 = i * big
-        src = sources(m32, r0, big, frames, len_ref)
-        src = jnp.concatenate([v.astype(BF16) for v in src], axis=1)
-        cot = split_pair(cot_ref[pl.ds(pl.multiple_of(r0, 8), big), :].astype(F32))
-        cot = jnp.concatenate(cot, axis=0).astype(BF16)
-        total[...] += lax.dot_general(
-            cot, src, (((0,), (0,)), ((), ())), preferred_element_type=F32
-        )
-        return 0
-
-    lax.fori_loop(0, rows // big, step, 0)
     for j in range(3):
-        o_ref[j * ch : (j + 1) * ch, :] = total[:, j * pad : (j + 1) * pad].T[:ch, :ch]
+        full[j * ch : (j + 1) * ch, :] = grad[:, j * pad : (j + 1) * pad].T[:ch, :ch]
+    core = core_ref[0]
+    n = mine_ref.shape[0]
+    mine_ref[...] = full[pl.ds(pl.multiple_of(core * n, 8), n), :]
+    other_ref[...] = full[pl.ds(pl.multiple_of((1 - core) * n, 8), n), :].astype(BF16)
 
 
 def tree(parts):
@@ -376,28 +431,27 @@
     return [(i, i ^ k) for i in range(n)]
 
 
-def reduce_all(g):
+def reduce_all(g, other):
     core = lax.axis_index("c")
     n_plane = lax.axis_size("y") * lax.axis_size("x")
     place = lax.axis_index("y") * lax.axis_size("x") + lax.axis_index("x")
     n_z = lax.axis_size("z")
-    half = g.shape[0] // 2
-    share = half // n_plane
+    share = g.shape[0] // n_plane
 
     def cut(v, i, size):
         return lax.dynamic_slice_in_dim(v, i * size, size, 0)
 
-    other = lax.ppermute(cut(g, 1 - core, half).astype(BF16), "c", swaps(2, 1))
-    g = cut(g, core, half) + other.astype(F32)
+    g = g + lax.ppermute(other, "c", swaps(2, 1)).astype(F32)
     parts = [cut(g, place, share)]
     for k in range(1, n_plane):
         sent = cut(g, place ^ k, share).astype(BF16)
         parts.append(lax.ppermute(sent, PLANE, swaps(n_plane, k)).astype(F32))
-    mine = tree(parts).astype(BF16)
-    parts = [mine.astype(F32)]
-    for k in range(1, n_z):
-        parts.append(lax.ppermute(mine, "z", swaps(n_z, k)).astype(F32))
     total = tree(parts).astype(BF16)
+    step = 1
+    while step < n_z:
+        got = lax.ppermute(total, "z", swaps(n_z, step))
+        total = (total.astype(F32) + got.astype(F32)).astype(BF16)
+        step *= 2
     parts = [total] + [lax.ppermute(total, PLANE, swaps(n_plane, k)) for k in range(1, n_plane)]
     stacked = jnp.stack(parts)
     ordered = jnp.concatenate(
@@ -448,27 +502,27 @@
         up = [(i, i + 1) for i in range(n_rows - 1)]
         top = lax.ppermute(latents[:, rows - 1], "x", up)
         bot = lax.ppermute(latents[:, 0], "x", [(j, i) for i, j in up])
-    flags = jnp.stack([row > 0, row < n_rows - 1]).astype(jnp.int32)
-
+    seq = (lax.axis_index("z") * lax.axis_size("y") + lax.axis_index("y")) * 2 + lax.axis_index("c")
+    flags = jnp.stack([row > 0, row < n_rows - 1, seq * f_dev]).astype(jnp.int32)
     table = time_table(timesteps, time_weight)
-    seq = (lax.axis_index("z") * lax.axis_size("y") + lax.axis_index("y")) * 2 + lax.axis_index("c")
-    frame = seq * f_dev + jnp.arange(f_dev, dtype=jnp.int32)
-    local_ids = jnp.sum(
-        (frame[:, None] >= jnp.cumsum(clip_lengths)[None, :]).astype(jnp.int32), axis=1
-    )
+    taps = call(
+        conv_weight_kernel,
+        jax.ShapeDtypeStruct((1024, 1024), BF16),
+        [VMEM],
+        bytes_accessed=2 * size,
+    )(spatial_weight)
     active = call(
         conv_kernel,
         packed,
         [SMEM, SMEM, VMEM, VMEM, VMEM, VMEM, VMEM],
         flops=9 * dense,
         bytes_accessed=2 * size + 9 * ch * ch * 2,
-    )(flags, local_ids, latents, top, bot, spatial_weight, table)
+    )(flags, clip_lengths, latents, top, bot, taps, table)
+    part = jax.ShapeDtypeStruct((shards, half // 2, PIX, 2 * ch), BF16)
+    early, late = call(pack_kernel, (part, part), [VMEM], bytes_accessed=2 * size)(cotangent)
+    early = exchange(early)
+    early, active = lax.optimization_barrier((early, active))
     active = exchange(active)
-
-    cot = call(pack_kernel, packed, [VMEM], bytes_accessed=2 * size)(cotangent)
-    cot, active = lax.optimization_barrier((cot, active))
-    cot = exchange(cot)
-
     n_packed = shards * half * PIX
     flat = jax.ShapeDtypeStruct((n_packed, 2 * ch), BF16)
     units = n_packed // PIX
@@ -476,40 +530,48 @@
     columns = pltpu.VMEM((5, n_packed, 128), F32)
     shifted = pltpu.VMEM((n_packed + 2 * PIX, 2 * ch), F32)
     pad = tiles * 128
-    block, mixed = call(
+    weights = [
+        jax.ShapeDtypeStruct((pad, 3 * pad), BF16),
+        jax.ShapeDtypeStruct((pad, pad), BF16),
+        jax.ShapeDtypeStruct((3 * pad, pad), BF16),
+        jax.ShapeDtypeStruct((2 * units, 2 * units), F32),
+    ]
+    prepared = call(prepare_kernel, weights, [SMEM] + [VMEM] * 5, bytes_accessed=4 * size)(
+        clip_lengths, query_weight, key_weight, value_weight, out_weight, temporal_weight
+    )
+    late, active, prepared = lax.optimization_barrier((late, active, prepared))
+    wqkv, wo, tw, bias = prepared
+    late = exchange(late)
+    mixed = call(
         attention_kernel,
-        (flat, flat),
-        [SMEM] + [VMEM] * 6,
+        flat,
+        [VMEM] * 4,
+        scratch=[columns, columns],
+        flops=7 * dense,
+        bytes_accessed=4 * size,
+    )(active.reshape(flat.shape), wqkv, wo, bias)
+    half_grad = (3 * ch // 2, ch)
+    block, mine, other = call(
+        temporal_kernel,
+        (flat, jax.ShapeDtypeStruct(half_grad, F32), jax.ShapeDtypeStruct(half_grad, BF16)),
+        [SMEM, SMEM] + [VMEM] * 4,
         scratch=[
-            columns,
-            columns,
             shifted,
-            pltpu.VMEM((2 * units, 2 * units), F32),
-            pltpu.VMEM((pad, 3 * pad), BF16),
-            pltpu.VMEM((pad, pad), BF16),
-            pltpu.VMEM((3 * pad, pad), BF16),
+            pltpu.VMEM((pad, 3 * pad), F32),
+            pltpu.VMEM((3 * ch, ch), F32),
         ],
-        flops=10 * dense,
-        bytes_accessed=3 * size,
+        flops=6 * dense,
+        bytes_accessed=4 * size,
     )(
+        lax.axis_index("c")[None],
         clip_lengths,
-        active.reshape(flat.shape),
-        query_weight,
-        key_weight,
-        value_weight,
-        out_weight,
-        temporal_weight,
+        mixed,
+        early.reshape(shards, half // 2 * PIX, 2 * ch),
+        late.reshape(shards, half // 2 * PIX, 2 * ch),
+        tw,
     )
     block = exchange(block.reshape(packed.shape))
-    grads = call(
-        grad_kernel,
-        jax.ShapeDtypeStruct((3 * ch, ch), F32),
-        [SMEM, VMEM, VMEM],
-        scratch=[shifted, pltpu.VMEM((pad, 3 * pad), F32)],
-        flops=3 * dense,
-        bytes_accessed=2 * size + 3 * ch * ch * 4,
-    )(clip_lengths, mixed, cot.reshape(flat.shape))
-    grads = reduce_all(grads).reshape(3, ch, ch)
+    grads = reduce_all(mine, other).reshape(3, ch, ch)
     block_out = call(
         unpack_kernel,
         jax.ShapeDtypeStruct(latents.shape, BF16),

time: 142 us -> 138 us (0.972)
  Pallas kernels: 42.7 us -> 27.7 us
  local copies, waits for them, and re-layouts: 3.99 us -> 10.6 us
  starting transfers between devices: 34.3 us -> 39.6 us
  other arithmetic: 6.77 us -> 3.92 us
  waiting for transfers between devices: 52.3 us -> 53.8 us
    ppermute x4 -> x3, waiting for transfers between devices: 12.1 us -> 24 us  [the longest x2 22.4 us: reduce_all(): got = lax.ppermute(total, 'z', swaps(n_z, step))]
    ppermute x3, waiting for transfers between devices: 10.2 us -> 0.01 us  [reduce_all(): parts.append(lax.ppermute(sent, PLANE, swaps(n_plane, k)).astype(F32))]
    pallas_call x3 -> x5, Pallas kernels: 28.6 us -> 20.3 us  [the longest x1 11.5 us: body(): call(attention_kernel, flat, [VMEM] * 4, scratch=[columns, columns], flop...]
    unnamed x12 -> x42, local copies, waits for them, and re-layouts: 2.61 us -> 10.5 us
    pallas_call x1, Pallas kernels: 11.3 us -> 5.75 us  [body(): call(conv_kernel, packed, [SMEM, SMEM, VMEM, VMEM, VMEM, VMEM, VMEM], flo...]
    all_to_all x3 -> x4, starting transfers between devices: 19 us -> 22.5 us  [exchange(): flat = lax.all_to_all(flat, SEQ, split_axis=0, concat_axis=0, tiled=True)]
    ppermute x1, waiting for transfers between devices: 3.25 us -> 0.01 us  [body(): got = lax.ppermute(edge, 'x', swaps(2, 1))]
    all_to_all x3 -> x4, waiting for transfers between devices: 21.9 us -> 24.2 us  [exchange(): flat = lax.all_to_all(flat, SEQ, split_axis=0, concat_axis=0, tiled=True)]
  transfers between devices with their start and end apart: 15 -> 15, of which waited for: 10 -> 9; matrix products, arithmetic and copies ran while one was open for 4% -> 2% of each run, Pallas kernels for 17% -> 14%
where the time goes in v2:
time: 138 us; the launch traced here: 137 us
  waiting for transfers between devices  53.8 us (39%)
  starting transfers between devices  39.6 us (29%)
  Pallas kernels  27.7 us (20%)
  local copies, waits for them, and re-layouts  10.6 us (8%)
  other arithmetic  3.92 us (3%)
    all_to_all x4, waiting for transfers between devices, exchange(): flat = lax.all_to_all(flat, SEQ, split_axis=0, concat_axis=0, tiled=True)  24.2 us
    all_to_all x4, starting transfers between devices, exchange(): flat = lax.all_to_all(flat, SEQ, split_axis=0, concat_axis=0, tiled=True)  22.5 us
    ppermute x2, waiting for transfers between devices, reduce_all(): got = lax.ppermute(total, 'z', swaps(n_z, step))  22.4 us
    pallas_call x1, Pallas kernels, body(): call(attention_kernel, flat, [VMEM] * 4, scratch=[columns, columns], flop...  11.5 us
    unnamed x42, local copies, waits for them, and re-layouts  10.5 us
    ppermute x2, starting transfers between devices, reduce_all(): got = lax.ppermute(total, 'z', swaps(n_z, step))  6.53 us
    pallas_call x1, Pallas kernels, body(): call(temporal_kernel, (flat, jax.ShapeDtypeStruct(half_grad, F32), jax.Sh...  6.39 us
    pallas_call x1, Pallas kernels, body(): call(conv_kernel, packed, [SMEM, SMEM, VMEM, VMEM, VMEM, VMEM, VMEM], flo...  5.75 us
  transfers between devices with their start and end apart: 15, of which 9 were waited for; matrix products, arithmetic and copies ran while one was open for 2% of the time, Pallas kernels for 14%

profile of v2, /device:TPU:0, one launch (start us, length us, event | category | flops | bytes accessed | tf_op | source)
XLA Modules:
  0.0 136.8 jit_solution(16296290177390302906)
XLA Ops:
  0.7 2.0 %fusion = bf16[12,32,320]{2,1,0:T(8,128)(2,1)} fusion(bf16[12,4,32,320]{3,2,1,0:T(8,128)(2,1)} %lat_ref.1, pred[]{:T(512)S(6)} %eq.7), kind=kLoop, calls=%fused_computation.7 | loop fusion | flops 122880 | bytes 737281 | tf_op jit(solution)/shard_map/jit(_where)/select_n | solution.py:498
  2.6 2.9 %collective-permute-start = (bf16[12,32,320]{2,1,0:T(8,128)(2,1)}, bf16[12,32,320]{2,1,0:T(8,128)(2,1)S(1)}, u32[]{:S(2)}, u32[]{:S(2)}) collective-permute-start(bf16[12,32,320]{2,1,0:T(8,128)(2,1)} %fusion), channel_id=1, source_target_pairs={{0,1},{1,0},{2,3},{3,2},{4,5},{5,4},{6,7},{7,6},{8,9},{9,8},{10,11... | collective-permute-start | bytes 737288 | tf_op jit(solution)/shard_map/ppermute | solution.py:499
  5.6 1.3 copy-done.2
  6.8 1.3 shard_map.122
  8.2 5.9 %all-to-all-start = ((bf16[16,24,640]{2,1,0:T(8,128)(2,1)}), bf16[16,24,640]{2,1,0:T(8,128)(2,1)S(1)}, u32[]{:S(2)}, u32[]{:S(2)}) async-start(bf16[16,24,640]{2,1,0:T(8,128)(2,1)} %bitcast.1), calls=%async_computation | async-start | bytes 983040 | tf_op jit(solution)/shard_map/all_to_all | solution.py:469
  15.7 5.8 %shard_map.124 = bf16[16,6,8,640]{3,2,1,0:T(8,128)(2,1)} custom-call(s32[3]{0:T(128)S(1)} %pad_add_fusion.flag_ref, s32[4]{0:T(128)S(1)} %copy-done.9, bf16[12,4,32,320]{3,2,1,0:T(8,128)(2,1)S(1)} %copy-done.4, bf16[12,32,320]{2,1,0:T(8,128)(2,1)S(1)} %collective-permute-done.top_ref.bot_ref, bf16[12,32,320]{2,1,0:T(8,128)(2,1)S(1)} %collective-permute-done.top_ref.bot_ref, ...), custom_call_target="tpu_custom_call" | custom-call | flops 2831155200 | bytes 3809280 | tf_op jit(solution)/shard_map/pallas_call | solution.py:514
  21.4 6.5 %all-to-all-done = bf16[16,24,640]{2,1,0:T(8,128)(2,1)S(1)} async-done(((bf16[16,24,640]{2,1,0:T(8,128)(2,1)}), bf16[16,24,640]{2,1,0:T(8,128)(2,1)S(1)}, u32[]{:S(2)}, u32[]{:S(2)}) %all-to-all-start) | async-done | bytes 491552 | tf_op jit(solution)/shard_map/all_to_all | solution.py:469
  27.9 4.1 %all-to-all-start.1 = ((bf16[16,48,640]{2,1,0:T(8,128)(2,1)}), bf16[16,48,640]{2,1,0:T(8,128)(2,1)S(1)}, u32[]{:S(2)}, u32[]{:S(2)}) async-start(bf16[16,48,640]{2,1,0:T(8,128)(2,1)} %bitcast.7), calls=%async_computation.1 | async-start | bytes 1966080 | tf_op jit(solution)/shard_map/all_to_all | solution.py:469
  36.1 17.7 %all-to-all-done.1 = bf16[16,48,640]{2,1,0:T(8,128)(2,1)S(1)} async-done(((bf16[16,48,640]{2,1,0:T(8,128)(2,1)}), bf16[16,48,640]{2,1,0:T(8,128)(2,1)S(1)}, u32[]{:S(2)}, u32[]{:S(2)}) %all-to-all-start.1) | async-done | bytes 983072 | tf_op jit(solution)/shard_map/all_to_all | solution.py:469
  53.9 6.5 %all-to-all-start.2 = ((bf16[16,24,640]{2,1,0:T(8,128)(2,1)}), bf16[16,24,640]{2,1,0:T(8,128)(2,1)S(1)}, u32[]{:S(2)}, u32[]{:S(2)}) async-start(bf16[16,24,640]{2,1,0:T(8,128)(2,1)} %bitcast.11), calls=%async_computation.2 | async-start | bytes 983040 | tf_op jit(solution)/shard_map/all_to_all | solution.py:469
  60.4 1.2 copy-done.13
  61.6 1.0 copy-done.15
  62.5 0.9 copy-done.17
  63.5 11.5 %shard_map.126.m_ref = bf16[768,640]{1,0:T(8,128)(2,1)S(1)} custom-call(bf16[768,640]{1,0:T(8,128)(2,1)S(1)} %bitcast.37, bf16[384,1152]{1,0:T(8,128)(2,1)S(1)} %copy-done.13, bf16[384,384]{1,0:T(8,128)(2,1)S(1)} %copy-done.15, f32[192,192]{1,0:T(8,128)S(1)} %copy-done.17), custom_call_target="tpu_custom_call" | custom-call | flops 2202009600 | bytes 3932160 | tf_op jit(solution)/shard_map/pallas_call | solution.py:545
  75.0 0.9 copy-done.18
  75.9 1.2 copy-done.19
  77.1 6.4 %shard_map.127 = (bf16[768,640]{1,0:T(8,128)(2,1)}, f32[480,320]{1,0:T(8,128)S(1)}, bf16[480,320]{1,0:T(8,128)(2,1)}) custom-call(s32[1]{0:T(128)} %bitcast.core_ref, s32[4]{0:T(128)S(1)} %copy-done.9, bf16[768,640]{1,0:T(8,128)(2,1)S(1)} %copy-done.19, bf16[16,24,640]{2,1,0:T(8,128)(2,1)S(1)} %all-to-all-done, ...), custom_call_target="tpu_custom_call" | custom-call | flops 1887436800 | bytes 3932160 | tf_op jit(solution)/shard_map/pallas_call | solution.py:554
  83.9 1.5 %collective-permute-done.1 = bf16[480,320]{1,0:T(8,128)(2,1)S(1)} collective-permute-done((bf16[480,320]{1,0:T(8,128)(2,1)}, bf16[480,320]{1,0:T(8,128)(2,1)S(1)}, u32[]{:S(2)}, u32[]{:S(2)}) %collective-permute-start.1) | collective-permute-done | bytes 307232 | tf_op jit(solution)/shard_map/ppermute | solution.py:444
  86.2 1.9 %collective-permute-start.3 = (bf16[120,320]{1,0:T(8,128)(2,1)S(1)}, bf16[120,320]{1,0:T(8,128)(2,1)S(1)}, u32[]{:S(2)}, u32[]{:S(2)}) collective-permute-start(bf16[120,320]{1,0:T(8,128)(2,1)S(1)} %get-tuple-element.40), channel_id=1, source_target_pairs={{0,4},{1,5},{4,0},{5,1},{2,6},{3,7},{6,2},{7,3},{8,12},{9,13},{12,... | collective-permute-start | bytes 230408 | tf_op jit(solution)/shard_map/ppermute | solution.py:448
  88.1 1.1 collective-permute-start.4
  89.2 6.0 %all-to-all-start.3 = ((bf16[16,48,640]{2,1,0:T(8,128)(2,1)}), bf16[16,48,640]{2,1,0:T(8,128)(2,1)S(1)}, u32[]{:S(2)}, u32[]{:S(2)}) async-start(bf16[16,48,640]{2,1,0:T(8,128)(2,1)} %bitcast.12), calls=%async_computation.3 | async-start | bytes 1966080 | tf_op jit(solution)/shard_map/all_to_all | solution.py:469
  95.2 2.0 %collective-permute-start.5 = (bf16[120,320]{1,0:T(8,128)(2,1)S(1)}, bf16[120,320]{1,0:T(8,128)(2,1)S(1)}, u32[]{:S(2)}, u32[]{:S(2)}) collective-permute-start(bf16[120,320]{1,0:T(8,128)(2,1)S(1)} %add_convert_fusion.2), channel_id=1, source_target_pairs={{0,8},{8,0},{16,24},{24,16},{1,9},{9,1},{17,25},{25,17},{2,10},{10... | collective-permute-start | bytes 230408 | tf_op jit(solution)/shard_map/ppermute | solution.py:452
  97.2 16.9 %collective-permute-done.5 = bf16[120,320]{1,0:T(8,128)(2,1)S(1)} collective-permute-done((bf16[120,320]{1,0:T(8,128)(2,1)S(1)}, bf16[120,320]{1,0:T(8,128)(2,1)S(1)}, u32[]{:S(2)}, u32[]{:S(2)}) %collective-permute-start.5) | collective-permute-done | bytes 76832 | tf_op jit(solution)/shard_map/ppermute | solution.py:452
  114.1 4.5 %collective-permute-start.6 = (bf16[120,320]{1,0:T(8,128)(2,1)S(1)}, bf16[120,320]{1,0:T(8,128)(2,1)S(1)}, u32[]{:S(2)}, u32[]{:S(2)}) collective-permute-start(bf16[120,320]{1,0:T(8,128)(2,1)S(1)} %add_convert_fusion.1), channel_id=1, source_target_pairs={{0,16},{8,24},{16,0},{24,8},{1,17},{9,25},{17,1},{25,9},{2,18},{10... | collective-permute-start | bytes 230408 | tf_op jit(solution)/shard_map/ppermute | solution.py:452
  118.6 5.6 %collective-permute-done.6 = bf16[120,320]{1,0:T(8,128)(2,1)S(1)} collective-permute-done((bf16[120,320]{1,0:T(8,128)(2,1)S(1)}, bf16[120,320]{1,0:T(8,128)(2,1)S(1)}, u32[]{:S(2)}, u32[]{:S(2)}) %collective-permute-start.6) | collective-permute-done | bytes 76832 | tf_op jit(solution)/shard_map/ppermute | solution.py:452
  124.9 1.5 %collective-permute-start.8 = (bf16[120,320]{1,0:T(8,128)(2,1)S(1)}, bf16[120,320]{1,0:T(8,128)(2,1)S(1)}, u32[]{:S(2)}, u32[]{:S(2)}) collective-permute-start(bf16[120,320]{1,0:T(8,128)(2,1)S(1)} %add_convert_fusion), channel_id=1, source_target_pairs={{0,4},{1,5},{4,0},{5,1},{2,6},{3,7},{6,2},{7,3},{8,12},{9,13},{12,... | collective-permute-start | bytes 230408 | tf_op jit(solution)/shard_map/ppermute | solution.py:455
  126.3 1.5 %collective-permute-start.9 = (bf16[120,320]{1,0:T(8,128)(2,1)S(1)}, bf16[120,320]{1,0:T(8,128)(2,1)S(1)}, u32[]{:S(2)}, u32[]{:S(2)}) collective-permute-start(bf16[120,320]{1,0:T(8,128)(2,1)S(1)} %add_convert_fusion), channel_id=1, source_target_pairs={{0,5},{1,4},{4,1},{5,0},{2,7},{3,6},{6,3},{7,2},{8,13},{9,12},{12,... | collective-permute-start | bytes 230408 | tf_op jit(solution)/shard_map/ppermute | solution.py:455
  127.8 1.9 %collective-permute-done.7 = bf16[120,320]{1,0:T(8,128)(2,1)S(1)} collective-permute-done((bf16[120,320]{1,0:T(8,128)(2,1)S(1)}, bf16[120,320]{1,0:T(8,128)(2,1)S(1)}, u32[]{:S(2)}, u32[]{:S(2)}) %collective-permute-start.7) | collective-permute-done | bytes 76832 | tf_op jit(solution)/shard_map/ppermute | solution.py:455
  130.2 1.6 %collective-permute-done.9 = bf16[120,320]{1,0:T(8,128)(2,1)S(1)} collective-permute-done((bf16[120,320]{1,0:T(8,128)(2,1)S(1)}, bf16[120,320]{1,0:T(8,128)(2,1)S(1)}, u32[]{:S(2)}, u32[]{:S(2)}) %collective-permute-start.9) | collective-permute-done | bytes 76832 | tf_op jit(solution)/shard_map/ppermute | solution.py:455
  132.1 1.7 %collective-permute-done.10 = bf16[480,320]{1,0:T(8,128)(2,1)S(1)} collective-permute-done((bf16[480,320]{1,0:T(8,128)(2,1)S(1)}, bf16[480,320]{1,0:T(8,128)(2,1)S(1)}, u32[]{:S(2)}, u32[]{:S(2)}) %collective-permute-start.10) | collective-permute-done | bytes 307232 | tf_op jit(solution)/shard_map/ppermute | solution.py:460
  134.0 1.2 convert.3
  135.2 1.6 %shard_map.128 = bf16[12,4,32,320]{3,2,1,0:T(8,128)(2,1)} custom-call(bf16[16,6,8,640]{3,2,1,0:T(8,128)(2,1)S(1)} %bitcast.36), custom_call_target="tpu_custom_call" | custom-call | bytes 1966080 | tf_op jit(solution)/shard_map/pallas_call | solution.py:575
  (64 shorter events, 8.4 us)
Async XLA Ops:
  0.6 14.0 %copy-start = (bf16[320,320]{1,0:T(8,128)(2,1)S(1)}, bf16[320,320]{1,0:T(8,128)(2,1)}, u32[]{:S(2)}) copy-start(bf16[320,320]{1,0:T(8,128)(2,1)} %param.15) | copy-start | bytes 614404
  0.7 13.5 %copy-start.20 = (s32[4]{0:T(128)S(1)}, s32[4]{0:T(128)}, u32[]{:S(2)}) copy-start(s32[4]{0:T(128)} %param.13) | copy-start | bytes 52
  0.7 13.7 %copy-start.1 = (bf16[3,3,320,320]{3,2,1,0:T(8,128)(2,1)S(1)}, bf16[3,3,320,320]{3,2,1,0:T(8,128)(2,1)}, u32[]{:S(2)}) copy-start(bf16[3,3,320,320]{3,2,1,0:T(8,128)(2,1)} %w_ref.1) | copy-start | bytes 5529604
  2.6 12.3 %collective-permute-start = (bf16[12,32,320]{2,1,0:T(8,128)(2,1)}, bf16[12,32,320]{2,1,0:T(8,128)(2,1)S(1)}, u32[]{:S(2)}, u32[]{:S(2)}) collective-permute-start(bf16[12,32,320]{2,1,0:T(8,128)(2,1)} %fusion), channel_id=1, source_target_pairs={{0,1},{1,0},{2,3},{3,2},{4,5},{5,4},{6,7},{7,6},{8,9},{9,8},{10,11... | collective-permute-start | bytes 737288 | tf_op jit(solution)/shard_map/ppermute | solution.py:499
  5.6 1.3 copy-start.2
  8.2 19.7 %all-to-all-start = ((bf16[16,24,640]{2,1,0:T(8,128)(2,1)}), bf16[16,24,640]{2,1,0:T(8,128)(2,1)S(1)}, u32[]{:S(2)}, u32[]{:S(2)}) async-start(bf16[16,24,640]{2,1,0:T(8,128)(2,1)} %bitcast.1), calls=%async_computation | async-start | bytes 983040 | tf_op jit(solution)/shard_map/all_to_all | solution.py:469
  14.4 1.3 copy-start.4
  14.4 1.3 copy-start.9
  21.4 10.6 %copy-start.3 = (bf16[3,320,320]{2,1,0:T(8,128)(2,1)S(1)}, bf16[3,320,320]{2,1,0:T(8,128)(2,1)}, u32[]{:S(2)}) copy-start(bf16[3,320,320]{2,1,0:T(8,128)(2,1)} %tw_ref.1) | copy-start | bytes 1843204
  21.4 10.6 %copy-start.5 = (bf16[320,320]{1,0:T(8,128)(2,1)S(1)}, bf16[320,320]{1,0:T(8,128)(2,1)}, u32[]{:S(2)}) copy-start(bf16[320,320]{1,0:T(8,128)(2,1)} %wq_ref.1) | copy-start | bytes 614404
  21.4 10.6 %copy-start.6 = (bf16[320,320]{1,0:T(8,128)(2,1)S(1)}, bf16[320,320]{1,0:T(8,128)(2,1)}, u32[]{:S(2)}) copy-start(bf16[320,320]{1,0:T(8,128)(2,1)} %wk_ref.1) | copy-start | bytes 614404
  21.4 10.6 %copy-start.7 = (bf16[320,320]{1,0:T(8,128)(2,1)S(1)}, bf16[320,320]{1,0:T(8,128)(2,1)}, u32[]{:S(2)}) copy-start(bf16[320,320]{1,0:T(8,128)(2,1)} %wv_ref.1) | copy-start | bytes 614404
  21.4 10.6 %copy-start.8 = (bf16[320,320]{1,0:T(8,128)(2,1)S(1)}, bf16[320,320]{1,0:T(8,128)(2,1)}, u32[]{:S(2)}) copy-start(bf16[320,320]{1,0:T(8,128)(2,1)} %wo_ref.1) | copy-start | bytes 614404
  27.9 26.0 %all-to-all-start.1 = ((bf16[16,48,640]{2,1,0:T(8,128)(2,1)}), bf16[16,48,640]{2,1,0:T(8,128)(2,1)S(1)}, u32[]{:S(2)}, u32[]{:S(2)}) async-start(bf16[16,48,640]{2,1,0:T(8,128)(2,1)} %bitcast.7), calls=%async_computation.1 | async-start | bytes 1966080 | tf_op jit(solution)/shard_map/all_to_all | solution.py:469
  32.9 0.9 copy-start.10
  53.9 22.1 %all-to-all-start.2 = ((bf16[16,24,640]{2,1,0:T(8,128)(2,1)}), bf16[16,24,640]{2,1,0:T(8,128)(2,1)S(1)}, u32[]{:S(2)}, u32[]{:S(2)}) async-start(bf16[16,24,640]{2,1,0:T(8,128)(2,1)} %bitcast.11), calls=%async_computation.2 | async-start | bytes 983040 | tf_op jit(solution)/shard_map/all_to_all | solution.py:469
  60.4 1.2 copy-start.13
  61.6 1.0 copy-start.15
  63.5 12.5 %copy-start.11 = (bf16[1152,384]{1,0:T(8,128)(2,1)S(1)}, bf16[1152,384]{1,0:T(8,128)(2,1)}, u32[]{:S(2)}) copy-start(bf16[1152,384]{1,0:T(8,128)(2,1)} %copy-done.10) | copy-start | bytes 2654212
  75.0 0.9 copy-start.18
  75.9 1.2 copy-start.19
  83.5 1.9 %collective-permute-start.1 = (bf16[480,320]{1,0:T(8,128)(2,1)}, bf16[480,320]{1,0:T(8,128)(2,1)S(1)}, u32[]{:S(2)}, u32[]{:S(2)}) collective-permute-start(bf16[480,320]{1,0:T(8,128)(2,1)} %get-tuple-element.35), channel_id=1, source_target_pairs={{0,2},{2,0},{1,3},{3,1},{4,6},{6,4},{5,7},{7,5},{8,10},{10,8},{9,1... | collective-permute-start | bytes 921608 | tf_op jit(solution)/shard_map/ppermute | solution.py:444
  85.6 9.5 %collective-permute-start.2 = (bf16[120,320]{1,0:T(8,128)(2,1)S(1)}, bf16[120,320]{1,0:T(8,128)(2,1)S(1)}, u32[]{:S(2)}, u32[]{:S(2)}) collective-permute-start(bf16[120,320]{1,0:T(8,128)(2,1)S(1)} %get-tuple-element.38), channel_id=1, source_target_pairs={{0,1},{1,0},{4,5},{5,4},{2,3},{3,2},{6,7},{7,6},{8,9},{9,8},{12,13... | collective-permute-start | bytes 230408 | tf_op jit(solution)/shard_map/ppermute | solution.py:448
  86.2 8.9 %collective-permute-start.3 = (bf16[120,320]{1,0:T(8,128)(2,1)S(1)}, bf16[120,320]{1,0:T(8,128)(2,1)S(1)}, u32[]{:S(2)}, u32[]{:S(2)}) collective-permute-start(bf16[120,320]{1,0:T(8,128)(2,1)S(1)} %get-tuple-element.40), channel_id=1, source_target_pairs={{0,4},{1,5},{4,0},{5,1},{2,6},{3,7},{6,2},{7,3},{8,12},{9,13},{12,... | collective-permute-start | bytes 230408 | tf_op jit(solution)/shard_map/ppermute | solution.py:448
  88.1 7.1 %collective-permute-start.4 = (bf16[120,320]{1,0:T(8,128)(2,1)S(1)}, bf16[120,320]{1,0:T(8,128)(2,1)S(1)}, u32[]{:S(2)}, u32[]{:S(2)}) collective-permute-start(bf16[120,320]{1,0:T(8,128)(2,1)S(1)} %get-tuple-element.39), channel_id=1, source_target_pairs={{0,5},{1,4},{4,1},{5,0},{2,7},{3,6},{6,3},{7,2},{8,13},{9,12},{12,... | collective-permute-start | bytes 230408 | tf_op jit(solution)/shard_map/ppermute | solution.py:448
  89.2 46.0 %all-to-all-start.3 = ((bf16[16,48,640]{2,1,0:T(8,128)(2,1)}), bf16[16,48,640]{2,1,0:T(8,128)(2,1)S(1)}, u32[]{:S(2)}, u32[]{:S(2)}) async-start(bf16[16,48,640]{2,1,0:T(8,128)(2,1)} %bitcast.12), calls=%async_computation.3 | async-start | bytes 1966080 | tf_op jit(solution)/shard_map/all_to_all | solution.py:469
  95.2 18.8 %collective-permute-start.5 = (bf16[120,320]{1,0:T(8,128)(2,1)S(1)}, bf16[120,320]{1,0:T(8,128)(2,1)S(1)}, u32[]{:S(2)}, u32[]{:S(2)}) collective-permute-start(bf16[120,320]{1,0:T(8,128)(2,1)S(1)} %add_convert_fusion.2), channel_id=1, source_target_pairs={{0,8},{8,0},{16,24},{24,16},{1,9},{9,1},{17,25},{25,17},{2,10},{10... | collective-permute-start | bytes 230408 | tf_op jit(solution)/shard_map/ppermute | solution.py:452
  114.1 10.1 %collective-permute-start.6 = (bf16[120,320]{1,0:T(8,128)(2,1)S(1)}, bf16[120,320]{1,0:T(8,128)(2,1)S(1)}, u32[]{:S(2)}, u32[]{:S(2)}) collective-permute-start(bf16[120,320]{1,0:T(8,128)(2,1)S(1)} %add_convert_fusion.1), channel_id=1, source_target_pairs={{0,16},{8,24},{16,0},{24,8},{1,17},{9,25},{17,1},{25,9},{2,18},{10... | collective-permute-start | bytes 230408 | tf_op jit(solution)/shard_map/ppermute | solution.py:452
  124.2 5.5 %collective-permute-start.7 = (bf16[120,320]{1,0:T(8,128)(2,1)S(1)}, bf16[120,320]{1,0:T(8,128)(2,1)S(1)}, u32[]{:S(2)}, u32[]{:S(2)}) collective-permute-start(bf16[120,320]{1,0:T(8,128)(2,1)S(1)} %add_convert_fusion), channel_id=1, source_target_pairs={{0,1},{1,0},{4,5},{5,4},{2,3},{3,2},{6,7},{7,6},{8,9},{9,8},{12,13... | collective-permute-start | bytes 230408 | tf_op jit(solution)/shard_map/ppermute | solution.py:455
  124.9 5.3 %collective-permute-start.8 = (bf16[120,320]{1,0:T(8,128)(2,1)S(1)}, bf16[120,320]{1,0:T(8,128)(2,1)S(1)}, u32[]{:S(2)}, u32[]{:S(2)}) collective-permute-start(bf16[120,320]{1,0:T(8,128)(2,1)S(1)} %add_convert_fusion), channel_id=1, source_target_pairs={{0,4},{1,5},{4,0},{5,1},{2,6},{3,7},{6,2},{7,3},{8,12},{9,13},{12,... | collective-permute-start | bytes 230408 | tf_op jit(solution)/shard_map/ppermute | solution.py:455
  126.3 5.5 %collective-permute-start.9 = (bf16[120,320]{1,0:T(8,128)(2,1)S(1)}, bf16[120,320]{1,0:T(8,128)(2,1)S(1)}, u32[]{:S(2)}, u32[]{:S(2)}) collective-permute-start(bf16[120,320]{1,0:T(8,128)(2,1)S(1)} %add_convert_fusion), channel_id=1, source_target_pairs={{0,5},{1,4},{4,1},{5,0},{2,7},{3,6},{6,3},{7,2},{8,13},{9,12},{12,... | collective-permute-start | bytes 230408 | tf_op jit(solution)/shard_map/ppermute | solution.py:455
  132.0 1.8 %collective-permute-start.10 = (bf16[480,320]{1,0:T(8,128)(2,1)S(1)}, bf16[480,320]{1,0:T(8,128)(2,1)S(1)}, u32[]{:S(2)}, u32[]{:S(2)}) collective-permute-start(bf16[480,320]{1,0:T(8,128)(2,1)S(1)} %pad_maximum_fusion.2), channel_id=1, source_target_pairs={{0,2},{2,0},{1,3},{3,1},{4,6},{6,4},{5,7},{7,5},{8,10},{10,8},{9,1... | collective-permute-start | bytes 921608 | tf_op jit(solution)/shard_map/ppermute | solution.py:460
  (4 other events, 3.3 us)

commit v3 on v2

--- a/solution.py
+++ b/solution.py
@@ -16,8 +16,11 @@
 F32 = jnp.float32
 VMEM = pltpu.VMEM
 SMEM = pltpu.SMEM
+ANY = pl.ANY
 PIX = 8
 BIG = 384
+VMEM_LIMIT = 24 * 2**20
+WHOLE_VMEM = 60 * 2**20
 
 
 def time_table(timesteps, time_weight):
@@ -28,18 +31,17 @@
     return jnp.dot(embedded, time_weight.astype(F32), precision=lax.Precision.HIGHEST)
 
 
-def call(kernel, out_shape, in_spaces, scratch=(), flops=0, bytes_accessed=0, grid=None, **kw):
+def call(kernel, out_shape, in_spaces, scratch=(), flops=0, bytes_accessed=0, out_space=VMEM):
     return pl.pallas_call(
         kernel,
         out_shape=out_shape,
         in_specs=[pl.BlockSpec(memory_space=s) for s in in_spaces],
-        out_specs=jax.tree.map(lambda _: pl.BlockSpec(memory_space=VMEM), out_shape),
+        out_specs=jax.tree.map(lambda _: pl.BlockSpec(memory_space=out_space), out_shape),
         scratch_shapes=scratch,
         cost_estimate=pl.CostEstimate(
             flops=flops, bytes_accessed=bytes_accessed, transcendentals=0
         ),
-        compiler_params=pltpu.CompilerParams(vmem_limit_bytes=40 * 2**20),
-        **kw,
+        compiler_params=pltpu.CompilerParams(vmem_limit_bytes=VMEM_LIMIT if ANY not in in_spaces else WHOLE_VMEM),
     )
 
 
@@ -281,7 +283,7 @@
 
 
 def attention_kernel(
-    act_ref, wqkv, wo, bias, m_ref, n5, d5
+    act_ref, wqkv_hbm, wo_hbm, bias_hbm, m_hbm, n5, d5, wqkv, wo, bias, m_ref, sems
 ):
     rows, ch2 = act_ref.shape
     ch = ch2 // 2
@@ -289,6 +291,12 @@
     units = rows // PIX
     frames = units * 2
     head = ch // HEADS
+    fetches = [
+        pltpu.make_async_copy(src, dst, sems.at[k])
+        for k, (src, dst) in enumerate(((wqkv_hbm, wqkv), (wo_hbm, wo), (bias_hbm, bias)))
+    ]
+    for f in fetches:
+        f.start()
     chunk = 96
     low = low_lanes()
 
@@ -313,6 +321,8 @@
         return 0
 
     lax.fori_loop(0, rows // chunk, norm, 0)
+    for f in fetches:
+        f.wait()
 
     factor = head ** (-0.5) * math.log2(math.e)
     lane = lax.broadcasted_iota(jnp.int32, (1, pad), 1)
@@ -376,43 +386,89 @@
         return 0
 
     lax.fori_loop(0, rows // chunk, mix, 0)
-
-
-def temporal_kernel(
-    core_ref, len_ref, m_ref, early_ref, late_ref, tw,
-    o_ref, mine_ref, other_ref, m32, grad, full
+    out = pltpu.make_async_copy(m_ref, m_hbm, sems.at[3])
+    out.start()
+    out.wait()
+
+
+def shift_store(m_ref, m32):
+    rows, ch2 = m_ref.shape
+    m32[0:PIX, :] = jnp.zeros((PIX, ch2), F32)
+    m32[rows + PIX : rows + 2 * PIX, :] = jnp.zeros((PIX, ch2), F32)
+    m32[PIX : rows + PIX, :] = m_ref[...].astype(F32)
+
+
+def temporal_kernel(len_ref, m_hbm, tw_hbm, o_ref, m32, m_ref, tw, sems):
+    fetches = [
+        pltpu.make_async_copy(src, dst, sems.at[k])
+        for k, (src, dst) in enumerate(((m_hbm, m_ref), (tw_hbm, tw)))
+    ]
+    for f in fetches:
+        f.start()
+    for f in fetches:
+        f.wait()
+    rows, ch2 = m_ref.shape
+    frames = rows // PIX * 2
+    shift_store(m_ref, m32)
+
+    def step(i, _):
+        r0 = i * BIG
+        src = sources(m32, r0, BIG, frames, len_ref)
+        rounded = jnp.concatenate([v.astype(BF16) for v in src], axis=1)
+        total = src[1] + jnp.dot(rounded, tw[...], preferred_element_type=F32)
+        even, odd, tail = join_pair(total[:BIG], total[BIG:])
+        at = pl.ds(pl.multiple_of(r0, 8), BIG)
+        o_ref[at, 0:256] = even.astype(BF16)
+        o_ref[at, 256:512] = odd.astype(BF16)
+        o_ref[at, 512:640] = tail.astype(BF16)
+        return 0
+
+    lax.fori_loop(0, rows // BIG, step, 0)
+
+
+def grad_kernel(
+    core_ref, len_ref, m_hbm, early_hbm, late_hbm, mine_ref, other_ref,
+    m32, grad, full, m_ref, early_ref, late_ref, sems,
 ):
+    fetches = [
+        pltpu.make_async_copy(src, dst, sems.at[k])
+        for k, (src, dst) in enumerate(
+            ((m_hbm, m_ref), (early_hbm, early_ref), (late_hbm, late_ref))
+        )
+    ]
+    for f in fetches:
+        f.start()
+    fetches[0].wait()
     rows, ch2 = m_ref.shape
     ch = ch2 // 2
     pad = dst_tile(ch)
     frames = rows // PIX * 2
-    big = BIG
-    m32[0:PIX, :] = jnp.zeros((PIX, ch2), F32)
-    m32[rows + PIX : rows + 2 * PIX, :] = jnp.zeros((PIX, ch2), F32)
-    m32[PIX : rows + PIX, :] = m_ref[...].astype(F32)
-    grad[...] = jnp.zeros_like(grad)
-
-    def temporal(i, _):
-        r0 = i * big
-        src = sources(m32, r0, big, frames, len_ref)
+    shift_store(m_ref, m32)
+    fetches[1].wait()
+    fetches[2].wait()
+    each = early_ref.shape[1]
+    spans = BIG // (2 * each)
+
+    def step(i, _):
+        r0 = i * BIG
+        src = sources(m32, r0, BIG, frames, len_ref)
         rounded = jnp.concatenate([v.astype(BF16) for v in src], axis=1)
-        total = src[1] + jnp.dot(rounded, tw[...], preferred_element_type=F32)
-        each = early_ref.shape[1]
-        spans = big // (2 * each)
         cot = [ref[i * spans + k] for k in range(spans) for ref in (early_ref, late_ref)]
         cot = split_pair(jnp.concatenate([c.astype(F32) for c in cot], axis=0))
         cot = jnp.concatenate(cot, axis=0).astype(BF16)
-        grad[...] += lax.dot_general(
-            cot, rounded, (((0,), (0,)), ((), ())), preferred_element_type=F32
-        )
-        even, odd, tail = join_pair(total[:big], total[big:])
-        at = pl.ds(pl.multiple_of(r0, 8), big)
-        o_ref[at, 0:256] = even.astype(BF16)
-        o_ref[at, 256:512] = odd.astype(BF16)
-        o_ref[at, 512:640] = tail.astype(BF16)
+        got = lax.dot_general(cot, rounded, (((0,), (0,)), ((), ())), preferred_element_type=F32)
+
+        @pl.when(i == 0)
+        def _():
+            grad[...] = got
+
+        @pl.when(i > 0)
+        def _():
+            grad[...] += got
+
         return 0
 
-    lax.fori_loop(0, rows // big, temporal, 0)
+    lax.fori_loop(0, rows // BIG, step, 0)
     for j in range(3):
         full[j * ch : (j + 1) * ch, :] = grad[:, j * pad : (j + 1) * pad].T[:ch, :ch]
     core = core_ref[0]
@@ -431,6 +487,13 @@
     return [(i, i ^ k) for i in range(n)]
 
 
+def ordered(parts, place):
+    stacked = jnp.stack(parts)
+    return jnp.concatenate(
+        [lax.dynamic_index_in_dim(stacked, place ^ j, 0, False) for j in range(len(parts))], 0
+    )
+
+
 def reduce_all(g, other):
     core = lax.axis_index("c")
     n_plane = lax.axis_size("y") * lax.axis_size("x")
@@ -446,20 +509,22 @@
     for k in range(1, n_plane):
         sent = cut(g, place ^ k, share).astype(BF16)
         parts.append(lax.ppermute(sent, PLANE, swaps(n_plane, k)).astype(F32))
+    total = tree(parts)
+    level = lax.axis_index("z")
+    piece = -(-share // n_z // 8) * 8
+    total = jnp.pad(total, ((0, piece * n_z - share), (0, 0)))
+    parts = [cut(total, level, piece)]
+    for k in range(1, n_z):
+        sent = cut(total, level ^ k, piece).astype(BF16)
+        parts.append(lax.ppermute(sent, "z", swaps(n_z, k)).astype(F32))
     total = tree(parts).astype(BF16)
-    step = 1
-    while step < n_z:
-        got = lax.ppermute(total, "z", swaps(n_z, step))
-        total = (total.astype(F32) + got.astype(F32)).astype(BF16)
-        step *= 2
+    parts = [total] + [lax.ppermute(total, "z", swaps(n_z, k)) for k in range(1, n_z)]
+    total = ordered(parts, level)[:share]
     parts = [total] + [lax.ppermute(total, PLANE, swaps(n_plane, k)) for k in range(1, n_plane)]
-    stacked = jnp.stack(parts)
-    ordered = jnp.concatenate(
-        [lax.dynamic_index_in_dim(stacked, place ^ j, 0, False) for j in range(n_plane)], 0
-    )
-    other = lax.ppermute(ordered, "c", swaps(2, 1))
-    low = jnp.where(core == 0, ordered, other)
-    high = jnp.where(core == 0, other, ordered)
+    own = ordered(parts, place)
+    other = lax.ppermute(own, "c", swaps(2, 1))
+    low = jnp.where(core == 0, own, other)
+    high = jnp.where(core == 0, other, own)
     return jnp.concatenate([low, high], 0).astype(F32)
 
 
@@ -495,7 +560,7 @@
 
     row = lax.axis_index("x")
     if n_rows == 2:
-        edge = jnp.where(row == 0, latents[:, rows - 1], latents[:, 0])
+        edge = lax.dynamic_index_in_dim(latents, (1 - row) * (rows - 1), 1, False)
         got = lax.ppermute(edge, "x", swaps(2, 1))
         top, bot = got, got
     else:
@@ -528,6 +593,7 @@
     units = n_packed // PIX
     tiles = -(-ch // 128)
     columns = pltpu.VMEM((5, n_packed, 128), F32)
+    whole = pltpu.VMEM(flat.shape, BF16)
     shifted = pltpu.VMEM((n_packed + 2 * PIX, 2 * ch), F32)
     pad = tiles * 128
     weights = [
@@ -545,39 +611,59 @@
     mixed = call(
         attention_kernel,
         flat,
-        [VMEM] * 4,
-        scratch=[columns, columns],
+        [VMEM] + [ANY] * 3,
+        scratch=[columns, columns]
+        + [pltpu.VMEM(w.shape, w.dtype) for w in (weights[0], weights[1], weights[3])]
+        + [whole, pltpu.SemaphoreType.DMA((4,))],
+        out_space=ANY,
         flops=7 * dense,
         bytes_accessed=4 * size,
     )(active.reshape(flat.shape), wqkv, wo, bias)
     half_grad = (3 * ch // 2, ch)
-    block, mine, other = call(
-        temporal_kernel,
-        (flat, jax.ShapeDtypeStruct(half_grad, F32), jax.ShapeDtypeStruct(half_grad, BF16)),
-        [SMEM, SMEM] + [VMEM] * 4,
+    mine, other = call(
+        grad_kernel,
+        (jax.ShapeDtypeStruct(half_grad, F32), jax.ShapeDtypeStruct(half_grad, BF16)),
+        [SMEM, SMEM, ANY, ANY, ANY],
         scratch=[
             shifted,
             pltpu.VMEM((pad, 3 * pad), F32),
             pltpu.VMEM((3 * ch, ch), F32),
+            whole,
+            pltpu.VMEM((shards, half // 2 * PIX, 2 * ch), BF16),
+            pltpu.VMEM((shards, half // 2 * PIX, 2 * ch), BF16),
+            pltpu.SemaphoreType.DMA((3,)),
         ],
-        flops=6 * dense,
-        bytes_accessed=4 * size,
+        flops=3 * dense,
+        bytes_accessed=3 * size,
     )(
         lax.axis_index("c")[None],
         clip_lengths,
         mixed,
         early.reshape(shards, half // 2 * PIX, 2 * ch),
         late.reshape(shards, half // 2 * PIX, 2 * ch),
-        tw,
     )
+    mixed, mine, other = lax.optimization_barrier((mixed, mine, other))
+    block = call(
+        temporal_kernel,
+        flat,
+        [SMEM, ANY, ANY],
+        scratch=[
+            shifted,
+            whole,
+            pltpu.VMEM(weights[2].shape, BF16),
+            pltpu.SemaphoreType.DMA((2,)),
+        ],
+        flops=3 * dense,
+        bytes_accessed=3 * size,
+    )(clip_lengths, mixed, tw)
     block = exchange(block.reshape(packed.shape))
-    grads = reduce_all(mine, other).reshape(3, ch, ch)
     block_out = call(
         unpack_kernel,
         jax.ShapeDtypeStruct(latents.shape, BF16),
         [VMEM],
         bytes_accessed=2 * size,
     )(block)
+    grads = reduce_all(mine, other).reshape(3, ch, ch)
     return block_out, grads
 
 

time: 138 us -> 148 us (1.072)
  Pallas kernels: 27.7 us -> 36.3 us
  waiting for transfers between devices: 53.8 us -> 57.8 us
  local copies, waits for them, and re-layouts: 10.6 us -> 6.67 us
  starting transfers between devices: 39.6 us -> 42.3 us
    pallas_call x2 -> x3, Pallas kernels: 17.9 us -> 26.4 us  [the longest x1 13.7 us: body(): call(attention_kernel, flat, [VMEM] + [ANY] * 3, scratch=[columns, column...]
    unnamed x42 -> x34, local copies, waits for them, and re-layouts: 10.5 us -> 5.36 us
    ppermute x3 -> x7, waiting for transfers between devices: 24.1 us -> 27.3 us  [the longest x3 22.4 us: reduce_all(): parts.append(lax.ppermute(sent, 'z', swaps(n_z, k)).astype(F32))]
    ppermute x3 -> x7, starting transfers between devices: 6.6 us -> 8.98 us  [the longest x3 4.45 us: reduce_all(): parts.append(lax.ppermute(sent, 'z', swaps(n_z, k)).astype(F32))]
    select_n x2 -> x1, other arithmetic: 2.11 us -> 0.15 us  [reduce_all(): low = jnp.where(core == 0, own, other)]
  transfers between devices with their start and end apart: 15 -> 19, of which waited for: 9 -> 11; matrix products, arithmetic and copies ran while one was open for 2% -> 2% of each run, Pallas kernels for 14% -> 19%
where the time goes in v3:
time: 148 us; the launch traced here: 147 us
  waiting for transfers between devices  57.8 us (39%)
  starting transfers between devices  42.3 us (29%)
  Pallas kernels  36.3 us (25%)
  local copies, waits for them, and re-layouts  6.67 us (5%)
  other arithmetic  3.08 us (2%)
    all_to_all x4, waiting for transfers between devices, exchange(): flat = lax.all_to_all(flat, SEQ, split_axis=0, concat_axis=0, tiled=True)  24.9 us
    all_to_all x4, starting transfers between devices, exchange(): flat = lax.all_to_all(flat, SEQ, split_axis=0, concat_axis=0, tiled=True)  22.7 us
    ppermute x3, waiting for transfers between devices, reduce_all(): parts.append(lax.ppermute(sent, 'z', swaps(n_z, k)).astype(F32))  22.4 us
    pallas_call x1, Pallas kernels, body(): call(attention_kernel, flat, [VMEM] + [ANY] * 3, scratch=[columns, column...  13.7 us
    pallas_call x1, Pallas kernels, body(): call(grad_kernel, (jax.ShapeDtypeStruct(half_grad, F32), jax.ShapeDtypeSt...  6.65 us
    pallas_call x1, Pallas kernels, body(): call(temporal_kernel, flat, [SMEM, ANY, ANY], scratch=[shifted, whole, pl...  6.05 us
    pallas_call x1, Pallas kernels, body(): call(conv_kernel, packed, [SMEM, SMEM, VMEM, VMEM, VMEM, VMEM, VMEM], flo...  5.79 us
    unnamed x34, local copies, waits for them, and re-layouts  5.36 us
  transfers between devices with their start and end apart: 19, of which 11 were waited for; matrix products, arithmetic and copies ran while one was open for 2% of the time, Pallas kernels for 19%

profile of v3, /device:TPU:0, one launch (start us, length us, event | category | flops | bytes accessed | tf_op | source)
XLA Modules:
  0.0 147.3 jit_solution(15215266655601990409)
XLA Ops:
  0.7 1.2 dynamic-slice_bitcast_fusion
  1.8 3.0 %collective-permute-start = (bf16[12,32,320]{2,1,0:T(8,128)(2,1)S(1)}, bf16[12,32,320]{2,1,0:T(8,128)(2,1)S(1)}, u32[]{:S(2)}, u32[]{:S(2)}) collective-permute-start(bf16[12,32,320]{2,1,0:T(8,128)(2,1)S(1)} %dynamic-slice_bitcast_fusion), channel_id=1, source_target_pairs={{0,1},{1,0},{2,3},{3,2},{4,5},{5,4},{6,7},{7,6},{8,9},{9,8},{10,11... | collective-permute-start | bytes 737288 | tf_op jit(solution)/shard_map/ppermute | solution.py:564
  4.8 1.3 copy-done.2
  6.1 1.4 shard_map.122
  7.5 5.9 %all-to-all-start = ((bf16[16,24,640]{2,1,0:T(8,128)(2,1)}), bf16[16,24,640]{2,1,0:T(8,128)(2,1)S(1)}, u32[]{:S(2)}, u32[]{:S(2)}) async-start(bf16[16,24,640]{2,1,0:T(8,128)(2,1)} %bitcast), calls=%async_computation | async-start | bytes 983040 | tf_op jit(solution)/shard_map/all_to_all | solution.py:534
  14.9 5.8 %shard_map.124 = bf16[16,6,8,640]{3,2,1,0:T(8,128)(2,1)} custom-call(s32[3]{0:T(128)S(1)} %pad_add_fusion.flag_ref, s32[4]{0:T(128)S(1)} %copy-done.9, bf16[12,4,32,320]{3,2,1,0:T(8,128)(2,1)S(1)} %copy-done.8, bf16[12,32,320]{2,1,0:T(8,128)(2,1)S(1)} %collective-permute-done.top_ref.bot_ref, bf16[12,32,320]{2,1,0:T(8,128)(2,1)S(1)} %collective-permute-done.top_ref.bot_ref, ...), custom_call_target="tpu_custom_call" | custom-call | flops 2831155200 | bytes 3809280 | tf_op jit(solution)/shard_map/pallas_call | solution.py:579
  20.8 6.4 %all-to-all-done = bf16[16,24,640]{2,1,0:T(8,128)(2,1)S(1)} async-done(((bf16[16,24,640]{2,1,0:T(8,128)(2,1)}), bf16[16,24,640]{2,1,0:T(8,128)(2,1)S(1)}, u32[]{:S(2)}, u32[]{:S(2)}) %all-to-all-start) | async-done | bytes 491552 | tf_op jit(solution)/shard_map/all_to_all | solution.py:534
  27.2 4.3 %all-to-all-start.1 = ((bf16[16,48,640]{2,1,0:T(8,128)(2,1)}), bf16[16,48,640]{2,1,0:T(8,128)(2,1)}, u32[]{:S(2)}, u32[]{:S(2)}) async-start(bf16[16,48,640]{2,1,0:T(8,128)(2,1)} %bitcast.6), calls=%async_computation.1 | async-start | bytes 1966080 | tf_op jit(solution)/shard_map/all_to_all | solution.py:534
  34.9 18.4 %all-to-all-done.1 = bf16[16,48,640]{2,1,0:T(8,128)(2,1)} async-done(((bf16[16,48,640]{2,1,0:T(8,128)(2,1)}), bf16[16,48,640]{2,1,0:T(8,128)(2,1)}, u32[]{:S(2)}, u32[]{:S(2)}) %all-to-all-start.1) | async-done | bytes 983072 | tf_op jit(solution)/shard_map/all_to_all | solution.py:534
  53.4 6.5 %all-to-all-start.2 = ((bf16[16,24,640]{2,1,0:T(8,128)(2,1)}), bf16[16,24,640]{2,1,0:T(8,128)(2,1)S(1)}, u32[]{:S(2)}, u32[]{:S(2)}) async-start(bf16[16,24,640]{2,1,0:T(8,128)(2,1)} %bitcast.11), calls=%async_computation.2 | async-start | bytes 983040 | tf_op jit(solution)/shard_map/all_to_all | solution.py:534
  59.9 13.7 %shard_map.126.m_hbm = bf16[768,640]{1,0:T(8,128)(2,1)} custom-call(bf16[768,640]{1,0:T(8,128)(2,1)} %bitcast.8.act_ref, bf16[384,1152]{1,0:T(8,128)(2,1)} %copy-done.11, bf16[384,384]{1,0:T(8,128)(2,1)} %copy-done.12, f32[192,192]{1,0:T(8,128)} %copy-done.13), custom_call_target="tpu_custom_call" | custom-call | flops 2202009600 | bytes 3932160 | tf_op jit(solution)/shard_map/pallas_call | solution.py:611
  74.5 6.7 %shard_map.127 = (f32[480,320]{1,0:T(8,128)}, bf16[480,320]{1,0:T(8,128)(2,1)}) custom-call(s32[1]{0:T(128)} %bitcast.9.core_ref, s32[4]{0:T(128)} %len_ref.7, bf16[768,640]{1,0:T(8,128)(2,1)} %shard_map.126.m_hbm, bf16[16,24,640]{2,1,0:T(8,128)(2,1)} %copy-done.14, bf16[16,24,640]{2,1,0:T(8,128)(2,1)} %copy-done.15), custom_call_target="tpu_custom_call" | custom-call | flops 943718400 | bytes 2949120 | tf_op jit(solution)/shard_map/pallas_call | solution.py:623
  81.6 1.5 %collective-permute-done.1 = bf16[480,320]{1,0:T(8,128)(2,1)S(1)} collective-permute-done((bf16[480,320]{1,0:T(8,128)(2,1)}, bf16[480,320]{1,0:T(8,128)(2,1)S(1)}, u32[]{:S(2)}, u32[]{:S(2)}) %collective-permute-start.1) | collective-permute-done | bytes 307232 | tf_op jit(solution)/shard_map/ppermute | solution.py:507
  83.1 1.2 convert_add_fusion
  84.9 1.9 %collective-permute-start.3 = (bf16[120,320]{1,0:T(8,128)(2,1)S(1)}, bf16[120,320]{1,0:T(8,128)(2,1)S(1)}, u32[]{:S(2)}, u32[]{:S(2)}) collective-permute-start(bf16[120,320]{1,0:T(8,128)(2,1)S(1)} %get-tuple-element.44), channel_id=1, source_target_pairs={{0,4},{1,5},{4,0},{5,1},{2,6},{3,7},{6,2},{7,3},{8,12},{9,13},{12,... | collective-permute-start | bytes 230408 | tf_op jit(solution)/shard_map/ppermute | solution.py:511
  86.8 1.1 collective-permute-start.4
  87.9 6.0 %shard_map.128 = bf16[768,640]{1,0:T(8,128)(2,1)} custom-call(s32[4]{0:T(128)} %len_ref.7, bf16[768,640]{1,0:T(8,128)(2,1)} %shard_map.126.m_hbm, bf16[1152,384]{1,0:T(8,128)(2,1)} %copy-done.10), custom_call_target="tpu_custom_call" | custom-call | flops 943718400 | bytes 2949120 | tf_op jit(solution)/shard_map/pallas_call | solution.py:646
  93.9 6.0 %all-to-all-start.3 = ((bf16[16,48,640]{2,1,0:T(8,128)(2,1)}), bf16[16,48,640]{2,1,0:T(8,128)(2,1)S(1)}, u32[]{:S(2)}, u32[]{:S(2)}) async-start(bf16[16,48,640]{2,1,0:T(8,128)(2,1)} %bitcast.44), calls=%async_computation.3 | async-start | bytes 1966080 | tf_op jit(solution)/shard_map/all_to_all | solution.py:534
  100.0 2.0 %collective-permute-start.5 = (bf16[32,320]{1,0:T(8,128)(2,1)S(1)}, bf16[32,320]{1,0:T(8,128)(2,1)S(1)}, u32[]{:S(2)}, u32[]{:S(2)}) collective-permute-start(bf16[32,320]{1,0:T(8,128)(2,1)S(1)} %get-tuple-element.49), channel_id=1, source_target_pairs={{0,8},{8,0},{16,24},{24,16},{1,9},{9,1},{17,25},{25,17},{2,10},{10... | collective-permute-start | bytes 61448 | tf_op jit(solution)/shard_map/ppermute | solution.py:519
  102.0 2.4 %collective-permute-start.6 = (bf16[32,320]{1,0:T(8,128)(2,1)S(1)}, bf16[32,320]{1,0:T(8,128)(2,1)S(1)}, u32[]{:S(2)}, u32[]{:S(2)}) collective-permute-start(bf16[32,320]{1,0:T(8,128)(2,1)S(1)} %get-tuple-element.50), channel_id=1, source_target_pairs={{0,16},{8,24},{16,0},{24,8},{1,17},{9,25},{17,1},{25,9},{2,18},{10... | collective-permute-start | bytes 61448 | tf_op jit(solution)/shard_map/ppermute | solution.py:519
  104.5 13.1 %collective-permute-done.5 = bf16[32,320]{1,0:T(8,128)(2,1)S(1)} collective-permute-done((bf16[32,320]{1,0:T(8,128)(2,1)S(1)}, bf16[32,320]{1,0:T(8,128)(2,1)S(1)}, u32[]{:S(2)}, u32[]{:S(2)}) %collective-permute-start.5) | collective-permute-done | bytes 20512 | tf_op jit(solution)/shard_map/ppermute | solution.py:519
  117.6 9.3 %collective-permute-done.6 = bf16[32,320]{1,0:T(8,128)(2,1)S(1)} collective-permute-done((bf16[32,320]{1,0:T(8,128)(2,1)S(1)}, bf16[32,320]{1,0:T(8,128)(2,1)S(1)}, u32[]{:S(2)}, u32[]{:S(2)}) %collective-permute-start.6) | collective-permute-done | bytes 20512 | tf_op jit(solution)/shard_map/ppermute | solution.py:519
  127.8 1.2 collective-permute-start.9
  129.0 2.4 %collective-permute-start.10 = (bf16[32,320]{1,0:T(8,128)(2,1)S(1)}, bf16[32,320]{1,0:T(8,128)(2,1)S(1)}, u32[]{:S(2)}, u32[]{:S(2)}) collective-permute-start(bf16[32,320]{1,0:T(8,128)(2,1)S(1)} %fusion.2), channel_id=1, source_target_pairs={{0,24},{8,16},{16,8},{24,0},{1,25},{9,17},{17,9},{25,1},{2,26},{10... | collective-permute-start | bytes 61448 | tf_op jit(solution)/shard_map/ppermute | solution.py:521
  131.4 1.2 collective-permute-done.9
  132.5 2.1 %collective-permute-done.10 = bf16[32,320]{1,0:T(8,128)(2,1)S(1)} collective-permute-done((bf16[32,320]{1,0:T(8,128)(2,1)S(1)}, bf16[32,320]{1,0:T(8,128)(2,1)S(1)}, u32[]{:S(2)}, u32[]{:S(2)}) %collective-permute-start.10) | collective-permute-done | bytes 20512 | tf_op jit(solution)/shard_map/ppermute | solution.py:521
  135.3 1.5 collective-permute-start.12
  136.8 1.5 %collective-permute-start.13 = (bf16[120,320]{1,0:T(8,128)(2,1)S(1)}, bf16[120,320]{1,0:T(8,128)(2,1)S(1)}, u32[]{:S(2)}, u32[]{:S(2)}) collective-permute-start(bf16[120,320]{1,0:T(8,128)(2,1)S(1)} %pad_maximum_fusion.4), channel_id=1, source_target_pairs={{0,5},{1,4},{4,1},{5,0},{2,7},{3,6},{6,3},{7,2},{8,13},{9,12},{12,... | collective-permute-start | bytes 230408 | tf_op jit(solution)/shard_map/ppermute | solution.py:523
  139.9 2.4 %collective-permute-done.13 = bf16[120,320]{1,0:T(8,128)(2,1)S(1)} collective-permute-done((bf16[120,320]{1,0:T(8,128)(2,1)S(1)}, bf16[120,320]{1,0:T(8,128)(2,1)S(1)}, u32[]{:S(2)}, u32[]{:S(2)}) %collective-permute-start.13) | collective-permute-done | bytes 76832 | tf_op jit(solution)/shard_map/ppermute | solution.py:523
  142.5 1.7 %collective-permute-done.14 = bf16[480,320]{1,0:T(8,128)(2,1)S(1)} collective-permute-done((bf16[480,320]{1,0:T(8,128)(2,1)S(1)}, bf16[480,320]{1,0:T(8,128)(2,1)S(1)}, u32[]{:S(2)}, u32[]{:S(2)}) %collective-permute-start.14) | collective-permute-done | bytes 307232 | tf_op jit(solution)/shard_map/ppermute | solution.py:525
  144.5 1.2 convert.3
  145.7 1.6 %shard_map.129 = bf16[12,4,32,320]{3,2,1,0:T(8,128)(2,1)} custom-call(bf16[16,6,8,640]{3,2,1,0:T(8,128)(2,1)S(1)} %bitcast.42), custom_call_target="tpu_custom_call" | custom-call | bytes 1966080 | tf_op jit(solution)/shard_map/pallas_call | solution.py:660
  (68 shorter events, 10.7 us)
Async XLA Ops:
  0.6 13.3 %copy-start = (bf16[320,320]{1,0:T(8,128)(2,1)S(1)}, bf16[320,320]{1,0:T(8,128)(2,1)}, u32[]{:S(2)}) copy-start(bf16[320,320]{1,0:T(8,128)(2,1)} %param.15) | copy-start | bytes 614404
  0.6 13.0 %copy-start.1 = (bf16[3,3,320,320]{3,2,1,0:T(8,128)(2,1)S(1)}, bf16[3,3,320,320]{3,2,1,0:T(8,128)(2,1)}, u32[]{:S(2)}) copy-start(bf16[3,3,320,320]{3,2,1,0:T(8,128)(2,1)} %w_ref.1) | copy-start | bytes 5529604
  1.8 12.4 %collective-permute-start = (bf16[12,32,320]{2,1,0:T(8,128)(2,1)S(1)}, bf16[12,32,320]{2,1,0:T(8,128)(2,1)S(1)}, u32[]{:S(2)}, u32[]{:S(2)}) collective-permute-start(bf16[12,32,320]{2,1,0:T(8,128)(2,1)S(1)} %dynamic-slice_bitcast_fusion), channel_id=1, source_target_pairs={{0,1},{1,0},{2,3},{3,2},{4,5},{5,4},{6,7},{7,6},{8,9},{9,8},{10,11... | collective-permute-start | bytes 737288 | tf_op jit(solution)/shard_map/ppermute | solution.py:564
  4.8 1.3 copy-start.2
  6.1 7.3 %copy-start.16 = (s32[4]{0:T(128)S(1)}, s32[4]{0:T(128)}, u32[]{:S(2)}) copy-start(s32[4]{0:T(128)} %param.13) | copy-start | bytes 52
  7.5 19.7 %all-to-all-start = ((bf16[16,24,640]{2,1,0:T(8,128)(2,1)}), bf16[16,24,640]{2,1,0:T(8,128)(2,1)S(1)}, u32[]{:S(2)}, u32[]{:S(2)}) async-start(bf16[16,24,640]{2,1,0:T(8,128)(2,1)} %bitcast), calls=%async_computation | async-start | bytes 983040 | tf_op jit(solution)/shard_map/all_to_all | solution.py:534
  13.7 1.3 copy-start.8
  13.7 1.3 copy-start.9
  20.7 10.8 %copy-start.3 = (bf16[3,320,320]{2,1,0:T(8,128)(2,1)S(1)}, bf16[3,320,320]{2,1,0:T(8,128)(2,1)}, u32[]{:S(2)}) copy-start(bf16[3,320,320]{2,1,0:T(8,128)(2,1)} %tw_ref.1) | copy-start | bytes 1843204
  20.7 10.8 %copy-start.4 = (bf16[320,320]{1,0:T(8,128)(2,1)S(1)}, bf16[320,320]{1,0:T(8,128)(2,1)}, u32[]{:S(2)}) copy-start(bf16[320,320]{1,0:T(8,128)(2,1)} %wq_ref.1) | copy-start | bytes 614404
  20.7 10.8 %copy-start.5 = (bf16[320,320]{1,0:T(8,128)(2,1)S(1)}, bf16[320,320]{1,0:T(8,128)(2,1)}, u32[]{:S(2)}) copy-start(bf16[320,320]{1,0:T(8,128)(2,1)} %wk_ref.1) | copy-start | bytes 614404
  20.7 10.8 %copy-start.6 = (bf16[320,320]{1,0:T(8,128)(2,1)S(1)}, bf16[320,320]{1,0:T(8,128)(2,1)}, u32[]{:S(2)}) copy-start(bf16[320,320]{1,0:T(8,128)(2,1)} %wv_ref.1) | copy-start | bytes 614404
  20.7 10.8 %copy-start.7 = (bf16[320,320]{1,0:T(8,128)(2,1)S(1)}, bf16[320,320]{1,0:T(8,128)(2,1)}, u32[]{:S(2)}) copy-start(bf16[320,320]{1,0:T(8,128)(2,1)} %wo_ref.1) | copy-start | bytes 614404
  27.2 5.2 %copy-start.14 = (bf16[16,24,640]{2,1,0:T(8,128)(2,1)}, bf16[16,24,640]{2,1,0:T(8,128)(2,1)S(1)}, u32[]{:S(2)}) copy-start(bf16[16,24,640]{2,1,0:T(8,128)(2,1)S(1)} %all-to-all-done) | copy-start | bytes 1474564
  27.2 26.2 %all-to-all-start.1 = ((bf16[16,48,640]{2,1,0:T(8,128)(2,1)}), bf16[16,48,640]{2,1,0:T(8,128)(2,1)}, u32[]{:S(2)}, u32[]{:S(2)}) async-start(bf16[16,48,640]{2,1,0:T(8,128)(2,1)} %bitcast.6), calls=%async_computation.1 | async-start | bytes 1966080 | tf_op jit(solution)/shard_map/all_to_all | solution.py:534
  34.9 24.9 %copy-start.13 = (f32[192,192]{1,0:T(8,128)}, f32[192,192]{1,0:T(8,128)S(1)}, u32[]{:S(2)}) copy-start(f32[192,192]{1,0:T(8,128)S(1)} %get-tuple-element.31.bias_hbm) | copy-start | bytes 442372
  53.4 20.3 %all-to-all-start.2 = ((bf16[16,24,640]{2,1,0:T(8,128)(2,1)}), bf16[16,24,640]{2,1,0:T(8,128)(2,1)S(1)}, u32[]{:S(2)}, u32[]{:S(2)}) async-start(bf16[16,24,640]{2,1,0:T(8,128)(2,1)} %bitcast.11), calls=%async_computation.2 | async-start | bytes 983040 | tf_op jit(solution)/shard_map/all_to_all | solution.py:534
  81.1 2.0 %collective-permute-start.1 = (bf16[480,320]{1,0:T(8,128)(2,1)}, bf16[480,320]{1,0:T(8,128)(2,1)S(1)}, u32[]{:S(2)}, u32[]{:S(2)}) collective-permute-start(bf16[480,320]{1,0:T(8,128)(2,1)} %get-tuple-element.39), channel_id=1, source_target_pairs={{0,2},{2,0},{1,3},{3,1},{4,6},{6,4},{5,7},{7,5},{8,10},{10,8},{9,1... | collective-permute-start | bytes 921608 | tf_op jit(solution)/shard_map/ppermute | solution.py:507
  84.3 15.6 %collective-permute-start.2 = (bf16[120,320]{1,0:T(8,128)(2,1)S(1)}, bf16[120,320]{1,0:T(8,128)(2,1)S(1)}, u32[]{:S(2)}, u32[]{:S(2)}) collective-permute-start(bf16[120,320]{1,0:T(8,128)(2,1)S(1)} %get-tuple-element.42), channel_id=1, source_target_pairs={{0,1},{1,0},{4,5},{5,4},{2,3},{3,2},{6,7},{7,6},{8,9},{9,8},{12,13... | collective-permute-start | bytes 230408 | tf_op jit(solution)/shard_map/ppermute | solution.py:511
  84.9 15.0 %collective-permute-start.3 = (bf16[120,320]{1,0:T(8,128)(2,1)S(1)}, bf16[120,320]{1,0:T(8,128)(2,1)S(1)}, u32[]{:S(2)}, u32[]{:S(2)}) collective-permute-start(bf16[120,320]{1,0:T(8,128)(2,1)S(1)} %get-tuple-element.44), channel_id=1, source_target_pairs={{0,4},{1,5},{4,0},{5,1},{2,6},{3,7},{6,2},{7,3},{8,12},{9,13},{12,... | collective-permute-start | bytes 230408 | tf_op jit(solution)/shard_map/ppermute | solution.py:511
  86.8 13.1 %collective-permute-start.4 = (bf16[120,320]{1,0:T(8,128)(2,1)S(1)}, bf16[120,320]{1,0:T(8,128)(2,1)S(1)}, u32[]{:S(2)}, u32[]{:S(2)}) collective-permute-start(bf16[120,320]{1,0:T(8,128)(2,1)S(1)} %get-tuple-element.43), channel_id=1, source_target_pairs={{0,5},{1,4},{4,1},{5,0},{2,7},{3,6},{6,3},{7,2},{8,13},{9,12},{12,... | collective-permute-start | bytes 230408 | tf_op jit(solution)/shard_map/ppermute | solution.py:511
  93.9 51.7 %all-to-all-start.3 = ((bf16[16,48,640]{2,1,0:T(8,128)(2,1)}), bf16[16,48,640]{2,1,0:T(8,128)(2,1)S(1)}, u32[]{:S(2)}, u32[]{:S(2)}) async-start(bf16[16,48,640]{2,1,0:T(8,128)(2,1)} %bitcast.44), calls=%async_computation.3 | async-start | bytes 1966080 | tf_op jit(solution)/shard_map/all_to_all | solution.py:534
  100.0 17.6 %collective-permute-start.5 = (bf16[32,320]{1,0:T(8,128)(2,1)S(1)}, bf16[32,320]{1,0:T(8,128)(2,1)S(1)}, u32[]{:S(2)}, u32[]{:S(2)}) collective-permute-start(bf16[32,320]{1,0:T(8,128)(2,1)S(1)} %get-tuple-element.49), channel_id=1, source_target_pairs={{0,8},{8,0},{16,24},{24,16},{1,9},{9,1},{17,25},{25,17},{2,10},{10... | collective-permute-start | bytes 61448 | tf_op jit(solution)/shard_map/ppermute | solution.py:519
  102.0 24.9 %collective-permute-start.6 = (bf16[32,320]{1,0:T(8,128)(2,1)S(1)}, bf16[32,320]{1,0:T(8,128)(2,1)S(1)}, u32[]{:S(2)}, u32[]{:S(2)}) collective-permute-start(bf16[32,320]{1,0:T(8,128)(2,1)S(1)} %get-tuple-element.50), channel_id=1, source_target_pairs={{0,16},{8,24},{16,0},{24,8},{1,17},{9,25},{17,1},{25,9},{2,18},{10... | collective-permute-start | bytes 61448 | tf_op jit(solution)/shard_map/ppermute | solution.py:519
  104.4 22.5 %collective-permute-start.7 = (bf16[32,320]{1,0:T(8,128)(2,1)S(1)}, bf16[32,320]{1,0:T(8,128)(2,1)S(1)}, u32[]{:S(2)}, u32[]{:S(2)}) collective-permute-start(bf16[32,320]{1,0:T(8,128)(2,1)S(1)} %get-tuple-element.51), channel_id=1, source_target_pairs={{0,24},{8,16},{16,8},{24,0},{1,25},{9,17},{17,9},{25,1},{2,26},{10... | collective-permute-start | bytes 61448 | tf_op jit(solution)/shard_map/ppermute | solution.py:519
  126.9 4.5 %collective-permute-start.8 = (bf16[32,320]{1,0:T(8,128)(2,1)S(1)}, bf16[32,320]{1,0:T(8,128)(2,1)S(1)}, u32[]{:S(2)}, u32[]{:S(2)}) collective-permute-start(bf16[32,320]{1,0:T(8,128)(2,1)S(1)} %fusion.2), channel_id=1, source_target_pairs={{0,8},{8,0},{16,24},{24,16},{1,9},{9,1},{17,25},{25,17},{2,10},{10... | collective-permute-start | bytes 61448 | tf_op jit(solution)/shard_map/ppermute | solution.py:521
  127.8 4.7 %collective-permute-start.9 = (bf16[32,320]{1,0:T(8,128)(2,1)S(1)}, bf16[32,320]{1,0:T(8,128)(2,1)S(1)}, u32[]{:S(2)}, u32[]{:S(2)}) collective-permute-start(bf16[32,320]{1,0:T(8,128)(2,1)S(1)} %fusion.2), channel_id=1, source_target_pairs={{0,16},{8,24},{16,0},{24,8},{1,17},{9,25},{17,1},{25,9},{2,18},{10... | collective-permute-start | bytes 61448 | tf_op jit(solution)/shard_map/ppermute | solution.py:521
  129.0 5.6 %collective-permute-start.10 = (bf16[32,320]{1,0:T(8,128)(2,1)S(1)}, bf16[32,320]{1,0:T(8,128)(2,1)S(1)}, u32[]{:S(2)}, u32[]{:S(2)}) collective-permute-start(bf16[32,320]{1,0:T(8,128)(2,1)S(1)} %fusion.2), channel_id=1, source_target_pairs={{0,24},{8,16},{16,8},{24,0},{1,25},{9,17},{17,9},{25,1},{2,26},{10... | collective-permute-start | bytes 61448 | tf_op jit(solution)/shard_map/ppermute | solution.py:521
  134.7 4.6 %collective-permute-start.11 = (bf16[120,320]{1,0:T(8,128)(2,1)S(1)}, bf16[120,320]{1,0:T(8,128)(2,1)S(1)}, u32[]{:S(2)}, u32[]{:S(2)}) collective-permute-start(bf16[120,320]{1,0:T(8,128)(2,1)S(1)} %pad_maximum_fusion.4), channel_id=1, source_target_pairs={{0,1},{1,0},{4,5},{5,4},{2,3},{3,2},{6,7},{7,6},{8,9},{9,8},{12,13... | collective-permute-start | bytes 230408 | tf_op jit(solution)/shard_map/ppermute | solution.py:523
  135.3 4.6 %collective-permute-start.12 = (bf16[120,320]{1,0:T(8,128)(2,1)S(1)}, bf16[120,320]{1,0:T(8,128)(2,1)S(1)}, u32[]{:S(2)}, u32[]{:S(2)}) collective-permute-start(bf16[120,320]{1,0:T(8,128)(2,1)S(1)} %pad_maximum_fusion.4), channel_id=1, source_target_pairs={{0,4},{1,5},{4,0},{5,1},{2,6},{3,7},{6,2},{7,3},{8,12},{9,13},{12,... | collective-permute-start | bytes 230408 | tf_op jit(solution)/shard_map/ppermute | solution.py:523
  136.8 5.5 %collective-permute-start.13 = (bf16[120,320]{1,0:T(8,128)(2,1)S(1)}, bf16[120,320]{1,0:T(8,128)(2,1)S(1)}, u32[]{:S(2)}, u32[]{:S(2)}) collective-permute-start(bf16[120,320]{1,0:T(8,128)(2,1)S(1)} %pad_maximum_fusion.4), channel_id=1, source_target_pairs={{0,5},{1,4},{4,1},{5,0},{2,7},{3,6},{6,3},{7,2},{8,13},{9,12},{12,... | collective-permute-start | bytes 230408 | tf_op jit(solution)/shard_map/ppermute | solution.py:523
  142.5 1.8 %collective-permute-start.14 = (bf16[480,320]{1,0:T(8,128)(2,1)S(1)}, bf16[480,320]{1,0:T(8,128)(2,1)S(1)}, u32[]{:S(2)}, u32[]{:S(2)}) collective-permute-start(bf16[480,320]{1,0:T(8,128)(2,1)S(1)} %pad_maximum_fusion.2), channel_id=1, source_target_pairs={{0,2},{2,0},{1,3},{3,1},{4,6},{6,4},{5,7},{7,5},{8,10},{10,8},{9,1... | collective-permute-start | bytes 921608 | tf_op jit(solution)/shard_map/ppermute | solution.py:525
  (4 other events, 3.3 us)

commit v4 on v3

--- a/solution.py
+++ b/solution.py
@@ -18,7 +18,6 @@
 SMEM = pltpu.SMEM
 ANY = pl.ANY
 PIX = 8
-BIG = 384
 VMEM_LIMIT = 24 * 2**20
 WHOLE_VMEM = 60 * 2**20
 
@@ -61,49 +60,22 @@
     return jnp.concatenate([piece, jnp.zeros((PIX - real, row.shape[-1]), F32)], 0).astype(BF16)
 
 
-def pack_kernel(x_ref, early_ref, late_ref):
+def pack_kernel(x_ref, o_ref):
     frames, rows, across, ch = x_ref.shape
-    half = frames // 2
-    real = across * rows // early_ref.shape[0]
+    real = across * rows // o_ref.shape[0]
     wide = 256
-    for o_ref, start in ((early_ref, 0), (late_ref, half // 2)):
-
-        def step(t, _, o_ref=o_ref, start=start):
-            flat = [
-                jnp.concatenate([x_ref[2 * (t + start) + q, i] for i in range(rows)], axis=0)
-                for q in range(2)
-            ]
-            for q in range(2):
-                store_groups(o_ref, t, slice(q * wide, (q + 1) * wide), flat[q][:, :wide], real)
-            tail = jnp.concatenate([flat[0][:, wide:], flat[1][:, wide:]], axis=1)
-            store_groups(o_ref, t, slice(2 * wide, 2 * ch), tail, real)
-            return 0
-
-        lax.fori_loop(0, half // 2, step, 0)
-
-
-def unpack_kernel(x_ref, o_ref):
-    frames, rows, across, ch = o_ref.shape
-    half = frames // 2
-    groups = x_ref.shape[0] // rows
-    real = across // groups
-    wide = ch // 128 * 128
-
-    def join(blocks, low, high):
-        if real == PIX:
-            return jnp.concatenate([b[:, low:high] for b in blocks], 0)
-        return jnp.concatenate([b[:real, low:high].astype(F32) for b in blocks], 0).astype(BF16)
 
     def step(t, _):
-        for i in range(rows):
-            blocks = [x_ref[i * groups + g, t] for g in range(groups)]
-            o_ref[2 * t, i, :, 0:wide] = join(blocks, 0, wide)
-            o_ref[2 * t, i, :, wide:ch] = join(blocks, 2 * wide, wide + ch)
-            o_ref[2 * t + 1, i, :, 0:wide] = join(blocks, wide, 2 * wide)
-            o_ref[2 * t + 1, i, :, wide:ch] = join(blocks, wide + ch, 2 * ch)
-        return 0
-
-    lax.fori_loop(0, half, step, 0)
+        flat = [
+            jnp.concatenate([x_ref[2 * t + q, i] for i in range(rows)], axis=0) for q in range(2)
+        ]
+        for q in range(2):
+            store_groups(o_ref, t, slice(q * wide, (q + 1) * wide), flat[q][:, :wide], real)
+        tail = jnp.concatenate([flat[0][:, wide:], flat[1][:, wide:]], axis=1)
+        store_groups(o_ref, t, slice(2 * wide, 2 * ch), tail, real)
+        return 0
+
+    lax.fori_loop(0, frames // 2, step, 0)
 
 
 def conv_weight_kernel(w_ref, o_ref):
@@ -252,11 +224,25 @@
     return -(-ch // 128) * 128
 
 
-def sources(m32, r0, n, frames, len_ref):
-    cur = split_pair(m32[pl.ds(pl.multiple_of(r0 + PIX, 8), n), :])
-    before = split_pair(m32[pl.ds(pl.multiple_of(r0, 8), n), :])[1]
-    after = split_pair(m32[pl.ds(pl.multiple_of(r0 + 2 * PIX, 8), n), :])[0]
-    even = ((r0 + lax.broadcasted_iota(jnp.int32, (n, 1), 0)) >> 3) * 2
+def spread_units(m_ref, m32):
+    own = m_ref.shape[1] - PIX
+    for s in range(m_ref.shape[0]):
+        x = m_ref[s].astype(F32)
+        m32[s, PIX : PIX + own, :] = x[:own]
+        m32[s, 0:PIX, :] = x[own:]
+        m32[s, PIX + own :, :] = x[own:]
+
+
+def sources(m32, start, count, base, frames, len_ref):
+    own = m32.shape[1] - 2 * PIX
+
+    def rows(first):
+        x = m32[pl.ds(start, count), first : first + own, :]
+        return split_pair(x.reshape(count * own, x.shape[-1]))
+
+    cur, before, after = rows(PIX), rows(0)[1], rows(2 * PIX)[0]
+    unit = lax.broadcasted_iota(jnp.int32, (count, own, 1), 1).reshape(count * own, 1) >> 3
+    even = base + 2 * unit
     ids = [clip_ids(even + k, len_ref) for k in (-1, 0, 1, 2)]
     into = jnp.where((ids[0] == ids[1]) & (even > 0), 1.0, 0.0)
     inside = jnp.where(ids[1] == ids[2], 1.0, 0.0)
@@ -283,7 +269,7 @@
 
 
 def attention_kernel(
-    act_ref, wqkv_hbm, wo_hbm, bias_hbm, m_hbm, n5, d5, wqkv, wo, bias, m_ref, sems
+    act_ref, wqkv_hbm, wo_hbm, bias_hbm, o_ref, n5, d5, wqkv, wo, bias, m32, sems
 ):
     rows, ch2 = act_ref.shape
     ch = ch2 // 2
@@ -379,82 +365,67 @@
 
     lax.fori_loop(0, PIX // group, pixels, 0)
 
+    own = o_ref.shape[1] - PIX
+
     def mix(i, _):
-        at = pl.ds(pl.multiple_of(i * chunk, 8), chunk)
+        at = pl.ds(pl.multiple_of(i * own, 8), own)
         delta = jnp.concatenate([d5[c, at, :] for c in range(5)], axis=1)
-        m_ref[at, :] = (act_ref[at, :].astype(F32) + delta).astype(BF16)
-        return 0
-
-    lax.fori_loop(0, rows // chunk, mix, 0)
-    out = pltpu.make_async_copy(m_ref, m_hbm, sems.at[3])
-    out.start()
-    out.wait()
-
-
-def shift_store(m_ref, m32):
-    rows, ch2 = m_ref.shape
-    m32[0:PIX, :] = jnp.zeros((PIX, ch2), F32)
-    m32[rows + PIX : rows + 2 * PIX, :] = jnp.zeros((PIX, ch2), F32)
-    m32[PIX : rows + PIX, :] = m_ref[...].astype(F32)
-
-
-def temporal_kernel(len_ref, m_hbm, tw_hbm, o_ref, m32, m_ref, tw, sems):
-    fetches = [
-        pltpu.make_async_copy(src, dst, sems.at[k])
-        for k, (src, dst) in enumerate(((m_hbm, m_ref), (tw_hbm, tw)))
-    ]
-    for f in fetches:
-        f.start()
-    for f in fetches:
-        f.wait()
-    rows, ch2 = m_ref.shape
-    frames = rows // PIX * 2
-    shift_store(m_ref, m32)
+        m = (act_ref[at, :].astype(F32) + delta).astype(BF16)
+        o_ref[i, 0:own, :] = m
+        m32[at, :] = m.astype(F32)
+        return 0
+
+    lax.fori_loop(0, rows // own, mix, 0)
+
+    def edges(i, _):
+        after = m32[pl.ds(pl.multiple_of(jnp.minimum((i + 1) * own, rows - PIX), 8), PIX), :]
+        before = m32[pl.ds(pl.multiple_of(jnp.maximum(i * own - PIX, 0), 8), PIX), :]
+        tail = jnp.where(low, after[:, 512:640], before[:, 512:640])
+        edge = jnp.concatenate([after[:, 0:256], before[:, 256:512], tail], axis=1)
+        o_ref[i, own : own + PIX, :] = edge.astype(BF16)
+        return 0
+
+    lax.fori_loop(0, rows // own, edges, 0)
+
+
+def temporal_kernel(flag_ref, len_ref, m_ref, tw, o_ref, m32):
+    shards = m_ref.shape[0]
+    frames, rows, across, ch = o_ref.shape
+    units = frames // 2
+    groups = shards // rows
+    real = across // groups
+    total_frames = flag_ref[3]
+    spread_units(m_ref, m32)
+
+    def join(blocks):
+        return jnp.concatenate([b[:real] for b in blocks], axis=0).astype(BF16)
 
     def step(i, _):
-        r0 = i * BIG
-        src = sources(m32, r0, BIG, frames, len_ref)
+        src = sources(m32, i * groups, groups, flag_ref[2], total_frames, len_ref)
         rounded = jnp.concatenate([v.astype(BF16) for v in src], axis=1)
         total = src[1] + jnp.dot(rounded, tw[...], preferred_element_type=F32)
-        even, odd, tail = join_pair(total[:BIG], total[BIG:])
-        at = pl.ds(pl.multiple_of(r0, 8), BIG)
-        o_ref[at, 0:256] = even.astype(BF16)
-        o_ref[at, 256:512] = odd.astype(BF16)
-        o_ref[at, 512:640] = tail.astype(BF16)
-        return 0
-
-    lax.fori_loop(0, rows // BIG, step, 0)
-
-
-def grad_kernel(
-    core_ref, len_ref, m_hbm, early_hbm, late_hbm, mine_ref, other_ref,
-    m32, grad, full, m_ref, early_ref, late_ref, sems,
-):
-    fetches = [
-        pltpu.make_async_copy(src, dst, sems.at[k])
-        for k, (src, dst) in enumerate(
-            ((m_hbm, m_ref), (early_hbm, early_ref), (late_hbm, late_ref))
-        )
-    ]
-    for f in fetches:
-        f.start()
-    fetches[0].wait()
-    rows, ch2 = m_ref.shape
-    ch = ch2 // 2
+        total = total.reshape(2, groups, units, PIX, total.shape[-1])
+        for u in range(units):
+            for q in range(2):
+                got = join([total[q, g, u] for g in range(groups)])
+                o_ref[2 * u + q, i] = got[:, :ch]
+        return 0
+
+    lax.fori_loop(0, rows, step, 0)
+
+
+def grad_kernel(flag_ref, len_ref, m_ref, cot_ref, mine_ref, other_ref, m32, grad, full):
+    shards = m_ref.shape[0]
+    ch = m_ref.shape[-1] // 2
     pad = dst_tile(ch)
-    frames = rows // PIX * 2
-    shift_store(m_ref, m32)
-    fetches[1].wait()
-    fetches[2].wait()
-    each = early_ref.shape[1]
-    spans = BIG // (2 * each)
+    count = 8
+    spread_units(m_ref, m32)
 
     def step(i, _):
-        r0 = i * BIG
-        src = sources(m32, r0, BIG, frames, len_ref)
+        src = sources(m32, i * count, count, flag_ref[2], flag_ref[3], len_ref)
         rounded = jnp.concatenate([v.astype(BF16) for v in src], axis=1)
-        cot = [ref[i * spans + k] for k in range(spans) for ref in (early_ref, late_ref)]
-        cot = split_pair(jnp.concatenate([c.astype(F32) for c in cot], axis=0))
+        cot = cot_ref[pl.ds(i * count, count), :, :].astype(F32)
+        cot = split_pair(cot.reshape(-1, 2 * ch))
         cot = jnp.concatenate(cot, axis=0).astype(BF16)
         got = lax.dot_general(cot, rounded, (((0,), (0,)), ((), ())), preferred_element_type=F32)
 
@@ -468,10 +439,10 @@
 
         return 0
 
-    lax.fori_loop(0, rows // BIG, step, 0)
+    lax.fori_loop(0, shards // count, step, 0)
     for j in range(3):
         full[j * ch : (j + 1) * ch, :] = grad[:, j * pad : (j + 1) * pad].T[:ch, :ch]
-    core = core_ref[0]
+    core = flag_ref[4]
     n = mine_ref.shape[0]
     mine_ref[...] = full[pl.ds(pl.multiple_of(core * n, 8), n), :]
     other_ref[...] = full[pl.ds(pl.multiple_of((1 - core) * n, 8), n), :].astype(BF16)
@@ -509,17 +480,11 @@
     for k in range(1, n_plane):
         sent = cut(g, place ^ k, share).astype(BF16)
         parts.append(lax.ppermute(sent, PLANE, swaps(n_plane, k)).astype(F32))
-    total = tree(parts)
-    level = lax.axis_index("z")
-    piece = -(-share // n_z // 8) * 8
-    total = jnp.pad(total, ((0, piece * n_z - share), (0, 0)))
-    parts = [cut(total, level, piece)]
+    mine = tree(parts).astype(BF16)
+    parts = [mine.astype(F32)]
     for k in range(1, n_z):
-        sent = cut(total, level ^ k, piece).astype(BF16)
-        parts.append(lax.ppermute(sent, "z", swaps(n_z, k)).astype(F32))
+        parts.append(lax.ppermute(mine, "z", swaps(n_z, k)).astype(F32))
     total = tree(parts).astype(BF16)
-    parts = [total] + [lax.ppermute(total, "z", swaps(n_z, k)) for k in range(1, n_z)]
-    total = ordered(parts, level)[:share]
     parts = [total] + [lax.ppermute(total, PLANE, swaps(n_plane, k)) for k in range(1, n_plane)]
     own = ordered(parts, place)
     other = lax.ppermute(own, "c", swaps(2, 1))
@@ -568,7 +533,9 @@
         top = lax.ppermute(latents[:, rows - 1], "x", up)
         bot = lax.ppermute(latents[:, 0], "x", [(j, i) for i, j in up])
     seq = (lax.axis_index("z") * lax.axis_size("y") + lax.axis_index("y")) * 2 + lax.axis_index("c")
-    flags = jnp.stack([row > 0, row < n_rows - 1, seq * f_dev]).astype(jnp.int32)
+    flags = jnp.stack(
+        [row > 0, row < n_rows - 1, seq * f_dev, shards * f_dev, lax.axis_index("c")]
+    ).astype(jnp.int32)
     table = time_table(timesteps, time_weight)
     taps = call(
         conv_weight_kernel,
@@ -583,18 +550,16 @@
         flops=9 * dense,
         bytes_accessed=2 * size + 9 * ch * ch * 2,
     )(flags, clip_lengths, latents, top, bot, taps, table)
-    part = jax.ShapeDtypeStruct((shards, half // 2, PIX, 2 * ch), BF16)
-    early, late = call(pack_kernel, (part, part), [VMEM], bytes_accessed=2 * size)(cotangent)
-    early = exchange(early)
-    early, active = lax.optimization_barrier((early, active))
     active = exchange(active)
+    cot = call(pack_kernel, packed, [VMEM], bytes_accessed=2 * size)(cotangent)
+
     n_packed = shards * half * PIX
     flat = jax.ShapeDtypeStruct((n_packed, 2 * ch), BF16)
     units = n_packed // PIX
     tiles = -(-ch // 128)
     columns = pltpu.VMEM((5, n_packed, 128), F32)
-    whole = pltpu.VMEM(flat.shape, BF16)
-    shifted = pltpu.VMEM((n_packed + 2 * PIX, 2 * ch), F32)
+    whole = pltpu.VMEM(flat.shape, F32)
+    around = pltpu.VMEM((shards, (half + 2) * PIX, 2 * ch), F32)
     pad = tiles * 128
     weights = [
         jax.ShapeDtypeStruct((pad, 3 * pad), BF16),
@@ -605,64 +570,37 @@
     prepared = call(prepare_kernel, weights, [SMEM] + [VMEM] * 5, bytes_accessed=4 * size)(
         clip_lengths, query_weight, key_weight, value_weight, out_weight, temporal_weight
     )
-    late, active, prepared = lax.optimization_barrier((late, active, prepared))
+    cot, active, prepared = lax.optimization_barrier((cot, active, prepared))
     wqkv, wo, tw, bias = prepared
-    late = exchange(late)
     mixed = call(
         attention_kernel,
-        flat,
+        jax.ShapeDtypeStruct((shards, (half + 1) * PIX, 2 * ch), BF16),
         [VMEM] + [ANY] * 3,
         scratch=[columns, columns]
         + [pltpu.VMEM(w.shape, w.dtype) for w in (weights[0], weights[1], weights[3])]
-        + [whole, pltpu.SemaphoreType.DMA((4,))],
-        out_space=ANY,
+        + [whole, pltpu.SemaphoreType.DMA((3,))],
         flops=7 * dense,
         bytes_accessed=4 * size,
     )(active.reshape(flat.shape), wqkv, wo, bias)
+    mixed = lax.all_to_all(mixed, SEQ, split_axis=0, concat_axis=0, tiled=True)
     half_grad = (3 * ch // 2, ch)
     mine, other = call(
         grad_kernel,
         (jax.ShapeDtypeStruct(half_grad, F32), jax.ShapeDtypeStruct(half_grad, BF16)),
-        [SMEM, SMEM, ANY, ANY, ANY],
-        scratch=[
-            shifted,
-            pltpu.VMEM((pad, 3 * pad), F32),
-            pltpu.VMEM((3 * ch, ch), F32),
-            whole,
-            pltpu.VMEM((shards, half // 2 * PIX, 2 * ch), BF16),
-            pltpu.VMEM((shards, half // 2 * PIX, 2 * ch), BF16),
-            pltpu.SemaphoreType.DMA((3,)),
-        ],
+        [SMEM, SMEM, VMEM, VMEM],
+        scratch=[around, pltpu.VMEM((pad, 3 * pad), F32), pltpu.VMEM((3 * ch, ch), F32)],
         flops=3 * dense,
         bytes_accessed=3 * size,
-    )(
-        lax.axis_index("c")[None],
-        clip_lengths,
-        mixed,
-        early.reshape(shards, half // 2 * PIX, 2 * ch),
-        late.reshape(shards, half // 2 * PIX, 2 * ch),
-    )
+    )(flags, clip_lengths, mixed, cot.reshape(shards, half * PIX, 2 * ch))
     mixed, mine, other = lax.optimization_barrier((mixed, mine, other))
-    block = call(
+    block_out = call(
         temporal_kernel,
-        flat,
-        [SMEM, ANY, ANY],
-        scratch=[
-            shifted,
-            whole,
-            pltpu.VMEM(weights[2].shape, BF16),
-            pltpu.SemaphoreType.DMA((2,)),
-        ],
+        jax.ShapeDtypeStruct(latents.shape, BF16),
+        [SMEM, SMEM, VMEM, VMEM],
+        scratch=[around],
         flops=3 * dense,
         bytes_accessed=3 * size,
-    )(clip_lengths, mixed, tw)
-    block = exchange(block.reshape(packed.shape))
-    block_out = call(
-        unpack_kernel,
-        jax.ShapeDtypeStruct(latents.shape, BF16),
-        [VMEM],
-        bytes_accessed=2 * size,
-    )(block)
+    )(flags, clip_lengths, mixed, tw)
     grads = reduce_all(mine, other).reshape(3, ch, ch)
     return block_out, grads
 

time: 148 us -> 135 us (0.912)
  blocking collectives: 0 us -> 35.6 us
  waiting for transfers between devices: 57.8 us -> 36 us
  starting transfers between devices: 42.3 us -> 21.1 us
  Pallas kernels: 36.3 us -> 30 us
    all_to_all x0 -> x1, blocking collectives: none -> 35.6 us  [body(): mixed = lax.all_to_all(mixed, SEQ, split_axis=0, concat_axis=0, tiled=True)]
    ppermute x6 -> x3, waiting for transfers between devices: 25.7 us -> 4.52 us  [reduce_all(): parts.append(lax.ppermute(mine, 'z', swaps(n_z, k)).astype(F32))]
    all_to_all x4 -> x1, starting transfers between devices: 22.7 us -> 6.37 us  [exchange(): flat = lax.all_to_all(flat, SEQ, split_axis=0, concat_axis=0, tiled=True)]
    all_to_all x4 -> x1, waiting for transfers between devices: 24.9 us -> 16.5 us  [exchange(): flat = lax.all_to_all(flat, SEQ, split_axis=0, concat_axis=0, tiled=True)]
    ppermute x3, waiting for transfers between devices: 0.01 us -> 4.54 us  [reduce_all(): parts.append(lax.ppermute(sent, PLANE, swaps(n_plane, k)).astype(F32))]
    ppermute x6 -> x3, starting transfers between devices: 8.9 us -> 4.45 us  [reduce_all(): parts.append(lax.ppermute(mine, 'z', swaps(n_z, k)).astype(F32))]
    ppermute x1, waiting for transfers between devices: 0.01 us -> 4.24 us  [body(): got = lax.ppermute(edge, 'x', swaps(2, 1))]
    pallas_call x4 -> x3, Pallas kernels: 22.8 us -> 18.9 us  [the longest x1 14.1 us: body(): call(attention_kernel, jax.ShapeDtypeStruct((shards, (half + 1) * PIX, 2...]
  transfers between devices with their start and end apart: 19 -> 13, of which waited for: 11 -> 10; matrix products, arithmetic and copies ran while one was open for 2% -> 1% of each run, Pallas kernels for 19% -> 4%
where the time goes in v4:
time: 135 us; the launch traced here: 134 us
  waiting for transfers between devices  36 us (27%)
  blocking collectives  35.6 us (26%)
  Pallas kernels  30 us (22%)
  starting transfers between devices  21.1 us (16%)
  local copies, waits for them, and re-layouts  7.72 us (6%)
  other arithmetic  2.54 us (2%)
    all_to_all x1, blocking collectives, body(): mixed = lax.all_to_all(mixed, SEQ, split_axis=0, concat_axis=0, tiled=True)  35.6 us
    all_to_all x1, waiting for transfers between devices, exchange(): flat = lax.all_to_all(flat, SEQ, split_axis=0, concat_axis=0, tiled=True)  16.5 us
    pallas_call x1, Pallas kernels, body(): call(attention_kernel, jax.ShapeDtypeStruct((shards, (half + 1) * PIX, 2...  14.1 us
    all_to_all x1, starting transfers between devices, exchange(): flat = lax.all_to_all(flat, SEQ, split_axis=0, concat_axis=0, tiled=True)  6.37 us
    pallas_call x1, Pallas kernels, body(): call(conv_kernel, packed, [SMEM, SMEM, VMEM, VMEM, VMEM, VMEM, VMEM], flo...  6.3 us
    unnamed x30, local copies, waits for them, and re-layouts  5.76 us
    ppermute x3, waiting for transfers between devices, reduce_all(): lax.ppermute(total, PLANE, swaps(n_plane, k))  4.7 us
    ppermute x3, waiting for transfers between devices, reduce_all(): parts.append(lax.ppermute(sent, PLANE, swaps(n_plane, k)).astype(F32))  4.54 us
  transfers between devices with their start and end apart: 13, of which 10 were waited for; matrix products, arithmetic and copies ran while one was open for 1% of the time, Pallas kernels for 4%

profile of v4, /device:TPU:0, one launch (start us, length us, event | category | flops | bytes accessed | tf_op | source)
XLA Modules:
  0.0 134.1 jit_solution(16753324927949222729)
XLA Ops:
  0.7 1.8 %dynamic-slice_bitcast_fusion = bf16[12,32,320]{2,1,0:T(8,128)(2,1)} fusion(bf16[12,4,32,320]{3,2,1,0:T(8,128)(2,1)} %lat_ref.1, s32[]{:T(128)S(6)} %select_n.41), kind=kLoop, calls=%fused_computation.6 | loop fusion | bytes 491524 | tf_op jit(solution)/shard_map/jit(dynamic_index_in_dim)/squeeze | solution.py:528
  2.4 2.9 %collective-permute-start = (bf16[12,32,320]{2,1,0:T(8,128)(2,1)}, bf16[12,32,320]{2,1,0:T(8,128)(2,1)}, u32[]{:S(2)}, u32[]{:S(2)}) collective-permute-start(bf16[12,32,320]{2,1,0:T(8,128)(2,1)} %dynamic-slice_bitcast_fusion), channel_id=1, source_target_pairs={{0,1},{1,0},{2,3},{3,2},{4,5},{5,4},{6,7},{7,6},{8,9},{9,8},{10,11... | collective-permute-start | bytes 737288 | tf_op jit(solution)/shard_map/ppermute | solution.py:529
  6.2 1.6 %copy-done.1 = bf16[3,3,320,320]{3,2,1,0:T(8,128)(2,1)S(1)} copy-done((bf16[3,3,320,320]{3,2,1,0:T(8,128)(2,1)S(1)}, bf16[3,3,320,320]{3,2,1,0:T(8,128)(2,1)}, u32[]{:S(2)}) %copy-start.1) | copy-done | bytes 1843224
  8.4 4.2 %collective-permute-done.top_ref.bot_ref = bf16[12,32,320]{2,1,0:T(8,128)(2,1)} collective-permute-done((bf16[12,32,320]{2,1,0:T(8,128)(2,1)}, bf16[12,32,320]{2,1,0:T(8,128)(2,1)}, u32[]{:S(2)}, u32[]{:S(2)}) %collective-permute-start) | collective-permute-done | bytes 245792 | tf_op jit(solution)/shard_map/ppermute | solution.py:529
  12.7 6.3 %shard_map.124 = bf16[16,6,8,640]{3,2,1,0:T(8,128)(2,1)} custom-call(s32[5]{0:T(128)S(1)} %stack.42.flag_ref, s32[4]{0:T(128)S(1)} %copy-done.9, bf16[12,4,32,320]{3,2,1,0:T(8,128)(2,1)S(1)} %copy-done.8, bf16[12,32,320]{2,1,0:T(8,128)(2,1)} %collective-permute-done.top_ref.bot_ref, bf16[12,32,320]{2,1,0:T(8,128)(2,1)} %collective-permute-done.top_ref.bot_ref, ...), custom_call_target="tpu_custom_call" | custom-call | flops 2831155200 | bytes 3809280 | tf_op jit(solution)/shard_map/pallas_call | solution.py:546
  19.0 6.4 %all-to-all-start = ((bf16[16,48,640]{2,1,0:T(8,128)(2,1)}), bf16[16,48,640]{2,1,0:T(8,128)(2,1)}, u32[]{:S(2)}, u32[]{:S(2)}) async-start(bf16[16,48,640]{2,1,0:T(8,128)(2,1)} %bitcast.5), calls=%async_computation | async-start | bytes 1966080 | tf_op jit(solution)/shard_map/all_to_all | solution.py:499
  26.8 0.8 shard_map.125
  27.6 0.9 copy-done.10
  28.5 0.9 copy-done.12
  29.4 0.7 copy-done.13
  30.8 16.5 %all-to-all-done = bf16[16,48,640]{2,1,0:T(8,128)(2,1)} async-done(((bf16[16,48,640]{2,1,0:T(8,128)(2,1)}), bf16[16,48,640]{2,1,0:T(8,128)(2,1)}, u32[]{:S(2)}, u32[]{:S(2)}) %all-to-all-start) | async-done | bytes 983072 | tf_op jit(solution)/shard_map/all_to_all | solution.py:499
  47.3 14.1 %shard_map.126 = bf16[16,56,640]{2,1,0:T(8,128)(2,1)} custom-call(bf16[768,640]{1,0:T(8,128)(2,1)} %bitcast.7.act_ref, bf16[384,1152]{1,0:T(8,128)(2,1)} %copy-done.12, bf16[384,384]{1,0:T(8,128)(2,1)} %copy-done.13, f32[192,192]{1,0:T(8,128)} %copy-done.14), custom_call_target="tpu_custom_call" | custom-call | flops 2202009600 | bytes 3932160 | tf_op jit(solution)/shard_map/pallas_call | solution.py:575
  61.4 35.6 %all_to_all.10.m_ref = bf16[16,56,640]{2,1,0:T(8,128)(2,1)S(1)} all-to-all(bf16[16,56,640]{2,1,0:T(8,128)(2,1)} %shard_map.126), channel_id=1, replica_groups=mesh['z'=4,'y'=2,'c'=2,'x'=2] {'z','y','c'}, dimensions={0} | all-to-all | bytes 2293760 | tf_op jit(solution)/shard_map/all_to_all | solution.py:585
  97.0 3.7 %shard_map.127 = (f32[480,320]{1,0:T(8,128)S(1)}, bf16[480,320]{1,0:T(8,128)(2,1)S(1)}) custom-call(s32[5]{0:T(128)S(1)} %stack.42.flag_ref, s32[4]{0:T(128)S(1)} %copy-done.9, bf16[16,56,640]{2,1,0:T(8,128)(2,1)S(1)} %all_to_all.10.m_ref, bf16[16,48,640]{2,1,0:T(8,128)(2,1)S(1)} %bitcast.25), custom_call_target="tpu_custom_call" | custom-call | flops 943718400 | bytes 2949120 | tf_op jit(solution)/shard_map/pallas_call | solution.py:587
  100.9 1.6 %collective-permute-done.1 = bf16[480,320]{1,0:T(8,128)(2,1)S(1)} collective-permute-done((bf16[480,320]{1,0:T(8,128)(2,1)S(1)}, bf16[480,320]{1,0:T(8,128)(2,1)S(1)}, u32[]{:S(2)}, u32[]{:S(2)}) %collective-permute-start.1) | collective-permute-done | bytes 307232 | tf_op jit(solution)/shard_map/ppermute | solution.py:478
  102.6 1.6 %collective-permute-start.2 = (bf16[120,320]{1,0:T(8,128)(2,1)S(1)}, bf16[120,320]{1,0:T(8,128)(2,1)S(1)}, u32[]{:S(2)}, u32[]{:S(2)}) collective-permute-start(bf16[120,320]{1,0:T(8,128)(2,1)S(1)} %get-tuple-element.34), channel_id=1, source_target_pairs={{0,1},{1,0},{4,5},{5,4},{2,3},{3,2},{6,7},{7,6},{8,9},{9,8},{12,13... | collective-permute-start | bytes 230408 | tf_op jit(solution)/shard_map/ppermute | solution.py:482
  104.8 1.4 %collective-permute-start.4 = (bf16[120,320]{1,0:T(8,128)(2,1)S(1)}, bf16[120,320]{1,0:T(8,128)(2,1)S(1)}, u32[]{:S(2)}, u32[]{:S(2)}) collective-permute-start(bf16[120,320]{1,0:T(8,128)(2,1)S(1)} %get-tuple-element.35), channel_id=1, source_target_pairs={{0,5},{1,4},{4,1},{5,0},{2,7},{3,6},{6,3},{7,2},{8,13},{9,12},{12,... | collective-permute-start | bytes 230408 | tf_op jit(solution)/shard_map/ppermute | solution.py:482
  106.1 1.2 collective-permute-done.2
  107.3 3.3 %collective-permute-done.3 = bf16[120,320]{1,0:T(8,128)(2,1)S(1)} collective-permute-done((bf16[120,320]{1,0:T(8,128)(2,1)S(1)}, bf16[120,320]{1,0:T(8,128)(2,1)S(1)}, u32[]{:S(2)}, u32[]{:S(2)}) %collective-permute-start.3) | collective-permute-done | bytes 76832 | tf_op jit(solution)/shard_map/ppermute | solution.py:482
  110.7 0.8 collective-permute-start.5
  111.5 1.3 %collective-permute-start.6 = (bf16[120,320]{1,0:T(8,128)(2,1)S(1)}, bf16[120,320]{1,0:T(8,128)(2,1)S(1)}, u32[]{:S(2)}, u32[]{:S(2)}) collective-permute-start(bf16[120,320]{1,0:T(8,128)(2,1)S(1)} %add_convert_fusion.1), channel_id=1, source_target_pairs={{0,16},{8,24},{16,0},{24,8},{1,17},{9,25},{17,1},{25,9},{2,18},{10... | collective-permute-start | bytes 230408 | tf_op jit(solution)/shard_map/ppermute | solution.py:486
  112.8 2.3 %collective-permute-start.7 = (bf16[120,320]{1,0:T(8,128)(2,1)S(1)}, bf16[120,320]{1,0:T(8,128)(2,1)S(1)}, u32[]{:S(2)}, u32[]{:S(2)}) collective-permute-start(bf16[120,320]{1,0:T(8,128)(2,1)S(1)} %add_convert_fusion.1), channel_id=1, source_target_pairs={{0,24},{8,16},{16,8},{24,0},{1,25},{9,17},{17,9},{25,1},{2,26},{10... | collective-permute-start | bytes 230408 | tf_op jit(solution)/shard_map/ppermute | solution.py:486
  115.2 0.8 collective-permute-done.5
  116.0 3.7 %collective-permute-done.6 = bf16[120,320]{1,0:T(8,128)(2,1)S(1)} collective-permute-done((bf16[120,320]{1,0:T(8,128)(2,1)S(1)}, bf16[120,320]{1,0:T(8,128)(2,1)S(1)}, u32[]{:S(2)}, u32[]{:S(2)}) %collective-permute-start.6) | collective-permute-done | bytes 76832 | tf_op jit(solution)/shard_map/ppermute | solution.py:486
  119.8 1.4 %collective-permute-start.8 = (bf16[120,320]{1,0:T(8,128)(2,1)S(1)}, bf16[120,320]{1,0:T(8,128)(2,1)S(1)}, u32[]{:S(2)}, u32[]{:S(2)}) collective-permute-start(bf16[120,320]{1,0:T(8,128)(2,1)S(1)} %add_convert_fusion), channel_id=1, source_target_pairs={{0,1},{1,0},{4,5},{5,4},{2,3},{3,2},{6,7},{7,6},{8,9},{9,8},{12,13... | collective-permute-start | bytes 230408 | tf_op jit(solution)/shard_map/ppermute | solution.py:488
  121.2 1.4 %collective-permute-start.9 = (bf16[120,320]{1,0:T(8,128)(2,1)S(1)}, bf16[120,320]{1,0:T(8,128)(2,1)S(1)}, u32[]{:S(2)}, u32[]{:S(2)}) collective-permute-start(bf16[120,320]{1,0:T(8,128)(2,1)S(1)} %add_convert_fusion), channel_id=1, source_target_pairs={{0,4},{1,5},{4,0},{5,1},{2,6},{3,7},{6,2},{7,3},{8,12},{9,13},{12,... | collective-permute-start | bytes 230408 | tf_op jit(solution)/shard_map/ppermute | solution.py:488
  122.6 0.8 collective-permute-start.10
  123.3 1.1 collective-permute-done.8
  124.4 1.3 %collective-permute-done.9 = bf16[120,320]{1,0:T(8,128)(2,1)S(1)} collective-permute-done((bf16[120,320]{1,0:T(8,128)(2,1)S(1)}, bf16[120,320]{1,0:T(8,128)(2,1)S(1)}, u32[]{:S(2)}, u32[]{:S(2)}) %collective-permute-start.9) | collective-permute-done | bytes 76832 | tf_op jit(solution)/shard_map/ppermute | solution.py:488
  125.7 2.3 %collective-permute-done.10 = bf16[120,320]{1,0:T(8,128)(2,1)S(1)} collective-permute-done((bf16[120,320]{1,0:T(8,128)(2,1)S(1)}, bf16[120,320]{1,0:T(8,128)(2,1)S(1)}, u32[]{:S(2)}, u32[]{:S(2)}) %collective-permute-start.10) | collective-permute-done | bytes 76832 | tf_op jit(solution)/shard_map/ppermute | solution.py:488
  128.3 4.4 %shard_map.128 = bf16[12,4,32,320]{3,2,1,0:T(8,128)(2,1)} custom-call(s32[5]{0:T(128)S(1)} %stack.42.flag_ref, s32[4]{0:T(128)S(1)} %copy-done.9, bf16[16,56,640]{2,1,0:T(8,128)(2,1)S(1)} %all_to_all.10.m_ref, bf16[1152,384]{1,0:T(8,128)(2,1)S(1)} %copy-done.11), custom_call_target="tpu_custom_call" | custom-call | flops 943718400 | bytes 2949120 | tf_op jit(solution)/shard_map/pallas_call | solution.py:596
  132.9 1.2 convert.3
  (48 shorter events, 5.0 us)
Async XLA Ops:
  0.6 7.5 %copy-start = (bf16[320,320]{1,0:T(8,128)(2,1)S(1)}, bf16[320,320]{1,0:T(8,128)(2,1)}, u32[]{:S(2)}) copy-start(bf16[320,320]{1,0:T(8,128)(2,1)} %param.15) | copy-start | bytes 614404
  2.4 10.3 %collective-permute-start = (bf16[12,32,320]{2,1,0:T(8,128)(2,1)}, bf16[12,32,320]{2,1,0:T(8,128)(2,1)}, u32[]{:S(2)}, u32[]{:S(2)}) collective-permute-start(bf16[12,32,320]{2,1,0:T(8,128)(2,1)} %dynamic-slice_bitcast_fusion), channel_id=1, source_target_pairs={{0,1},{1,0},{2,3},{3,2},{4,5},{5,4},{6,7},{7,6},{8,9},{9,8},{10,11... | collective-permute-start | bytes 737288 | tf_op jit(solution)/shard_map/ppermute | solution.py:529
  6.2 1.6 %copy-start.1 = (bf16[3,3,320,320]{3,2,1,0:T(8,128)(2,1)S(1)}, bf16[3,3,320,320]{3,2,1,0:T(8,128)(2,1)}, u32[]{:S(2)}) copy-start(bf16[3,3,320,320]{3,2,1,0:T(8,128)(2,1)} %w_ref.1) | copy-start | bytes 5529604
  7.8 4.9 %copy-start.8 = (bf16[12,4,32,320]{3,2,1,0:T(8,128)(2,1)S(1)}, bf16[12,4,32,320]{3,2,1,0:T(8,128)(2,1)}, u32[]{:S(2)}) copy-start(bf16[12,4,32,320]{3,2,1,0:T(8,128)(2,1)} %lat_ref.1) | copy-start | bytes 2949124
  7.8 4.9 %copy-start.9 = (s32[4]{0:T(128)S(1)}, s32[4]{0:T(128)}, u32[]{:S(2)}) copy-start(s32[4]{0:T(128)} %len_ref.7) | copy-start | bytes 52
  19.0 6.4 %copy-start.2 = (bf16[12,4,32,320]{3,2,1,0:T(8,128)(2,1)S(1)}, bf16[12,4,32,320]{3,2,1,0:T(8,128)(2,1)}, u32[]{:S(2)}) copy-start(bf16[12,4,32,320]{3,2,1,0:T(8,128)(2,1)} %x_ref.1) | copy-start | bytes 2949124
  19.0 28.3 %all-to-all-start = ((bf16[16,48,640]{2,1,0:T(8,128)(2,1)}), bf16[16,48,640]{2,1,0:T(8,128)(2,1)}, u32[]{:S(2)}, u32[]{:S(2)}) async-start(bf16[16,48,640]{2,1,0:T(8,128)(2,1)} %bitcast.5), calls=%async_computation | async-start | bytes 1966080 | tf_op jit(solution)/shard_map/all_to_all | solution.py:499
  25.4 1.1 copy-start.3
  25.4 1.2 copy-start.4
  25.4 1.2 copy-start.5
  25.4 1.3 copy-start.6
  25.4 1.3 %copy-start.7 = (bf16[320,320]{1,0:T(8,128)(2,1)S(1)}, bf16[320,320]{1,0:T(8,128)(2,1)}, u32[]{:S(2)}) copy-start(bf16[320,320]{1,0:T(8,128)(2,1)} %wo_ref.1) | copy-start | bytes 614404
  27.6 0.9 copy-start.10
  28.5 0.9 copy-start.12
  29.4 0.7 copy-start.13
  30.1 0.7 copy-start.14
  100.7 1.8 %collective-permute-start.1 = (bf16[480,320]{1,0:T(8,128)(2,1)S(1)}, bf16[480,320]{1,0:T(8,128)(2,1)S(1)}, u32[]{:S(2)}, u32[]{:S(2)}) collective-permute-start(bf16[480,320]{1,0:T(8,128)(2,1)S(1)} %get-tuple-element.31), channel_id=1, source_target_pairs={{0,2},{2,0},{1,3},{3,1},{4,6},{6,4},{5,7},{7,5},{8,10},{10,8},{9,1... | collective-permute-start | bytes 921608 | tf_op jit(solution)/shard_map/ppermute | solution.py:478
  102.6 4.8 %collective-permute-start.2 = (bf16[120,320]{1,0:T(8,128)(2,1)S(1)}, bf16[120,320]{1,0:T(8,128)(2,1)S(1)}, u32[]{:S(2)}, u32[]{:S(2)}) collective-permute-start(bf16[120,320]{1,0:T(8,128)(2,1)S(1)} %get-tuple-element.34), channel_id=1, source_target_pairs={{0,1},{1,0},{4,5},{5,4},{2,3},{3,2},{6,7},{7,6},{8,9},{9,8},{12,13... | collective-permute-start | bytes 230408 | tf_op jit(solution)/shard_map/ppermute | solution.py:482
  104.1 6.5 %collective-permute-start.3 = (bf16[120,320]{1,0:T(8,128)(2,1)S(1)}, bf16[120,320]{1,0:T(8,128)(2,1)S(1)}, u32[]{:S(2)}, u32[]{:S(2)}) collective-permute-start(bf16[120,320]{1,0:T(8,128)(2,1)S(1)} %get-tuple-element.36), channel_id=1, source_target_pairs={{0,4},{1,5},{4,0},{5,1},{2,6},{3,7},{6,2},{7,3},{8,12},{9,13},{12,... | collective-permute-start | bytes 230408 | tf_op jit(solution)/shard_map/ppermute | solution.py:482
  104.8 5.9 %collective-permute-start.4 = (bf16[120,320]{1,0:T(8,128)(2,1)S(1)}, bf16[120,320]{1,0:T(8,128)(2,1)S(1)}, u32[]{:S(2)}, u32[]{:S(2)}) collective-permute-start(bf16[120,320]{1,0:T(8,128)(2,1)S(1)} %get-tuple-element.35), channel_id=1, source_target_pairs={{0,5},{1,4},{4,1},{5,0},{2,7},{3,6},{6,3},{7,2},{8,13},{9,12},{12,... | collective-permute-start | bytes 230408 | tf_op jit(solution)/shard_map/ppermute | solution.py:482
  110.7 17.6 %copy-start.11 = (bf16[1152,384]{1,0:T(8,128)(2,1)S(1)}, bf16[1152,384]{1,0:T(8,128)(2,1)}, u32[]{:S(2)}) copy-start(bf16[1152,384]{1,0:T(8,128)(2,1)} %copy-done.10) | copy-start | bytes 2654212
  110.7 5.3 %collective-permute-start.5 = (bf16[120,320]{1,0:T(8,128)(2,1)S(1)}, bf16[120,320]{1,0:T(8,128)(2,1)S(1)}, u32[]{:S(2)}, u32[]{:S(2)}) collective-permute-start(bf16[120,320]{1,0:T(8,128)(2,1)S(1)} %add_convert_fusion.1), channel_id=1, source_target_pairs={{0,8},{8,0},{16,24},{24,16},{1,9},{9,1},{17,25},{25,17},{2,10},{10... | collective-permute-start | bytes 230408 | tf_op jit(solution)/shard_map/ppermute | solution.py:486
  111.5 8.2 %collective-permute-start.6 = (bf16[120,320]{1,0:T(8,128)(2,1)S(1)}, bf16[120,320]{1,0:T(8,128)(2,1)S(1)}, u32[]{:S(2)}, u32[]{:S(2)}) collective-permute-start(bf16[120,320]{1,0:T(8,128)(2,1)S(1)} %add_convert_fusion.1), channel_id=1, source_target_pairs={{0,16},{8,24},{16,0},{24,8},{1,17},{9,25},{17,1},{25,9},{2,18},{10... | collective-permute-start | bytes 230408 | tf_op jit(solution)/shard_map/ppermute | solution.py:486
  112.8 6.9 %collective-permute-start.7 = (bf16[120,320]{1,0:T(8,128)(2,1)S(1)}, bf16[120,320]{1,0:T(8,128)(2,1)S(1)}, u32[]{:S(2)}, u32[]{:S(2)}) collective-permute-start(bf16[120,320]{1,0:T(8,128)(2,1)S(1)} %add_convert_fusion.1), channel_id=1, source_target_pairs={{0,24},{8,16},{16,8},{24,0},{1,25},{9,17},{17,9},{25,1},{2,26},{10... | collective-permute-start | bytes 230408 | tf_op jit(solution)/shard_map/ppermute | solution.py:486
  119.8 4.6 %collective-permute-start.8 = (bf16[120,320]{1,0:T(8,128)(2,1)S(1)}, bf16[120,320]{1,0:T(8,128)(2,1)S(1)}, u32[]{:S(2)}, u32[]{:S(2)}) collective-permute-start(bf16[120,320]{1,0:T(8,128)(2,1)S(1)} %add_convert_fusion), channel_id=1, source_target_pairs={{0,1},{1,0},{4,5},{5,4},{2,3},{3,2},{6,7},{7,6},{8,9},{9,8},{12,13... | collective-permute-start | bytes 230408 | tf_op jit(solution)/shard_map/ppermute | solution.py:488
  121.2 4.6 %collective-permute-start.9 = (bf16[120,320]{1,0:T(8,128)(2,1)S(1)}, bf16[120,320]{1,0:T(8,128)(2,1)S(1)}, u32[]{:S(2)}, u32[]{:S(2)}) collective-permute-start(bf16[120,320]{1,0:T(8,128)(2,1)S(1)} %add_convert_fusion), channel_id=1, source_target_pairs={{0,4},{1,5},{4,0},{5,1},{2,6},{3,7},{6,2},{7,3},{8,12},{9,13},{12,... | collective-permute-start | bytes 230408 | tf_op jit(solution)/shard_map/ppermute | solution.py:488
  122.6 5.5 %collective-permute-start.10 = (bf16[120,320]{1,0:T(8,128)(2,1)S(1)}, bf16[120,320]{1,0:T(8,128)(2,1)S(1)}, u32[]{:S(2)}, u32[]{:S(2)}) collective-permute-start(bf16[120,320]{1,0:T(8,128)(2,1)S(1)} %add_convert_fusion), channel_id=1, source_target_pairs={{0,5},{1,4},{4,1},{5,0},{2,7},{3,6},{6,3},{7,2},{8,13},{9,12},{12,... | collective-permute-start | bytes 230408 | tf_op jit(solution)/shard_map/ppermute | solution.py:488
  128.2 4.5 %collective-permute-start.11 = (bf16[480,320]{1,0:T(8,128)(2,1)S(1)}, bf16[480,320]{1,0:T(8,128)(2,1)S(1)}, u32[]{:S(2)}, u32[]{:S(2)}) collective-permute-start(bf16[480,320]{1,0:T(8,128)(2,1)S(1)} %pad_maximum_fusion.2), channel_id=1, source_target_pairs={{0,2},{2,0},{1,3},{3,1},{4,6},{6,4},{5,7},{7,5},{8,10},{10,8},{9,1... | collective-permute-start | bytes 921608 | tf_op jit(solution)/shard_map/ppermute | solution.py:490

commit v5 on v4

--- a/solution.py
+++ b/solution.py
@@ -30,17 +30,20 @@
     return jnp.dot(embedded, time_weight.astype(F32), precision=lax.Precision.HIGHEST)
 
 
-def call(kernel, out_shape, in_spaces, scratch=(), flops=0, bytes_accessed=0, out_space=VMEM):
+def call(
+    kernel, out_shape, in_spaces, scratch=(), flops=0, bytes_accessed=0, out_space=VMEM, aliases=None, limit=VMEM_LIMIT
+):
     return pl.pallas_call(
         kernel,
         out_shape=out_shape,
         in_specs=[pl.BlockSpec(memory_space=s) for s in in_spaces],
         out_specs=jax.tree.map(lambda _: pl.BlockSpec(memory_space=out_space), out_shape),
         scratch_shapes=scratch,
+        input_output_aliases=aliases or {},
         cost_estimate=pl.CostEstimate(
             flops=flops, bytes_accessed=bytes_accessed, transcendentals=0
         ),
-        compiler_params=pltpu.CompilerParams(vmem_limit_bytes=VMEM_LIMIT if ANY not in in_spaces else WHOLE_VMEM),
+        compiler_params=pltpu.CompilerParams(vmem_limit_bytes=limit),
     )
 
 
@@ -114,14 +117,9 @@
     return 0.5 * v * (1.0 + jnp.tanh(0.5 * v))
 
 
-def conv_kernel(flag_ref, len_ref, lat_ref, top_ref, bot_ref, w_ref, table_ref, o_ref):
-    frames, rows, across, ch = lat_ref.shape
-    real = across * rows // o_ref.shape[0]
+def conv_rows(lines, store, count, n_rows, base, steps, len_ref, w_ref, table_ref):
     wide = 256
-    pos = rows * across
     low = low_lanes()
-    pairs = 3 if (frames // 2) % 3 == 0 else 1
-    count = 2 * pairs
 
     def clip_of(frame):
         bound = jnp.int32(0)
@@ -132,15 +130,11 @@
         return jnp.minimum(place, CLIPS - 1)
 
     def step(g, _):
-        kept = []
-        for k in range(count):
-            f = g * count + k
-            top, bot = top_ref[f], bot_ref[f]
-            top = jnp.where(flag_ref[0] > 0, top, jnp.zeros_like(top))
-            bot = jnp.where(flag_ref[1] > 0, bot, jnp.zeros_like(bot))
-            kept.append([top] + [lat_ref[f, i] for i in range(rows)] + [bot])
+        kept = [lines(g * count + k) for k in range(count)]
+        across = kept[0][0].shape[0]
+        pos = n_rows * across
         window = [
-            jnp.concatenate([r for lines in kept for r in lines[a : a + rows]], axis=0)
+            jnp.concatenate([r for one in kept for r in one[a : a + n_rows]], axis=0)
             for a in range(3)
         ]
         tails = [w[:, wide:] for w in window]
@@ -168,28 +162,88 @@
             cols.append(shifted(at(0), at(2)) + at(1))
         mid = y[:, 3 * wide : 3 * wide + 128]
         side = shifted(mid, y[:, 3 * wide + 128 :])
-        for k in range(pairs):
-            t = g * pairs + k
+        for k in range(count // 2):
+            t = g * (count // 2) + k
             even = slice(2 * k * pos, (2 * k + 1) * pos)
             odd = slice((2 * k + 1) * pos, (2 * k + 2) * pos)
-            base = flag_ref[2] + 2 * t
-            emb = [table_ref[pl.ds(clip_of(base + q), 1), :] for q in range(2)]
+            emb = [table_ref[pl.ds(clip_of(base + 2 * t + q), 1), :] for q in range(2)]
             for q, rs in enumerate((even, odd)):
                 for c in range(2):
                     lanes = slice(c * 128, (c + 1) * 128)
                     v = cols[c][rs] + emb[q][:, lanes]
                     got = window[1][rs, lanes].astype(F32) + silu(v)
-                    dst = slice(q * wide + c * 128, q * wide + (c + 1) * 128)
-                    store_groups(o_ref, t, dst, got, real)
+                    store(t, slice(q * wide + c * 128, q * wide + (c + 1) * 128), got)
             tail = jnp.where(
                 low, side[even] + swap_halves(mid[even]), swap_halves(side[odd]) + mid[odd]
             )
             tail = tail + jnp.concatenate([emb[0][:, wide:], emb[1][:, wide:]], axis=1)
             res = jnp.concatenate([tails[1][even], tails[1][odd]], axis=1).astype(F32)
-            store_groups(o_ref, t, slice(2 * wide, 2 * wide + 128), res + silu(tail), real)
+            store(t, slice(2 * wide, 2 * wide + 128), res + silu(tail))
         return 0
 
-    lax.fori_loop(0, frames // count, step, 0)
+    lax.fori_loop(0, steps, step, 0)
+
+
+def keep_if(condition, x):
+    return jnp.where(condition, x, jnp.zeros_like(x))
+
+
+def conv_kernel(flag_ref, len_ref, lat_ref, top_ref, bot_ref, w_ref, table_ref, o_ref):
+    frames, rows, across, _ = lat_ref.shape
+    real = across * rows // o_ref.shape[0]
+
+    def lines(f):
+        top = keep_if(flag_ref[0] > 0, top_ref[f])
+        bot = keep_if(flag_ref[1] > 0, bot_ref[f])
+        return [top] + [lat_ref[f, i] for i in range(rows)] + [bot]
+
+    def store(t, lanes, value):
+        store_groups(o_ref, t, lanes, value, real)
+
+    conv_rows(lines, store, 2, rows, flag_ref[2], frames // 2, len_ref, w_ref, table_ref)
+
+
+def inner_kernel(flag_ref, len_ref, lat_ref, w_ref, table_ref, o_ref):
+    frames, rows, across, _ = lat_ref.shape
+    groups = o_ref.shape[0] // rows
+    first = flag_ref[0]
+
+    def lines(f):
+        above = keep_if(first == 1, lat_ref[f, 0])
+        below = keep_if(first == 0, lat_ref[f, rows - 1])
+        return [above] + [lat_ref[f, k + first] for k in range(rows - 1)] + [below]
+
+    def store(t, lanes, value):
+        dst = o_ref.at[pl.ds(first * groups, (rows - 1) * groups)]
+        store_groups(dst, t, lanes, value, PIX)
+
+    count = 6 if frames % 6 == 0 else 2
+    conv_rows(
+        lines, store, count, rows - 1, flag_ref[2], frames // count, len_ref, w_ref, table_ref
+    )
+
+
+def edge_kernel(
+    flag_ref, len_ref, lat_ref, halo_ref, w_ref, table_ref, inner_hbm, o_hbm, edge, sem
+):
+    frames, rows, across, _ = lat_ref.shape
+    groups = edge.shape[0]
+    first = flag_ref[0]
+
+    def lines(f):
+        halo = halo_ref[f]
+        above = jnp.where(first == 1, halo, lat_ref[f, rows - 2])
+        below = jnp.where(first == 0, halo, lat_ref[f, 1])
+        return [above, lat_ref[f, (1 - first) * (rows - 1)], below]
+
+    def store(t, lanes, value):
+        store_groups(edge, t, lanes, value, PIX)
+
+    conv_rows(lines, store, frames, 1, flag_ref[2], 1, len_ref, w_ref, table_ref)
+    dst = o_hbm.at[pl.ds((1 - first) * (rows - 1) * groups, groups)]
+    out = pltpu.make_async_copy(edge, dst, sem)
+    out.start()
+    out.wait()
 
 
 def low_lanes():
@@ -465,7 +519,17 @@
     )
 
 
-def reduce_all(g, other):
+def finish_kernel(flag_ref, own_ref, other_ref, o_ref):
+    parts, share, _ = own_ref.shape
+    for k in range(parts):
+        at = (flag_ref[5] ^ k) * share
+        mine = at + flag_ref[4] * parts * share
+        theirs = at + (1 - flag_ref[4]) * parts * share
+        o_ref[pl.ds(pl.multiple_of(mine, 8), share), :] = own_ref[k].astype(F32)
+        o_ref[pl.ds(pl.multiple_of(theirs, 8), share), :] = other_ref[k].astype(F32)
+
+
+def reduce_all(g, other, block_out, flags):
     core = lax.axis_index("c")
     n_plane = lax.axis_size("y") * lax.axis_size("x")
     place = lax.axis_index("y") * lax.axis_size("x") + lax.axis_index("x")
@@ -481,16 +545,25 @@
         sent = cut(g, place ^ k, share).astype(BF16)
         parts.append(lax.ppermute(sent, PLANE, swaps(n_plane, k)).astype(F32))
     mine = tree(parts).astype(BF16)
+    mine, block_out = lax.optimization_barrier((mine, block_out))
     parts = [mine.astype(F32)]
     for k in range(1, n_z):
         parts.append(lax.ppermute(mine, "z", swaps(n_z, k)).astype(F32))
     total = tree(parts).astype(BF16)
     parts = [total] + [lax.ppermute(total, PLANE, swaps(n_plane, k)) for k in range(1, n_plane)]
-    own = ordered(parts, place)
+    if share % 8:
+        own = ordered(parts, place)
+        other = lax.ppermute(own, "c", swaps(2, 1))
+        low = jnp.where(core == 0, own, other)
+        high = jnp.where(core == 0, other, own)
+        return jnp.concatenate([low, high], 0).astype(F32), block_out
+    own = jnp.stack(parts)
     other = lax.ppermute(own, "c", swaps(2, 1))
-    low = jnp.where(core == 0, own, other)
-    high = jnp.where(core == 0, other, own)
-    return jnp.concatenate([low, high], 0).astype(F32)
+    whole = jax.ShapeDtypeStruct((2 * g.shape[0], g.shape[1]), F32)
+    grads = call(finish_kernel, whole, [SMEM, VMEM, VMEM], bytes_accessed=4 * g.size)(
+        flags, own, other
+    )
+    return grads, block_out
 
 
 def exchange(x):
@@ -533,8 +606,10 @@
         top = lax.ppermute(latents[:, rows - 1], "x", up)
         bot = lax.ppermute(latents[:, 0], "x", [(j, i) for i, j in up])
     seq = (lax.axis_index("z") * lax.axis_size("y") + lax.axis_index("y")) * 2 + lax.axis_index("c")
+    place = lax.axis_index("y") * n_rows + row
+    core = lax.axis_index("c")
     flags = jnp.stack(
-        [row > 0, row < n_rows - 1, seq * f_dev, shards * f_dev, lax.axis_index("c")]
+        [row > 0, row < n_rows - 1, seq * f_dev, shards * f_dev, core, place]
     ).astype(jnp.int32)
     table = time_table(timesteps, time_weight)
     taps = call(
@@ -543,13 +618,27 @@
         [VMEM],
         bytes_accessed=2 * size,
     )(spatial_weight)
-    active = call(
-        conv_kernel,
-        packed,
-        [SMEM, SMEM, VMEM, VMEM, VMEM, VMEM, VMEM],
-        flops=9 * dense,
-        bytes_accessed=2 * size + 9 * ch * ch * 2,
-    )(flags, clip_lengths, latents, top, bot, taps, table)
+    work = dict(flops=9 * dense, bytes_accessed=2 * size + 9 * ch * ch * 2)
+    if n_rows == 2 and rows * across == shards * PIX and rows > 2:
+        inner = call(inner_kernel, packed, [SMEM, SMEM] + [VMEM] * 3, **work)(
+            flags, clip_lengths, latents, taps, table
+        )
+        active = call(
+            edge_kernel,
+            packed,
+            [SMEM, SMEM] + [VMEM] * 4 + [ANY],
+            scratch=[
+                pltpu.VMEM((shards // rows, half, PIX, 2 * ch), BF16),
+                pltpu.SemaphoreType.DMA(()),
+            ],
+            out_space=ANY,
+            aliases={6: 0},
+            **work,
+        )(flags, clip_lengths, latents, top, taps, table, inner)
+    else:
+        active = call(conv_kernel, packed, [SMEM, SMEM] + [VMEM] * 5, **work)(
+            flags, clip_lengths, latents, top, bot, taps, table
+        )
     active = exchange(active)
     cot = call(pack_kernel, packed, [VMEM], bytes_accessed=2 * size)(cotangent)
 
@@ -581,6 +670,7 @@
         + [whole, pltpu.SemaphoreType.DMA((3,))],
         flops=7 * dense,
         bytes_accessed=4 * size,
+        limit=WHOLE_VMEM,
     )(active.reshape(flat.shape), wqkv, wo, bias)
     mixed = lax.all_to_all(mixed, SEQ, split_axis=0, concat_axis=0, tiled=True)
     half_grad = (3 * ch // 2, ch)
@@ -601,8 +691,8 @@
         flops=3 * dense,
         bytes_accessed=3 * size,
     )(flags, clip_lengths, mixed, tw)
-    grads = reduce_all(mine, other).reshape(3, ch, ch)
-    return block_out, grads
+    grads, block_out = reduce_all(mine, other, block_out, flags)
+    return block_out, grads.reshape(3, ch, ch)
 
 
 def solution(mesh):

time: 135 us -> 129 us (0.956)
  waiting for transfers between devices: 36 us -> 28.8 us
  Pallas kernels: 30 us -> 33.1 us
  other arithmetic: 2.54 us -> 1.08 us
    ppermute x3, waiting for transfers between devices: 4.54 us -> 0.01 us  [reduce_all(): parts.append(lax.ppermute(sent, PLANE, swaps(n_plane, k)).astype(F32))]
    ppermute x1, waiting for transfers between devices: 4.24 us -> 0.01 us  [body(): got = lax.ppermute(edge, 'x', swaps(2, 1))]
    pallas_call x1 -> x3, Pallas kernels: 6.3 us -> 9.39 us  [the longest x1 4.78 us: body(): call(inner_kernel, packed, [SMEM, SMEM] + [VMEM] * 3, **work)]
    ppermute x1, waiting for transfers between devices: 0.01 us -> 1.67 us  [reduce_all(): other = lax.ppermute(own, 'c', swaps(2, 1))]
    ppermute x3, waiting for transfers between devices: 4.7 us -> 3.31 us  [reduce_all(): lax.ppermute(total, PLANE, swaps(n_plane, k))]
  transfers between devices with their start and end apart: 13 -> 13, of which waited for: 10 -> 8; matrix products, arithmetic and copies ran while one was open for 1% -> 1% of each run, Pallas kernels for 4% -> 8%
where the time goes in v5:
time: 129 us
  blocking collectives  35.6 us (28%)
  Pallas kernels  33.1 us (26%)
  waiting for transfers between devices  28.8 us (22%)
  starting transfers between devices  20.9 us (16%)
  local copies, waits for them, and re-layouts  8.16 us (6%)
    all_to_all x1, blocking collectives, body(): mixed = lax.all_to_all(mixed, SEQ, split_axis=0, concat_axis=0, tiled=True)  35.6 us
    all_to_all x1, waiting for transfers between devices, exchange(): flat = lax.all_to_all(flat, SEQ, split_axis=0, concat_axis=0, tiled=True)  16.5 us
    pallas_call x1, Pallas kernels, body(): call(attention_kernel, jax.ShapeDtypeStruct((shards, (half + 1) * PIX, 2...  14.1 us
    unnamed x30, local copies, waits for them, and re-layouts  6.27 us
    all_to_all x1, starting transfers between devices, exchange(): flat = lax.all_to_all(flat, SEQ, split_axis=0, concat_axis=0, tiled=True)  6.11 us
    ppermute x3, waiting for transfers between devices, reduce_all(): parts.append(lax.ppermute(mine, 'z', swaps(n_z, k)).astype(F32))  5.73 us
    pallas_call x1, Pallas kernels, body(): call(inner_kernel, packed, [SMEM, SMEM] + [VMEM] * 3, **work)  4.78 us
    ppermute x3, starting transfers between devices, reduce_all(): parts.append(lax.ppermute(mine, 'z', swaps(n_z, k)).astype(F32))  4.45 us
  transfers between devices with their start and end apart: 13, of which 8 were waited for; matrix products, arithmetic and copies ran while one was open for 1% of the time, Pallas kernels for 8%

profile of v5, /device:TPU:0, one launch (start us, length us, event | category | flops | bytes accessed | tf_op | source)
XLA Modules:
  0.0 128.7 jit_solution(5976926927098581818)
XLA Ops:
  0.7 1.8 %dynamic-slice_bitcast_fusion = bf16[12,32,320]{2,1,0:T(8,128)(2,1)} fusion(bf16[12,4,32,320]{3,2,1,0:T(8,128)(2,1)} %lat_ref.3, s32[]{:T(128)S(6)} %select_n.16), kind=kLoop, calls=%fused_computation.2 | loop fusion | bytes 491524 | tf_op jit(solution)/shard_map/jit(dynamic_index_in_dim)/squeeze | solution.py:601
  2.4 2.9 %collective-permute-start = (bf16[12,32,320]{2,1,0:T(8,128)(2,1)}, bf16[12,32,320]{2,1,0:T(8,128)(2,1)}, u32[]{:S(2)}, u32[]{:S(2)}) collective-permute-start(bf16[12,32,320]{2,1,0:T(8,128)(2,1)} %dynamic-slice_bitcast_fusion), channel_id=1, source_target_pairs={{0,1},{1,0},{2,3},{3,2},{4,5},{5,4},{6,7},{7,6},{8,9},{9,8},{10,11... | collective-permute-start | bytes 737288 | tf_op jit(solution)/shard_map/ppermute | solution.py:602
  5.4 0.7 convert_element_type.45
  6.0 1.6 %copy-done.1 = bf16[3,3,320,320]{3,2,1,0:T(8,128)(2,1)S(1)} copy-done((bf16[3,3,320,320]{3,2,1,0:T(8,128)(2,1)S(1)}, bf16[3,3,320,320]{3,2,1,0:T(8,128)(2,1)}, u32[]{:S(2)}) %copy-start.1) | copy-done | bytes 1843224
  8.9 4.8 %shard_map.124.inner_hbm = bf16[16,6,8,640]{3,2,1,0:T(8,128)(2,1)} custom-call(s32[6]{0:T(128)S(1)} %stack.46.flag_ref, s32[4]{0:T(128)S(1)} %copy-done.9, bf16[12,4,32,320]{3,2,1,0:T(8,128)(2,1)S(1)} %copy-done.8, bf16[1024,1024]{1,0:T(8,128)(2,1)S(1)} %shard_map.123.w_ref, f32[4,320]{1,0:T(4,128)S(1)} %fusion.table_ref), custom_call_target="tpu_custom_call" | custom-call | flops 2831155200 | bytes 3809280 | tf_op jit(solution)/shard_map/pallas_call | solution.py:623
  13.7 2.9 %shard_map.125 = bf16[16,6,8,640]{3,2,1,0:T(8,128)(2,1)} custom-call(s32[6]{0:T(128)S(1)} %stack.46.flag_ref, s32[4]{0:T(128)S(1)} %copy-done.9, bf16[12,4,32,320]{3,2,1,0:T(8,128)(2,1)S(1)} %copy-done.8, bf16[12,32,320]{2,1,0:T(8,128)(2,1)} %collective-permute-done.halo_ref, ...), custom_call_target="tpu_custom_call", output_to_operand_aliasing={{}: (6, {})} | custom-call | flops 2831155200 | bytes 3809280 | tf_op jit(solution)/shard_map/pallas_call | solution.py:626
  16.6 6.1 %all-to-all-start = ((bf16[16,48,640]{2,1,0:T(8,128)(2,1)}), bf16[16,48,640]{2,1,0:T(8,128)(2,1)}, u32[]{:S(2)}, u32[]{:S(2)}) async-start(bf16[16,48,640]{2,1,0:T(8,128)(2,1)} %bitcast.6), calls=%async_computation | async-start | bytes 1966080 | tf_op jit(solution)/shard_map/all_to_all | solution.py:572
  24.1 0.8 shard_map.126
  24.9 0.9 copy-done.10
  25.9 0.9 copy-done.12
  26.8 0.7 copy-done.13
  27.5 0.7 copy-done.14
  28.2 16.5 %all-to-all-done = bf16[16,48,640]{2,1,0:T(8,128)(2,1)} async-done(((bf16[16,48,640]{2,1,0:T(8,128)(2,1)}), bf16[16,48,640]{2,1,0:T(8,128)(2,1)}, u32[]{:S(2)}, u32[]{:S(2)}) %all-to-all-start) | async-done | bytes 983072 | tf_op jit(solution)/shard_map/all_to_all | solution.py:572
  44.6 14.1 %shard_map.127 = bf16[16,56,640]{2,1,0:T(8,128)(2,1)} custom-call(bf16[768,640]{1,0:T(8,128)(2,1)} %bitcast.8.act_ref, bf16[384,1152]{1,0:T(8,128)(2,1)} %copy-done.12, bf16[384,384]{1,0:T(8,128)(2,1)} %copy-done.13, f32[192,192]{1,0:T(8,128)} %copy-done.14), custom_call_target="tpu_custom_call" | custom-call | flops 2202009600 | bytes 3932160 | tf_op jit(solution)/shard_map/pallas_call | solution.py:664
  58.7 35.6 %all_to_all.10.m_ref = bf16[16,56,640]{2,1,0:T(8,128)(2,1)S(1)} all-to-all(bf16[16,56,640]{2,1,0:T(8,128)(2,1)} %shard_map.127), channel_id=1, replica_groups=mesh['z'=4,'y'=2,'c'=2,'x'=2] {'z','y','c'}, dimensions={0} | all-to-all | bytes 2293760 | tf_op jit(solution)/shard_map/all_to_all | solution.py:675
  94.3 3.8 %shard_map.128 = (f32[480,320]{1,0:T(8,128)S(1)}, bf16[480,320]{1,0:T(8,128)(2,1)S(1)}) custom-call(s32[6]{0:T(128)S(1)} %stack.46.flag_ref, s32[4]{0:T(128)S(1)} %copy-done.9, bf16[16,56,640]{2,1,0:T(8,128)(2,1)S(1)} %all_to_all.10.m_ref, bf16[16,48,640]{2,1,0:T(8,128)(2,1)S(1)} %bitcast.17), custom_call_target="tpu_custom_call" | custom-call | flops 943718400 | bytes 2949120 | tf_op jit(solution)/shard_map/pallas_call | solution.py:677
  98.3 1.6 %collective-permute-done.1 = bf16[480,320]{1,0:T(8,128)(2,1)S(1)} collective-permute-done((bf16[480,320]{1,0:T(8,128)(2,1)S(1)}, bf16[480,320]{1,0:T(8,128)(2,1)S(1)}, u32[]{:S(2)}, u32[]{:S(2)}) %collective-permute-start.1) | collective-permute-done | bytes 307232 | tf_op jit(solution)/shard_map/ppermute | solution.py:542
  100.0 0.8 collective-permute-start.2
  101.4 2.1 %collective-permute-start.4 = (bf16[120,320]{1,0:T(8,128)(2,1)S(1)}, bf16[120,320]{1,0:T(8,128)(2,1)S(1)}, u32[]{:S(2)}, u32[]{:S(2)}) collective-permute-start(bf16[120,320]{1,0:T(8,128)(2,1)S(1)} %get-tuple-element.37), channel_id=1, source_target_pairs={{0,5},{1,4},{4,1},{5,0},{2,7},{3,6},{6,3},{7,2},{8,13},{9,12},{12,... | collective-permute-start | bytes 230408 | tf_op jit(solution)/shard_map/ppermute | solution.py:546
  103.6 4.3 %shard_map.129 = bf16[12,4,32,320]{3,2,1,0:T(8,128)(2,1)} custom-call(s32[6]{0:T(128)S(1)} %stack.46.flag_ref, s32[4]{0:T(128)S(1)} %copy-done.9, bf16[16,56,640]{2,1,0:T(8,128)(2,1)S(1)} %all_to_all.10.m_ref, bf16[1152,384]{1,0:T(8,128)(2,1)S(1)} %copy-done.11), custom_call_target="tpu_custom_call" | custom-call | flops 943718400 | bytes 2949120 | tf_op jit(solution)/shard_map/pallas_call | solution.py:686
  107.9 0.8 collective-permute-start.5
  108.7 1.3 %collective-permute-start.6 = (bf16[120,320]{1,0:T(8,128)(2,1)S(1)}, bf16[120,320]{1,0:T(8,128)(2,1)S(1)}, u32[]{:S(2)}, u32[]{:S(2)}) collective-permute-start(bf16[120,320]{1,0:T(8,128)(2,1)S(1)} %add_convert_fusion.1), channel_id=1, source_target_pairs={{0,16},{8,24},{16,0},{24,8},{1,17},{9,25},{17,1},{25,9},{2,18},{10... | collective-permute-start | bytes 230408 | tf_op jit(solution)/shard_map/ppermute | solution.py:551
  110.0 2.3 %collective-permute-start.7 = (bf16[120,320]{1,0:T(8,128)(2,1)S(1)}, bf16[120,320]{1,0:T(8,128)(2,1)S(1)}, u32[]{:S(2)}, u32[]{:S(2)}) collective-permute-start(bf16[120,320]{1,0:T(8,128)(2,1)S(1)} %add_convert_fusion.1), channel_id=1, source_target_pairs={{0,24},{8,16},{16,8},{24,0},{1,25},{9,17},{17,9},{25,1},{2,26},{10... | collective-permute-start | bytes 230408 | tf_op jit(solution)/shard_map/ppermute | solution.py:551
  112.4 0.8 collective-permute-done.5
  113.2 4.9 %collective-permute-done.6 = bf16[120,320]{1,0:T(8,128)(2,1)S(1)} collective-permute-done((bf16[120,320]{1,0:T(8,128)(2,1)S(1)}, bf16[120,320]{1,0:T(8,128)(2,1)S(1)}, u32[]{:S(2)}, u32[]{:S(2)}) %collective-permute-start.6) | collective-permute-done | bytes 76832 | tf_op jit(solution)/shard_map/ppermute | solution.py:551
  118.2 0.8 collective-permute-start.8
  119.6 2.1 %collective-permute-start.10 = (bf16[120,320]{1,0:T(8,128)(2,1)S(1)}, bf16[120,320]{1,0:T(8,128)(2,1)S(1)}, u32[]{:S(2)}, u32[]{:S(2)}) collective-permute-start(bf16[120,320]{1,0:T(8,128)(2,1)S(1)} %add_convert_fusion), channel_id=1, source_target_pairs={{0,5},{1,4},{4,1},{5,0},{2,7},{3,6},{6,3},{7,2},{8,13},{9,12},{12,... | collective-permute-start | bytes 230408 | tf_op jit(solution)/shard_map/ppermute | solution.py:553
  121.7 1.1 collective-permute-done.8
  122.8 0.7 collective-permute-done.9
  123.5 1.5 %collective-permute-done.10 = bf16[120,320]{1,0:T(8,128)(2,1)S(1)} collective-permute-done((bf16[120,320]{1,0:T(8,128)(2,1)S(1)}, bf16[120,320]{1,0:T(8,128)(2,1)S(1)}, u32[]{:S(2)}, u32[]{:S(2)}) %collective-permute-start.10) | collective-permute-done | bytes 76832 | tf_op jit(solution)/shard_map/ppermute | solution.py:553
  125.2 1.7 %collective-permute-done.11.other_ref = bf16[4,120,320]{2,1,0:T(8,128)(2,1)S(1)} collective-permute-done((bf16[4,120,320]{2,1,0:T(8,128)(2,1)S(1)}, bf16[4,120,320]{2,1,0:T(8,128)(2,1)S(1)}, u32[]{:S(2)}, u32[]{:S(2)}) %collective-permute-start.11) | collective-permute-done | bytes 307232 | tf_op jit(solution)/shard_map/ppermute | solution.py:561
  126.9 1.8 %shard_map.130 = f32[960,320]{1,0:T(8,128)} custom-call(s32[6]{0:T(128)S(1)} %stack.46.flag_ref, bf16[4,120,320]{2,1,0:T(8,128)(2,1)S(1)} %pad_maximum_fusion.own_ref, bf16[4,120,320]{2,1,0:T(8,128)(2,1)S(1)} %collective-permute-done.11.other_ref), custom_call_target="tpu_custom_call" | custom-call | bytes 614400 | tf_op jit(solution)/shard_map/pallas_call | solution.py:563
  (45 shorter events, 4.5 us)
Async XLA Ops:
  0.6 7.4 %copy-start = (bf16[320,320]{1,0:T(8,128)(2,1)S(1)}, bf16[320,320]{1,0:T(8,128)(2,1)}, u32[]{:S(2)}) copy-start(bf16[320,320]{1,0:T(8,128)(2,1)} %param.15) | copy-start | bytes 614404
  2.4 11.3 %collective-permute-start = (bf16[12,32,320]{2,1,0:T(8,128)(2,1)}, bf16[12,32,320]{2,1,0:T(8,128)(2,1)}, u32[]{:S(2)}, u32[]{:S(2)}) collective-permute-start(bf16[12,32,320]{2,1,0:T(8,128)(2,1)} %dynamic-slice_bitcast_fusion), channel_id=1, source_target_pairs={{0,1},{1,0},{2,3},{3,2},{4,5},{5,4},{6,7},{7,6},{8,9},{9,8},{10,11... | collective-permute-start | bytes 737288 | tf_op jit(solution)/shard_map/ppermute | solution.py:602
  6.0 1.6 %copy-start.1 = (bf16[3,3,320,320]{3,2,1,0:T(8,128)(2,1)S(1)}, bf16[3,3,320,320]{3,2,1,0:T(8,128)(2,1)}, u32[]{:S(2)}) copy-start(bf16[3,3,320,320]{3,2,1,0:T(8,128)(2,1)} %w_ref.1) | copy-start | bytes 5529604
  7.6 1.3 copy-start.8
  7.6 1.3 copy-start.9
  16.6 6.1 %copy-start.2 = (bf16[12,4,32,320]{3,2,1,0:T(8,128)(2,1)S(1)}, bf16[12,4,32,320]{3,2,1,0:T(8,128)(2,1)}, u32[]{:S(2)}) copy-start(bf16[12,4,32,320]{3,2,1,0:T(8,128)(2,1)} %x_ref.1) | copy-start | bytes 2949124
  16.6 28.0 %all-to-all-start = ((bf16[16,48,640]{2,1,0:T(8,128)(2,1)}), bf16[16,48,640]{2,1,0:T(8,128)(2,1)}, u32[]{:S(2)}, u32[]{:S(2)}) async-start(bf16[16,48,640]{2,1,0:T(8,128)(2,1)} %bitcast.6), calls=%async_computation | async-start | bytes 1966080 | tf_op jit(solution)/shard_map/all_to_all | solution.py:572
  22.7 1.1 copy-start.3
  22.7 1.2 copy-start.4
  22.7 1.2 copy-start.5
  22.7 1.3 copy-start.6
  22.8 1.3 %copy-start.7 = (bf16[320,320]{1,0:T(8,128)(2,1)S(1)}, bf16[320,320]{1,0:T(8,128)(2,1)}, u32[]{:S(2)}) copy-start(bf16[320,320]{1,0:T(8,128)(2,1)} %wo_ref.1) | copy-start | bytes 614404
  24.9 0.9 copy-start.10
  25.8 0.9 copy-start.12
  26.8 0.7 copy-start.13
  27.5 0.7 copy-start.14
  98.1 1.8 %collective-permute-start.1 = (bf16[480,320]{1,0:T(8,128)(2,1)S(1)}, bf16[480,320]{1,0:T(8,128)(2,1)S(1)}, u32[]{:S(2)}, u32[]{:S(2)}) collective-permute-start(bf16[480,320]{1,0:T(8,128)(2,1)S(1)} %get-tuple-element.31), channel_id=1, source_target_pairs={{0,2},{2,0},{1,3},{3,1},{4,6},{6,4},{5,7},{7,5},{8,10},{10,8},{9,1... | collective-permute-start | bytes 921608 | tf_op jit(solution)/shard_map/ppermute | solution.py:542
  98.3 5.3 %copy-start.11 = (bf16[1152,384]{1,0:T(8,128)(2,1)S(1)}, bf16[1152,384]{1,0:T(8,128)(2,1)}, u32[]{:S(2)}) copy-start(bf16[1152,384]{1,0:T(8,128)(2,1)} %copy-done.10) | copy-start | bytes 2654212
  100.0 7.9 %collective-permute-start.2 = (bf16[120,320]{1,0:T(8,128)(2,1)S(1)}, bf16[120,320]{1,0:T(8,128)(2,1)S(1)}, u32[]{:S(2)}, u32[]{:S(2)}) collective-permute-start(bf16[120,320]{1,0:T(8,128)(2,1)S(1)} %get-tuple-element.36), channel_id=1, source_target_pairs={{0,1},{1,0},{4,5},{5,4},{2,3},{3,2},{6,7},{7,6},{8,9},{9,8},{12,13... | collective-permute-start | bytes 230408 | tf_op jit(solution)/shard_map/ppermute | solution.py:546
  100.8 7.1 %collective-permute-start.3 = (bf16[120,320]{1,0:T(8,128)(2,1)S(1)}, bf16[120,320]{1,0:T(8,128)(2,1)S(1)}, u32[]{:S(2)}, u32[]{:S(2)}) collective-permute-start(bf16[120,320]{1,0:T(8,128)(2,1)S(1)} %get-tuple-element.38), channel_id=1, source_target_pairs={{0,4},{1,5},{4,0},{5,1},{2,6},{3,7},{6,2},{7,3},{8,12},{9,13},{12,... | collective-permute-start | bytes 230408 | tf_op jit(solution)/shard_map/ppermute | solution.py:546
  101.4 6.5 %collective-permute-start.4 = (bf16[120,320]{1,0:T(8,128)(2,1)S(1)}, bf16[120,320]{1,0:T(8,128)(2,1)S(1)}, u32[]{:S(2)}, u32[]{:S(2)}) collective-permute-start(bf16[120,320]{1,0:T(8,128)(2,1)S(1)} %get-tuple-element.37), channel_id=1, source_target_pairs={{0,5},{1,4},{4,1},{5,0},{2,7},{3,6},{6,3},{7,2},{8,13},{9,12},{12,... | collective-permute-start | bytes 230408 | tf_op jit(solution)/shard_map/ppermute | solution.py:546
  107.9 5.2 %collective-permute-start.5 = (bf16[120,320]{1,0:T(8,128)(2,1)S(1)}, bf16[120,320]{1,0:T(8,128)(2,1)S(1)}, u32[]{:S(2)}, u32[]{:S(2)}) collective-permute-start(bf16[120,320]{1,0:T(8,128)(2,1)S(1)} %add_convert_fusion.1), channel_id=1, source_target_pairs={{0,8},{8,0},{16,24},{24,16},{1,9},{9,1},{17,25},{25,17},{2,10},{10... | collective-permute-start | bytes 230408 | tf_op jit(solution)/shard_map/ppermute | solution.py:551
  108.7 9.4 %collective-permute-start.6 = (bf16[120,320]{1,0:T(8,128)(2,1)S(1)}, bf16[120,320]{1,0:T(8,128)(2,1)S(1)}, u32[]{:S(2)}, u32[]{:S(2)}) collective-permute-start(bf16[120,320]{1,0:T(8,128)(2,1)S(1)} %add_convert_fusion.1), channel_id=1, source_target_pairs={{0,16},{8,24},{16,0},{24,8},{1,17},{9,25},{17,1},{25,9},{2,18},{10... | collective-permute-start | bytes 230408 | tf_op jit(solution)/shard_map/ppermute | solution.py:551
  110.0 8.1 %collective-permute-start.7 = (bf16[120,320]{1,0:T(8,128)(2,1)S(1)}, bf16[120,320]{1,0:T(8,128)(2,1)S(1)}, u32[]{:S(2)}, u32[]{:S(2)}) collective-permute-start(bf16[120,320]{1,0:T(8,128)(2,1)S(1)} %add_convert_fusion.1), channel_id=1, source_target_pairs={{0,24},{8,16},{16,8},{24,0},{1,25},{9,17},{17,9},{25,1},{2,26},{10... | collective-permute-start | bytes 230408 | tf_op jit(solution)/shard_map/ppermute | solution.py:551
  118.2 4.6 %collective-permute-start.8 = (bf16[120,320]{1,0:T(8,128)(2,1)S(1)}, bf16[120,320]{1,0:T(8,128)(2,1)S(1)}, u32[]{:S(2)}, u32[]{:S(2)}) collective-permute-start(bf16[120,320]{1,0:T(8,128)(2,1)S(1)} %add_convert_fusion), channel_id=1, source_target_pairs={{0,1},{1,0},{4,5},{5,4},{2,3},{3,2},{6,7},{7,6},{8,9},{9,8},{12,13... | collective-permute-start | bytes 230408 | tf_op jit(solution)/shard_map/ppermute | solution.py:553
  119.0 4.6 %collective-permute-start.9 = (bf16[120,320]{1,0:T(8,128)(2,1)S(1)}, bf16[120,320]{1,0:T(8,128)(2,1)S(1)}, u32[]{:S(2)}, u32[]{:S(2)}) collective-permute-start(bf16[120,320]{1,0:T(8,128)(2,1)S(1)} %add_convert_fusion), channel_id=1, source_target_pairs={{0,4},{1,5},{4,0},{5,1},{2,6},{3,7},{6,2},{7,3},{8,12},{9,13},{12,... | collective-permute-start | bytes 230408 | tf_op jit(solution)/shard_map/ppermute | solution.py:553
  119.6 5.5 %collective-permute-start.10 = (bf16[120,320]{1,0:T(8,128)(2,1)S(1)}, bf16[120,320]{1,0:T(8,128)(2,1)S(1)}, u32[]{:S(2)}, u32[]{:S(2)}) collective-permute-start(bf16[120,320]{1,0:T(8,128)(2,1)S(1)} %add_convert_fusion), channel_id=1, source_target_pairs={{0,5},{1,4},{4,1},{5,0},{2,7},{3,6},{6,3},{7,2},{8,13},{9,12},{12,... | collective-permute-start | bytes 230408 | tf_op jit(solution)/shard_map/ppermute | solution.py:553
  125.1 1.8 %collective-permute-start.11 = (bf16[4,120,320]{2,1,0:T(8,128)(2,1)S(1)}, bf16[4,120,320]{2,1,0:T(8,128)(2,1)S(1)}, u32[]{:S(2)}, u32[]{:S(2)}) collective-permute-start(bf16[4,120,320]{2,1,0:T(8,128)(2,1)S(1)} %pad_maximum_fusion.own_ref), channel_id=1, source_target_pairs={{0,2},{2,0},{1,3},{3,1},{4,6},{6,4},{5,7},{7,5},{8,10},{10,8},{9,1... | collective-permute-start | bytes 921608 | tf_op jit(solution)/shard_map/ppermute | solution.py:561

commit v6 on v5

--- a/solution.py
+++ b/solution.py
@@ -22,12 +22,10 @@
 WHOLE_VMEM = 60 * 2**20
 
 
-def time_table(timesteps, time_weight):
-    half_width = time_weight.shape[0] // 2
+def angles_of(timesteps, half_width):
     frequency = jnp.exp(-math.log(10000.0) * jnp.arange(half_width, dtype=F32) / half_width)
     angles = timesteps.astype(F32)[:, None] * frequency[None, :]
-    embedded = jnp.concatenate([jnp.cos(angles), jnp.sin(angles)], axis=1)
-    return jnp.dot(embedded, time_weight.astype(F32), precision=lax.Precision.HIGHEST)
+    return jnp.cos(angles), jnp.sin(angles)
 
 
 def call(
@@ -81,7 +79,20 @@
     lax.fori_loop(0, frames // 2, step, 0)
 
 
-def conv_weight_kernel(w_ref, o_ref):
+def exact_product(x, w):
+    total = 0.0
+    for _ in range(3):
+        part = x.astype(BF16)
+        total = total + jnp.dot(part, w, preferred_element_type=F32)
+        x = x - part.astype(F32)
+    return total
+
+
+def conv_weight_kernel(w_ref, cos_ref, sin_ref, time_ref, o_ref, table_ref):
+    half_width = cos_ref.shape[1]
+    table_ref[...] = exact_product(cos_ref[...], time_ref[:half_width]) + exact_product(
+        sin_ref[...], time_ref[half_width:]
+    )
     ch = w_ref.shape[-1]
     wide = 256
     rest = ch - wide
@@ -278,23 +289,16 @@
     return -(-ch // 128) * 128
 
 
-def spread_units(m_ref, m32):
+def sources(m_ref, start, count, base, frames, len_ref):
     own = m_ref.shape[1] - PIX
-    for s in range(m_ref.shape[0]):
-        x = m_ref[s].astype(F32)
-        m32[s, PIX : PIX + own, :] = x[:own]
-        m32[s, 0:PIX, :] = x[own:]
-        m32[s, PIX + own :, :] = x[own:]
-
-
-def sources(m32, start, count, base, frames, len_ref):
-    own = m32.shape[1] - 2 * PIX
-
-    def rows(first):
-        x = m32[pl.ds(start, count), first : first + own, :]
-        return split_pair(x.reshape(count * own, x.shape[-1]))
-
-    cur, before, after = rows(PIX), rows(0)[1], rows(2 * PIX)[0]
+    x = m_ref[pl.ds(start, count)].astype(F32)
+
+    def pair(v):
+        return split_pair(v.reshape(count * own, v.shape[-1]))
+
+    cur = pair(x[:, :own])
+    before = pair(jnp.concatenate([x[:, own:], x[:, : own - PIX]], axis=1))[1]
+    after = pair(x[:, PIX:])[0]
     unit = lax.broadcasted_iota(jnp.int32, (count, own, 1), 1).reshape(count * own, 1) >> 3
     even = base + 2 * unit
     ids = [clip_ids(even + k, len_ref) for k in (-1, 0, 1, 2)]
@@ -323,7 +327,8 @@
 
 
 def attention_kernel(
-    act_ref, wqkv_hbm, wo_hbm, bias_hbm, o_ref, n5, d5, wqkv, wo, bias, m32, sems
+    act_hbm, wqkv_hbm, wo_hbm, bias_hbm, o_hbm,
+    n5, d5, wqkv, wo, bias, m32, act_ref, o_ref, sems, in_sems, out_sems
 ):
     rows, ch2 = act_ref.shape
     ch = ch2 // 2
@@ -331,16 +336,24 @@
     units = rows // PIX
     frames = units * 2
     head = ch // HEADS
+    chunk = 96
+
+    def arriving(i):
+        at = pl.ds(pl.multiple_of(i * chunk, 8), chunk)
+        return pltpu.make_async_copy(act_hbm.at[at], act_ref.at[at], in_sems.at[i])
+
+    for i in range(rows // chunk):
+        arriving(i).start()
     fetches = [
         pltpu.make_async_copy(src, dst, sems.at[k])
         for k, (src, dst) in enumerate(((wqkv_hbm, wqkv), (wo_hbm, wo), (bias_hbm, bias)))
     ]
     for f in fetches:
         f.start()
-    chunk = 96
     low = low_lanes()
 
     def norm(i, _):
+        arriving(i).wait()
         at = pl.ds(pl.multiple_of(i * chunk, 8), chunk)
         x = act_ref[at, :].astype(F32)
         cols = [x[:, c * 128 : (c + 1) * 128] for c in range(5)]
@@ -421,12 +434,17 @@
 
     own = o_ref.shape[1] - PIX
 
+    def leaving(i):
+        at = (i, pl.ds(0, own))
+        return pltpu.make_async_copy(o_ref.at[at], o_hbm.at[at], out_sems.at[i])
+
     def mix(i, _):
         at = pl.ds(pl.multiple_of(i * own, 8), own)
         delta = jnp.concatenate([d5[c, at, :] for c in range(5)], axis=1)
         m = (act_ref[at, :].astype(F32) + delta).astype(BF16)
         o_ref[i, 0:own, :] = m
         m32[at, :] = m.astype(F32)
+        leaving(i).start()
         return 0
 
     lax.fori_loop(0, rows // own, mix, 0)
@@ -440,22 +458,27 @@
         return 0
 
     lax.fori_loop(0, rows // own, edges, 0)
-
-
-def temporal_kernel(flag_ref, len_ref, m_ref, tw, o_ref, m32):
+    at = (slice(None), pl.ds(own, PIX))
+    last = pltpu.make_async_copy(o_ref.at[at], o_hbm.at[at], sems.at[3])
+    last.start()
+    for i in range(rows // own):
+        leaving(i).wait()
+    last.wait()
+
+
+def temporal_kernel(flag_ref, len_ref, m_ref, tw, o_ref):
     shards = m_ref.shape[0]
     frames, rows, across, ch = o_ref.shape
     units = frames // 2
     groups = shards // rows
     real = across // groups
     total_frames = flag_ref[3]
-    spread_units(m_ref, m32)
 
     def join(blocks):
         return jnp.concatenate([b[:real] for b in blocks], axis=0).astype(BF16)
 
     def step(i, _):
-        src = sources(m32, i * groups, groups, flag_ref[2], total_frames, len_ref)
+        src = sources(m_ref, i * groups, groups, flag_ref[2], total_frames, len_ref)
         rounded = jnp.concatenate([v.astype(BF16) for v in src], axis=1)
         total = src[1] + jnp.dot(rounded, tw[...], preferred_element_type=F32)
         total = total.reshape(2, groups, units, PIX, total.shape[-1])
@@ -468,15 +491,14 @@
     lax.fori_loop(0, rows, step, 0)
 
 
-def grad_kernel(flag_ref, len_ref, m_ref, cot_ref, mine_ref, other_ref, m32, grad, full):
+def grad_kernel(flag_ref, len_ref, m_ref, cot_ref, mine_ref, other_ref, grad, full):
     shards = m_ref.shape[0]
     ch = m_ref.shape[-1] // 2
     pad = dst_tile(ch)
     count = 8
-    spread_units(m_ref, m32)
 
     def step(i, _):
-        src = sources(m32, i * count, count, flag_ref[2], flag_ref[3], len_ref)
+        src = sources(m_ref, i * count, count, flag_ref[2], flag_ref[3], len_ref)
         rounded = jnp.concatenate([v.astype(BF16) for v in src], axis=1)
         cot = cot_ref[pl.ds(i * count, count), :, :].astype(F32)
         cot = split_pair(cot.reshape(-1, 2 * ch))
@@ -517,6 +539,15 @@
     return jnp.concatenate(
         [lax.dynamic_index_in_dim(stacked, place ^ j, 0, False) for j in range(len(parts))], 0
     )
+
+
+def shares_kernel(flag_ref, g_ref, got_ref, *refs):
+    outs, total = refs[:-1], refs[-1]
+    total[...] = g_ref[...] + got_ref[...].astype(F32)
+    for k, o_ref in enumerate(outs):
+        share = o_ref.shape[0]
+        at = pl.ds(pl.multiple_of((flag_ref[5] ^ k) * share, 8), share)
+        o_ref[...] = total[at, :].astype(o_ref.dtype)
 
 
 def finish_kernel(flag_ref, own_ref, other_ref, o_ref):
@@ -539,10 +570,23 @@
     def cut(v, i, size):
         return lax.dynamic_slice_in_dim(v, i * size, size, 0)
 
-    g = g + lax.ppermute(other, "c", swaps(2, 1)).astype(F32)
-    parts = [cut(g, place, share)]
-    for k in range(1, n_plane):
-        sent = cut(g, place ^ k, share).astype(BF16)
+    got = lax.ppermute(other, "c", swaps(2, 1))
+    if share % 8:
+        g = g + got.astype(F32)
+        cuts = [cut(g, place, share)]
+        cuts += [cut(g, place ^ k, share).astype(BF16) for k in range(1, n_plane)]
+    else:
+        kinds = [jax.ShapeDtypeStruct((share, g.shape[1]), F32 if k == 0 else BF16) for k in range(n_plane)]
+        cuts = call(
+            shares_kernel,
+            kinds,
+            [SMEM, VMEM, VMEM],
+            scratch=[pltpu.VMEM(g.shape, F32)],
+            bytes_accessed=10 * g.size,
+        )(flags, g, got)
+    parts = [cuts[0]]
+    for sent in cuts[1:]:
+        k = len(parts)
         parts.append(lax.ppermute(sent, PLANE, swaps(n_plane, k)).astype(F32))
     mine = tree(parts).astype(BF16)
     mine, block_out = lax.optimization_barrier((mine, block_out))
@@ -611,13 +655,12 @@
     flags = jnp.stack(
         [row > 0, row < n_rows - 1, seq * f_dev, shards * f_dev, core, place]
     ).astype(jnp.int32)
-    table = time_table(timesteps, time_weight)
-    taps = call(
+    taps, table = call(
         conv_weight_kernel,
-        jax.ShapeDtypeStruct((1024, 1024), BF16),
-        [VMEM],
+        (jax.ShapeDtypeStruct((1024, 1024), BF16), jax.ShapeDtypeStruct((CLIPS, ch), F32)),
+        [VMEM] * 4,
         bytes_accessed=2 * size,
-    )(spatial_weight)
+    )(spatial_weight, *angles_of(timesteps, ch // 2), time_weight)
     work = dict(flops=9 * dense, bytes_accessed=2 * size + 9 * ch * ch * 2)
     if n_rows == 2 and rows * across == shards * PIX and rows > 2:
         inner = call(inner_kernel, packed, [SMEM, SMEM] + [VMEM] * 3, **work)(
@@ -648,7 +691,6 @@
     tiles = -(-ch // 128)
     columns = pltpu.VMEM((5, n_packed, 128), F32)
     whole = pltpu.VMEM(flat.shape, F32)
-    around = pltpu.VMEM((shards, (half + 2) * PIX, 2 * ch), F32)
     pad = tiles * 128
     weights = [
         jax.ShapeDtypeStruct((pad, 3 * pad), BF16),
@@ -664,10 +706,18 @@
     mixed = call(
         attention_kernel,
         jax.ShapeDtypeStruct((shards, (half + 1) * PIX, 2 * ch), BF16),
-        [VMEM] + [ANY] * 3,
+        [ANY] * 4,
         scratch=[columns, columns]
         + [pltpu.VMEM(w.shape, w.dtype) for w in (weights[0], weights[1], weights[3])]
-        + [whole, pltpu.SemaphoreType.DMA((3,))],
+        + [
+            whole,
+            pltpu.VMEM(flat.shape, BF16),
+            pltpu.VMEM((shards, (half + 1) * PIX, 2 * ch), BF16),
+            pltpu.SemaphoreType.DMA((4,)),
+            pltpu.SemaphoreType.DMA((n_packed // 96,)),
+            pltpu.SemaphoreType.DMA((shards,)),
+        ],
+        out_space=ANY,
         flops=7 * dense,
         bytes_accessed=4 * size,
         limit=WHOLE_VMEM,
@@ -678,7 +728,7 @@
         grad_kernel,
         (jax.ShapeDtypeStruct(half_grad, F32), jax.ShapeDtypeStruct(half_grad, BF16)),
         [SMEM, SMEM, VMEM, VMEM],
-        scratch=[around, pltpu.VMEM((pad, 3 * pad), F32), pltpu.VMEM((3 * ch, ch), F32)],
+        scratch=[pltpu.VMEM((pad, 3 * pad), F32), pltpu.VMEM((3 * ch, ch), F32)],
         flops=3 * dense,
         bytes_accessed=3 * size,
     )(flags, clip_lengths, mixed, cot.reshape(shards, half * PIX, 2 * ch))
@@ -687,7 +737,6 @@
         temporal_kernel,
         jax.ShapeDtypeStruct(latents.shape, BF16),
         [SMEM, SMEM, VMEM, VMEM],
-        scratch=[around],
         flops=3 * dense,
         bytes_accessed=3 * size,
     )(flags, clip_lengths, mixed, tw)

time: 129 us -> 131 us (1.016)
  local copies, waits for them, and re-layouts: 8.16 us -> 9.78 us
    unnamed x30, local copies, waits for them, and re-layouts: 6.27 us -> 8.7 us
where the time goes in v6:
time: 131 us
  blocking collectives  35.6 us (27%)
  Pallas kernels  32.7 us (25%)
  waiting for transfers between devices  29.9 us (23%)
  starting transfers between devices  20.9 us (16%)
  local copies, waits for them, and re-layouts  9.78 us (7%)
    all_to_all x1, blocking collectives, body(): mixed = lax.all_to_all(mixed, SEQ, split_axis=0, concat_axis=0, tiled=True)  35.6 us
    all_to_all x1, waiting for transfers between devices, exchange(): flat = lax.all_to_all(flat, SEQ, split_axis=0, concat_axis=0, tiled=True)  17.4 us
    pallas_call x1, Pallas kernels, body(): call(attention_kernel, jax.ShapeDtypeStruct((shards, (half + 1) * PIX, 2...  13.6 us
    unnamed x30, local copies, waits for them, and re-layouts  8.7 us
    ppermute x3, waiting for transfers between devices, reduce_all(): parts.append(lax.ppermute(mine, 'z', swaps(n_z, k)).astype(F32))  6.21 us
    all_to_all x1, starting transfers between devices, exchange(): flat = lax.all_to_all(flat, SEQ, split_axis=0, concat_axis=0, tiled=True)  6.13 us
    pallas_call x1, Pallas kernels, body(): call(inner_kernel, packed, [SMEM, SMEM] + [VMEM] * 3, **work)  4.79 us
    ppermute x3, starting transfers between devices, reduce_all(): parts.append(lax.ppermute(mine, 'z', swaps(n_z, k)).astype(F32))  4.45 us
  transfers between devices with their start and end apart: 13, of which 8 were waited for; matrix products, arithmetic and copies ran while one was open for 1% of the time, Pallas kernels for 8%

profile of v6, /device:TPU:0, one launch (start us, length us, event | category | flops | bytes accessed | tf_op | source)
XLA Modules:
  0.0 130.8 jit_solution(4296747178675121611)
XLA Ops:
  0.6 1.0 dynamic-slice_bitcast_fusion
  1.6 3.0 %collective-permute-start = (bf16[12,32,320]{2,1,0:T(8,128)(2,1)S(1)}, bf16[12,32,320]{2,1,0:T(8,128)(2,1)S(1)}, u32[]{:S(2)}, u32[]{:S(2)}) collective-permute-start(bf16[12,32,320]{2,1,0:T(8,128)(2,1)S(1)} %dynamic-slice_bitcast_fusion), channel_id=1, source_target_pairs={{0,1},{1,0},{2,3},{3,2},{4,5},{5,4},{6,7},{7,6},{8,9},{9,8},{10,11... | collective-permute-start | bytes 737288 | tf_op jit(solution)/shard_map/ppermute | solution.py:646
  4.7 0.7 convert_element_type.32
  5.5 1.6 %copy-done = bf16[3,3,320,320]{3,2,1,0:T(8,128)(2,1)S(1)} copy-done((bf16[3,3,320,320]{3,2,1,0:T(8,128)(2,1)S(1)}, bf16[3,3,320,320]{3,2,1,0:T(8,128)(2,1)}, u32[]{:S(2)}) %copy-start) | copy-done | bytes 1843224
  7.1 0.9 copy-done.7
  8.4 1.4 %copy-done.10 = bf16[1024,1024]{1,0:T(8,128)(2,1)} copy-done((bf16[1024,1024]{1,0:T(8,128)(2,1)}, bf16[1024,1024]{1,0:T(8,128)(2,1)S(1)}, u32[]{:S(2)}) %copy-start.10) | copy-done | bytes 2097176
  9.9 1.6 %copy-done.11 = bf16[1024,1024]{1,0:T(8,128)(2,1)S(1)} copy-done((bf16[1024,1024]{1,0:T(8,128)(2,1)S(1)}, bf16[1024,1024]{1,0:T(8,128)(2,1)}, u32[]{:S(2)}) %copy-start.11) | copy-done | bytes 2097176
  11.4 4.8 %shard_map.124.inner_hbm = bf16[16,6,8,640]{3,2,1,0:T(8,128)(2,1)} custom-call(s32[6]{0:T(128)S(1)} %stack.46.flag_ref, s32[4]{0:T(128)S(1)} %copy-done.9, bf16[12,4,32,320]{3,2,1,0:T(8,128)(2,1)S(1)} %copy-done.8, bf16[1024,1024]{1,0:T(8,128)(2,1)S(1)} %copy-done.11, f32[4,320]{1,0:T(4,128)S(1)} %get-tuple-element.26.table_ref), custom_call_target="tpu_custom_call" | custom-call | flops 2831155200 | bytes 3809280 | tf_op jit(solution)/shard_map/pallas_call | solution.py:666
  16.2 2.4 %shard_map.125 = bf16[16,6,8,640]{3,2,1,0:T(8,128)(2,1)} custom-call(s32[6]{0:T(128)S(1)} %stack.46.flag_ref, s32[4]{0:T(128)S(1)} %copy-done.9, bf16[12,4,32,320]{3,2,1,0:T(8,128)(2,1)S(1)} %copy-done.8, bf16[12,32,320]{2,1,0:T(8,128)(2,1)S(1)} %collective-permute-done.halo_ref, bf16[1024,1024]{1,0:T(8,128)(2,1)S(1)} %copy-done.11, ...), custom_call_target="tpu_custom_call", output_to_operand_aliasing={{}: (6, {})} | custom-call | flops 2831155200 | bytes 3809280 | tf_op jit(solution)/shard_map/pallas_call | solution.py:669
  18.7 6.1 %all-to-all-start = ((bf16[16,48,640]{2,1,0:T(8,128)(2,1)}), bf16[16,48,640]{2,1,0:T(8,128)(2,1)}, u32[]{:S(2)}, u32[]{:S(2)}) async-start(bf16[16,48,640]{2,1,0:T(8,128)(2,1)} %bitcast.6), calls=%async_computation | async-start | bytes 1966080 | tf_op jit(solution)/shard_map/all_to_all | solution.py:616
  26.2 0.8 shard_map.126
  27.1 0.9 copy-done.12
  28.0 0.7 copy-done.13
  28.7 0.7 copy-done.14
  29.4 17.4 %all-to-all-done = bf16[16,48,640]{2,1,0:T(8,128)(2,1)} async-done(((bf16[16,48,640]{2,1,0:T(8,128)(2,1)}), bf16[16,48,640]{2,1,0:T(8,128)(2,1)}, u32[]{:S(2)}, u32[]{:S(2)}) %all-to-all-start) | async-done | bytes 983072 | tf_op jit(solution)/shard_map/all_to_all | solution.py:616
  46.7 13.6 %shard_map.127 = bf16[16,56,640]{2,1,0:T(8,128)(2,1)} custom-call(bf16[768,640]{1,0:T(8,128)(2,1)} %bitcast.8.act_hbm, bf16[384,1152]{1,0:T(8,128)(2,1)} %copy-done.12, bf16[384,384]{1,0:T(8,128)(2,1)} %copy-done.13, f32[192,192]{1,0:T(8,128)} %copy-done.14), custom_call_target="tpu_custom_call" | custom-call | flops 2202009600 | bytes 3932160 | tf_op jit(solution)/shard_map/pallas_call | solution.py:706
  60.4 35.6 %all_to_all.10.m_ref = bf16[16,56,640]{2,1,0:T(8,128)(2,1)S(1)} all-to-all(bf16[16,56,640]{2,1,0:T(8,128)(2,1)} %shard_map.127), channel_id=1, replica_groups=mesh['z'=4,'y'=2,'c'=2,'x'=2] {'z','y','c'}, dimensions={0} | all-to-all | bytes 2293760 | tf_op jit(solution)/shard_map/all_to_all | solution.py:725
  96.0 3.6 %shard_map.128 = (f32[480,320]{1,0:T(8,128)S(1)}, bf16[480,320]{1,0:T(8,128)(2,1)S(1)}) custom-call(s32[6]{0:T(128)S(1)} %stack.46.flag_ref, s32[4]{0:T(128)S(1)} %copy-done.9, bf16[16,56,640]{2,1,0:T(8,128)(2,1)S(1)} %all_to_all.10.m_ref, bf16[16,48,640]{2,1,0:T(8,128)(2,1)S(1)} %bitcast.16), custom_call_target="tpu_custom_call" | custom-call | flops 943718400 | bytes 2949120 | tf_op jit(solution)/shard_map/pallas_call | solution.py:727
  99.8 1.6 %collective-permute-done.1.got_ref = bf16[480,320]{1,0:T(8,128)(2,1)S(1)} collective-permute-done((bf16[480,320]{1,0:T(8,128)(2,1)S(1)}, bf16[480,320]{1,0:T(8,128)(2,1)S(1)}, u32[]{:S(2)}, u32[]{:S(2)}) %collective-permute-start.1) | collective-permute-done | bytes 307232 | tf_op jit(solution)/shard_map/ppermute | solution.py:573
  101.4 0.7 shard_map.129
  103.3 2.3 %collective-permute-start.4 = (bf16[120,320]{1,0:T(8,128)(2,1)S(1)}, bf16[120,320]{1,0:T(8,128)(2,1)S(1)}, u32[]{:S(2)}, u32[]{:S(2)}) collective-permute-start(bf16[120,320]{1,0:T(8,128)(2,1)S(1)} %get-tuple-element.43), channel_id=1, source_target_pairs={{0,5},{1,4},{4,1},{5,0},{2,7},{3,6},{6,3},{7,2},{8,13},{9,12},{12,... | collective-permute-start | bytes 230408 | tf_op jit(solution)/shard_map/ppermute | solution.py:590
  105.6 4.2 %shard_map.130 = bf16[12,4,32,320]{3,2,1,0:T(8,128)(2,1)} custom-call(s32[6]{0:T(128)S(1)} %stack.46.flag_ref, s32[4]{0:T(128)S(1)} %copy-done.9, bf16[16,56,640]{2,1,0:T(8,128)(2,1)S(1)} %all_to_all.10.m_ref, bf16[1152,384]{1,0:T(8,128)(2,1)S(1)} %get-tuple-element.45.tw), custom_call_target="tpu_custom_call" | custom-call | flops 943718400 | bytes 2949120 | tf_op jit(solution)/shard_map/pallas_call | solution.py:736
  109.9 1.5 %collective-permute-start.7 = (bf16[120,320]{1,0:T(8,128)(2,1)S(1)}, bf16[120,320]{1,0:T(8,128)(2,1)S(1)}, u32[]{:S(2)}, u32[]{:S(2)}) collective-permute-start(bf16[120,320]{1,0:T(8,128)(2,1)S(1)} %add_convert_fusion.1), channel_id=1, source_target_pairs={{0,24},{8,16},{16,8},{24,0},{1,25},{9,17},{17,9},{25,1},{2,26},{10... | collective-permute-start | bytes 230408 | tf_op jit(solution)/shard_map/ppermute | solution.py:595
  111.4 0.7 collective-permute-start.6
  112.1 2.2 %collective-permute-start.5 = (bf16[120,320]{1,0:T(8,128)(2,1)S(1)}, bf16[120,320]{1,0:T(8,128)(2,1)S(1)}, u32[]{:S(2)}, u32[]{:S(2)}) collective-permute-start(bf16[120,320]{1,0:T(8,128)(2,1)S(1)} %add_convert_fusion.1), channel_id=1, source_target_pairs={{0,8},{8,0},{16,24},{24,16},{1,9},{9,1},{17,25},{25,17},{2,10},{10... | collective-permute-start | bytes 230408 | tf_op jit(solution)/shard_map/ppermute | solution.py:595
  114.3 3.0 %collective-permute-done.7 = bf16[120,320]{1,0:T(8,128)(2,1)S(1)} collective-permute-done((bf16[120,320]{1,0:T(8,128)(2,1)S(1)}, bf16[120,320]{1,0:T(8,128)(2,1)S(1)}, u32[]{:S(2)}, u32[]{:S(2)}) %collective-permute-start.7) | collective-permute-done | bytes 76832 | tf_op jit(solution)/shard_map/ppermute | solution.py:595
  117.4 3.2 %collective-permute-done.6 = bf16[120,320]{1,0:T(8,128)(2,1)S(1)} collective-permute-done((bf16[120,320]{1,0:T(8,128)(2,1)S(1)}, bf16[120,320]{1,0:T(8,128)(2,1)S(1)}, u32[]{:S(2)}, u32[]{:S(2)}) %collective-permute-start.6) | collective-permute-done | bytes 76832 | tf_op jit(solution)/shard_map/ppermute | solution.py:595
  121.2 1.4 %collective-permute-start.9 = (bf16[120,320]{1,0:T(8,128)(2,1)S(1)}, bf16[120,320]{1,0:T(8,128)(2,1)S(1)}, u32[]{:S(2)}, u32[]{:S(2)}) collective-permute-start(bf16[120,320]{1,0:T(8,128)(2,1)S(1)} %add_convert_fusion), channel_id=1, source_target_pairs={{0,4},{1,5},{4,0},{5,1},{2,6},{3,7},{6,2},{7,3},{8,12},{9,13},{12,... | collective-permute-start | bytes 230408 | tf_op jit(solution)/shard_map/ppermute | solution.py:597
  122.6 1.5 %collective-permute-start.8 = (bf16[120,320]{1,0:T(8,128)(2,1)S(1)}, bf16[120,320]{1,0:T(8,128)(2,1)S(1)}, u32[]{:S(2)}, u32[]{:S(2)}) collective-permute-start(bf16[120,320]{1,0:T(8,128)(2,1)S(1)} %add_convert_fusion), channel_id=1, source_target_pairs={{0,1},{1,0},{4,5},{5,4},{2,3},{3,2},{6,7},{7,6},{8,9},{9,8},{12,13... | collective-permute-start | bytes 230408 | tf_op jit(solution)/shard_map/ppermute | solution.py:597
  124.1 2.3 %collective-permute-done.10 = bf16[120,320]{1,0:T(8,128)(2,1)S(1)} collective-permute-done((bf16[120,320]{1,0:T(8,128)(2,1)S(1)}, bf16[120,320]{1,0:T(8,128)(2,1)S(1)}, u32[]{:S(2)}, u32[]{:S(2)}) %collective-permute-start.10) | collective-permute-done | bytes 76832 | tf_op jit(solution)/shard_map/ppermute | solution.py:597
  127.4 1.7 %collective-permute-done.11.other_ref = bf16[4,120,320]{2,1,0:T(8,128)(2,1)S(1)} collective-permute-done((bf16[4,120,320]{2,1,0:T(8,128)(2,1)S(1)}, bf16[4,120,320]{2,1,0:T(8,128)(2,1)S(1)}, u32[]{:S(2)}, u32[]{:S(2)}) %collective-permute-start.11) | collective-permute-done | bytes 307232 | tf_op jit(solution)/shard_map/ppermute | solution.py:605
  129.0 1.8 %shard_map.131 = f32[960,320]{1,0:T(8,128)} custom-call(s32[6]{0:T(128)S(1)} %stack.46.flag_ref, bf16[4,120,320]{2,1,0:T(8,128)(2,1)S(1)} %pad_maximum_fusion.own_ref, bf16[4,120,320]{2,1,0:T(8,128)(2,1)S(1)} %collective-permute-done.11.other_ref), custom_call_target="tpu_custom_call" | custom-call | bytes 614400 | tf_op jit(solution)/shard_map/pallas_call | solution.py:607
  (43 shorter events, 5.1 us)
Async XLA Ops:
  1.6 14.6 %collective-permute-start = (bf16[12,32,320]{2,1,0:T(8,128)(2,1)S(1)}, bf16[12,32,320]{2,1,0:T(8,128)(2,1)S(1)}, u32[]{:S(2)}, u32[]{:S(2)}) collective-permute-start(bf16[12,32,320]{2,1,0:T(8,128)(2,1)S(1)} %dynamic-slice_bitcast_fusion), channel_id=1, source_target_pairs={{0,1},{1,0},{2,3},{3,2},{4,5},{5,4},{6,7},{7,6},{8,9},{9,8},{10,11... | collective-permute-start | bytes 737288 | tf_op jit(solution)/shard_map/ppermute | solution.py:646
  5.4 1.6 %copy-start = (bf16[3,3,320,320]{3,2,1,0:T(8,128)(2,1)S(1)}, bf16[3,3,320,320]{3,2,1,0:T(8,128)(2,1)}, u32[]{:S(2)}) copy-start(bf16[3,3,320,320]{3,2,1,0:T(8,128)(2,1)} %w_ref.1) | copy-start | bytes 5529604
  7.1 0.9 copy-start.7
  8.0 1.8 %copy-start.8 = (bf16[12,4,32,320]{3,2,1,0:T(8,128)(2,1)S(1)}, bf16[12,4,32,320]{3,2,1,0:T(8,128)(2,1)}, u32[]{:S(2)}) copy-start(bf16[12,4,32,320]{3,2,1,0:T(8,128)(2,1)} %lat_ref.3) | copy-start | bytes 2949124
  8.0 1.8 %copy-start.9 = (s32[4]{0:T(128)S(1)}, s32[4]{0:T(128)}, u32[]{:S(2)}) copy-start(s32[4]{0:T(128)} %len_ref.9) | copy-start | bytes 52
  8.4 1.4 %copy-start.10 = (bf16[1024,1024]{1,0:T(8,128)(2,1)}, bf16[1024,1024]{1,0:T(8,128)(2,1)S(1)}, u32[]{:S(2)}) copy-start(bf16[1024,1024]{1,0:T(8,128)(2,1)S(1)} %get-tuple-element.25.w_ref) | copy-start | bytes 6291460
  9.9 1.6 %copy-start.11 = (bf16[1024,1024]{1,0:T(8,128)(2,1)S(1)}, bf16[1024,1024]{1,0:T(8,128)(2,1)}, u32[]{:S(2)}) copy-start(bf16[1024,1024]{1,0:T(8,128)(2,1)} %copy-done.10) | copy-start | bytes 6291460
  18.7 6.1 %copy-start.1 = (bf16[12,4,32,320]{3,2,1,0:T(8,128)(2,1)S(1)}, bf16[12,4,32,320]{3,2,1,0:T(8,128)(2,1)}, u32[]{:S(2)}) copy-start(bf16[12,4,32,320]{3,2,1,0:T(8,128)(2,1)} %x_ref.1) | copy-start | bytes 2949124
  18.7 28.1 %all-to-all-start = ((bf16[16,48,640]{2,1,0:T(8,128)(2,1)}), bf16[16,48,640]{2,1,0:T(8,128)(2,1)}, u32[]{:S(2)}, u32[]{:S(2)}) async-start(bf16[16,48,640]{2,1,0:T(8,128)(2,1)} %bitcast.6), calls=%async_computation | async-start | bytes 1966080 | tf_op jit(solution)/shard_map/all_to_all | solution.py:616
  24.8 1.1 copy-start.2
  24.8 1.2 copy-start.3
  24.9 1.2 copy-start.4
  24.9 1.3 copy-start.5
  24.9 1.3 %copy-start.6 = (bf16[320,320]{1,0:T(8,128)(2,1)S(1)}, bf16[320,320]{1,0:T(8,128)(2,1)}, u32[]{:S(2)}) copy-start(bf16[320,320]{1,0:T(8,128)(2,1)} %wo_ref.1) | copy-start | bytes 614404
  27.0 0.9 copy-start.12
  28.0 0.7 copy-start.13
  28.7 0.7 copy-start.14
  99.6 1.8 %collective-permute-start.1 = (bf16[480,320]{1,0:T(8,128)(2,1)S(1)}, bf16[480,320]{1,0:T(8,128)(2,1)S(1)}, u32[]{:S(2)}, u32[]{:S(2)}) collective-permute-start(bf16[480,320]{1,0:T(8,128)(2,1)S(1)} %get-tuple-element.39), channel_id=1, source_target_pairs={{0,2},{2,0},{1,3},{3,1},{4,6},{6,4},{5,7},{7,5},{8,10},{10,8},{9,1... | collective-permute-start | bytes 921608 | tf_op jit(solution)/shard_map/ppermute | solution.py:573
  102.0 7.7 %collective-permute-start.2 = (bf16[120,320]{1,0:T(8,128)(2,1)S(1)}, bf16[120,320]{1,0:T(8,128)(2,1)S(1)}, u32[]{:S(2)}, u32[]{:S(2)}) collective-permute-start(bf16[120,320]{1,0:T(8,128)(2,1)S(1)} %get-tuple-element.41), channel_id=1, source_target_pairs={{0,1},{1,0},{4,5},{5,4},{2,3},{3,2},{6,7},{7,6},{8,9},{9,8},{12,13... | collective-permute-start | bytes 230408 | tf_op jit(solution)/shard_map/ppermute | solution.py:590
  102.6 7.2 %collective-permute-start.3 = (bf16[120,320]{1,0:T(8,128)(2,1)S(1)}, bf16[120,320]{1,0:T(8,128)(2,1)S(1)}, u32[]{:S(2)}, u32[]{:S(2)}) collective-permute-start(bf16[120,320]{1,0:T(8,128)(2,1)S(1)} %get-tuple-element.42), channel_id=1, source_target_pairs={{0,4},{1,5},{4,0},{5,1},{2,6},{3,7},{6,2},{7,3},{8,12},{9,13},{12,... | collective-permute-start | bytes 230408 | tf_op jit(solution)/shard_map/ppermute | solution.py:590
  103.3 6.5 %collective-permute-start.4 = (bf16[120,320]{1,0:T(8,128)(2,1)S(1)}, bf16[120,320]{1,0:T(8,128)(2,1)S(1)}, u32[]{:S(2)}, u32[]{:S(2)}) collective-permute-start(bf16[120,320]{1,0:T(8,128)(2,1)S(1)} %get-tuple-element.43), channel_id=1, source_target_pairs={{0,5},{1,4},{4,1},{5,0},{2,7},{3,6},{6,3},{7,2},{8,13},{9,12},{12,... | collective-permute-start | bytes 230408 | tf_op jit(solution)/shard_map/ppermute | solution.py:590
  109.9 7.5 %collective-permute-start.7 = (bf16[120,320]{1,0:T(8,128)(2,1)S(1)}, bf16[120,320]{1,0:T(8,128)(2,1)S(1)}, u32[]{:S(2)}, u32[]{:S(2)}) collective-permute-start(bf16[120,320]{1,0:T(8,128)(2,1)S(1)} %add_convert_fusion.1), channel_id=1, source_target_pairs={{0,24},{8,16},{16,8},{24,0},{1,25},{9,17},{17,9},{25,1},{2,26},{10... | collective-permute-start | bytes 230408 | tf_op jit(solution)/shard_map/ppermute | solution.py:595
  111.4 9.1 %collective-permute-start.6 = (bf16[120,320]{1,0:T(8,128)(2,1)S(1)}, bf16[120,320]{1,0:T(8,128)(2,1)S(1)}, u32[]{:S(2)}, u32[]{:S(2)}) collective-permute-start(bf16[120,320]{1,0:T(8,128)(2,1)S(1)} %add_convert_fusion.1), channel_id=1, source_target_pairs={{0,16},{8,24},{16,0},{24,8},{1,17},{9,25},{17,1},{25,9},{2,18},{10... | collective-permute-start | bytes 230408 | tf_op jit(solution)/shard_map/ppermute | solution.py:595
  112.1 8.4 %collective-permute-start.5 = (bf16[120,320]{1,0:T(8,128)(2,1)S(1)}, bf16[120,320]{1,0:T(8,128)(2,1)S(1)}, u32[]{:S(2)}, u32[]{:S(2)}) collective-permute-start(bf16[120,320]{1,0:T(8,128)(2,1)S(1)} %add_convert_fusion.1), channel_id=1, source_target_pairs={{0,8},{8,0},{16,24},{24,16},{1,9},{9,1},{17,25},{25,17},{2,10},{10... | collective-permute-start | bytes 230408 | tf_op jit(solution)/shard_map/ppermute | solution.py:595
  120.6 5.8 %collective-permute-start.10 = (bf16[120,320]{1,0:T(8,128)(2,1)S(1)}, bf16[120,320]{1,0:T(8,128)(2,1)S(1)}, u32[]{:S(2)}, u32[]{:S(2)}) collective-permute-start(bf16[120,320]{1,0:T(8,128)(2,1)S(1)} %add_convert_fusion), channel_id=1, source_target_pairs={{0,5},{1,4},{4,1},{5,0},{2,7},{3,6},{6,3},{7,2},{8,13},{9,12},{12,... | collective-permute-start | bytes 230408 | tf_op jit(solution)/shard_map/ppermute | solution.py:597
  121.2 5.5 %collective-permute-start.9 = (bf16[120,320]{1,0:T(8,128)(2,1)S(1)}, bf16[120,320]{1,0:T(8,128)(2,1)S(1)}, u32[]{:S(2)}, u32[]{:S(2)}) collective-permute-start(bf16[120,320]{1,0:T(8,128)(2,1)S(1)} %add_convert_fusion), channel_id=1, source_target_pairs={{0,4},{1,5},{4,0},{5,1},{2,6},{3,7},{6,2},{7,3},{8,12},{9,13},{12,... | collective-permute-start | bytes 230408 | tf_op jit(solution)/shard_map/ppermute | solution.py:597
  122.6 4.6 %collective-permute-start.8 = (bf16[120,320]{1,0:T(8,128)(2,1)S(1)}, bf16[120,320]{1,0:T(8,128)(2,1)S(1)}, u32[]{:S(2)}, u32[]{:S(2)}) collective-permute-start(bf16[120,320]{1,0:T(8,128)(2,1)S(1)} %add_convert_fusion), channel_id=1, source_target_pairs={{0,1},{1,0},{4,5},{5,4},{2,3},{3,2},{6,7},{7,6},{8,9},{9,8},{12,13... | collective-permute-start | bytes 230408 | tf_op jit(solution)/shard_map/ppermute | solution.py:597
  127.3 1.8 %collective-permute-start.11 = (bf16[4,120,320]{2,1,0:T(8,128)(2,1)S(1)}, bf16[4,120,320]{2,1,0:T(8,128)(2,1)S(1)}, u32[]{:S(2)}, u32[]{:S(2)}) collective-permute-start(bf16[4,120,320]{2,1,0:T(8,128)(2,1)S(1)} %pad_maximum_fusion.own_ref), channel_id=1, source_target_pairs={{0,2},{2,0},{1,3},{3,1},{4,6},{6,4},{5,7},{7,5},{8,10},{10,8},{9,1... | collective-permute-start | bytes 921608 | tf_op jit(solution)/shard_map/ppermute | solution.py:605

commit v7 on v6

--- a/solution.py
+++ b/solution.py
@@ -22,10 +22,12 @@
 WHOLE_VMEM = 60 * 2**20
 
 
-def angles_of(timesteps, half_width):
+def time_table(timesteps, time_weight):
+    half_width = time_weight.shape[0] // 2
     frequency = jnp.exp(-math.log(10000.0) * jnp.arange(half_width, dtype=F32) / half_width)
     angles = timesteps.astype(F32)[:, None] * frequency[None, :]
-    return jnp.cos(angles), jnp.sin(angles)
+    embedded = jnp.concatenate([jnp.cos(angles), jnp.sin(angles)], axis=1)
+    return jnp.dot(embedded, time_weight.astype(F32), precision=lax.Precision.HIGHEST)
 
 
 def call(
@@ -79,20 +81,7 @@
     lax.fori_loop(0, frames // 2, step, 0)
 
 
-def exact_product(x, w):
-    total = 0.0
-    for _ in range(3):
-        part = x.astype(BF16)
-        total = total + jnp.dot(part, w, preferred_element_type=F32)
-        x = x - part.astype(F32)
-    return total
-
-
-def conv_weight_kernel(w_ref, cos_ref, sin_ref, time_ref, o_ref, table_ref):
-    half_width = cos_ref.shape[1]
-    table_ref[...] = exact_product(cos_ref[...], time_ref[:half_width]) + exact_product(
-        sin_ref[...], time_ref[half_width:]
-    )
+def conv_weight_kernel(w_ref, o_ref):
     ch = w_ref.shape[-1]
     wide = 256
     rest = ch - wide
@@ -641,8 +630,15 @@
     dense = 2 * positions * ch * ch
 
     row = lax.axis_index("x")
+    taps = call(
+        conv_weight_kernel,
+        jax.ShapeDtypeStruct((1024, 1024), BF16),
+        [VMEM],
+        bytes_accessed=2 * size,
+    )(spatial_weight)
     if n_rows == 2:
         edge = lax.dynamic_index_in_dim(latents, (1 - row) * (rows - 1), 1, False)
+        edge, taps = lax.optimization_barrier((edge, taps))
         got = lax.ppermute(edge, "x", swaps(2, 1))
         top, bot = got, got
     else:
@@ -655,12 +651,7 @@
     flags = jnp.stack(
         [row > 0, row < n_rows - 1, seq * f_dev, shards * f_dev, core, place]
     ).astype(jnp.int32)
-    taps, table = call(
-        conv_weight_kernel,
-        (jax.ShapeDtypeStruct((1024, 1024), BF16), jax.ShapeDtypeStruct((CLIPS, ch), F32)),
-        [VMEM] * 4,
-        bytes_accessed=2 * size,
-    )(spatial_weight, *angles_of(timesteps, ch // 2), time_weight)
+    table = time_table(timesteps, time_weight)
     work = dict(flops=9 * dense, bytes_accessed=2 * size + 9 * ch * ch * 2)
     if n_rows == 2 and rows * across == shards * PIX and rows > 2:
         inner = call(inner_kernel, packed, [SMEM, SMEM] + [VMEM] * 3, **work)(

time: 131 us -> 131 us (level)
  local copies, waits for them, and re-layouts: 9.78 us -> 6.67 us
  waiting for transfers between devices: 29.9 us -> 32.9 us
    unnamed x30 -> x28, local copies, waits for them, and re-layouts: 8.7 us -> 5.84 us
    ppermute x1, waiting for transfers between devices: 0.01 us -> 2.02 us  [body(): got = lax.ppermute(edge, 'x', swaps(2, 1))]
  transfers between devices with their start and end apart: 13 -> 13, of which waited for: 8 -> 10; matrix products, arithmetic and copies ran while one was open for 1% -> 0% of each run, Pallas kernels for 8% -> 8%
where the time goes in v7:
time: 131 us
  blocking collectives  35.6 us (27%)
  Pallas kernels  33 us (25%)
  waiting for transfers between devices  32.9 us (25%)
  starting transfers between devices  21.1 us (16%)
  local copies, waits for them, and re-layouts  6.67 us (5%)
    all_to_all x1, blocking collectives, body(): mixed = lax.all_to_all(mixed, SEQ, split_axis=0, concat_axis=0, tiled=True)  35.6 us
    all_to_all x1, waiting for transfers between devices, exchange(): flat = lax.all_to_all(flat, SEQ, split_axis=0, concat_axis=0, tiled=True)  17.4 us
    pallas_call x1, Pallas kernels, body(): call(attention_kernel, jax.ShapeDtypeStruct((shards, (half + 1) * PIX, 2...  13.6 us
    all_to_all x1, starting transfers between devices, exchange(): flat = lax.all_to_all(flat, SEQ, split_axis=0, concat_axis=0, tiled=True)  6.38 us
    ppermute x3, waiting for transfers between devices, reduce_all(): parts.append(lax.ppermute(mine, 'z', swaps(n_z, k)).astype(F32))  5.88 us
    unnamed x28, local copies, waits for them, and re-layouts  5.84 us
    pallas_call x1, Pallas kernels, body(): call(inner_kernel, packed, [SMEM, SMEM] + [VMEM] * 3, **work)  4.79 us
    ppermute x3, starting transfers between devices, reduce_all(): parts.append(lax.ppermute(mine, 'z', swaps(n_z, k)).astype(F32))  4.45 us
  transfers between devices with their start and end apart: 13, of which 10 were waited for; matrix products, arithmetic and copies ran while one was open for 0% of the time, Pallas kernels for 8%

profile of v7, /device:TPU:0, one launch (start us, length us, event | category | flops | bytes accessed | tf_op | source)
XLA Modules:
  0.0 130.8 jit_solution(7890332392638084689)
XLA Ops:
  0.7 1.7 %copy-done.1 = bf16[3,3,320,320]{3,2,1,0:T(8,128)(2,1)S(1)} copy-done((bf16[3,3,320,320]{3,2,1,0:T(8,128)(2,1)S(1)}, bf16[3,3,320,320]{3,2,1,0:T(8,128)(2,1)}, u32[]{:S(2)}) %copy-start.1) | copy-done | bytes 1843224
  2.6 1.0 copy-done.8
  3.6 0.7 dynamic-slice_bitcast_fusion
  4.3 2.9 %collective-permute-start = (bf16[12,32,320]{2,1,0:T(8,128)(2,1)}, bf16[12,32,320]{2,1,0:T(8,128)(2,1)}, u32[]{:S(2)}, u32[]{:S(2)}) collective-permute-start(bf16[12,32,320]{2,1,0:T(8,128)(2,1)} %dynamic-slice_bitcast_fusion), channel_id=1, source_target_pairs={{0,1},{1,0},{2,3},{3,2},{4,5},{5,4},{6,7},{7,6},{8,9},{9,8},{10,11... | collective-permute-start | bytes 737288 | tf_op jit(solution)/shard_map/ppermute | solution.py:642
  7.8 4.8 %shard_map.124.inner_hbm = bf16[16,6,8,640]{3,2,1,0:T(8,128)(2,1)} custom-call(s32[6]{0:T(128)S(1)} %stack.46.flag_ref, s32[4]{0:T(128)S(1)} %copy-done.9, bf16[12,4,32,320]{3,2,1,0:T(8,128)(2,1)S(1)} %copy-done.8, bf16[1024,1024]{1,0:T(8,128)(2,1)S(1)} %shard_map.123.w_ref, f32[4,320]{1,0:T(4,128)S(1)} %fusion.table_ref), custom_call_target="tpu_custom_call" | custom-call | flops 2831155200 | bytes 3809280 | tf_op jit(solution)/shard_map/pallas_call | solution.py:657
  12.6 2.0 %collective-permute-done.halo_ref = bf16[12,32,320]{2,1,0:T(8,128)(2,1)} collective-permute-done((bf16[12,32,320]{2,1,0:T(8,128)(2,1)}, bf16[12,32,320]{2,1,0:T(8,128)(2,1)}, u32[]{:S(2)}, u32[]{:S(2)}) %collective-permute-start) | collective-permute-done | bytes 245792 | tf_op jit(solution)/shard_map/ppermute | solution.py:642
  14.6 2.9 %shard_map.125 = bf16[16,6,8,640]{3,2,1,0:T(8,128)(2,1)} custom-call(s32[6]{0:T(128)S(1)} %stack.46.flag_ref, s32[4]{0:T(128)S(1)} %copy-done.9, bf16[12,4,32,320]{3,2,1,0:T(8,128)(2,1)S(1)} %copy-done.8, bf16[12,32,320]{2,1,0:T(8,128)(2,1)} %collective-permute-done.halo_ref, ...), custom_call_target="tpu_custom_call", output_to_operand_aliasing={{}: (6, {})} | custom-call | flops 2831155200 | bytes 3809280 | tf_op jit(solution)/shard_map/pallas_call | solution.py:660
  17.5 6.4 %all-to-all-start = ((bf16[16,48,640]{2,1,0:T(8,128)(2,1)}), bf16[16,48,640]{2,1,0:T(8,128)(2,1)}, u32[]{:S(2)}, u32[]{:S(2)}) async-start(bf16[16,48,640]{2,1,0:T(8,128)(2,1)} %bitcast.6), calls=%async_computation | async-start | bytes 1966080 | tf_op jit(solution)/shard_map/all_to_all | solution.py:605
  25.3 0.8 shard_map.126
  26.1 0.9 copy-done.10
  27.0 0.7 copy-done.11
  27.7 0.7 copy-done.12
  28.4 17.4 %all-to-all-done = bf16[16,48,640]{2,1,0:T(8,128)(2,1)} async-done(((bf16[16,48,640]{2,1,0:T(8,128)(2,1)}), bf16[16,48,640]{2,1,0:T(8,128)(2,1)}, u32[]{:S(2)}, u32[]{:S(2)}) %all-to-all-start) | async-done | bytes 983072 | tf_op jit(solution)/shard_map/all_to_all | solution.py:605
  45.8 13.6 %shard_map.127 = bf16[16,56,640]{2,1,0:T(8,128)(2,1)} custom-call(bf16[768,640]{1,0:T(8,128)(2,1)} %bitcast.8.act_hbm, bf16[384,1152]{1,0:T(8,128)(2,1)} %copy-done.10, bf16[384,384]{1,0:T(8,128)(2,1)} %copy-done.11, f32[192,192]{1,0:T(8,128)} %copy-done.12), custom_call_target="tpu_custom_call" | custom-call | flops 2202009600 | bytes 3932160 | tf_op jit(solution)/shard_map/pallas_call | solution.py:697
  59.4 35.6 %all_to_all.10.m_ref = bf16[16,56,640]{2,1,0:T(8,128)(2,1)S(1)} all-to-all(bf16[16,56,640]{2,1,0:T(8,128)(2,1)} %shard_map.127), channel_id=1, replica_groups=mesh['z'=4,'y'=2,'c'=2,'x'=2] {'z','y','c'}, dimensions={0} | all-to-all | bytes 2293760 | tf_op jit(solution)/shard_map/all_to_all | solution.py:716
  95.1 3.6 %shard_map.128 = (f32[480,320]{1,0:T(8,128)S(1)}, bf16[480,320]{1,0:T(8,128)(2,1)S(1)}) custom-call(s32[6]{0:T(128)S(1)} %stack.46.flag_ref, s32[4]{0:T(128)S(1)} %copy-done.9, bf16[16,56,640]{2,1,0:T(8,128)(2,1)S(1)} %all_to_all.10.m_ref, bf16[16,48,640]{2,1,0:T(8,128)(2,1)S(1)} %bitcast.17), custom_call_target="tpu_custom_call" | custom-call | flops 943718400 | bytes 2949120 | tf_op jit(solution)/shard_map/pallas_call | solution.py:718
  98.8 1.6 %collective-permute-done.1.got_ref = bf16[480,320]{1,0:T(8,128)(2,1)S(1)} collective-permute-done((bf16[480,320]{1,0:T(8,128)(2,1)S(1)}, bf16[480,320]{1,0:T(8,128)(2,1)S(1)}, u32[]{:S(2)}, u32[]{:S(2)}) %collective-permute-start.1) | collective-permute-done | bytes 307232 | tf_op jit(solution)/shard_map/ppermute | solution.py:562
  100.4 0.7 shard_map.129
  101.1 1.6 %collective-permute-start.2 = (bf16[120,320]{1,0:T(8,128)(2,1)S(1)}, bf16[120,320]{1,0:T(8,128)(2,1)S(1)}, u32[]{:S(2)}, u32[]{:S(2)}) collective-permute-start(bf16[120,320]{1,0:T(8,128)(2,1)S(1)} %get-tuple-element.41), channel_id=1, source_target_pairs={{0,1},{1,0},{4,5},{5,4},{2,3},{3,2},{6,7},{7,6},{8,9},{9,8},{12,13... | collective-permute-start | bytes 230408 | tf_op jit(solution)/shard_map/ppermute | solution.py:579
  103.3 1.4 %collective-permute-start.4 = (bf16[120,320]{1,0:T(8,128)(2,1)S(1)}, bf16[120,320]{1,0:T(8,128)(2,1)S(1)}, u32[]{:S(2)}, u32[]{:S(2)}) collective-permute-start(bf16[120,320]{1,0:T(8,128)(2,1)S(1)} %get-tuple-element.43), channel_id=1, source_target_pairs={{0,5},{1,4},{4,1},{5,0},{2,7},{3,6},{6,3},{7,2},{8,13},{9,12},{12,... | collective-permute-start | bytes 230408 | tf_op jit(solution)/shard_map/ppermute | solution.py:579
  104.6 4.2 %shard_map.130 = bf16[12,4,32,320]{3,2,1,0:T(8,128)(2,1)} custom-call(s32[6]{0:T(128)S(1)} %stack.46.flag_ref, s32[4]{0:T(128)S(1)} %copy-done.9, bf16[16,56,640]{2,1,0:T(8,128)(2,1)S(1)} %all_to_all.10.m_ref, bf16[1152,384]{1,0:T(8,128)(2,1)S(1)} %get-tuple-element.45.tw), custom_call_target="tpu_custom_call" | custom-call | flops 943718400 | bytes 2949120 | tf_op jit(solution)/shard_map/pallas_call | solution.py:727
  109.2 1.5 %collective-permute-start.7 = (bf16[120,320]{1,0:T(8,128)(2,1)S(1)}, bf16[120,320]{1,0:T(8,128)(2,1)S(1)}, u32[]{:S(2)}, u32[]{:S(2)}) collective-permute-start(bf16[120,320]{1,0:T(8,128)(2,1)S(1)} %add_convert_fusion.1), channel_id=1, source_target_pairs={{0,24},{8,16},{16,8},{24,0},{1,25},{9,17},{17,9},{25,1},{2,26},{10... | collective-permute-start | bytes 230408 | tf_op jit(solution)/shard_map/ppermute | solution.py:584
  110.8 0.7 collective-permute-start.6
  111.4 2.2 %collective-permute-start.5 = (bf16[120,320]{1,0:T(8,128)(2,1)S(1)}, bf16[120,320]{1,0:T(8,128)(2,1)S(1)}, u32[]{:S(2)}, u32[]{:S(2)}) collective-permute-start(bf16[120,320]{1,0:T(8,128)(2,1)S(1)} %add_convert_fusion.1), channel_id=1, source_target_pairs={{0,8},{8,0},{16,24},{24,16},{1,9},{9,1},{17,25},{25,17},{2,10},{10... | collective-permute-start | bytes 230408 | tf_op jit(solution)/shard_map/ppermute | solution.py:584
  113.7 2.9 %collective-permute-done.7 = bf16[120,320]{1,0:T(8,128)(2,1)S(1)} collective-permute-done((bf16[120,320]{1,0:T(8,128)(2,1)S(1)}, bf16[120,320]{1,0:T(8,128)(2,1)S(1)}, u32[]{:S(2)}, u32[]{:S(2)}) %collective-permute-start.7) | collective-permute-done | bytes 76832 | tf_op jit(solution)/shard_map/ppermute | solution.py:584
  116.6 2.9 %collective-permute-done.6 = bf16[120,320]{1,0:T(8,128)(2,1)S(1)} collective-permute-done((bf16[120,320]{1,0:T(8,128)(2,1)S(1)}, bf16[120,320]{1,0:T(8,128)(2,1)S(1)}, u32[]{:S(2)}, u32[]{:S(2)}) %collective-permute-start.6) | collective-permute-done | bytes 76832 | tf_op jit(solution)/shard_map/ppermute | solution.py:584
  119.6 1.6 %collective-permute-start.10 = (bf16[120,320]{1,0:T(8,128)(2,1)S(1)}, bf16[120,320]{1,0:T(8,128)(2,1)S(1)}, u32[]{:S(2)}, u32[]{:S(2)}) collective-permute-start(bf16[120,320]{1,0:T(8,128)(2,1)S(1)} %add_convert_fusion), channel_id=1, source_target_pairs={{0,5},{1,4},{4,1},{5,0},{2,7},{3,6},{6,3},{7,2},{8,13},{9,12},{12,... | collective-permute-start | bytes 230408 | tf_op jit(solution)/shard_map/ppermute | solution.py:586
  121.2 1.4 %collective-permute-start.9 = (bf16[120,320]{1,0:T(8,128)(2,1)S(1)}, bf16[120,320]{1,0:T(8,128)(2,1)S(1)}, u32[]{:S(2)}, u32[]{:S(2)}) collective-permute-start(bf16[120,320]{1,0:T(8,128)(2,1)S(1)} %add_convert_fusion), channel_id=1, source_target_pairs={{0,4},{1,5},{4,0},{5,1},{2,6},{3,7},{6,2},{7,3},{8,12},{9,13},{12,... | collective-permute-start | bytes 230408 | tf_op jit(solution)/shard_map/ppermute | solution.py:586
  123.2 2.8 %collective-permute-done.10 = bf16[120,320]{1,0:T(8,128)(2,1)S(1)} collective-permute-done((bf16[120,320]{1,0:T(8,128)(2,1)S(1)}, bf16[120,320]{1,0:T(8,128)(2,1)S(1)}, u32[]{:S(2)}, u32[]{:S(2)}) %collective-permute-start.10) | collective-permute-done | bytes 76832 | tf_op jit(solution)/shard_map/ppermute | solution.py:586
  126.4 0.7 collective-permute-done.8
  127.4 1.7 %collective-permute-done.11.other_ref = bf16[4,120,320]{2,1,0:T(8,128)(2,1)S(1)} collective-permute-done((bf16[4,120,320]{2,1,0:T(8,128)(2,1)S(1)}, bf16[4,120,320]{2,1,0:T(8,128)(2,1)S(1)}, u32[]{:S(2)}, u32[]{:S(2)}) %collective-permute-start.11) | collective-permute-done | bytes 307232 | tf_op jit(solution)/shard_map/ppermute | solution.py:594
  129.0 1.8 %shard_map.131 = f32[960,320]{1,0:T(8,128)} custom-call(s32[6]{0:T(128)S(1)} %stack.46.flag_ref, bf16[4,120,320]{2,1,0:T(8,128)(2,1)S(1)} %pad_maximum_fusion.own_ref, bf16[4,120,320]{2,1,0:T(8,128)(2,1)S(1)} %collective-permute-done.11.other_ref), custom_call_target="tpu_custom_call" | custom-call | bytes 614400 | tf_op jit(solution)/shard_map/pallas_call | solution.py:596
  (42 shorter events, 4.6 us)
Async XLA Ops:
  0.6 6.8 %copy-start = (bf16[320,320]{1,0:T(8,128)(2,1)S(1)}, bf16[320,320]{1,0:T(8,128)(2,1)}, u32[]{:S(2)}) copy-start(bf16[320,320]{1,0:T(8,128)(2,1)} %param.15) | copy-start | bytes 614404
  0.7 1.7 %copy-start.1 = (bf16[3,3,320,320]{3,2,1,0:T(8,128)(2,1)S(1)}, bf16[3,3,320,320]{3,2,1,0:T(8,128)(2,1)}, u32[]{:S(2)}) copy-start(bf16[3,3,320,320]{3,2,1,0:T(8,128)(2,1)} %w_ref.1) | copy-start | bytes 5529604
  2.3 1.3 copy-start.8
  2.3 5.0 %copy-start.13 = (s32[4]{0:T(128)S(1)}, s32[4]{0:T(128)}, u32[]{:S(2)}) copy-start(s32[4]{0:T(128)} %param.13) | copy-start | bytes 52
  2.3 5.5 %copy-start.9 = (s32[4]{0:T(128)S(1)}, s32[4]{0:T(128)}, u32[]{:S(2)}) copy-start(s32[4]{0:T(128)} %len_ref.9) | copy-start | bytes 52
  4.3 10.3 %collective-permute-start = (bf16[12,32,320]{2,1,0:T(8,128)(2,1)}, bf16[12,32,320]{2,1,0:T(8,128)(2,1)}, u32[]{:S(2)}, u32[]{:S(2)}) collective-permute-start(bf16[12,32,320]{2,1,0:T(8,128)(2,1)} %dynamic-slice_bitcast_fusion), channel_id=1, source_target_pairs={{0,1},{1,0},{2,3},{3,2},{4,5},{5,4},{6,7},{7,6},{8,9},{9,8},{10,11... | collective-permute-start | bytes 737288 | tf_op jit(solution)/shard_map/ppermute | solution.py:642
  17.5 6.4 %copy-start.2 = (bf16[12,4,32,320]{3,2,1,0:T(8,128)(2,1)S(1)}, bf16[12,4,32,320]{3,2,1,0:T(8,128)(2,1)}, u32[]{:S(2)}) copy-start(bf16[12,4,32,320]{3,2,1,0:T(8,128)(2,1)} %x_ref.1) | copy-start | bytes 2949124
  17.5 28.3 %all-to-all-start = ((bf16[16,48,640]{2,1,0:T(8,128)(2,1)}), bf16[16,48,640]{2,1,0:T(8,128)(2,1)}, u32[]{:S(2)}, u32[]{:S(2)}) async-start(bf16[16,48,640]{2,1,0:T(8,128)(2,1)} %bitcast.6), calls=%async_computation | async-start | bytes 1966080 | tf_op jit(solution)/shard_map/all_to_all | solution.py:605
  23.9 1.1 copy-start.3
  23.9 1.2 copy-start.4
  23.9 1.2 copy-start.5
  23.9 1.3 copy-start.6
  23.9 1.3 %copy-start.7 = (bf16[320,320]{1,0:T(8,128)(2,1)S(1)}, bf16[320,320]{1,0:T(8,128)(2,1)}, u32[]{:S(2)}) copy-start(bf16[320,320]{1,0:T(8,128)(2,1)} %wo_ref.1) | copy-start | bytes 614404
  26.1 0.9 copy-start.10
  27.0 0.7 copy-start.11
  27.7 0.7 copy-start.12
  98.6 1.8 %collective-permute-start.1 = (bf16[480,320]{1,0:T(8,128)(2,1)S(1)}, bf16[480,320]{1,0:T(8,128)(2,1)S(1)}, u32[]{:S(2)}, u32[]{:S(2)}) collective-permute-start(bf16[480,320]{1,0:T(8,128)(2,1)S(1)} %get-tuple-element.39), channel_id=1, source_target_pairs={{0,2},{2,0},{1,3},{3,1},{4,6},{6,4},{5,7},{7,5},{8,10},{10,8},{9,1... | collective-permute-start | bytes 921608 | tf_op jit(solution)/shard_map/ppermute | solution.py:562
  101.1 7.7 %collective-permute-start.2 = (bf16[120,320]{1,0:T(8,128)(2,1)S(1)}, bf16[120,320]{1,0:T(8,128)(2,1)S(1)}, u32[]{:S(2)}, u32[]{:S(2)}) collective-permute-start(bf16[120,320]{1,0:T(8,128)(2,1)S(1)} %get-tuple-element.41), channel_id=1, source_target_pairs={{0,1},{1,0},{4,5},{5,4},{2,3},{3,2},{6,7},{7,6},{8,9},{9,8},{12,13... | collective-permute-start | bytes 230408 | tf_op jit(solution)/shard_map/ppermute | solution.py:579
  102.6 6.5 %collective-permute-start.3 = (bf16[120,320]{1,0:T(8,128)(2,1)S(1)}, bf16[120,320]{1,0:T(8,128)(2,1)S(1)}, u32[]{:S(2)}, u32[]{:S(2)}) collective-permute-start(bf16[120,320]{1,0:T(8,128)(2,1)S(1)} %get-tuple-element.42), channel_id=1, source_target_pairs={{0,4},{1,5},{4,0},{5,1},{2,6},{3,7},{6,2},{7,3},{8,12},{9,13},{12,... | collective-permute-start | bytes 230408 | tf_op jit(solution)/shard_map/ppermute | solution.py:579
  103.3 5.9 %collective-permute-start.4 = (bf16[120,320]{1,0:T(8,128)(2,1)S(1)}, bf16[120,320]{1,0:T(8,128)(2,1)S(1)}, u32[]{:S(2)}, u32[]{:S(2)}) collective-permute-start(bf16[120,320]{1,0:T(8,128)(2,1)S(1)} %get-tuple-element.43), channel_id=1, source_target_pairs={{0,5},{1,4},{4,1},{5,0},{2,7},{3,6},{6,3},{7,2},{8,13},{9,12},{12,... | collective-permute-start | bytes 230408 | tf_op jit(solution)/shard_map/ppermute | solution.py:579
  109.2 7.4 %collective-permute-start.7 = (bf16[120,320]{1,0:T(8,128)(2,1)S(1)}, bf16[120,320]{1,0:T(8,128)(2,1)S(1)}, u32[]{:S(2)}, u32[]{:S(2)}) collective-permute-start(bf16[120,320]{1,0:T(8,128)(2,1)S(1)} %add_convert_fusion.1), channel_id=1, source_target_pairs={{0,24},{8,16},{16,8},{24,0},{1,25},{9,17},{17,9},{25,1},{2,26},{10... | collective-permute-start | bytes 230408 | tf_op jit(solution)/shard_map/ppermute | solution.py:584
  110.8 8.8 %collective-permute-start.6 = (bf16[120,320]{1,0:T(8,128)(2,1)S(1)}, bf16[120,320]{1,0:T(8,128)(2,1)S(1)}, u32[]{:S(2)}, u32[]{:S(2)}) collective-permute-start(bf16[120,320]{1,0:T(8,128)(2,1)S(1)} %add_convert_fusion.1), channel_id=1, source_target_pairs={{0,16},{8,24},{16,0},{24,8},{1,17},{9,25},{17,1},{25,9},{2,18},{10... | collective-permute-start | bytes 230408 | tf_op jit(solution)/shard_map/ppermute | solution.py:584
  111.4 8.1 %collective-permute-start.5 = (bf16[120,320]{1,0:T(8,128)(2,1)S(1)}, bf16[120,320]{1,0:T(8,128)(2,1)S(1)}, u32[]{:S(2)}, u32[]{:S(2)}) collective-permute-start(bf16[120,320]{1,0:T(8,128)(2,1)S(1)} %add_convert_fusion.1), channel_id=1, source_target_pairs={{0,8},{8,0},{16,24},{24,16},{1,9},{9,1},{17,25},{25,17},{2,10},{10... | collective-permute-start | bytes 230408 | tf_op jit(solution)/shard_map/ppermute | solution.py:584
  119.6 6.4 %collective-permute-start.10 = (bf16[120,320]{1,0:T(8,128)(2,1)S(1)}, bf16[120,320]{1,0:T(8,128)(2,1)S(1)}, u32[]{:S(2)}, u32[]{:S(2)}) collective-permute-start(bf16[120,320]{1,0:T(8,128)(2,1)S(1)} %add_convert_fusion), channel_id=1, source_target_pairs={{0,5},{1,4},{4,1},{5,0},{2,7},{3,6},{6,3},{7,2},{8,13},{9,12},{12,... | collective-permute-start | bytes 230408 | tf_op jit(solution)/shard_map/ppermute | solution.py:586
  121.2 5.2 %collective-permute-start.9 = (bf16[120,320]{1,0:T(8,128)(2,1)S(1)}, bf16[120,320]{1,0:T(8,128)(2,1)S(1)}, u32[]{:S(2)}, u32[]{:S(2)}) collective-permute-start(bf16[120,320]{1,0:T(8,128)(2,1)S(1)} %add_convert_fusion), channel_id=1, source_target_pairs={{0,4},{1,5},{4,0},{5,1},{2,6},{3,7},{6,2},{7,3},{8,12},{9,13},{12,... | collective-permute-start | bytes 230408 | tf_op jit(solution)/shard_map/ppermute | solution.py:586
  122.6 4.6 %collective-permute-start.8 = (bf16[120,320]{1,0:T(8,128)(2,1)S(1)}, bf16[120,320]{1,0:T(8,128)(2,1)S(1)}, u32[]{:S(2)}, u32[]{:S(2)}) collective-permute-start(bf16[120,320]{1,0:T(8,128)(2,1)S(1)} %add_convert_fusion), channel_id=1, source_target_pairs={{0,1},{1,0},{4,5},{5,4},{2,3},{3,2},{6,7},{7,6},{8,9},{9,8},{12,13... | collective-permute-start | bytes 230408 | tf_op jit(solution)/shard_map/ppermute | solution.py:586
  127.3 1.8 %collective-permute-start.11 = (bf16[4,120,320]{2,1,0:T(8,128)(2,1)S(1)}, bf16[4,120,320]{2,1,0:T(8,128)(2,1)S(1)}, u32[]{:S(2)}, u32[]{:S(2)}) collective-permute-start(bf16[4,120,320]{2,1,0:T(8,128)(2,1)S(1)} %pad_maximum_fusion.own_ref), channel_id=1, source_target_pairs={{0,2},{2,0},{1,3},{3,1},{4,6},{6,4},{5,7},{7,5},{8,10},{10,8},{9,1... | collective-permute-start | bytes 921608 | tf_op jit(solution)/shard_map/ppermute | solution.py:594

commit v8 on v7

--- a/solution.py
+++ b/solution.py
@@ -530,15 +530,6 @@
     )
 
 
-def shares_kernel(flag_ref, g_ref, got_ref, *refs):
-    outs, total = refs[:-1], refs[-1]
-    total[...] = g_ref[...] + got_ref[...].astype(F32)
-    for k, o_ref in enumerate(outs):
-        share = o_ref.shape[0]
-        at = pl.ds(pl.multiple_of((flag_ref[5] ^ k) * share, 8), share)
-        o_ref[...] = total[at, :].astype(o_ref.dtype)
-
-
 def finish_kernel(flag_ref, own_ref, other_ref, o_ref):
     parts, share, _ = own_ref.shape
     for k in range(parts):
@@ -559,23 +550,10 @@
     def cut(v, i, size):
         return lax.dynamic_slice_in_dim(v, i * size, size, 0)
 
-    got = lax.ppermute(other, "c", swaps(2, 1))
-    if share % 8:
-        g = g + got.astype(F32)
-        cuts = [cut(g, place, share)]
-        cuts += [cut(g, place ^ k, share).astype(BF16) for k in range(1, n_plane)]
-    else:
-        kinds = [jax.ShapeDtypeStruct((share, g.shape[1]), F32 if k == 0 else BF16) for k in range(n_plane)]
-        cuts = call(
-            shares_kernel,
-            kinds,
-            [SMEM, VMEM, VMEM],
-            scratch=[pltpu.VMEM(g.shape, F32)],
-            bytes_accessed=10 * g.size,
-        )(flags, g, got)
-    parts = [cuts[0]]
-    for sent in cuts[1:]:
-        k = len(parts)
+    g = g + lax.ppermute(other, "c", swaps(2, 1)).astype(F32)
+    parts = [cut(g, place, share)]
+    for k in range(1, n_plane):
+        sent = cut(g, place ^ k, share).astype(BF16)
         parts.append(lax.ppermute(sent, PLANE, swaps(n_plane, k)).astype(F32))
     mine = tree(parts).astype(BF16)
     mine, block_out = lax.optimization_barrier((mine, block_out))
@@ -630,15 +608,8 @@
     dense = 2 * positions * ch * ch
 
     row = lax.axis_index("x")
-    taps = call(
-        conv_weight_kernel,
-        jax.ShapeDtypeStruct((1024, 1024), BF16),
-        [VMEM],
-        bytes_accessed=2 * size,
-    )(spatial_weight)
     if n_rows == 2:
         edge = lax.dynamic_index_in_dim(latents, (1 - row) * (rows - 1), 1, False)
-        edge, taps = lax.optimization_barrier((edge, taps))
         got = lax.ppermute(edge, "x", swaps(2, 1))
         top, bot = got, got
     else:
@@ -652,6 +623,12 @@
         [row > 0, row < n_rows - 1, seq * f_dev, shards * f_dev, core, place]
     ).astype(jnp.int32)
     table = time_table(timesteps, time_weight)
+    taps = call(
+        conv_weight_kernel,
+        jax.ShapeDtypeStruct((1024, 1024), BF16),
+        [VMEM],
+        bytes_accessed=2 * size,
+    )(spatial_weight)
     work = dict(flops=9 * dense, bytes_accessed=2 * size + 9 * ch * ch * 2)
     if n_rows == 2 and rows * across == shards * PIX and rows > 2:
         inner = call(inner_kernel, packed, [SMEM, SMEM] + [VMEM] * 3, **work)(

time: 131 us -> 128 us (0.977)
  waiting for transfers between devices: 32.9 us -> 28.7 us
  local copies, waits for them, and re-layouts: 6.67 us -> 8.16 us
    ppermute x1, waiting for transfers between devices: 2.02 us -> 0.01 us  [body(): got = lax.ppermute(edge, 'x', swaps(2, 1))]
    unnamed x28 -> x30, local copies, waits for them, and re-layouts: 5.84 us -> 6.27 us
  transfers between devices with their start and end apart: 13 -> 13, of which waited for: 10 -> 8; matrix products, arithmetic and copies ran while one was open for 0% -> 1% of each run, Pallas kernels for 8% -> 8%
where the time goes in v8:
time: 128 us
  blocking collectives  35.6 us (28%)
  Pallas kernels  32.4 us (25%)
  waiting for transfers between devices  28.7 us (22%)
  starting transfers between devices  20.9 us (16%)
  local copies, waits for them, and re-layouts  8.16 us (6%)
    all_to_all x1, blocking collectives, body(): mixed = lax.all_to_all(mixed, SEQ, split_axis=0, concat_axis=0, tiled=True)  35.6 us
    all_to_all x1, waiting for transfers between devices, exchange(): flat = lax.all_to_all(flat, SEQ, split_axis=0, concat_axis=0, tiled=True)  16.5 us
    pallas_call x1, Pallas kernels, body(): call(attention_kernel, jax.ShapeDtypeStruct((shards, (half + 1) * PIX, 2...  13.6 us
    unnamed x30, local copies, waits for them, and re-layouts  6.27 us
    all_to_all x1, starting transfers between devices, exchange(): flat = lax.all_to_all(flat, SEQ, split_axis=0, concat_axis=0, tiled=True)  6.13 us
    ppermute x3, waiting for transfers between devices, reduce_all(): parts.append(lax.ppermute(mine, 'z', swaps(n_z, k)).astype(F32))  5.73 us
    pallas_call x1, Pallas kernels, body(): call(inner_kernel, packed, [SMEM, SMEM] + [VMEM] * 3, **work)  4.77 us
    ppermute x3, starting transfers between devices, reduce_all(): parts.append(lax.ppermute(mine, 'z', swaps(n_z, k)).astype(F32))  4.45 us
  transfers between devices with their start and end apart: 13, of which 8 were waited for; matrix products, arithmetic and copies ran while one was open for 1% of the time, Pallas kernels for 8%

profile of v8, /device:TPU:0, one launch (start us, length us, event | category | flops | bytes accessed | tf_op | source)
XLA Modules:
  0.0 127.9 jit_solution(4646247867760496958)
XLA Ops:
  0.7 1.8 %dynamic-slice_bitcast_fusion = bf16[12,32,320]{2,1,0:T(8,128)(2,1)} fusion(bf16[12,4,32,320]{3,2,1,0:T(8,128)(2,1)} %lat_ref.3, s32[]{:T(128)S(6)} %select_n.16), kind=kLoop, calls=%fused_computation.2 | loop fusion | bytes 491524 | tf_op jit(solution)/shard_map/jit(dynamic_index_in_dim)/squeeze | solution.py:612
  2.4 2.9 %collective-permute-start = (bf16[12,32,320]{2,1,0:T(8,128)(2,1)}, bf16[12,32,320]{2,1,0:T(8,128)(2,1)}, u32[]{:S(2)}, u32[]{:S(2)}) collective-permute-start(bf16[12,32,320]{2,1,0:T(8,128)(2,1)} %dynamic-slice_bitcast_fusion), channel_id=1, source_target_pairs={{0,1},{1,0},{2,3},{3,2},{4,5},{5,4},{6,7},{7,6},{8,9},{9,8},{10,11... | collective-permute-start | bytes 737288 | tf_op jit(solution)/shard_map/ppermute | solution.py:613
  5.4 0.7 convert_element_type.45
  6.0 1.6 %copy-done.1 = bf16[3,3,320,320]{3,2,1,0:T(8,128)(2,1)S(1)} copy-done((bf16[3,3,320,320]{3,2,1,0:T(8,128)(2,1)S(1)}, bf16[3,3,320,320]{3,2,1,0:T(8,128)(2,1)}, u32[]{:S(2)}) %copy-start.1) | copy-done | bytes 1843224
  8.9 4.8 %shard_map.124.inner_hbm = bf16[16,6,8,640]{3,2,1,0:T(8,128)(2,1)} custom-call(s32[6]{0:T(128)S(1)} %stack.46.flag_ref, s32[4]{0:T(128)S(1)} %copy-done.9, bf16[12,4,32,320]{3,2,1,0:T(8,128)(2,1)S(1)} %copy-done.8, bf16[1024,1024]{1,0:T(8,128)(2,1)S(1)} %shard_map.123.w_ref, f32[4,320]{1,0:T(4,128)S(1)} %fusion.table_ref), custom_call_target="tpu_custom_call" | custom-call | flops 2831155200 | bytes 3809280 | tf_op jit(solution)/shard_map/pallas_call | solution.py:634
  13.7 2.9 %shard_map.125 = bf16[16,6,8,640]{3,2,1,0:T(8,128)(2,1)} custom-call(s32[6]{0:T(128)S(1)} %stack.46.flag_ref, s32[4]{0:T(128)S(1)} %copy-done.9, bf16[12,4,32,320]{3,2,1,0:T(8,128)(2,1)S(1)} %copy-done.8, bf16[12,32,320]{2,1,0:T(8,128)(2,1)} %collective-permute-done.halo_ref, ...), custom_call_target="tpu_custom_call", output_to_operand_aliasing={{}: (6, {})} | custom-call | flops 2831155200 | bytes 3809280 | tf_op jit(solution)/shard_map/pallas_call | solution.py:637
  16.6 6.1 %all-to-all-start = ((bf16[16,48,640]{2,1,0:T(8,128)(2,1)}), bf16[16,48,640]{2,1,0:T(8,128)(2,1)}, u32[]{:S(2)}, u32[]{:S(2)}) async-start(bf16[16,48,640]{2,1,0:T(8,128)(2,1)} %bitcast.6), calls=%async_computation | async-start | bytes 1966080 | tf_op jit(solution)/shard_map/all_to_all | solution.py:583
  24.1 0.8 shard_map.126
  24.9 0.9 copy-done.10
  25.9 0.9 copy-done.12
  26.8 0.7 copy-done.13
  27.5 0.7 copy-done.14
  28.2 16.5 %all-to-all-done = bf16[16,48,640]{2,1,0:T(8,128)(2,1)} async-done(((bf16[16,48,640]{2,1,0:T(8,128)(2,1)}), bf16[16,48,640]{2,1,0:T(8,128)(2,1)}, u32[]{:S(2)}, u32[]{:S(2)}) %all-to-all-start) | async-done | bytes 983072 | tf_op jit(solution)/shard_map/all_to_all | solution.py:583
  44.6 13.6 %shard_map.127 = bf16[16,56,640]{2,1,0:T(8,128)(2,1)} custom-call(bf16[768,640]{1,0:T(8,128)(2,1)} %bitcast.8.act_hbm, bf16[384,1152]{1,0:T(8,128)(2,1)} %copy-done.12, bf16[384,384]{1,0:T(8,128)(2,1)} %copy-done.13, f32[192,192]{1,0:T(8,128)} %copy-done.14), custom_call_target="tpu_custom_call" | custom-call | flops 2202009600 | bytes 3932160 | tf_op jit(solution)/shard_map/pallas_call | solution.py:674
  58.3 35.6 %all_to_all.10.m_ref = bf16[16,56,640]{2,1,0:T(8,128)(2,1)S(1)} all-to-all(bf16[16,56,640]{2,1,0:T(8,128)(2,1)} %shard_map.127), channel_id=1, replica_groups=mesh['z'=4,'y'=2,'c'=2,'x'=2] {'z','y','c'}, dimensions={0} | all-to-all | bytes 2293760 | tf_op jit(solution)/shard_map/all_to_all | solution.py:693
  93.9 3.6 %shard_map.128 = (f32[480,320]{1,0:T(8,128)S(1)}, bf16[480,320]{1,0:T(8,128)(2,1)S(1)}) custom-call(s32[6]{0:T(128)S(1)} %stack.46.flag_ref, s32[4]{0:T(128)S(1)} %copy-done.9, bf16[16,56,640]{2,1,0:T(8,128)(2,1)S(1)} %all_to_all.10.m_ref, bf16[16,48,640]{2,1,0:T(8,128)(2,1)S(1)} %bitcast.17), custom_call_target="tpu_custom_call" | custom-call | flops 943718400 | bytes 2949120 | tf_op jit(solution)/shard_map/pallas_call | solution.py:695
  97.7 1.6 %collective-permute-done.1 = bf16[480,320]{1,0:T(8,128)(2,1)S(1)} collective-permute-done((bf16[480,320]{1,0:T(8,128)(2,1)S(1)}, bf16[480,320]{1,0:T(8,128)(2,1)S(1)}, u32[]{:S(2)}, u32[]{:S(2)}) %collective-permute-start.1) | collective-permute-done | bytes 307232 | tf_op jit(solution)/shard_map/ppermute | solution.py:553
  99.4 0.8 collective-permute-start.2
  100.8 2.1 %collective-permute-start.4 = (bf16[120,320]{1,0:T(8,128)(2,1)S(1)}, bf16[120,320]{1,0:T(8,128)(2,1)S(1)}, u32[]{:S(2)}, u32[]{:S(2)}) collective-permute-start(bf16[120,320]{1,0:T(8,128)(2,1)S(1)} %get-tuple-element.37), channel_id=1, source_target_pairs={{0,5},{1,4},{4,1},{5,0},{2,7},{3,6},{6,3},{7,2},{8,13},{9,12},{12,... | collective-permute-start | bytes 230408 | tf_op jit(solution)/shard_map/ppermute | solution.py:557
  102.9 4.2 %shard_map.129 = bf16[12,4,32,320]{3,2,1,0:T(8,128)(2,1)} custom-call(s32[6]{0:T(128)S(1)} %stack.46.flag_ref, s32[4]{0:T(128)S(1)} %copy-done.9, bf16[16,56,640]{2,1,0:T(8,128)(2,1)S(1)} %all_to_all.10.m_ref, bf16[1152,384]{1,0:T(8,128)(2,1)S(1)} %copy-done.11), custom_call_target="tpu_custom_call" | custom-call | flops 943718400 | bytes 2949120 | tf_op jit(solution)/shard_map/pallas_call | solution.py:704
  107.2 0.8 collective-permute-start.5
  108.0 1.3 %collective-permute-start.6 = (bf16[120,320]{1,0:T(8,128)(2,1)S(1)}, bf16[120,320]{1,0:T(8,128)(2,1)S(1)}, u32[]{:S(2)}, u32[]{:S(2)}) collective-permute-start(bf16[120,320]{1,0:T(8,128)(2,1)S(1)} %add_convert_fusion.1), channel_id=1, source_target_pairs={{0,16},{8,24},{16,0},{24,8},{1,17},{9,25},{17,1},{25,9},{2,18},{10... | collective-permute-start | bytes 230408 | tf_op jit(solution)/shard_map/ppermute | solution.py:562
  109.3 2.3 %collective-permute-start.7 = (bf16[120,320]{1,0:T(8,128)(2,1)S(1)}, bf16[120,320]{1,0:T(8,128)(2,1)S(1)}, u32[]{:S(2)}, u32[]{:S(2)}) collective-permute-start(bf16[120,320]{1,0:T(8,128)(2,1)S(1)} %add_convert_fusion.1), channel_id=1, source_target_pairs={{0,24},{8,16},{16,8},{24,0},{1,25},{9,17},{17,9},{25,1},{2,26},{10... | collective-permute-start | bytes 230408 | tf_op jit(solution)/shard_map/ppermute | solution.py:562
  111.7 0.8 collective-permute-done.5
  112.5 4.9 %collective-permute-done.6 = bf16[120,320]{1,0:T(8,128)(2,1)S(1)} collective-permute-done((bf16[120,320]{1,0:T(8,128)(2,1)S(1)}, bf16[120,320]{1,0:T(8,128)(2,1)S(1)}, u32[]{:S(2)}, u32[]{:S(2)}) %collective-permute-start.6) | collective-permute-done | bytes 76832 | tf_op jit(solution)/shard_map/ppermute | solution.py:562
  117.5 0.8 collective-permute-start.8
  118.9 2.1 %collective-permute-start.10 = (bf16[120,320]{1,0:T(8,128)(2,1)S(1)}, bf16[120,320]{1,0:T(8,128)(2,1)S(1)}, u32[]{:S(2)}, u32[]{:S(2)}) collective-permute-start(bf16[120,320]{1,0:T(8,128)(2,1)S(1)} %add_convert_fusion), channel_id=1, source_target_pairs={{0,5},{1,4},{4,1},{5,0},{2,7},{3,6},{6,3},{7,2},{8,13},{9,12},{12,... | collective-permute-start | bytes 230408 | tf_op jit(solution)/shard_map/ppermute | solution.py:564
  121.0 1.1 collective-permute-done.8
  122.1 0.7 collective-permute-done.9
  122.8 1.5 %collective-permute-done.10 = bf16[120,320]{1,0:T(8,128)(2,1)S(1)} collective-permute-done((bf16[120,320]{1,0:T(8,128)(2,1)S(1)}, bf16[120,320]{1,0:T(8,128)(2,1)S(1)}, u32[]{:S(2)}, u32[]{:S(2)}) %collective-permute-start.10) | collective-permute-done | bytes 76832 | tf_op jit(solution)/shard_map/ppermute | solution.py:564
  124.5 1.7 %collective-permute-done.11.other_ref = bf16[4,120,320]{2,1,0:T(8,128)(2,1)S(1)} collective-permute-done((bf16[4,120,320]{2,1,0:T(8,128)(2,1)S(1)}, bf16[4,120,320]{2,1,0:T(8,128)(2,1)S(1)}, u32[]{:S(2)}, u32[]{:S(2)}) %collective-permute-start.11) | collective-permute-done | bytes 307232 | tf_op jit(solution)/shard_map/ppermute | solution.py:572
  126.2 1.8 %shard_map.130 = f32[960,320]{1,0:T(8,128)} custom-call(s32[6]{0:T(128)S(1)} %stack.46.flag_ref, bf16[4,120,320]{2,1,0:T(8,128)(2,1)S(1)} %pad_maximum_fusion.own_ref, bf16[4,120,320]{2,1,0:T(8,128)(2,1)S(1)} %collective-permute-done.11.other_ref), custom_call_target="tpu_custom_call" | custom-call | bytes 614400 | tf_op jit(solution)/shard_map/pallas_call | solution.py:574
  (45 shorter events, 4.5 us)
Async XLA Ops:
  0.6 7.4 %copy-start = (bf16[320,320]{1,0:T(8,128)(2,1)S(1)}, bf16[320,320]{1,0:T(8,128)(2,1)}, u32[]{:S(2)}) copy-start(bf16[320,320]{1,0:T(8,128)(2,1)} %param.15) | copy-start | bytes 614404
  2.4 11.3 %collective-permute-start = (bf16[12,32,320]{2,1,0:T(8,128)(2,1)}, bf16[12,32,320]{2,1,0:T(8,128)(2,1)}, u32[]{:S(2)}, u32[]{:S(2)}) collective-permute-start(bf16[12,32,320]{2,1,0:T(8,128)(2,1)} %dynamic-slice_bitcast_fusion), channel_id=1, source_target_pairs={{0,1},{1,0},{2,3},{3,2},{4,5},{5,4},{6,7},{7,6},{8,9},{9,8},{10,11... | collective-permute-start | bytes 737288 | tf_op jit(solution)/shard_map/ppermute | solution.py:613
  6.0 1.6 %copy-start.1 = (bf16[3,3,320,320]{3,2,1,0:T(8,128)(2,1)S(1)}, bf16[3,3,320,320]{3,2,1,0:T(8,128)(2,1)}, u32[]{:S(2)}) copy-start(bf16[3,3,320,320]{3,2,1,0:T(8,128)(2,1)} %w_ref.1) | copy-start | bytes 5529604
  7.6 1.3 copy-start.8
  7.6 1.3 copy-start.9
  16.5 6.2 %copy-start.2 = (bf16[12,4,32,320]{3,2,1,0:T(8,128)(2,1)S(1)}, bf16[12,4,32,320]{3,2,1,0:T(8,128)(2,1)}, u32[]{:S(2)}) copy-start(bf16[12,4,32,320]{3,2,1,0:T(8,128)(2,1)} %x_ref.1) | copy-start | bytes 2949124
  16.6 28.1 %all-to-all-start = ((bf16[16,48,640]{2,1,0:T(8,128)(2,1)}), bf16[16,48,640]{2,1,0:T(8,128)(2,1)}, u32[]{:S(2)}, u32[]{:S(2)}) async-start(bf16[16,48,640]{2,1,0:T(8,128)(2,1)} %bitcast.6), calls=%async_computation | async-start | bytes 1966080 | tf_op jit(solution)/shard_map/all_to_all | solution.py:583
  22.7 1.1 copy-start.3
  22.7 1.2 copy-start.4
  22.7 1.2 copy-start.5
  22.7 1.3 %copy-start.6 = (bf16[320,320]{1,0:T(8,128)(2,1)S(1)}, bf16[320,320]{1,0:T(8,128)(2,1)}, u32[]{:S(2)}) copy-start(bf16[320,320]{1,0:T(8,128)(2,1)} %wv_ref.1) | copy-start | bytes 614404
  22.8 1.3 %copy-start.7 = (bf16[320,320]{1,0:T(8,128)(2,1)S(1)}, bf16[320,320]{1,0:T(8,128)(2,1)}, u32[]{:S(2)}) copy-start(bf16[320,320]{1,0:T(8,128)(2,1)} %wo_ref.1) | copy-start | bytes 614404
  24.9 0.9 copy-start.10
  25.9 0.9 copy-start.12
  26.8 0.7 copy-start.13
  27.5 0.7 copy-start.14
  97.5 1.8 %collective-permute-start.1 = (bf16[480,320]{1,0:T(8,128)(2,1)S(1)}, bf16[480,320]{1,0:T(8,128)(2,1)S(1)}, u32[]{:S(2)}, u32[]{:S(2)}) collective-permute-start(bf16[480,320]{1,0:T(8,128)(2,1)S(1)} %get-tuple-element.31), channel_id=1, source_target_pairs={{0,2},{2,0},{1,3},{3,1},{4,6},{6,4},{5,7},{7,5},{8,10},{10,8},{9,1... | collective-permute-start | bytes 921608 | tf_op jit(solution)/shard_map/ppermute | solution.py:553
  97.7 5.3 %copy-start.11 = (bf16[1152,384]{1,0:T(8,128)(2,1)S(1)}, bf16[1152,384]{1,0:T(8,128)(2,1)}, u32[]{:S(2)}) copy-start(bf16[1152,384]{1,0:T(8,128)(2,1)} %copy-done.10) | copy-start | bytes 2654212
  99.4 7.8 %collective-permute-start.2 = (bf16[120,320]{1,0:T(8,128)(2,1)S(1)}, bf16[120,320]{1,0:T(8,128)(2,1)S(1)}, u32[]{:S(2)}, u32[]{:S(2)}) collective-permute-start(bf16[120,320]{1,0:T(8,128)(2,1)S(1)} %get-tuple-element.36), channel_id=1, source_target_pairs={{0,1},{1,0},{4,5},{5,4},{2,3},{3,2},{6,7},{7,6},{8,9},{9,8},{12,13... | collective-permute-start | bytes 230408 | tf_op jit(solution)/shard_map/ppermute | solution.py:557
  100.2 7.0 %collective-permute-start.3 = (bf16[120,320]{1,0:T(8,128)(2,1)S(1)}, bf16[120,320]{1,0:T(8,128)(2,1)S(1)}, u32[]{:S(2)}, u32[]{:S(2)}) collective-permute-start(bf16[120,320]{1,0:T(8,128)(2,1)S(1)} %get-tuple-element.38), channel_id=1, source_target_pairs={{0,4},{1,5},{4,0},{5,1},{2,6},{3,7},{6,2},{7,3},{8,12},{9,13},{12,... | collective-permute-start | bytes 230408 | tf_op jit(solution)/shard_map/ppermute | solution.py:557
  100.8 6.4 %collective-permute-start.4 = (bf16[120,320]{1,0:T(8,128)(2,1)S(1)}, bf16[120,320]{1,0:T(8,128)(2,1)S(1)}, u32[]{:S(2)}, u32[]{:S(2)}) collective-permute-start(bf16[120,320]{1,0:T(8,128)(2,1)S(1)} %get-tuple-element.37), channel_id=1, source_target_pairs={{0,5},{1,4},{4,1},{5,0},{2,7},{3,6},{6,3},{7,2},{8,13},{9,12},{12,... | collective-permute-start | bytes 230408 | tf_op jit(solution)/shard_map/ppermute | solution.py:557
  107.2 5.2 %collective-permute-start.5 = (bf16[120,320]{1,0:T(8,128)(2,1)S(1)}, bf16[120,320]{1,0:T(8,128)(2,1)S(1)}, u32[]{:S(2)}, u32[]{:S(2)}) collective-permute-start(bf16[120,320]{1,0:T(8,128)(2,1)S(1)} %add_convert_fusion.1), channel_id=1, source_target_pairs={{0,8},{8,0},{16,24},{24,16},{1,9},{9,1},{17,25},{25,17},{2,10},{10... | collective-permute-start | bytes 230408 | tf_op jit(solution)/shard_map/ppermute | solution.py:562
  108.0 9.4 %collective-permute-start.6 = (bf16[120,320]{1,0:T(8,128)(2,1)S(1)}, bf16[120,320]{1,0:T(8,128)(2,1)S(1)}, u32[]{:S(2)}, u32[]{:S(2)}) collective-permute-start(bf16[120,320]{1,0:T(8,128)(2,1)S(1)} %add_convert_fusion.1), channel_id=1, source_target_pairs={{0,16},{8,24},{16,0},{24,8},{1,17},{9,25},{17,1},{25,9},{2,18},{10... | collective-permute-start | bytes 230408 | tf_op jit(solution)/shard_map/ppermute | solution.py:562
  109.3 8.1 %collective-permute-start.7 = (bf16[120,320]{1,0:T(8,128)(2,1)S(1)}, bf16[120,320]{1,0:T(8,128)(2,1)S(1)}, u32[]{:S(2)}, u32[]{:S(2)}) collective-permute-start(bf16[120,320]{1,0:T(8,128)(2,1)S(1)} %add_convert_fusion.1), channel_id=1, source_target_pairs={{0,24},{8,16},{16,8},{24,0},{1,25},{9,17},{17,9},{25,1},{2,26},{10... | collective-permute-start | bytes 230408 | tf_op jit(solution)/shard_map/ppermute | solution.py:562
  117.5 4.6 %collective-permute-start.8 = (bf16[120,320]{1,0:T(8,128)(2,1)S(1)}, bf16[120,320]{1,0:T(8,128)(2,1)S(1)}, u32[]{:S(2)}, u32[]{:S(2)}) collective-permute-start(bf16[120,320]{1,0:T(8,128)(2,1)S(1)} %add_convert_fusion), channel_id=1, source_target_pairs={{0,1},{1,0},{4,5},{5,4},{2,3},{3,2},{6,7},{7,6},{8,9},{9,8},{12,13... | collective-permute-start | bytes 230408 | tf_op jit(solution)/shard_map/ppermute | solution.py:564
  118.2 4.6 %collective-permute-start.9 = (bf16[120,320]{1,0:T(8,128)(2,1)S(1)}, bf16[120,320]{1,0:T(8,128)(2,1)S(1)}, u32[]{:S(2)}, u32[]{:S(2)}) collective-permute-start(bf16[120,320]{1,0:T(8,128)(2,1)S(1)} %add_convert_fusion), channel_id=1, source_target_pairs={{0,4},{1,5},{4,0},{5,1},{2,6},{3,7},{6,2},{7,3},{8,12},{9,13},{12,... | collective-permute-start | bytes 230408 | tf_op jit(solution)/shard_map/ppermute | solution.py:564
  118.9 5.5 %collective-permute-start.10 = (bf16[120,320]{1,0:T(8,128)(2,1)S(1)}, bf16[120,320]{1,0:T(8,128)(2,1)S(1)}, u32[]{:S(2)}, u32[]{:S(2)}) collective-permute-start(bf16[120,320]{1,0:T(8,128)(2,1)S(1)} %add_convert_fusion), channel_id=1, source_target_pairs={{0,5},{1,4},{4,1},{5,0},{2,7},{3,6},{6,3},{7,2},{8,13},{9,12},{12,... | collective-permute-start | bytes 230408 | tf_op jit(solution)/shard_map/ppermute | solution.py:564
  124.4 1.8 %collective-permute-start.11 = (bf16[4,120,320]{2,1,0:T(8,128)(2,1)S(1)}, bf16[4,120,320]{2,1,0:T(8,128)(2,1)S(1)}, u32[]{:S(2)}, u32[]{:S(2)}) collective-permute-start(bf16[4,120,320]{2,1,0:T(8,128)(2,1)S(1)} %pad_maximum_fusion.own_ref), channel_id=1, source_target_pairs={{0,2},{2,0},{1,3},{3,1},{4,6},{6,4},{5,7},{7,5},{8,10},{10,8},{9,1... | collective-permute-start | bytes 921608 | tf_op jit(solution)/shard_map/ppermute | solution.py:572

commit v9 on v8

--- a/solution.py
+++ b/solution.py
@@ -325,7 +325,7 @@
     units = rows // PIX
     frames = units * 2
     head = ch // HEADS
-    chunk = 96
+    chunk = 192
 
     def arriving(i):
         at = pl.ds(pl.multiple_of(i * chunk, 8), chunk)
@@ -436,7 +436,7 @@
         leaving(i).start()
         return 0
 
-    lax.fori_loop(0, rows // own, mix, 0)
+    lax.fori_loop(0, rows // own, mix, 0, unroll=4)
 
     def edges(i, _):
         after = m32[pl.ds(pl.multiple_of(jnp.minimum((i + 1) * own, rows - PIX), 8), PIX), :]
@@ -446,7 +446,7 @@
         o_ref[i, own : own + PIX, :] = edge.astype(BF16)
         return 0
 
-    lax.fori_loop(0, rows // own, edges, 0)
+    lax.fori_loop(0, rows // own, edges, 0, unroll=4)
     at = (slice(None), pl.ds(own, PIX))
     last = pltpu.make_async_copy(o_ref.at[at], o_hbm.at[at], sems.at[3])
     last.start()
@@ -484,7 +484,7 @@
     shards = m_ref.shape[0]
     ch = m_ref.shape[-1] // 2
     pad = dst_tile(ch)
-    count = 8
+    count = 16
 
     def step(i, _):
         src = sources(m_ref, i * count, count, flag_ref[2], flag_ref[3], len_ref)
@@ -682,7 +682,7 @@
             pltpu.VMEM(flat.shape, BF16),
             pltpu.VMEM((shards, (half + 1) * PIX, 2 * ch), BF16),
             pltpu.SemaphoreType.DMA((4,)),
-            pltpu.SemaphoreType.DMA((n_packed // 96,)),
+            pltpu.SemaphoreType.DMA((n_packed // 192,)),
             pltpu.SemaphoreType.DMA((shards,)),
         ],
         out_space=ANY,

time: 128 us -> 127 us (level)
  Pallas kernels: 32.4 us -> 30.7 us
where the time goes in v9:
time: 127 us; the launch traced here: 126 us
  blocking collectives  35.6 us (28%)
  Pallas kernels  30.7 us (24%)
  waiting for transfers between devices  28.7 us (23%)
  starting transfers between devices  20.9 us (16%)
  local copies, waits for them, and re-layouts  8.16 us (6%)
    all_to_all x1, blocking collectives, body(): mixed = lax.all_to_all(mixed, SEQ, split_axis=0, concat_axis=0, tiled=True)  35.6 us
    all_to_all x1, waiting for transfers between devices, exchange(): flat = lax.all_to_all(flat, SEQ, split_axis=0, concat_axis=0, tiled=True)  16.5 us
    pallas_call x1, Pallas kernels, body(): call(attention_kernel, jax.ShapeDtypeStruct((shards, (half + 1) * PIX, 2...  12.8 us
    unnamed x30, local copies, waits for them, and re-layouts  6.27 us
    all_to_all x1, starting transfers between devices, exchange(): flat = lax.all_to_all(flat, SEQ, split_axis=0, concat_axis=0, tiled=True)  6.11 us
    ppermute x3, waiting for transfers between devices, reduce_all(): parts.append(lax.ppermute(mine, 'z', swaps(n_z, k)).astype(F32))  5.73 us
    pallas_call x1, Pallas kernels, body(): call(inner_kernel, packed, [SMEM, SMEM] + [VMEM] * 3, **work)  4.78 us
    ppermute x3, starting transfers between devices, reduce_all(): parts.append(lax.ppermute(mine, 'z', swaps(n_z, k)).astype(F32))  4.45 us
  transfers between devices with their start and end apart: 13, of which 8 were waited for; matrix products, arithmetic and copies ran while one was open for 1% of the time, Pallas kernels for 8%

profile of v9, /device:TPU:0, one launch (start us, length us, event | category | flops | bytes accessed | tf_op | source)
XLA Modules:
  0.0 126.2 jit_solution(17903468894630202593)
XLA Ops:
  0.7 1.8 %dynamic-slice_bitcast_fusion = bf16[12,32,320]{2,1,0:T(8,128)(2,1)} fusion(bf16[12,4,32,320]{3,2,1,0:T(8,128)(2,1)} %lat_ref.3, s32[]{:T(128)S(6)} %select_n.16), kind=kLoop, calls=%fused_computation.2 | loop fusion | bytes 491524 | tf_op jit(solution)/shard_map/jit(dynamic_index_in_dim)/squeeze | solution.py:612
  2.4 2.9 %collective-permute-start = (bf16[12,32,320]{2,1,0:T(8,128)(2,1)}, bf16[12,32,320]{2,1,0:T(8,128)(2,1)}, u32[]{:S(2)}, u32[]{:S(2)}) collective-permute-start(bf16[12,32,320]{2,1,0:T(8,128)(2,1)} %dynamic-slice_bitcast_fusion), channel_id=1, source_target_pairs={{0,1},{1,0},{2,3},{3,2},{4,5},{5,4},{6,7},{7,6},{8,9},{9,8},{10,11... | collective-permute-start | bytes 737288 | tf_op jit(solution)/shard_map/ppermute | solution.py:613
  5.4 0.7 convert_element_type.45
  6.0 1.6 %copy-done.1 = bf16[3,3,320,320]{3,2,1,0:T(8,128)(2,1)S(1)} copy-done((bf16[3,3,320,320]{3,2,1,0:T(8,128)(2,1)S(1)}, bf16[3,3,320,320]{3,2,1,0:T(8,128)(2,1)}, u32[]{:S(2)}) %copy-start.1) | copy-done | bytes 1843224
  8.9 4.8 %shard_map.124.inner_hbm = bf16[16,6,8,640]{3,2,1,0:T(8,128)(2,1)} custom-call(s32[6]{0:T(128)S(1)} %stack.46.flag_ref, s32[4]{0:T(128)S(1)} %copy-done.9, bf16[12,4,32,320]{3,2,1,0:T(8,128)(2,1)S(1)} %copy-done.8, bf16[1024,1024]{1,0:T(8,128)(2,1)S(1)} %shard_map.123.w_ref, f32[4,320]{1,0:T(4,128)S(1)} %fusion.table_ref), custom_call_target="tpu_custom_call" | custom-call | flops 2831155200 | bytes 3809280 | tf_op jit(solution)/shard_map/pallas_call | solution.py:634
  13.7 2.9 %shard_map.125 = bf16[16,6,8,640]{3,2,1,0:T(8,128)(2,1)} custom-call(s32[6]{0:T(128)S(1)} %stack.46.flag_ref, s32[4]{0:T(128)S(1)} %copy-done.9, bf16[12,4,32,320]{3,2,1,0:T(8,128)(2,1)S(1)} %copy-done.8, bf16[12,32,320]{2,1,0:T(8,128)(2,1)} %collective-permute-done.halo_ref, ...), custom_call_target="tpu_custom_call", output_to_operand_aliasing={{}: (6, {})} | custom-call | flops 2831155200 | bytes 3809280 | tf_op jit(solution)/shard_map/pallas_call | solution.py:637
  16.6 6.1 %all-to-all-start = ((bf16[16,48,640]{2,1,0:T(8,128)(2,1)}), bf16[16,48,640]{2,1,0:T(8,128)(2,1)}, u32[]{:S(2)}, u32[]{:S(2)}) async-start(bf16[16,48,640]{2,1,0:T(8,128)(2,1)} %bitcast.6), calls=%async_computation | async-start | bytes 1966080 | tf_op jit(solution)/shard_map/all_to_all | solution.py:583
  24.1 0.8 shard_map.126
  24.9 0.9 copy-done.10
  25.9 0.9 copy-done.12
  26.8 0.7 copy-done.13
  27.5 0.7 copy-done.14
  28.2 16.5 %all-to-all-done = bf16[16,48,640]{2,1,0:T(8,128)(2,1)} async-done(((bf16[16,48,640]{2,1,0:T(8,128)(2,1)}), bf16[16,48,640]{2,1,0:T(8,128)(2,1)}, u32[]{:S(2)}, u32[]{:S(2)}) %all-to-all-start) | async-done | bytes 983072 | tf_op jit(solution)/shard_map/all_to_all | solution.py:583
  44.6 12.8 %shard_map.127 = bf16[16,56,640]{2,1,0:T(8,128)(2,1)} custom-call(bf16[768,640]{1,0:T(8,128)(2,1)} %bitcast.8.act_hbm, bf16[384,1152]{1,0:T(8,128)(2,1)} %copy-done.12, bf16[384,384]{1,0:T(8,128)(2,1)} %copy-done.13, f32[192,192]{1,0:T(8,128)} %copy-done.14), custom_call_target="tpu_custom_call" | custom-call | flops 2202009600 | bytes 3932160 | tf_op jit(solution)/shard_map/pallas_call | solution.py:674
  57.4 35.6 %all_to_all.10.m_ref = bf16[16,56,640]{2,1,0:T(8,128)(2,1)S(1)} all-to-all(bf16[16,56,640]{2,1,0:T(8,128)(2,1)} %shard_map.127), channel_id=1, replica_groups=mesh['z'=4,'y'=2,'c'=2,'x'=2] {'z','y','c'}, dimensions={0} | all-to-all | bytes 2293760 | tf_op jit(solution)/shard_map/all_to_all | solution.py:693
  93.1 2.7 %shard_map.128 = (f32[480,320]{1,0:T(8,128)S(1)}, bf16[480,320]{1,0:T(8,128)(2,1)S(1)}) custom-call(s32[6]{0:T(128)S(1)} %stack.46.flag_ref, s32[4]{0:T(128)S(1)} %copy-done.9, bf16[16,56,640]{2,1,0:T(8,128)(2,1)S(1)} %all_to_all.10.m_ref, bf16[16,48,640]{2,1,0:T(8,128)(2,1)S(1)} %bitcast.17), custom_call_target="tpu_custom_call" | custom-call | flops 943718400 | bytes 2949120 | tf_op jit(solution)/shard_map/pallas_call | solution.py:695
  96.0 1.6 %collective-permute-done.1 = bf16[480,320]{1,0:T(8,128)(2,1)S(1)} collective-permute-done((bf16[480,320]{1,0:T(8,128)(2,1)S(1)}, bf16[480,320]{1,0:T(8,128)(2,1)S(1)}, u32[]{:S(2)}, u32[]{:S(2)}) %collective-permute-start.1) | collective-permute-done | bytes 307232 | tf_op jit(solution)/shard_map/ppermute | solution.py:553
  97.7 0.8 collective-permute-start.2
  99.1 2.1 %collective-permute-start.4 = (bf16[120,320]{1,0:T(8,128)(2,1)S(1)}, bf16[120,320]{1,0:T(8,128)(2,1)S(1)}, u32[]{:S(2)}, u32[]{:S(2)}) collective-permute-start(bf16[120,320]{1,0:T(8,128)(2,1)S(1)} %get-tuple-element.37), channel_id=1, source_target_pairs={{0,5},{1,4},{4,1},{5,0},{2,7},{3,6},{6,3},{7,2},{8,13},{9,12},{12,... | collective-permute-start | bytes 230408 | tf_op jit(solution)/shard_map/ppermute | solution.py:557
  101.2 4.2 %shard_map.129 = bf16[12,4,32,320]{3,2,1,0:T(8,128)(2,1)} custom-call(s32[6]{0:T(128)S(1)} %stack.46.flag_ref, s32[4]{0:T(128)S(1)} %copy-done.9, bf16[16,56,640]{2,1,0:T(8,128)(2,1)S(1)} %all_to_all.10.m_ref, bf16[1152,384]{1,0:T(8,128)(2,1)S(1)} %copy-done.11), custom_call_target="tpu_custom_call" | custom-call | flops 943718400 | bytes 2949120 | tf_op jit(solution)/shard_map/pallas_call | solution.py:704
  105.5 0.8 collective-permute-start.5
  106.2 1.3 %collective-permute-start.6 = (bf16[120,320]{1,0:T(8,128)(2,1)S(1)}, bf16[120,320]{1,0:T(8,128)(2,1)S(1)}, u32[]{:S(2)}, u32[]{:S(2)}) collective-permute-start(bf16[120,320]{1,0:T(8,128)(2,1)S(1)} %add_convert_fusion.1), channel_id=1, source_target_pairs={{0,16},{8,24},{16,0},{24,8},{1,17},{9,25},{17,1},{25,9},{2,18},{10... | collective-permute-start | bytes 230408 | tf_op jit(solution)/shard_map/ppermute | solution.py:562
  107.6 2.3 %collective-permute-start.7 = (bf16[120,320]{1,0:T(8,128)(2,1)S(1)}, bf16[120,320]{1,0:T(8,128)(2,1)S(1)}, u32[]{:S(2)}, u32[]{:S(2)}) collective-permute-start(bf16[120,320]{1,0:T(8,128)(2,1)S(1)} %add_convert_fusion.1), channel_id=1, source_target_pairs={{0,24},{8,16},{16,8},{24,0},{1,25},{9,17},{17,9},{25,1},{2,26},{10... | collective-permute-start | bytes 230408 | tf_op jit(solution)/shard_map/ppermute | solution.py:562
  109.9 0.8 collective-permute-done.5
  110.7 4.9 %collective-permute-done.6 = bf16[120,320]{1,0:T(8,128)(2,1)S(1)} collective-permute-done((bf16[120,320]{1,0:T(8,128)(2,1)S(1)}, bf16[120,320]{1,0:T(8,128)(2,1)S(1)}, u32[]{:S(2)}, u32[]{:S(2)}) %collective-permute-start.6) | collective-permute-done | bytes 76832 | tf_op jit(solution)/shard_map/ppermute | solution.py:562
  115.7 0.8 collective-permute-start.8
  117.1 2.1 %collective-permute-start.10 = (bf16[120,320]{1,0:T(8,128)(2,1)S(1)}, bf16[120,320]{1,0:T(8,128)(2,1)S(1)}, u32[]{:S(2)}, u32[]{:S(2)}) collective-permute-start(bf16[120,320]{1,0:T(8,128)(2,1)S(1)} %add_convert_fusion), channel_id=1, source_target_pairs={{0,5},{1,4},{4,1},{5,0},{2,7},{3,6},{6,3},{7,2},{8,13},{9,12},{12,... | collective-permute-start | bytes 230408 | tf_op jit(solution)/shard_map/ppermute | solution.py:564
  119.3 1.1 collective-permute-done.8
  120.3 0.7 collective-permute-done.9
  121.1 1.5 %collective-permute-done.10 = bf16[120,320]{1,0:T(8,128)(2,1)S(1)} collective-permute-done((bf16[120,320]{1,0:T(8,128)(2,1)S(1)}, bf16[120,320]{1,0:T(8,128)(2,1)S(1)}, u32[]{:S(2)}, u32[]{:S(2)}) %collective-permute-start.10) | collective-permute-done | bytes 76832 | tf_op jit(solution)/shard_map/ppermute | solution.py:564
  122.8 1.7 %collective-permute-done.11.other_ref = bf16[4,120,320]{2,1,0:T(8,128)(2,1)S(1)} collective-permute-done((bf16[4,120,320]{2,1,0:T(8,128)(2,1)S(1)}, bf16[4,120,320]{2,1,0:T(8,128)(2,1)S(1)}, u32[]{:S(2)}, u32[]{:S(2)}) %collective-permute-start.11) | collective-permute-done | bytes 307232 | tf_op jit(solution)/shard_map/ppermute | solution.py:572
  124.4 1.8 %shard_map.130 = f32[960,320]{1,0:T(8,128)} custom-call(s32[6]{0:T(128)S(1)} %stack.46.flag_ref, bf16[4,120,320]{2,1,0:T(8,128)(2,1)S(1)} %pad_maximum_fusion.own_ref, bf16[4,120,320]{2,1,0:T(8,128)(2,1)S(1)} %collective-permute-done.11.other_ref), custom_call_target="tpu_custom_call" | custom-call | bytes 614400 | tf_op jit(solution)/shard_map/pallas_call | solution.py:574
  (45 shorter events, 4.5 us)
Async XLA Ops:
  0.6 7.4 %copy-start = (bf16[320,320]{1,0:T(8,128)(2,1)S(1)}, bf16[320,320]{1,0:T(8,128)(2,1)}, u32[]{:S(2)}) copy-start(bf16[320,320]{1,0:T(8,128)(2,1)} %param.15) | copy-start | bytes 614404
  2.4 11.3 %collective-permute-start = (bf16[12,32,320]{2,1,0:T(8,128)(2,1)}, bf16[12,32,320]{2,1,0:T(8,128)(2,1)}, u32[]{:S(2)}, u32[]{:S(2)}) collective-permute-start(bf16[12,32,320]{2,1,0:T(8,128)(2,1)} %dynamic-slice_bitcast_fusion), channel_id=1, source_target_pairs={{0,1},{1,0},{2,3},{3,2},{4,5},{5,4},{6,7},{7,6},{8,9},{9,8},{10,11... | collective-permute-start | bytes 737288 | tf_op jit(solution)/shard_map/ppermute | solution.py:613
  6.0 1.6 %copy-start.1 = (bf16[3,3,320,320]{3,2,1,0:T(8,128)(2,1)S(1)}, bf16[3,3,320,320]{3,2,1,0:T(8,128)(2,1)}, u32[]{:S(2)}) copy-start(bf16[3,3,320,320]{3,2,1,0:T(8,128)(2,1)} %w_ref.1) | copy-start | bytes 5529604
  7.6 1.3 %copy-start.8 = (bf16[12,4,32,320]{3,2,1,0:T(8,128)(2,1)S(1)}, bf16[12,4,32,320]{3,2,1,0:T(8,128)(2,1)}, u32[]{:S(2)}) copy-start(bf16[12,4,32,320]{3,2,1,0:T(8,128)(2,1)} %lat_ref.3) | copy-start | bytes 2949124
  7.6 1.3 %copy-start.9 = (s32[4]{0:T(128)S(1)}, s32[4]{0:T(128)}, u32[]{:S(2)}) copy-start(s32[4]{0:T(128)} %len_ref.9) | copy-start | bytes 52
  16.6 6.1 %copy-start.2 = (bf16[12,4,32,320]{3,2,1,0:T(8,128)(2,1)S(1)}, bf16[12,4,32,320]{3,2,1,0:T(8,128)(2,1)}, u32[]{:S(2)}) copy-start(bf16[12,4,32,320]{3,2,1,0:T(8,128)(2,1)} %x_ref.1) | copy-start | bytes 2949124
  16.6 28.0 %all-to-all-start = ((bf16[16,48,640]{2,1,0:T(8,128)(2,1)}), bf16[16,48,640]{2,1,0:T(8,128)(2,1)}, u32[]{:S(2)}, u32[]{:S(2)}) async-start(bf16[16,48,640]{2,1,0:T(8,128)(2,1)} %bitcast.6), calls=%async_computation | async-start | bytes 1966080 | tf_op jit(solution)/shard_map/all_to_all | solution.py:583
  22.7 1.1 copy-start.3
  22.7 1.2 copy-start.4
  22.7 1.2 copy-start.5
  22.7 1.3 %copy-start.6 = (bf16[320,320]{1,0:T(8,128)(2,1)S(1)}, bf16[320,320]{1,0:T(8,128)(2,1)}, u32[]{:S(2)}) copy-start(bf16[320,320]{1,0:T(8,128)(2,1)} %wv_ref.1) | copy-start | bytes 614404
  22.8 1.3 %copy-start.7 = (bf16[320,320]{1,0:T(8,128)(2,1)S(1)}, bf16[320,320]{1,0:T(8,128)(2,1)}, u32[]{:S(2)}) copy-start(bf16[320,320]{1,0:T(8,128)(2,1)} %wo_ref.1) | copy-start | bytes 614404
  24.9 0.9 copy-start.10
  25.8 0.9 copy-start.12
  26.8 0.7 copy-start.13
  27.5 0.7 copy-start.14
  95.8 1.8 %collective-permute-start.1 = (bf16[480,320]{1,0:T(8,128)(2,1)S(1)}, bf16[480,320]{1,0:T(8,128)(2,1)S(1)}, u32[]{:S(2)}, u32[]{:S(2)}) collective-permute-start(bf16[480,320]{1,0:T(8,128)(2,1)S(1)} %get-tuple-element.31), channel_id=1, source_target_pairs={{0,2},{2,0},{1,3},{3,1},{4,6},{6,4},{5,7},{7,5},{8,10},{10,8},{9,1... | collective-permute-start | bytes 921608 | tf_op jit(solution)/shard_map/ppermute | solution.py:553
  95.9 5.3 %copy-start.11 = (bf16[1152,384]{1,0:T(8,128)(2,1)S(1)}, bf16[1152,384]{1,0:T(8,128)(2,1)}, u32[]{:S(2)}) copy-start(bf16[1152,384]{1,0:T(8,128)(2,1)} %copy-done.10) | copy-start | bytes 2654212
  97.7 7.8 %collective-permute-start.2 = (bf16[120,320]{1,0:T(8,128)(2,1)S(1)}, bf16[120,320]{1,0:T(8,128)(2,1)S(1)}, u32[]{:S(2)}, u32[]{:S(2)}) collective-permute-start(bf16[120,320]{1,0:T(8,128)(2,1)S(1)} %get-tuple-element.36), channel_id=1, source_target_pairs={{0,1},{1,0},{4,5},{5,4},{2,3},{3,2},{6,7},{7,6},{8,9},{9,8},{12,13... | collective-permute-start | bytes 230408 | tf_op jit(solution)/shard_map/ppermute | solution.py:557
  98.4 7.0 %collective-permute-start.3 = (bf16[120,320]{1,0:T(8,128)(2,1)S(1)}, bf16[120,320]{1,0:T(8,128)(2,1)S(1)}, u32[]{:S(2)}, u32[]{:S(2)}) collective-permute-start(bf16[120,320]{1,0:T(8,128)(2,1)S(1)} %get-tuple-element.38), channel_id=1, source_target_pairs={{0,4},{1,5},{4,0},{5,1},{2,6},{3,7},{6,2},{7,3},{8,12},{9,13},{12,... | collective-permute-start | bytes 230408 | tf_op jit(solution)/shard_map/ppermute | solution.py:557
  99.1 6.4 %collective-permute-start.4 = (bf16[120,320]{1,0:T(8,128)(2,1)S(1)}, bf16[120,320]{1,0:T(8,128)(2,1)S(1)}, u32[]{:S(2)}, u32[]{:S(2)}) collective-permute-start(bf16[120,320]{1,0:T(8,128)(2,1)S(1)} %get-tuple-element.37), channel_id=1, source_target_pairs={{0,5},{1,4},{4,1},{5,0},{2,7},{3,6},{6,3},{7,2},{8,13},{9,12},{12,... | collective-permute-start | bytes 230408 | tf_op jit(solution)/shard_map/ppermute | solution.py:557
  105.5 5.2 %collective-permute-start.5 = (bf16[120,320]{1,0:T(8,128)(2,1)S(1)}, bf16[120,320]{1,0:T(8,128)(2,1)S(1)}, u32[]{:S(2)}, u32[]{:S(2)}) collective-permute-start(bf16[120,320]{1,0:T(8,128)(2,1)S(1)} %add_convert_fusion.1), channel_id=1, source_target_pairs={{0,8},{8,0},{16,24},{24,16},{1,9},{9,1},{17,25},{25,17},{2,10},{10... | collective-permute-start | bytes 230408 | tf_op jit(solution)/shard_map/ppermute | solution.py:562
  106.2 9.4 %collective-permute-start.6 = (bf16[120,320]{1,0:T(8,128)(2,1)S(1)}, bf16[120,320]{1,0:T(8,128)(2,1)S(1)}, u32[]{:S(2)}, u32[]{:S(2)}) collective-permute-start(bf16[120,320]{1,0:T(8,128)(2,1)S(1)} %add_convert_fusion.1), channel_id=1, source_target_pairs={{0,16},{8,24},{16,0},{24,8},{1,17},{9,25},{17,1},{25,9},{2,18},{10... | collective-permute-start | bytes 230408 | tf_op jit(solution)/shard_map/ppermute | solution.py:562
  107.6 8.1 %collective-permute-start.7 = (bf16[120,320]{1,0:T(8,128)(2,1)S(1)}, bf16[120,320]{1,0:T(8,128)(2,1)S(1)}, u32[]{:S(2)}, u32[]{:S(2)}) collective-permute-start(bf16[120,320]{1,0:T(8,128)(2,1)S(1)} %add_convert_fusion.1), channel_id=1, source_target_pairs={{0,24},{8,16},{16,8},{24,0},{1,25},{9,17},{17,9},{25,1},{2,26},{10... | collective-permute-start | bytes 230408 | tf_op jit(solution)/shard_map/ppermute | solution.py:562
  115.7 4.6 %collective-permute-start.8 = (bf16[120,320]{1,0:T(8,128)(2,1)S(1)}, bf16[120,320]{1,0:T(8,128)(2,1)S(1)}, u32[]{:S(2)}, u32[]{:S(2)}) collective-permute-start(bf16[120,320]{1,0:T(8,128)(2,1)S(1)} %add_convert_fusion), channel_id=1, source_target_pairs={{0,1},{1,0},{4,5},{5,4},{2,3},{3,2},{6,7},{7,6},{8,9},{9,8},{12,13... | collective-permute-start | bytes 230408 | tf_op jit(solution)/shard_map/ppermute | solution.py:564
  116.5 4.6 %collective-permute-start.9 = (bf16[120,320]{1,0:T(8,128)(2,1)S(1)}, bf16[120,320]{1,0:T(8,128)(2,1)S(1)}, u32[]{:S(2)}, u32[]{:S(2)}) collective-permute-start(bf16[120,320]{1,0:T(8,128)(2,1)S(1)} %add_convert_fusion), channel_id=1, source_target_pairs={{0,4},{1,5},{4,0},{5,1},{2,6},{3,7},{6,2},{7,3},{8,12},{9,13},{12,... | collective-permute-start | bytes 230408 | tf_op jit(solution)/shard_map/ppermute | solution.py:564
  117.1 5.5 %collective-permute-start.10 = (bf16[120,320]{1,0:T(8,128)(2,1)S(1)}, bf16[120,320]{1,0:T(8,128)(2,1)S(1)}, u32[]{:S(2)}, u32[]{:S(2)}) collective-permute-start(bf16[120,320]{1,0:T(8,128)(2,1)S(1)} %add_convert_fusion), channel_id=1, source_target_pairs={{0,5},{1,4},{4,1},{5,0},{2,7},{3,6},{6,3},{7,2},{8,13},{9,12},{12,... | collective-permute-start | bytes 230408 | tf_op jit(solution)/shard_map/ppermute | solution.py:564
  122.7 1.8 %collective-permute-start.11 = (bf16[4,120,320]{2,1,0:T(8,128)(2,1)S(1)}, bf16[4,120,320]{2,1,0:T(8,128)(2,1)S(1)}, u32[]{:S(2)}, u32[]{:S(2)}) collective-permute-start(bf16[4,120,320]{2,1,0:T(8,128)(2,1)S(1)} %pad_maximum_fusion.own_ref), channel_id=1, source_target_pairs={{0,2},{2,0},{1,3},{3,1},{4,6},{6,4},{5,7},{7,5},{8,10},{10,8},{9,1... | collective-permute-start | bytes 921608 | tf_op jit(solution)/shard_map/ppermute | solution.py:572

commit v10 on v9

--- a/solution.py
+++ b/solution.py
@@ -462,22 +462,25 @@
     groups = shards // rows
     real = across // groups
     total_frames = flag_ref[3]
+    lines = 4 if rows % 4 == 0 else 1
+    count = groups * lines
 
     def join(blocks):
         return jnp.concatenate([b[:real] for b in blocks], axis=0).astype(BF16)
 
     def step(i, _):
-        src = sources(m_ref, i * groups, groups, flag_ref[2], total_frames, len_ref)
+        src = sources(m_ref, i * count, count, flag_ref[2], total_frames, len_ref)
         rounded = jnp.concatenate([v.astype(BF16) for v in src], axis=1)
         total = src[1] + jnp.dot(rounded, tw[...], preferred_element_type=F32)
-        total = total.reshape(2, groups, units, PIX, total.shape[-1])
+        total = total.reshape(2, count, units, PIX, total.shape[-1])
         for u in range(units):
             for q in range(2):
-                got = join([total[q, g, u] for g in range(groups)])
-                o_ref[2 * u + q, i] = got[:, :ch]
+                for r in range(lines):
+                    got = join([total[q, r * groups + g, u] for g in range(groups)])
+                    o_ref[2 * u + q, i * lines + r] = got[:, :ch]
         return 0
 
-    lax.fori_loop(0, rows, step, 0)
+    lax.fori_loop(0, rows // lines, step, 0)
 
 
 def grad_kernel(flag_ref, len_ref, m_ref, cot_ref, mine_ref, other_ref, grad, full):

time: 127 us -> 126 us (level)
  transfers between devices with their start and end apart: 13 -> 13, of which waited for: 8 -> 9; matrix products, arithmetic and copies ran while one was open for 1% -> 1% of each run, Pallas kernels for 8% -> 8%
where the time goes in v10:
time: 126 us
  blocking collectives  35.6 us (28%)
  Pallas kernels  30.1 us (24%)
  waiting for transfers between devices  28.9 us (23%)
  starting transfers between devices  20.9 us (17%)
  local copies, waits for them, and re-layouts  8.16 us (6%)
    all_to_all x1, blocking collectives, body(): mixed = lax.all_to_all(mixed, SEQ, split_axis=0, concat_axis=0, tiled=True)  35.6 us
    all_to_all x1, waiting for transfers between devices, exchange(): flat = lax.all_to_all(flat, SEQ, split_axis=0, concat_axis=0, tiled=True)  16.5 us
    pallas_call x1, Pallas kernels, body(): call(attention_kernel, jax.ShapeDtypeStruct((shards, (half + 1) * PIX, 2...  12.8 us
    unnamed x30, local copies, waits for them, and re-layouts  6.27 us
    all_to_all x1, starting transfers between devices, exchange(): flat = lax.all_to_all(flat, SEQ, split_axis=0, concat_axis=0, tiled=True)  6.11 us
    ppermute x3, waiting for transfers between devices, reduce_all(): parts.append(lax.ppermute(mine, 'z', swaps(n_z, k)).astype(F32))  5.68 us
    pallas_call x1, Pallas kernels, body(): call(inner_kernel, packed, [SMEM, SMEM] + [VMEM] * 3, **work)  4.78 us
    ppermute x3, starting transfers between devices, reduce_all(): parts.append(lax.ppermute(mine, 'z', swaps(n_z, k)).astype(F32))  4.45 us
  transfers between devices with their start and end apart: 13, of which 9 were waited for; matrix products, arithmetic and copies ran while one was open for 1% of the time, Pallas kernels for 8%

profile of v10, /device:TPU:0, one launch (start us, length us, event | category | flops | bytes accessed | tf_op | source)
XLA Modules:
  0.0 125.9 jit_solution(1863869564366614890)
XLA Ops:
  0.7 1.8 %dynamic-slice_bitcast_fusion = bf16[12,32,320]{2,1,0:T(8,128)(2,1)} fusion(bf16[12,4,32,320]{3,2,1,0:T(8,128)(2,1)} %lat_ref.3, s32[]{:T(128)S(6)} %select_n.16), kind=kLoop, calls=%fused_computation.2 | loop fusion | bytes 491524 | tf_op jit(solution)/shard_map/jit(dynamic_index_in_dim)/squeeze | solution.py:615
  2.4 2.9 %collective-permute-start = (bf16[12,32,320]{2,1,0:T(8,128)(2,1)}, bf16[12,32,320]{2,1,0:T(8,128)(2,1)}, u32[]{:S(2)}, u32[]{:S(2)}) collective-permute-start(bf16[12,32,320]{2,1,0:T(8,128)(2,1)} %dynamic-slice_bitcast_fusion), channel_id=1, source_target_pairs={{0,1},{1,0},{2,3},{3,2},{4,5},{5,4},{6,7},{7,6},{8,9},{9,8},{10,11... | collective-permute-start | bytes 737288 | tf_op jit(solution)/shard_map/ppermute | solution.py:616
  6.0 1.6 %copy-done.1 = bf16[3,3,320,320]{3,2,1,0:T(8,128)(2,1)S(1)} copy-done((bf16[3,3,320,320]{3,2,1,0:T(8,128)(2,1)S(1)}, bf16[3,3,320,320]{3,2,1,0:T(8,128)(2,1)}, u32[]{:S(2)}) %copy-start.1) | copy-done | bytes 1843224
  8.9 4.8 %shard_map.124.inner_hbm = bf16[16,6,8,640]{3,2,1,0:T(8,128)(2,1)} custom-call(s32[6]{0:T(128)S(1)} %stack.46.flag_ref, s32[4]{0:T(128)S(1)} %copy-done.9, bf16[12,4,32,320]{3,2,1,0:T(8,128)(2,1)S(1)} %copy-done.8, bf16[1024,1024]{1,0:T(8,128)(2,1)S(1)} %shard_map.123.w_ref, f32[4,320]{1,0:T(4,128)S(1)} %fusion.table_ref), custom_call_target="tpu_custom_call" | custom-call | flops 2831155200 | bytes 3809280 | tf_op jit(solution)/shard_map/pallas_call | solution.py:637
  13.7 2.9 %shard_map.125 = bf16[16,6,8,640]{3,2,1,0:T(8,128)(2,1)} custom-call(s32[6]{0:T(128)S(1)} %stack.46.flag_ref, s32[4]{0:T(128)S(1)} %copy-done.9, bf16[12,4,32,320]{3,2,1,0:T(8,128)(2,1)S(1)} %copy-done.8, bf16[12,32,320]{2,1,0:T(8,128)(2,1)} %collective-permute-done.halo_ref, ...), custom_call_target="tpu_custom_call", output_to_operand_aliasing={{}: (6, {})} | custom-call | flops 2831155200 | bytes 3809280 | tf_op jit(solution)/shard_map/pallas_call | solution.py:640
  16.6 6.1 %all-to-all-start = ((bf16[16,48,640]{2,1,0:T(8,128)(2,1)}), bf16[16,48,640]{2,1,0:T(8,128)(2,1)}, u32[]{:S(2)}, u32[]{:S(2)}) async-start(bf16[16,48,640]{2,1,0:T(8,128)(2,1)} %bitcast.6), calls=%async_computation | async-start | bytes 1966080 | tf_op jit(solution)/shard_map/all_to_all | solution.py:586
  24.1 0.8 shard_map.126
  24.9 0.9 copy-done.10
  25.9 0.9 copy-done.12
  26.8 0.7 copy-done.13
  27.5 0.7 copy-done.14
  28.2 16.5 %all-to-all-done = bf16[16,48,640]{2,1,0:T(8,128)(2,1)} async-done(((bf16[16,48,640]{2,1,0:T(8,128)(2,1)}), bf16[16,48,640]{2,1,0:T(8,128)(2,1)}, u32[]{:S(2)}, u32[]{:S(2)}) %all-to-all-start) | async-done | bytes 983072 | tf_op jit(solution)/shard_map/all_to_all | solution.py:586
  44.6 12.8 %shard_map.127 = bf16[16,56,640]{2,1,0:T(8,128)(2,1)} custom-call(bf16[768,640]{1,0:T(8,128)(2,1)} %bitcast.8.act_hbm, bf16[384,1152]{1,0:T(8,128)(2,1)} %copy-done.12, bf16[384,384]{1,0:T(8,128)(2,1)} %copy-done.13, f32[192,192]{1,0:T(8,128)} %copy-done.14), custom_call_target="tpu_custom_call" | custom-call | flops 2202009600 | bytes 3932160 | tf_op jit(solution)/shard_map/pallas_call | solution.py:677
  57.4 35.6 %all_to_all.10.m_ref = bf16[16,56,640]{2,1,0:T(8,128)(2,1)S(1)} all-to-all(bf16[16,56,640]{2,1,0:T(8,128)(2,1)} %shard_map.127), channel_id=1, replica_groups=mesh['z'=4,'y'=2,'c'=2,'x'=2] {'z','y','c'}, dimensions={0} | all-to-all | bytes 2293760 | tf_op jit(solution)/shard_map/all_to_all | solution.py:696
  93.1 2.7 %shard_map.128 = (f32[480,320]{1,0:T(8,128)S(1)}, bf16[480,320]{1,0:T(8,128)(2,1)S(1)}) custom-call(s32[6]{0:T(128)S(1)} %stack.46.flag_ref, s32[4]{0:T(128)S(1)} %copy-done.9, bf16[16,56,640]{2,1,0:T(8,128)(2,1)S(1)} %all_to_all.10.m_ref, bf16[16,48,640]{2,1,0:T(8,128)(2,1)S(1)} %bitcast.17), custom_call_target="tpu_custom_call" | custom-call | flops 943718400 | bytes 2949120 | tf_op jit(solution)/shard_map/pallas_call | solution.py:698
  96.0 1.6 %collective-permute-done.1 = bf16[480,320]{1,0:T(8,128)(2,1)S(1)} collective-permute-done((bf16[480,320]{1,0:T(8,128)(2,1)S(1)}, bf16[480,320]{1,0:T(8,128)(2,1)S(1)}, u32[]{:S(2)}, u32[]{:S(2)}) %collective-permute-start.1) | collective-permute-done | bytes 307232 | tf_op jit(solution)/shard_map/ppermute | solution.py:556
  97.7 0.8 collective-permute-start.2
  99.1 2.1 %collective-permute-start.4 = (bf16[120,320]{1,0:T(8,128)(2,1)S(1)}, bf16[120,320]{1,0:T(8,128)(2,1)S(1)}, u32[]{:S(2)}, u32[]{:S(2)}) collective-permute-start(bf16[120,320]{1,0:T(8,128)(2,1)S(1)} %get-tuple-element.37), channel_id=1, source_target_pairs={{0,5},{1,4},{4,1},{5,0},{2,7},{3,6},{6,3},{7,2},{8,13},{9,12},{12,... | collective-permute-start | bytes 230408 | tf_op jit(solution)/shard_map/ppermute | solution.py:560
  101.2 3.7 %shard_map.129 = bf16[12,4,32,320]{3,2,1,0:T(8,128)(2,1)} custom-call(s32[6]{0:T(128)S(1)} %stack.46.flag_ref, s32[4]{0:T(128)S(1)} %copy-done.9, bf16[16,56,640]{2,1,0:T(8,128)(2,1)S(1)} %all_to_all.10.m_ref, bf16[1152,384]{1,0:T(8,128)(2,1)S(1)} %copy-done.11), custom_call_target="tpu_custom_call" | custom-call | flops 943718400 | bytes 2949120 | tf_op jit(solution)/shard_map/pallas_call | solution.py:707
  105.0 0.8 collective-permute-start.5
  105.8 1.3 %collective-permute-start.6 = (bf16[120,320]{1,0:T(8,128)(2,1)S(1)}, bf16[120,320]{1,0:T(8,128)(2,1)S(1)}, u32[]{:S(2)}, u32[]{:S(2)}) collective-permute-start(bf16[120,320]{1,0:T(8,128)(2,1)S(1)} %add_convert_fusion.1), channel_id=1, source_target_pairs={{0,16},{8,24},{16,0},{24,8},{1,17},{9,25},{17,1},{25,9},{2,18},{10... | collective-permute-start | bytes 230408 | tf_op jit(solution)/shard_map/ppermute | solution.py:565
  107.1 2.3 %collective-permute-start.7 = (bf16[120,320]{1,0:T(8,128)(2,1)S(1)}, bf16[120,320]{1,0:T(8,128)(2,1)S(1)}, u32[]{:S(2)}, u32[]{:S(2)}) collective-permute-start(bf16[120,320]{1,0:T(8,128)(2,1)S(1)} %add_convert_fusion.1), channel_id=1, source_target_pairs={{0,24},{8,16},{16,8},{24,0},{1,25},{9,17},{17,9},{25,1},{2,26},{10... | collective-permute-start | bytes 230408 | tf_op jit(solution)/shard_map/ppermute | solution.py:565
  109.5 0.7 collective-permute-done.5
  110.2 4.9 %collective-permute-done.6 = bf16[120,320]{1,0:T(8,128)(2,1)S(1)} collective-permute-done((bf16[120,320]{1,0:T(8,128)(2,1)S(1)}, bf16[120,320]{1,0:T(8,128)(2,1)S(1)}, u32[]{:S(2)}, u32[]{:S(2)}) %collective-permute-start.6) | collective-permute-done | bytes 76832 | tf_op jit(solution)/shard_map/ppermute | solution.py:565
  115.2 0.8 collective-permute-start.8
  116.0 0.8 collective-permute-start.9
  116.8 2.0 %collective-permute-start.10 = (bf16[120,320]{1,0:T(8,128)(2,1)S(1)}, bf16[120,320]{1,0:T(8,128)(2,1)S(1)}, u32[]{:S(2)}, u32[]{:S(2)}) collective-permute-start(bf16[120,320]{1,0:T(8,128)(2,1)S(1)} %add_convert_fusion), channel_id=1, source_target_pairs={{0,5},{1,4},{4,1},{5,0},{2,7},{3,6},{6,3},{7,2},{8,13},{9,12},{12,... | collective-permute-start | bytes 230408 | tf_op jit(solution)/shard_map/ppermute | solution.py:567
  118.8 1.1 collective-permute-done.8
  119.8 0.7 collective-permute-done.9
  120.5 1.7 %collective-permute-done.10 = bf16[120,320]{1,0:T(8,128)(2,1)S(1)} collective-permute-done((bf16[120,320]{1,0:T(8,128)(2,1)S(1)}, bf16[120,320]{1,0:T(8,128)(2,1)S(1)}, u32[]{:S(2)}, u32[]{:S(2)}) %collective-permute-start.10) | collective-permute-done | bytes 76832 | tf_op jit(solution)/shard_map/ppermute | solution.py:567
  122.4 1.7 %collective-permute-done.11.other_ref = bf16[4,120,320]{2,1,0:T(8,128)(2,1)S(1)} collective-permute-done((bf16[4,120,320]{2,1,0:T(8,128)(2,1)S(1)}, bf16[4,120,320]{2,1,0:T(8,128)(2,1)S(1)}, u32[]{:S(2)}, u32[]{:S(2)}) %collective-permute-start.11) | collective-permute-done | bytes 307232 | tf_op jit(solution)/shard_map/ppermute | solution.py:575
  124.1 1.8 %shard_map.130 = f32[960,320]{1,0:T(8,128)} custom-call(s32[6]{0:T(128)S(1)} %stack.46.flag_ref, bf16[4,120,320]{2,1,0:T(8,128)(2,1)S(1)} %pad_maximum_fusion.own_ref, bf16[4,120,320]{2,1,0:T(8,128)(2,1)S(1)} %collective-permute-done.11.other_ref), custom_call_target="tpu_custom_call" | custom-call | bytes 614400 | tf_op jit(solution)/shard_map/pallas_call | solution.py:577
  (45 shorter events, 4.6 us)
Async XLA Ops:
  0.6 7.4 %copy-start = (bf16[320,320]{1,0:T(8,128)(2,1)S(1)}, bf16[320,320]{1,0:T(8,128)(2,1)}, u32[]{:S(2)}) copy-start(bf16[320,320]{1,0:T(8,128)(2,1)} %param.15) | copy-start | bytes 614404
  2.4 11.3 %collective-permute-start = (bf16[12,32,320]{2,1,0:T(8,128)(2,1)}, bf16[12,32,320]{2,1,0:T(8,128)(2,1)}, u32[]{:S(2)}, u32[]{:S(2)}) collective-permute-start(bf16[12,32,320]{2,1,0:T(8,128)(2,1)} %dynamic-slice_bitcast_fusion), channel_id=1, source_target_pairs={{0,1},{1,0},{2,3},{3,2},{4,5},{5,4},{6,7},{7,6},{8,9},{9,8},{10,11... | collective-permute-start | bytes 737288 | tf_op jit(solution)/shard_map/ppermute | solution.py:616
  6.0 1.6 %copy-start.1 = (bf16[3,3,320,320]{3,2,1,0:T(8,128)(2,1)S(1)}, bf16[3,3,320,320]{3,2,1,0:T(8,128)(2,1)}, u32[]{:S(2)}) copy-start(bf16[3,3,320,320]{3,2,1,0:T(8,128)(2,1)} %w_ref.1) | copy-start | bytes 5529604
  7.6 1.3 %copy-start.8 = (bf16[12,4,32,320]{3,2,1,0:T(8,128)(2,1)S(1)}, bf16[12,4,32,320]{3,2,1,0:T(8,128)(2,1)}, u32[]{:S(2)}) copy-start(bf16[12,4,32,320]{3,2,1,0:T(8,128)(2,1)} %lat_ref.3) | copy-start | bytes 2949124
  7.6 1.3 %copy-start.9 = (s32[4]{0:T(128)S(1)}, s32[4]{0:T(128)}, u32[]{:S(2)}) copy-start(s32[4]{0:T(128)} %len_ref.9) | copy-start | bytes 52
  16.6 6.1 %copy-start.2 = (bf16[12,4,32,320]{3,2,1,0:T(8,128)(2,1)S(1)}, bf16[12,4,32,320]{3,2,1,0:T(8,128)(2,1)}, u32[]{:S(2)}) copy-start(bf16[12,4,32,320]{3,2,1,0:T(8,128)(2,1)} %x_ref.1) | copy-start | bytes 2949124
  16.6 28.0 %all-to-all-start = ((bf16[16,48,640]{2,1,0:T(8,128)(2,1)}), bf16[16,48,640]{2,1,0:T(8,128)(2,1)}, u32[]{:S(2)}, u32[]{:S(2)}) async-start(bf16[16,48,640]{2,1,0:T(8,128)(2,1)} %bitcast.6), calls=%async_computation | async-start | bytes 1966080 | tf_op jit(solution)/shard_map/all_to_all | solution.py:586
  22.7 1.1 copy-start.3
  22.7 1.2 copy-start.4
  22.7 1.2 copy-start.5
  22.7 1.3 %copy-start.6 = (bf16[320,320]{1,0:T(8,128)(2,1)S(1)}, bf16[320,320]{1,0:T(8,128)(2,1)}, u32[]{:S(2)}) copy-start(bf16[320,320]{1,0:T(8,128)(2,1)} %wv_ref.1) | copy-start | bytes 614404
  22.8 1.3 %copy-start.7 = (bf16[320,320]{1,0:T(8,128)(2,1)S(1)}, bf16[320,320]{1,0:T(8,128)(2,1)}, u32[]{:S(2)}) copy-start(bf16[320,320]{1,0:T(8,128)(2,1)} %wo_ref.1) | copy-start | bytes 614404
  24.9 0.9 copy-start.10
  25.8 0.9 copy-start.12
  26.8 0.7 copy-start.13
  27.5 0.7 copy-start.14
  95.8 1.8 %collective-permute-start.1 = (bf16[480,320]{1,0:T(8,128)(2,1)S(1)}, bf16[480,320]{1,0:T(8,128)(2,1)S(1)}, u32[]{:S(2)}, u32[]{:S(2)}) collective-permute-start(bf16[480,320]{1,0:T(8,128)(2,1)S(1)} %get-tuple-element.31), channel_id=1, source_target_pairs={{0,2},{2,0},{1,3},{3,1},{4,6},{6,4},{5,7},{7,5},{8,10},{10,8},{9,1... | collective-permute-start | bytes 921608 | tf_op jit(solution)/shard_map/ppermute | solution.py:556
  95.9 5.3 %copy-start.11 = (bf16[1152,384]{1,0:T(8,128)(2,1)S(1)}, bf16[1152,384]{1,0:T(8,128)(2,1)}, u32[]{:S(2)}) copy-start(bf16[1152,384]{1,0:T(8,128)(2,1)} %copy-done.10) | copy-start | bytes 2654212
  97.7 7.2 %collective-permute-start.2 = (bf16[120,320]{1,0:T(8,128)(2,1)S(1)}, bf16[120,320]{1,0:T(8,128)(2,1)S(1)}, u32[]{:S(2)}, u32[]{:S(2)}) collective-permute-start(bf16[120,320]{1,0:T(8,128)(2,1)S(1)} %get-tuple-element.36), channel_id=1, source_target_pairs={{0,1},{1,0},{4,5},{5,4},{2,3},{3,2},{6,7},{7,6},{8,9},{9,8},{12,13... | collective-permute-start | bytes 230408 | tf_op jit(solution)/shard_map/ppermute | solution.py:560
  98.4 6.5 %collective-permute-start.3 = (bf16[120,320]{1,0:T(8,128)(2,1)S(1)}, bf16[120,320]{1,0:T(8,128)(2,1)S(1)}, u32[]{:S(2)}, u32[]{:S(2)}) collective-permute-start(bf16[120,320]{1,0:T(8,128)(2,1)S(1)} %get-tuple-element.38), channel_id=1, source_target_pairs={{0,4},{1,5},{4,0},{5,1},{2,6},{3,7},{6,2},{7,3},{8,12},{9,13},{12,... | collective-permute-start | bytes 230408 | tf_op jit(solution)/shard_map/ppermute | solution.py:560
  99.1 5.9 %collective-permute-start.4 = (bf16[120,320]{1,0:T(8,128)(2,1)S(1)}, bf16[120,320]{1,0:T(8,128)(2,1)S(1)}, u32[]{:S(2)}, u32[]{:S(2)}) collective-permute-start(bf16[120,320]{1,0:T(8,128)(2,1)S(1)} %get-tuple-element.37), channel_id=1, source_target_pairs={{0,5},{1,4},{4,1},{5,0},{2,7},{3,6},{6,3},{7,2},{8,13},{9,12},{12,... | collective-permute-start | bytes 230408 | tf_op jit(solution)/shard_map/ppermute | solution.py:560
  105.0 5.2 %collective-permute-start.5 = (bf16[120,320]{1,0:T(8,128)(2,1)S(1)}, bf16[120,320]{1,0:T(8,128)(2,1)S(1)}, u32[]{:S(2)}, u32[]{:S(2)}) collective-permute-start(bf16[120,320]{1,0:T(8,128)(2,1)S(1)} %add_convert_fusion.1), channel_id=1, source_target_pairs={{0,8},{8,0},{16,24},{24,16},{1,9},{9,1},{17,25},{25,17},{2,10},{10... | collective-permute-start | bytes 230408 | tf_op jit(solution)/shard_map/ppermute | solution.py:565
  105.8 9.4 %collective-permute-start.6 = (bf16[120,320]{1,0:T(8,128)(2,1)S(1)}, bf16[120,320]{1,0:T(8,128)(2,1)S(1)}, u32[]{:S(2)}, u32[]{:S(2)}) collective-permute-start(bf16[120,320]{1,0:T(8,128)(2,1)S(1)} %add_convert_fusion.1), channel_id=1, source_target_pairs={{0,16},{8,24},{16,0},{24,8},{1,17},{9,25},{17,1},{25,9},{2,18},{10... | collective-permute-start | bytes 230408 | tf_op jit(solution)/shard_map/ppermute | solution.py:565
  107.1 8.0 %collective-permute-start.7 = (bf16[120,320]{1,0:T(8,128)(2,1)S(1)}, bf16[120,320]{1,0:T(8,128)(2,1)S(1)}, u32[]{:S(2)}, u32[]{:S(2)}) collective-permute-start(bf16[120,320]{1,0:T(8,128)(2,1)S(1)} %add_convert_fusion.1), channel_id=1, source_target_pairs={{0,24},{8,16},{16,8},{24,0},{1,25},{9,17},{17,9},{25,1},{2,26},{10... | collective-permute-start | bytes 230408 | tf_op jit(solution)/shard_map/ppermute | solution.py:565
  115.2 4.6 %collective-permute-start.8 = (bf16[120,320]{1,0:T(8,128)(2,1)S(1)}, bf16[120,320]{1,0:T(8,128)(2,1)S(1)}, u32[]{:S(2)}, u32[]{:S(2)}) collective-permute-start(bf16[120,320]{1,0:T(8,128)(2,1)S(1)} %add_convert_fusion), channel_id=1, source_target_pairs={{0,1},{1,0},{4,5},{5,4},{2,3},{3,2},{6,7},{7,6},{8,9},{9,8},{12,13... | collective-permute-start | bytes 230408 | tf_op jit(solution)/shard_map/ppermute | solution.py:567
  116.0 4.6 %collective-permute-start.9 = (bf16[120,320]{1,0:T(8,128)(2,1)S(1)}, bf16[120,320]{1,0:T(8,128)(2,1)S(1)}, u32[]{:S(2)}, u32[]{:S(2)}) collective-permute-start(bf16[120,320]{1,0:T(8,128)(2,1)S(1)} %add_convert_fusion), channel_id=1, source_target_pairs={{0,4},{1,5},{4,0},{5,1},{2,6},{3,7},{6,2},{7,3},{8,12},{9,13},{12,... | collective-permute-start | bytes 230408 | tf_op jit(solution)/shard_map/ppermute | solution.py:567
  116.8 5.5 %collective-permute-start.10 = (bf16[120,320]{1,0:T(8,128)(2,1)S(1)}, bf16[120,320]{1,0:T(8,128)(2,1)S(1)}, u32[]{:S(2)}, u32[]{:S(2)}) collective-permute-start(bf16[120,320]{1,0:T(8,128)(2,1)S(1)} %add_convert_fusion), channel_id=1, source_target_pairs={{0,5},{1,4},{4,1},{5,0},{2,7},{3,6},{6,3},{7,2},{8,13},{9,12},{12,... | collective-permute-start | bytes 230408 | tf_op jit(solution)/shard_map/ppermute | solution.py:567
  122.3 1.8 %collective-permute-start.11 = (bf16[4,120,320]{2,1,0:T(8,128)(2,1)S(1)}, bf16[4,120,320]{2,1,0:T(8,128)(2,1)S(1)}, u32[]{:S(2)}, u32[]{:S(2)}) collective-permute-start(bf16[4,120,320]{2,1,0:T(8,128)(2,1)S(1)} %pad_maximum_fusion.own_ref), channel_id=1, source_target_pairs={{0,2},{2,0},{1,3},{3,1},{4,6},{6,4},{5,7},{7,5},{8,10},{10,8},{9,1... | collective-permute-start | bytes 921608 | tf_op jit(solution)/shard_map/ppermute | solution.py:575
